TPU v7x, 32 devices: a whole 2x2x4 slice. The times are simulated.
32 devices in a mesh: dp: 8 (over y, x, core), seq: 4 (over z).
Axes of the slice: x: 2, y: 2, z: 4, core: 2. Of those that a mesh axis runs over, the one named last changes fastest.
Arguments:
- tokens: bfloat16 [8, 2048, 1024], P('dp', 'seq'), may hold values from -6 to 6
- lengths: int32 [8], P('dp'), may hold values from 1024 to 2048, as said below
- cotangent: bfloat16 [8, 2048, 1024], P('dp', 'seq'), may hold values from -6 to 6
- w_query: bfloat16 [1024, 1024], P('seq'), may hold values from -0.1875 to 0.1875
- w_key: bfloat16 [1024, 512], P('seq'), may hold values from -0.1875 to 0.1875
- w_value: bfloat16 [1024, 512], P('seq'), may hold values from -0.1875 to 0.1875
- w_out: bfloat16 [1024, 1024], P('seq'), may hold values from -0.75 to 0.75
- w_gate: bfloat16 [1024, 4608], P('seq'), may hold values from -0.1875 to 0.1875
- w_up: bfloat16 [1024, 4608], P('seq'), may hold values from -0.1875 to 0.1875
- w_down: bfloat16 [4608, 1024], P('seq'), may hold values from -0.09375 to 0.09375
- gain_attn: bfloat16 [1024], P('seq'), may hold values from 0.5 to 1.5
- gain_ffn: bfloat16 [1024], P('seq'), may hold values from 0.5 to 1.5
- gain_query: bfloat16 [64], P('seq'), may hold values from 1 to 1.59375
- gain_key: bfloat16 [64], P('seq'), may hold values from 1 to 1.59375
Outputs:
- output: bfloat16 [8, 2048, 1024], P('dp', 'seq')
- grad_tokens: float32 [8, 2048, 1024], P('dp', 'seq')
- grad_query: float32 [1024, 1024], P('seq')
- grad_key: float32 [1024, 512], P('seq')
- grad_value: float32 [1024, 512], P('seq')
- grad_out: float32 [1024, 1024], P('seq')
- grad_gate: float32 [1024, 4608], P('seq')
- grad_up: float32 [1024, 4608], P('seq')
- grad_down: float32 [4608, 1024], P('seq')
- grad_gain_attn: float32 [1024], P('seq')
- grad_gain_ffn: float32 [1024], P('seq')
- grad_gain_query: float32 [64], P('seq')
- grad_gain_key: float32 [64], P('seq')
Inputs may be any that keep to these rules, and one draw needn't show every extreme that they name: `lengths`: valid positions of each slot; in every draw some slot is full and some slot has exactly 1024.
All inputs are finite; a program needn't handle non-finite values.
Results may differ from a plain program's by a relative error of at most 0.022.
Values may be sent and summed in bfloat16 or wider, within the bound.
No kernel may reach another device: no remote copies, remote signals or barrier semaphores. Data moves between devices by JAX's collectives and lax.ppermute only.
A program may use at most 320 MiB of HBM per device.

v0:
```python
import jax
import jax.numpy as jnp
from jax import lax
from jax.sharding import PartitionSpec as P

H = 16
KV = 8
HD = 64


EPS = 1e-05
rope_base = 1000000.0
negative = -1e30


def rms_scale(values):
    return lax.rsqrt(jnp.mean(values * values, axis=-1, keepdims=True) + EPS)


def norm_back(grads, normed, scale):
    return scale * (grads - normed * jnp.mean(grads * normed, axis=-1, keepdims=True))


def tables(positions, width):
    half = width // 2
    freq = rope_base ** (-(jnp.arange(half, dtype=jnp.float32) * 2.0 / width))
    angle = positions.astype(jnp.float32)[:, None] * freq[None, :]
    angle = jnp.concatenate([angle, angle], axis=1)
    return (jnp.cos(angle)[:, None, :], jnp.sin(angle)[:, None, :])


def rotate_half(values):
    half = values.shape[-1] // 2
    return jnp.concatenate([-values[..., half:], values[..., :half]], axis=-1)


def rotary(values, cosine, sine):
    return values * cosine + rotate_half(values) * sine


def rotary_back(grads, cosine, sine):
    return grads * cosine - rotate_half(grads * sine)


def outer(left, right):
    return lax.dot_general(
        left, right, (((0,), (0,)), ((), ())), preferred_element_type=jnp.float32
    )


def through(grads, weight):
    return lax.dot_general(
        grads, weight, (((1,), (1,)), ((), ())), preferred_element_type=jnp.float32
    )


def attend_forward(queries, keys, values, length, block):
    full_len = queries.shape[0]
    kv_local = keys.shape[1] // HD
    group = H // KV
    heads_local = kv_local * group
    scale = HD ** (-0.5)
    keys_split = keys.reshape(full_len, kv_local, HD)
    values_split = values.reshape(full_len, kv_local, HD)
    mixed_parts = []
    lse_parts = []
    for index in range(full_len // block):
        start = index * block
        finish = start + block
        q_block = queries[start:finish].reshape(block, kv_local, group, HD)
        key_part = keys_split[:finish]
        value_part = values_split[:finish]
        key_pos = jnp.arange(finish)
        row_pos = start + jnp.arange(block)

        def compute():
            raw = jnp.einsum(
                "bkgd,tkd->kgbt", q_block, key_part, preferred_element_type=jnp.float32
            )
            mask = (key_pos[None, :] <= row_pos[:, None]) & (key_pos[None, :] < length)
            scores = jnp.where(mask, raw * scale, negative)
            highest_score = jnp.max(scores, axis=-1, keepdims=True)
            powers = jnp.exp(scores - highest_score)
            total = jnp.sum(powers, axis=-1, keepdims=True)
            probs = (powers / total).astype(jnp.bfloat16)
            mixed = jnp.einsum(
                "kgbt,tkd->bkgd", probs, value_part, preferred_element_type=jnp.float32
            )
            return (
                mixed.reshape(block, heads_local * HD).astype(jnp.bfloat16),
                (highest_score + jnp.log(total))[..., 0],
            )

        mixed_block, lse_block = compute()
        mixed_parts.append(mixed_block)
        lse_parts.append(lse_block)
    return (jnp.concatenate(mixed_parts, axis=0), jnp.stack(lse_parts))


def attend_backward(queries, keys, values, grads, log_total, length, block):
    full_len = queries.shape[0]
    kv_local = keys.shape[1] // HD
    group = H // KV
    heads_local = kv_local * group
    scale = HD ** (-0.5)
    keys_split = keys.reshape(full_len, kv_local, HD)
    values_split = values.reshape(full_len, kv_local, HD)
    grad_k = jnp.zeros((full_len, kv_local, HD), jnp.float32)
    grad_v = jnp.zeros((full_len, kv_local, HD), jnp.float32)
    dq_parts = []
    for index in range(full_len // block):
        start = index * block
        finish = start + block
        q_block = queries[start:finish].reshape(block, kv_local, group, HD)
        g_block = grads[start:finish].reshape(block, kv_local, group, HD)
        lse_block = log_total[index]
        key_part = keys_split[:finish]
        value_part = values_split[:finish]
        key_pos = jnp.arange(finish)
        row_pos = start + jnp.arange(block)

        def compute():
            raw = jnp.einsum(
                "bkgd,tkd->kgbt", q_block, key_part, preferred_element_type=jnp.float32
            )
            mask = (key_pos[None, :] <= row_pos[:, None]) & (key_pos[None, :] < length)
            scores = jnp.where(mask, raw * scale, negative)
            probs = jnp.exp(scores - lse_block[..., None])
            probs_low = probs.astype(jnp.bfloat16)
            grad_probs = jnp.einsum(
                "bkgd,tkd->kgbt", g_block, value_part, preferred_element_type=jnp.float32
            )
            delta = jnp.sum(probs * grad_probs, axis=-1, keepdims=True)
            grad_scores = (probs * (grad_probs - delta) * scale).astype(jnp.bfloat16)
            grad_q = jnp.einsum(
                "kgbt,tkd->bkgd", grad_scores, key_part, preferred_element_type=jnp.float32
            )
            part_k = jnp.einsum(
                "kgbt,bkgd->tkd", grad_scores, q_block, preferred_element_type=jnp.float32
            )
            part_v = jnp.einsum(
                "kgbt,bkgd->tkd", probs_low, g_block, preferred_element_type=jnp.float32
            )
            return (grad_q.reshape(block, heads_local * HD).astype(jnp.bfloat16), part_k, part_v)

        dq_block, part_k, part_v = compute()
        padding = ((0, full_len - finish), (0, 0), (0, 0))
        grad_k = grad_k + jnp.pad(part_k, padding)
        grad_v = grad_v + jnp.pad(part_v, padding)
        dq_parts.append(dq_block)
    return (
        jnp.concatenate(dq_parts, axis=0),
        grad_k.reshape(full_len, kv_local * HD).astype(jnp.bfloat16),
        grad_v.reshape(full_len, kv_local * HD).astype(jnp.bfloat16),
    )


def per_device(
    tokens,
    lengths,
    cotangent,
    w_query,
    w_key,
    w_value,
    w_out,
    w_gate,
    w_up,
    w_down,
    gain_attn,
    gain_ffn,
    gain_query,
    gain_key,
):
    slots, local, width = tokens.shape
    row_count = slots * local
    weights = (
        w_query,
        w_key,
        w_value,
        w_out,
        w_gate,
        w_up,
        w_down,
        gain_attn,
        gain_ffn,
        gain_query,
        gain_key,
    )
    full = (
        lax.all_gather(weights[0], "seq", axis=0, tiled=True),
        lax.all_gather(weights[1], "seq", axis=0, tiled=True),
        lax.all_gather(weights[2], "seq", axis=0, tiled=True),
        lax.all_gather(weights[3], "seq", axis=0, tiled=True),
        lax.all_gather(weights[4], "seq", axis=0, tiled=True),
        lax.all_gather(weights[5], "seq", axis=0, tiled=True),
        lax.all_gather(weights[6], "seq", axis=0, tiled=True),
        lax.all_gather(weights[7], "seq", axis=0, tiled=True),
        lax.all_gather(weights[8], "seq", axis=0, tiled=True),
        lax.all_gather(weights[9], "seq", axis=0, tiled=True),
        lax.all_gather(weights[10], "seq", axis=0, tiled=True),
    )
    full_query, full_key, full_value, full_out, full_gate, full_up, full_down = full[:7]
    gain1 = full[7].astype(jnp.float32)
    gain2 = full[8].astype(jnp.float32)
    gainq = full[9].astype(jnp.float32)
    gaink = full[10].astype(jnp.float32)
    positions = lax.axis_index("seq") * local + jnp.arange(local, dtype=jnp.int32)
    cosine, sine = tables(positions, HD)
    valid = (positions[None, :] < lengths[:, None]).reshape(row_count, 1)
    inputs = tokens.astype(jnp.float32).reshape(row_count, width)
    scale1 = rms_scale(inputs)
    normed1 = inputs * scale1
    hidden1 = (normed1 * gain1).astype(jnp.bfloat16)
    query_raw = jnp.dot(hidden1, full_query, preferred_element_type=jnp.float32).reshape(
        slots, local, H, HD
    )
    key_raw = jnp.dot(hidden1, full_key, preferred_element_type=jnp.float32).reshape(
        slots, local, KV, HD
    )
    value_send = (
        jnp.dot(hidden1, full_value, preferred_element_type=jnp.float32)
        .astype(jnp.bfloat16)
        .reshape(slots, local, KV * HD)
    )
    q_scale = rms_scale(query_raw)
    q_hat = query_raw * q_scale
    k_scale = rms_scale(key_raw)
    k_hat = key_raw * k_scale
    query_send = (
        rotary(q_hat * gainq, cosine, sine).astype(jnp.bfloat16).reshape(slots, local, H * HD)
    )
    key_send = (
        rotary(k_hat * gaink, cosine, sine).astype(jnp.bfloat16).reshape(slots, local, KV * HD)
    )
    heads_q, heads_k, heads_v = (
        lax.all_to_all(query_send, "seq", split_axis=2, concat_axis=1, tiled=True),
        lax.all_to_all(key_send, "seq", split_axis=2, concat_axis=1, tiled=True),
        lax.all_to_all(value_send, "seq", split_axis=2, concat_axis=1, tiled=True),
    )
    full_len = heads_q.shape[1]
    block = min(512, full_len)
    slot = 0
    mixed_slot, lse_slot = attend_forward(
        heads_q[slot], heads_k[slot], heads_v[slot], lengths[slot], block
    )
    mixed_list = [mixed_slot]
    lse_list = [lse_slot]
    mixed_heads = jnp.stack(mixed_list)
    mixed_rows = lax.all_to_all(
        mixed_heads, "seq", split_axis=1, concat_axis=2, tiled=True
    ).reshape(row_count, H * HD)
    resid = inputs + jnp.dot(mixed_rows, full_out, preferred_element_type=jnp.float32)
    scale2 = rms_scale(resid)
    normed2 = resid * scale2
    hidden2 = (normed2 * gain2).astype(jnp.bfloat16)
    gate = jnp.dot(hidden2, full_gate, preferred_element_type=jnp.float32)
    up_proj = jnp.dot(hidden2, full_up, preferred_element_type=jnp.float32)
    sigma = jax.nn.sigmoid(gate)
    activated = gate * sigma
    inner = (activated * up_proj).astype(jnp.bfloat16)
    result = resid + jnp.dot(inner, full_down, preferred_element_type=jnp.float32)
    output = jnp.where(valid, result, 0.0).astype(jnp.bfloat16).reshape(slots, local, width)
    grad_y = jnp.where(valid, cotangent.astype(jnp.float32).reshape(row_count, width), 0.0)
    grad_y_low = grad_y.astype(jnp.bfloat16)
    term_down = outer(inner, grad_y_low)
    grad_inner = through(grad_y_low, full_down)
    grad_gate_act = (grad_inner * up_proj * sigma * (1.0 + gate * (1.0 - sigma))).astype(
        jnp.bfloat16
    )
    grad_up_act = (grad_inner * activated).astype(jnp.bfloat16)
    term_gate = outer(hidden2, grad_gate_act)
    term_up = outer(hidden2, grad_up_act)
    grad_hidden2 = through(grad_gate_act, full_gate) + through(grad_up_act, full_up)
    term_gain2 = jnp.sum(grad_hidden2 * normed2, axis=0)
    grad_resid = grad_y + norm_back(grad_hidden2 * gain2, normed2, scale2)
    grad_branch = grad_resid.astype(jnp.bfloat16)
    term_out = outer(mixed_rows, grad_branch)
    grad_mixed = through(grad_branch, full_out).astype(jnp.bfloat16).reshape(slots, local, H * HD)
    grad_heads = lax.all_to_all(grad_mixed, "seq", split_axis=2, concat_axis=1, tiled=True)
    slot = 0
    grad_q, grad_k, grad_v = attend_backward(
        heads_q[slot],
        heads_k[slot],
        heads_v[slot],
        grad_heads[slot],
        lse_list[slot],
        lengths[slot],
        block,
    )
    dq_list = [grad_q]
    dk_list = [grad_k]
    dv_list = [grad_v]
    back_q, back_k, back_v = (
        lax.all_to_all(jnp.stack(dq_list), "seq", split_axis=1, concat_axis=2, tiled=True),
        lax.all_to_all(jnp.stack(dk_list), "seq", split_axis=1, concat_axis=2, tiled=True),
        lax.all_to_all(jnp.stack(dv_list), "seq", split_axis=1, concat_axis=2, tiled=True),
    )
    grad_qhat = rotary_back(back_q.astype(jnp.float32).reshape(slots, local, H, HD), cosine, sine)
    term_gainq = jnp.sum(grad_qhat * q_hat, axis=(0, 1, 2))
    grad_qraw = (
        norm_back(grad_qhat * gainq, q_hat, q_scale).reshape(row_count, H * HD).astype(jnp.bfloat16)
    )
    grad_khat = rotary_back(back_k.astype(jnp.float32).reshape(slots, local, KV, HD), cosine, sine)
    term_gaink = jnp.sum(grad_khat * k_hat, axis=(0, 1, 2))
    grad_kraw = (
        norm_back(grad_khat * gaink, k_hat, k_scale)
        .reshape(row_count, KV * HD)
        .astype(jnp.bfloat16)
    )
    grad_vraw = back_v.reshape(row_count, KV * HD)
    term_query = outer(hidden1, grad_qraw)
    term_key = outer(hidden1, grad_kraw)
    term_value = outer(hidden1, grad_vraw)
    grad_hidden1 = (
        through(grad_qraw, full_query)
        + through(grad_kraw, full_key)
        + through(grad_vraw, full_value)
    )
    term_gain1 = jnp.sum(grad_hidden1 * normed1, axis=0)
    grad_tokens = (grad_resid + norm_back(grad_hidden1 * gain1, normed1, scale1)).reshape(
        slots, local, width
    )
    shards = (
        lax.psum_scatter(
            term_query.astype(jnp.bfloat16), "seq", scatter_dimension=0, tiled=True
        ).astype(jnp.float32),
        lax.psum_scatter(
            term_key.astype(jnp.bfloat16), "seq", scatter_dimension=0, tiled=True
        ).astype(jnp.float32),
        lax.psum_scatter(
            term_value.astype(jnp.bfloat16), "seq", scatter_dimension=0, tiled=True
        ).astype(jnp.float32),
        lax.psum_scatter(
            term_out.astype(jnp.bfloat16), "seq", scatter_dimension=0, tiled=True
        ).astype(jnp.float32),
        lax.psum_scatter(
            term_gate.astype(jnp.bfloat16), "seq", scatter_dimension=0, tiled=True
        ).astype(jnp.float32),
        lax.psum_scatter(
            term_up.astype(jnp.bfloat16), "seq", scatter_dimension=0, tiled=True
        ).astype(jnp.float32),
        lax.psum_scatter(
            term_down.astype(jnp.bfloat16), "seq", scatter_dimension=0, tiled=True
        ).astype(jnp.float32),
        lax.psum_scatter(
            term_gain1.astype(jnp.bfloat16), "seq", scatter_dimension=0, tiled=True
        ).astype(jnp.float32),
        lax.psum_scatter(
            term_gain2.astype(jnp.bfloat16), "seq", scatter_dimension=0, tiled=True
        ).astype(jnp.float32),
        lax.psum_scatter(
            term_gainq.astype(jnp.bfloat16), "seq", scatter_dimension=0, tiled=True
        ).astype(jnp.float32),
        lax.psum_scatter(
            term_gaink.astype(jnp.bfloat16), "seq", scatter_dimension=0, tiled=True
        ).astype(jnp.float32),
    )
    shards = (
        lax.psum(shards[0].astype(jnp.bfloat16), "dp").astype(jnp.float32),
        lax.psum(shards[1].astype(jnp.bfloat16), "dp").astype(jnp.float32),
        lax.psum(shards[2].astype(jnp.bfloat16), "dp").astype(jnp.float32),
        lax.psum(shards[3].astype(jnp.bfloat16), "dp").astype(jnp.float32),
        lax.psum(shards[4].astype(jnp.bfloat16), "dp").astype(jnp.float32),
        lax.psum(shards[5].astype(jnp.bfloat16), "dp").astype(jnp.float32),
        lax.psum(shards[6].astype(jnp.bfloat16), "dp").astype(jnp.float32),
        lax.psum(shards[7].astype(jnp.bfloat16), "dp").astype(jnp.float32),
        lax.psum(shards[8].astype(jnp.bfloat16), "dp").astype(jnp.float32),
        lax.psum(shards[9].astype(jnp.bfloat16), "dp").astype(jnp.float32),
        lax.psum(shards[10].astype(jnp.bfloat16), "dp").astype(jnp.float32),
    )
    (
        grad_query,
        grad_key,
        grad_value,
        grad_out,
        grad_gate,
        grad_up,
        grad_down,
        grad_gain_attn,
        grad_gain_ffn,
        grad_gain_query,
        grad_gain_key,
    ) = shards
    return (
        output,
        grad_tokens,
        grad_query,
        grad_key,
        grad_value,
        grad_out,
        grad_gate,
        grad_up,
        grad_down,
        grad_gain_attn,
        grad_gain_ffn,
        grad_gain_query,
        grad_gain_key,
    )


def solution(mesh):
    placed = (
        P("dp", "seq", None),
        P("dp"),
        P("dp", "seq", None),
        P("seq", None),
        P("seq", None),
        P("seq", None),
        P("seq", None),
        P("seq", None),
        P("seq", None),
        P("seq", None),
        P("seq"),
        P("seq"),
        P("seq"),
        P("seq"),
    )
    return jax.shard_map(
        per_device,
        mesh=mesh,
        in_specs=placed,
        out_specs=(
            P("dp", "seq", None),
            P("dp", "seq", None),
            P("seq", None),
            P("seq", None),
            P("seq", None),
            P("seq", None),
            P("seq", None),
            P("seq", None),
            P("seq", None),
            P("seq"),
            P("seq"),
            P("seq"),
            P("seq"),
        ),
        check_vma=False,
    )
```

profile of v0, /device:TPU:0, one launch (start us, length us, event | category | flops | bytes accessed | tf_op | source)
XLA Modules:
  0.0 1823.5 jit_solution(18416439332140908419)
XLA Ops:
  13.8 13.6 all-reduce.15
  27.4 7.7 all-gather
  50.7 4.4 all-to-all-start.1
  55.1 26.0 %all-gather.10.cloned.1.call-done = bf16[1024,512]{1,0:T(8,128)(2,1)} async-done(((bf16[256,512]{1,0:T(8,128)(2,1)}), bf16[1024,512]{1,0:T(8,128)(2,1)}) %all-gather.10.cloned.1.call-update) | async-done | bytes 1048592 | tf_op jit(solution)/shard_map/all_gather | solution.py:192
  89.0 38.5 %all-gather.14.cloned.1.call-done = bf16[1024,1024]{1,0:T(8,128)(2,1)} async-done(((bf16[256,1024]{1,0:T(8,128)(2,1)}), bf16[1024,1024]{1,0:T(8,128)(2,1)}) %all-gather.14.cloned.1.call-update) | async-done | bytes 2097168 | tf_op jit(solution)/shard_map/all_gather | solution.py:190
  127.4 4.2 fusion.168
  135.8 4.5 all-to-all-start
  148.7 6.1 fusion.118
  156.6 7.0 reduce.8
  165.7 4.4 all-to-all-done
  170.1 4.4 all-to-all-start.2
  195.2 11.7 all-to-all-done.2
  210.0 9.2 fusion.176
  219.2 8.1 fusion.7
  227.4 7.8 fusion.107
  255.2 11.7 copy.411
  266.9 10.6 reduce.11
  279.2 4.3 all-to-all-start.3
  283.5 40.6 %all-gather.1 = bf16[4,1,256]{2,1,0:T(2,128)(2,1)S(1)} all-gather(bf16[1,1,256]{2,1,0:T(2,128)(2,1)S(1)} %reshape.861), channel_id=1, replica_groups=mesh['dp'=8,'seq'=4] {'seq'}, dimensions={0}, use_global_device_ids=true | all-gather | bytes 2560 | tf_op jit(solution)/shard_map/all_gather | solution.py:198
  324.6 16.1 all-to-all-done.3
  350.5 39.8 %all-gather.18.cloned.1.call-done = bf16[1024,4608]{1,0:T(8,128)(2,1)} async-done(((bf16[256,4608]{1,0:T(8,128)(2,1)}), bf16[1024,4608]{1,0:T(8,128)(2,1)}) %all-gather.18.cloned.1.call-update) | async-done | bytes 9437200 | tf_op jit(solution)/shard_map/all_gather | solution.py:194
  390.3 11.0 fusion.180
  401.3 155.3 %all-gather.20.cloned.1.call-done = bf16[1024,4608]{1,0:T(8,128)(2,1)} async-done(((bf16[256,4608]{1,0:T(8,128)(2,1)}), bf16[1024,4608]{1,0:T(8,128)(2,1)}) %all-gather.20.cloned.1.call-update) | async-done | bytes 9437200 | tf_op jit(solution)/shard_map/all_gather | solution.py:195
  556.7 11.0 fusion.181
  567.7 155.5 %all-gather.22.cloned.1.call-done = bf16[4608,1024]{1,0:T(8,128)(2,1)} async-done(((bf16[1152,1024]{1,0:T(8,128)(2,1)}), bf16[4608,1024]{1,0:T(8,128)(2,1)}) %all-gather.22.cloned.1.call-update) | async-done | bytes 9437200 | tf_op jit(solution)/shard_map/all_gather | solution.py:196
  723.2 18.1 multiply_convert_fusion
  741.3 9.2 fusion.182
  750.5 8.9 multiply_reduce_fusion
  766.6 8.2 reduce.12
  788.3 33.3 %all-to-all-done.4 = bf16[4,2,65536]{2,1,0:T(2,128)(2,1)S(1)} async-done(((bf16[4,2,65536]{2,1,0:T(2,128)(2,1)}), bf16[4,2,65536]{2,1,0:T(2,128)(2,1)S(1)}, u32[]{:S(2)}, u32[]{:S(2)}) %all-to-all-start.4) | async-done | bytes 1048608 | tf_op jit(solution)/shard_map/all_to_all | solution.py:279
  827.6 8.1 fusion.126
  835.7 6.3 fusion.136
  842.1 4.6 fusion.141
  846.7 8.4 fusion.111
  855.2 19.0 %fusion.58 = f32[1536,2,64]{0,2,1:T(8,128)} fusion(bf16[512,2,2,64]{0,3,2,1:T(8,128)(2,1)S(1)} %bitcast.592, f32[2,1536,512,2]{2,1,3,0:T(8,128)} %fusion.136, f32[2,2,512,1536]{2,3,1,0:T(8,128)} %copy-done, f32[2,2,512]{2,1,0:T(2,128)S(1)} %log_add_fusion.1), kind=kOutput, calls=%fused_computation.88 | convolution fusion | flops 424676864 | bytes 26222592 | tf_op jit(solution)/shard_map/kgbt,bkgd->tkd/dot_general | solution.py:138
  874.2 15.4 fusion.96
  889.6 22.8 %fusion.70 = bf16[2048,2,64]{0,2,1:T(8,128)(2,1)S(1)} fusion(bf16[512,2,2,64]{0,3,2,1:T(8,128)(2,1)S(1)} %bitcast.588, f32[2,2048,512,2]{2,1,3,0:T(8,128)} %fusion.126, f32[2,2,512,2048]{2,3,1,0:T(8,128)} %get-tuple-element.68, f32[2,2,512]{2,1,0:T(2,128)S(1)} %copy-done.92, f32[1536,2,64]{0,2,1:T(8,128)} %fusion.58, f32[1024,2,64]{0,2,1:T(8,128)S(1)} %fusion.96, ...), kind=kOutput, calls=%fused_computation.94 | convolution fusion | flops 567283712 | bytes 35921920 | tf_op jit(solution)/shard_map/kgbt,bkgd->tkd/dot_general | solution.py:138
  913.2 11.5 reduce.15
  925.6 5.6 all-to-all-start.6
  931.2 4.8 fusion.97
  936.0 6.6 fusion.55
  942.6 8.5 fusion.67
  951.9 11.5 reduce.13
  964.3 22.7 %fusion.100 = bf16[2,64,2,512]{3,1,2,0:T(8,128)(2,1)} fusion(f32[2,1536,512,2]{2,1,3,0:T(8,128)} %fusion.136, f32[2,2,512,1536]{2,3,1,0:T(8,128)} %copy-done, f32[2,2,512]{2,1,0:T(2,128)S(1)} %log_add_fusion.1, bf16[1536,2,64,1]{0,2,1,3:T(8,128)(2,1)S(1)} %copy-done.65), kind=kOutput, calls=%fused_computation.149 | convolution fusion | flops 424807936 | bytes 25829376 | tf_op jit(solution)/shard_map/kgbt,tkd->bkgd/dot_general | solution.py:135
  987.0 23.1 %fusion.101 = bf16[2,64,2,512]{3,1,2,0:T(8,128)(2,1)} fusion(f32[2,2048,512,2]{2,1,3,0:T(8,128)} %fusion.126, f32[2,2,512,2048]{2,3,1,0:T(8,128)} %get-tuple-element.68, f32[2,2,512]{2,1,0:T(2,128)S(1)} %copy-done.92, bf16[2048,2,64,1]{0,2,1,3:T(8,128)(2,1)S(1)} %copy-done.62), kind=kOutput, calls=%fused_computation.150 | convolution fusion | flops 566366208 | bytes 34349056 | tf_op jit(solution)/shard_map/kgbt,tkd->bkgd/dot_general | solution.py:135
  1010.1 5.2 all-to-all-start.7
  1021.8 15.3 fusion.103
  1037.5 9.1 fusion.102
  1047.8 13.1 copy.410
  1060.9 11.6 reduce.14
  1074.2 5.1 all-to-all-start.5
  1089.9 8.8 all-to-all-done.5
  1128.0 9.8 convolution_convert_fusion.2
  1138.0 10.1 convolution_convert_fusion.1
  1149.3 10.0 convolution_convert_fusion
  1159.5 11.5 reduce-scatter.8.cloned.1.call-done
  1171.0 162.9 %reduce-scatter.16.cloned.1.call-done = bf16[256,4608]{1,0:T(8,128)(2,1)} async-done(((bf16[1024,4608]{1,0:T(8,128)(2,1)}), bf16[256,4608]{1,0:T(8,128)(2,1)}) %reduce-scatter.16.cloned.1.call-update) | async-done | bytes 2359312 | tf_op jit(solution)/shard_map/reduce_scatter | solution.py:336
  1333.8 164.5 %reduce-scatter.18.cloned.1.call-done = bf16[256,4608]{1,0:T(8,128)(2,1)} async-done(((bf16[1024,4608]{1,0:T(8,128)(2,1)}), bf16[256,4608]{1,0:T(8,128)(2,1)}) %reduce-scatter.18.cloned.1.call-update) | async-done | bytes 2359312 | tf_op jit(solution)/shard_map/reduce_scatter | solution.py:339
  1498.3 164.4 %reduce-scatter.20.cloned.1.call-done = bf16[1152,1024]{1,0:T(8,128)(2,1)} async-done(((bf16[4608,1024]{1,0:T(8,128)(2,1)}), bf16[1152,1024]{1,0:T(8,128)(2,1)}) %reduce-scatter.20.cloned.1.call-update) | async-done | bytes 2359312 | tf_op jit(solution)/shard_map/reduce_scatter | solution.py:342
  1678.8 10.0 fusion.93
  1698.7 4.5 fusion.86
  1709.1 11.4 all-reduce.14
  1720.8 12.4 all-reduce.12
  1738.8 61.3 %all-reduce.18.cloned.1.call-done = (bf16[256,1024]{1,0:T(8,128)(2,1)}, bf16[256,512]{1,0:T(8,128)(2,1)}, bf16[256,512]{1,0:T(8,128)(2,1)}, bf16[256,1024]{1,0:T...) async-done(((bf16[256,1024]{1,0:T(8,128)(2,1)}, bf16[256,512]{1,0:T(8,128)(2,1)}, bf16[256,512]{1,0:T(8,128)(2,1)}, ...) | async-done | bytes 8650768 | tf_op jit(solution)/shard_map/psum | solution.py:359
  (463 shorter events, 233.2 us)
Async XLA Ops:
  7.2 33.8 %all-gather.12.cloned.1.call-start = ((), (), s32[]{:S(2)}) async-start(), calls=%async_computation.16 | async-start | bytes 1310720 | tf_op jit(solution)/shard_map/all_gather | solution.py:191
  7.9 19.4 %copy-start.111 = (bf16[256]{0:T(256)(128)(2,1)S(1)}, bf16[256]{0:T(256)(128)(2,1)}, u32[]{:S(2)}) copy-start(bf16[256]{0:T(256)(128)(2,1)} %param.24) | copy-start | bytes 1540
  8.0 27.1 %copy-start.18 = (bf16[1,512,1024]{2,1,0:T(8,128)(2,1)S(1)}, bf16[1,512,1024]{2,1,0:T(8,128)(2,1)}, u32[]{:S(2)}) copy-start(bf16[1,512,1024]{2,1,0:T(8,128)(2,1)} %param.14) | copy-start | bytes 3145732
  8.0 73.1 %all-gather.10.cloned.1.call-start = ((), (), s32[]{:S(2)}) async-start(), calls=%async_computation.15 | async-start | bytes 1310720 | tf_op jit(solution)/shard_map/all_gather | solution.py:192
  8.7 118.7 %all-gather.14.cloned.1.call-start = ((), (), s32[]{:S(2)}) async-start(), calls=%async_computation.17 | async-start | bytes 2621440 | tf_op jit(solution)/shard_map/all_gather | solution.py:190
  9.5 337.4 %all-gather.16.cloned.1.call-start = ((), (), s32[]{:S(2)}) async-start(), calls=%async_computation.18 | async-start | bytes 2621440 | tf_op jit(solution)/shard_map/all_gather | solution.py:193
  10.0 380.3 %all-gather.18.cloned.1.call-start = ((), (), s32[]{:S(2)}) async-start(), calls=%async_computation.19 | async-start | bytes 11796480 | tf_op jit(solution)/shard_map/all_gather | solution.py:194
  10.6 546.0 %all-gather.20.cloned.1.call-start = ((), (), s32[]{:S(2)}) async-start(), calls=%async_computation.20 | async-start | bytes 11796480 | tf_op jit(solution)/shard_map/all_gather | solution.py:195
  11.2 712.0 %all-gather.22.cloned.1.call-start = ((), (), s32[]{:S(2)}) async-start(), calls=%async_computation.21 | async-start | bytes 11796480 | tf_op jit(solution)/shard_map/all_gather | solution.py:196
  27.4 106.5 %copy-start.101 = (f32[64]{0:T(128)}, f32[64]{0:T(128)S(1)}, u32[]{:S(2)}) copy-start(f32[64]{0:T(128)S(1)} %convert_element_type.411) | copy-start | bytes 772
  35.1 92.3 %copy-start.83 = (f32[4,1,256]{2,1,0:T(1,128)}, f32[4,1,256]{2,1,0:T(1,128)S(1)}, u32[]{:S(2)}) copy-start(f32[4,1,256]{2,1,0:T(1,128)S(1)} %convert_element_type.519) | copy-start | bytes 12292
  35.4 92.0 %copy-start.98 = (f32[512]{0:T(512)}, f32[512]{0:T(512)S(1)}, u32[]{:S(2)}) copy-start(f32[512]{0:T(512)S(1)} %add_rsqrt_fusion.3) | copy-start | bytes 6148
  35.8 8.3 copy-start.31
  35.8 8.3 copy-start.34
  40.2 108.5 %copy-start.81 = (f32[1024]{0:T(1024)}, f32[1024]{0:T(1024)S(1)}, u32[]{:S(2)}) copy-start(f32[1024]{0:T(1024)S(1)} %mul.681) | copy-start | bytes 12292
  44.1 37.0 %copy-start.19 = (bf16[1,512,1024]{2,1,0:T(8,128)(2,1)S(1)}, bf16[1,512,1024]{2,1,0:T(8,128)(2,1)}, u32[]{:S(2)}) copy-start(bf16[1,512,1024]{2,1,0:T(8,128)(2,1)} %param.14) | copy-start | bytes 3145732
  50.7 85.1 %all-to-all-start.1 = ((bf16[4,2,32768]{2,1,0:T(2,128)(2,1)}), bf16[4,2,32768]{2,1,0:T(2,128)(2,1)}, u32[]{:S(2)}, u32[]{:S(2)}) async-start(bf16[4,2,32768]{2,1,0:T(2,128)(2,1)} %reshape.897), calls=%async_computation.1 | async-start | bytes 1048576 | tf_op jit(solution)/shard_map/all_to_all | solution.py:237
  133.6 8.6 copy-start.4
  133.9 10.3 copy-start.58
  135.8 34.3 %all-to-all-start = ((bf16[4,2,32768]{2,1,0:T(2,128)(2,1)}), bf16[4,2,32768]{2,1,0:T(2,128)(2,1)}, u32[]{:S(2)}, u32[]{:S(2)}) async-start(bf16[4,2,32768]{2,1,0:T(2,128)(2,1)} %reshape.899), calls=%async_computation | async-start | bytes 1048576 | tf_op jit(solution)/shard_map/all_to_all | solution.py:238
  170.1 36.8 %all-to-all-start.2 = ((bf16[4,2,65536]{2,1,0:T(2,128)(2,1)}), bf16[4,2,65536]{2,1,0:T(2,128)(2,1)}, u32[]{:S(2)}, u32[]{:S(2)}) async-start(bf16[4,2,65536]{2,1,0:T(2,128)(2,1)} %reshape.895), calls=%async_computation.2 | async-start | bytes 2097152 | tf_op jit(solution)/shard_map/all_to_all | solution.py:236
  210.0 9.2 copy-start.71
  210.0 25.4 %copy-start.75 = (bf16[1,1,512,256]{2,3,1,0:T(8,128)(2,1)}, bf16[1,1,512,256]{2,3,1,0:T(8,128)(2,1)S(1)}, u32[]{:S(2)}) copy-start(bf16[1,1,512,256]{2,3,1,0:T(8,128)(2,1)S(1)} %get-tuple-element.59) | copy-start | bytes 786436
  210.0 35.4 %copy-start.73 = (bf16[1,1,512,256]{2,3,1,0:T(8,128)(2,1)}, bf16[1,1,512,256]{2,3,1,0:T(8,128)(2,1)S(1)}, u32[]{:S(2)}) copy-start(bf16[1,1,512,256]{2,3,1,0:T(8,128)(2,1)S(1)} %get-tuple-element.60) | copy-start | bytes 786436
  210.0 42.0 %copy-start.77 = (bf16[1,1,512,256]{2,3,1,0:T(8,128)(2,1)}, bf16[1,1,512,256]{2,3,1,0:T(8,128)(2,1)S(1)}, u32[]{:S(2)}) copy-start(bf16[1,1,512,256]{2,3,1,0:T(8,128)(2,1)S(1)} %get-tuple-element.57) | copy-start | bytes 786436
  219.2 8.2 copy-start.41
  227.4 8.0 copy-start.55
  266.9 16.5 copy-start.112
  279.2 61.5 %all-to-all-start.3 = ((bf16[4,2,65536]{2,1,0:T(2,128)(2,1)}), bf16[4,2,65536]{2,1,0:T(2,128)(2,1)}, u32[]{:S(2)}, u32[]{:S(2)}) async-start(bf16[4,2,65536]{2,1,0:T(2,128)(2,1)} %reshape.901), calls=%async_computation.3 | async-start | bytes 2097152 | tf_op jit(solution)/shard_map/all_to_all | solution.py:249
  324.6 22.3 %copy-start.20 = (bf16[1,512,1024]{2,1,0:T(8,128)(2,1)S(1)}, bf16[1,512,1024]{2,1,0:T(8,128)(2,1)}, u32[]{:S(2)}) copy-start(bf16[1,512,1024]{2,1,0:T(8,128)(2,1)} %param.14) | copy-start | bytes 3145732
  350.2 409.2 %copy-start.10 = (f32[512,1024]{1,0:T(8,128)}, f32[512,1024]{1,0:T(8,128)S(1)}, u32[]{:S(2)}) copy-start(f32[512,1024]{1,0:T(8,128)S(1)} %get-tuple-element.76) | copy-start | bytes 6291460
  350.4 206.2 %copy-start.48 = (bf16[512,1024]{1,0:T(8,128)(2,1)}, bf16[512,1024]{1,0:T(8,128)(2,1)S(1)}, u32[]{:S(2)}) copy-start(bf16[512,1024]{1,0:T(8,128)(2,1)S(1)} %multiply_convert_fusion.4) | copy-start | bytes 3145732
  741.3 9.2 copy-start.113
  750.5 8.9 copy-start.52
  750.5 8.9 copy-start.107
  766.6 17.8 copy-start.28
  776.8 44.9 %all-to-all-start.4 = ((bf16[4,2,65536]{2,1,0:T(2,128)(2,1)}), bf16[4,2,65536]{2,1,0:T(2,128)(2,1)S(1)}, u32[]{:S(2)}, u32[]{:S(2)}) async-start(bf16[4,2,65536]{2,1,0:T(2,128)(2,1)} %reshape.903), calls=%async_computation.4 | async-start | bytes 2097152 | tf_op jit(solution)/shard_map/all_to_all | solution.py:279
  780.3 379.1 %reduce-scatter.14.cloned.1.call-start = ((), (), s32[]{:S(2)}) async-start(), calls=%async_computation.25 | async-start | bytes 2621440 | tf_op jit(solution)/shard_map/reduce_scatter | solution.py:333
  784.4 62.3 %copy-start.87 = (f32[2,2,512]{2,1,0:T(2,128)}, f32[2,2,512]{2,1,0:T(2,128)S(1)}, u32[]{:S(2)}) copy-start(f32[2,2,512]{2,1,0:T(2,128)S(1)} %log_add_fusion.3) | copy-start | bytes 24580
  846.7 8.4 copy-start.76
  855.1 19.0 %copy-start.74 = (bf16[1,1,512,256]{2,3,1,0:T(8,128)(2,1)S(1)}, bf16[1,1,512,256]{2,3,1,0:T(8,128)(2,1)}, u32[]{:S(2)}) copy-start(bf16[1,1,512,256]{2,3,1,0:T(8,128)(2,1)} %copy-done.73) | copy-start | bytes 786436
  855.1 19.0 %copy-start.93 = (f32[2,2,512]{2,1,0:T(2,128)S(1)}, f32[2,2,512]{2,1,0:T(2,128)}, u32[]{:S(2)}) copy-start(f32[2,2,512]{2,1,0:T(2,128)} %log_add_fusion.2) | copy-start | bytes 24580
  874.2 15.4 copy-start.72
  874.2 15.4 copy-start.92
  925.6 84.4 %all-to-all-start.6 = ((bf16[4,2,32768]{2,1,0:T(2,128)(2,1)}), bf16[4,2,32768]{2,1,0:T(2,128)(2,1)S(1)}, u32[]{:S(2)}, u32[]{:S(2)}) async-start(bf16[4,2,32768]{2,1,0:T(2,128)(2,1)} %reshape.907), calls=%async_computation.6 | async-start | bytes 1048576 | tf_op jit(solution)/shard_map/all_to_all | solution.py:295
  951.1 13.2 copy-start.65
  964.3 22.7 %copy-start.62 = (bf16[2048,2,64,1]{0,2,1,3:T(8,128)(2,1)S(1)}, bf16[2048,2,64,1]{0,2,1,3:T(8,128)(2,1)}, u32[]{:S(2)}) copy-start(bf16[2048,2,64,1]{0,2,1,3:T(8,128)(2,1)} %reshape.875) | copy-start | bytes 1572868
  1010.1 64.1 %all-to-all-start.7 = ((bf16[4,2,32768]{2,1,0:T(2,128)(2,1)}), bf16[4,2,32768]{2,1,0:T(2,128)(2,1)}, u32[]{:S(2)}, u32[]{:S(2)}) async-start(bf16[4,2,32768]{2,1,0:T(2,128)(2,1)} %reshape.909), calls=%async_computation.7 | async-start | bytes 1048576 | tf_op jit(solution)/shard_map/all_to_all | solution.py:296
  1015.3 144.1 %reduce-scatter.10.cloned.1.call-start = ((), (), s32[]{:S(2)}) async-start(), calls=%async_computation.23 | async-start | bytes 1310720 | tf_op jit(solution)/shard_map/reduce_scatter | solution.py:327
  1021.8 15.3 copy-start.70
  1021.8 15.5 copy-start.69
  1021.8 15.7 copy-start.80
  1072.5 14.4 copy-start.85
  1072.6 14.3 copy-start.100
  1074.2 24.5 %all-to-all-start.5 = ((bf16[4,2,65536]{2,1,0:T(2,128)(2,1)}), bf16[4,2,65536]{2,1,0:T(2,128)(2,1)S(1)}, u32[]{:S(2)}, u32[]{:S(2)}) async-start(bf16[4,2,65536]{2,1,0:T(2,128)(2,1)} %reshape.905), calls=%async_computation.5 | async-start | bytes 2097152 | tf_op jit(solution)/shard_map/all_to_all | solution.py:294
  1079.3 80.2 %reduce-scatter.12.cloned.1.call-start = ((), (), s32[]{:S(2)}) async-start(), calls=%async_computation.24 | async-start | bytes 1310720 | tf_op jit(solution)/shard_map/reduce_scatter | solution.py:330
  1089.9 81.1 %reduce-scatter.8.cloned.1.call-start = ((), (), s32[]{:S(2)}) async-start(), calls=%async_computation.22 | async-start | bytes 2621440 | tf_op jit(solution)/shard_map/reduce_scatter | solution.py:324
  1128.0 205.8 %reduce-scatter.16.cloned.1.call-start = ((), (), s32[]{:S(2)}) async-start(), calls=%async_computation.26 | async-start | bytes 11796480 | tf_op jit(solution)/shard_map/reduce_scatter | solution.py:336
  1137.9 360.4 %reduce-scatter.18.cloned.1.call-start = ((), (), s32[]{:S(2)}) async-start(), calls=%async_computation.27 | async-start | bytes 11796480 | tf_op jit(solution)/shard_map/reduce_scatter | solution.py:339
  1148.1 514.6 %reduce-scatter.20.cloned.1.call-start = ((), (), s32[]{:S(2)}) async-start(), calls=%async_computation.28 | async-start | bytes 11796480 | tf_op jit(solution)/shard_map/reduce_scatter | solution.py:342
  1159.3 640.8 %all-reduce.18.cloned.1.call-start = ((), (), s32[]{:S(2)}) async-start(), calls=%async_computation.29 | async-start | bytes 17301504 | tf_op jit(solution)/shard_map/psum | solution.py:359
  1678.8 10.0 copy-start.25
  1706.5 28.8 %copy-start.29 = (f32[512,1024]{1,0:T(8,128)S(1)}, f32[512,1024]{1,0:T(8,128)}, u32[]{:S(2)}) copy-start(f32[512,1024]{1,0:T(8,128)} %copy-done.27) | copy-start | bytes 6291460
  1800.1 8.2 copy-start.38
  (73 other events, 236.9 us)
Sparse Core Ops, SparseCore 0:
  9.6 30.7 all-gather.11
  42.0 39.0 all-gather.9
  82.7 44.7 all-gather.13
  128.9 72.3 all-gather.15
  202.7 187.5 all-gather.17
  391.7 164.9 all-gather.19
  558.2 164.9 all-gather.21
  788.4 49.8 reduce-scatter.13
  1021.9 28.5 reduce-scatter.9
  1090.0 28.5 reduce-scatter.11
  1128.1 42.7 reduce-scatter.7
  1173.2 160.5 reduce-scatter.15
  1336.2 162.1 reduce-scatter.17
  1500.5 162.1 reduce-scatter.19
  1667.4 132.7 all-reduce.17
where the time goes:
time: 1830 us; the launch traced here: 1820 us
  waiting for transfers between devices  1060 us (58%)
  matrix products  338 us (18%)
  other arithmetic  143 us (8%)
  local copies, waits for them, and re-layouts  142 us (8%)
  blocking collectives  85.6 us (5%)
  starting transfers between devices  37.5 us (2%)
  between operations  18.9 us (1%)
    reduce_scatter x1, waiting for transfers between devices, per_device(): lax.psum_scatter(term_up.astype(jnp.bfloat16), 'seq', scatter_dimension=0...  165 us
    reduce_scatter x1, waiting for transfers between devices, per_device(): lax.psum_scatter(term_down.astype(jnp.bfloat16), 'seq', scatter_dimension...  164 us
    reduce_scatter x1, waiting for transfers between devices, per_device(): lax.psum_scatter(term_gate.astype(jnp.bfloat16), 'seq', scatter_dimension...  163 us
    all_gather x1, waiting for transfers between devices, per_device(): lax.all_gather(weights[6], 'seq', axis=0, tiled=True)  156 us
    all_gather x1, waiting for transfers between devices, per_device(): lax.all_gather(weights[5], 'seq', axis=0, tiled=True)  155 us
    dot_general x4, matrix products, compute(): jnp.einsum('kgbt,tkd->bkgd', grad_scores, key_part, preferred_element_typ...  70.1 us
    unnamed x8, other arithmetic  68.2 us
    dot_general x4, matrix products, compute(): jnp.einsum('kgbt,bkgd->tkd', grad_scores, q_block, preferred_element_type...  65.6 us
  transfers between devices with their start and end apart: 23, of which 15 were waited for; matrix products, arithmetic and copies ran while one was open for 30% of the time, Pallas kernels for 0%

commit v1 on v0

v1 whole, which is shorter than its diff:
```python
import functools
import math

import jax
import jax.numpy as jnp
from jax import lax
from jax.experimental import pallas as pl
from jax.experimental.pallas import tpu as pltpu
from jax.sharding import PartitionSpec as P

H = 16
KV = 8
HD = 64
EPS = 1e-05
ROPE_BASE = 1000000.0
LOG2E = math.log2(math.e)
SPLIT = 8
CHUNKS = 3

f32 = jnp.float32
bf16 = jnp.bfloat16
NN = (((1,), (0,)), ((), ()))
NT = (((1,), (1,)), ((), ()))
TN = (((0,), (0,)), ((), ()))


def dot(left, right, dims=NN):
    return lax.dot_general(left, right, dims, preferred_element_type=f32)


def rms_scale(values):
    return lax.rsqrt(jnp.mean(values * values, axis=-1, keepdims=True) + EPS)


def norm_back(grads, normed, scale):
    return scale * (grads - normed * jnp.mean(grads * normed, axis=-1, keepdims=True))


def tables(positions, width):
    half = width // 2
    freq = ROPE_BASE ** (-(jnp.arange(half, dtype=f32) * 2.0 / width))
    angle = positions.astype(f32)[:, None] * freq[None, :]
    angle = jnp.concatenate([angle, angle], axis=1)
    return (jnp.cos(angle)[:, None, :], jnp.sin(angle)[:, None, :])


def rotate_half(values):
    half = values.shape[-1] // 2
    return jnp.concatenate([-values[..., half:], values[..., :half]], axis=-1)


def rotary(values, cosine, sine):
    return values * cosine + rotate_half(values) * sine


def rotary_back(grads, cosine, sine):
    return grads * cosine - rotate_half(grads * sine)


def pair_half(x, first):
    lane = lax.broadcasted_iota(jnp.int32, x.shape, 1)
    rolled = pltpu.roll(x.astype(f32), HD, 1).astype(x.dtype)
    return jnp.where((lane < HD) == first, x, rolled)


def stack_pair(x):
    lane = lax.broadcasted_iota(jnp.int32, x.shape, 1)
    zero = jnp.zeros_like(x)
    return jnp.concatenate([jnp.where(lane < HD, x, zero), jnp.where(lane < HD, zero, x)], axis=0)


def causal(probs, block):
    key = lax.broadcasted_iota(jnp.int32, probs.shape, 0)
    query = lax.broadcasted_iota(jnp.int32, probs.shape, 1)
    query = jnp.where(query >= block, query - block, query)
    return jnp.where(key <= query, probs, 0.0)


def attend_fwd_kernel(block, q_ref, k_ref, v_ref, o_ref, lse_ref, keys, values):
    first = pl.program_id(0) % 2 == 0
    i = pl.program_id(1)

    @pl.when(i == 0)
    def _():
        keys[...] = pair_half(k_ref[...], first)
        values[...] = pair_half(v_ref[...], first)

    queries = stack_pair(q_ref[...])

    def tile(t, diagonal):
        rows = pl.ds(t * block, block)
        probs = jnp.exp2(dot(keys[rows, :], queries, NT) * (HD**-0.5 * LOG2E))
        if diagonal:
            probs = causal(probs, block)
        return dot(values[rows, :], probs.astype(bf16), TN), jnp.sum(probs, axis=0, keepdims=True)

    def body(t, carry):
        part, total = tile(t, False)
        return carry[0] + part, carry[1] + total

    mixed, total = lax.fori_loop(0, i, body, tile(i, True))
    mixed = mixed * (1.0 / total)
    pair = jnp.concatenate([mixed[:HD, :block], mixed[HD:, block:]], axis=0)
    o_ref[...] = pair.T.astype(bf16)
    lse_ref[0, 0] = jnp.log2(total)


def attend_forward(qkv, block):
    length, width = qkv.shape
    kv = width // (4 * HD)
    n = length // block
    key_at = lambda j, i: (0, kv + j // 2)
    value_at = lambda j, i: (0, kv + kv // 2 + j // 2)
    return pl.pallas_call(
        functools.partial(attend_fwd_kernel, block),
        grid=(kv, n),
        in_specs=[
            pl.BlockSpec((block, 2 * HD), lambda j, i: (i, j)),
            pl.BlockSpec((length, 2 * HD), key_at),
            pl.BlockSpec((length, 2 * HD), value_at),
        ],
        out_specs=[
            pl.BlockSpec((block, 2 * HD), lambda j, i: (i, j)),
            pl.BlockSpec((1, 1, 1, 2 * block), lambda j, i: (j, i, 0, 0)),
        ],
        out_shape=[
            jax.ShapeDtypeStruct((length, width // 2), bf16),
            jax.ShapeDtypeStruct((kv, n, 1, 2 * block), f32),
        ],
        scratch_shapes=[pltpu.VMEM((length, 2 * HD), bf16), pltpu.VMEM((length, 2 * HD), bf16)],
        cost_estimate=pl.CostEstimate(
            flops=8 * length * length * 2 * HD * kv,
            transcendentals=length * length * kv,
            bytes_accessed=3 * length * width,
        ),
        name="attend_forward",
    )(qkv, qkv, qkv)


def attend_bwd_kernel(
    block, q_ref, k_ref, v_ref, g_ref, o_ref, lse_ref, dq_ref, dk_ref, dv_ref,
    queries, grads, delta, keys, values, grad_q,
):
    first = pl.program_id(0) % 2 == 0
    n = q_ref.shape[0] // block
    keys[...] = pair_half(k_ref[...], first)
    values[...] = pair_half(v_ref[...], first)
    for i in range(n):
        rows = slice(i * block, (i + 1) * block)
        g = g_ref[rows, :]
        queries[i] = stack_pair(q_ref[rows, :])
        grads[i] = stack_pair(g)
        both = (g.astype(f32) * o_ref[rows, :].astype(f32)).T
        delta[i] = jnp.concatenate(
            [jnp.sum(both[:HD], axis=0, keepdims=True), jnp.sum(both[HD:], axis=0, keepdims=True)],
            axis=1,
        )
        grad_q[i] = jnp.zeros(grad_q.shape[1:], f32)

    def tile(key, value, key_t, i, diagonal):
        query, grad = queries[i], grads[i]
        probs = jnp.exp2(dot(key, query, NT) * (HD**-0.5 * LOG2E) - lse_ref[0, i])
        if diagonal:
            probs = causal(probs, block)
        grad_probs = dot(value, grad, NT)
        grad_scores = (probs * (grad_probs - delta[i]) * HD**-0.5).astype(bf16)
        grad_q[i] += dot(key_t, grad_scores)
        return dot(grad_scores, query), dot(probs.astype(bf16), grad)

    def step(t, _):
        rows = pl.ds(t * block, block)
        key, value = keys[rows, :], values[rows, :]
        key_t = key.astype(f32).T.astype(bf16)

        def body(i, carry):
            part_k, part_v = tile(key, value, key_t, i, False)
            return carry[0] + part_k, carry[1] + part_v

        part_k, part_v = lax.fori_loop(t + 1, n, body, tile(key, value, key_t, t, True))
        part_k = (part_k + pltpu.roll(part_k, HD, 1)).astype(bf16)
        part_v = (part_v + pltpu.roll(part_v, HD, 1)).astype(bf16)

        @pl.when(first)
        def _():
            dk_ref[rows, :] = part_k
            dv_ref[rows, :] = part_v

        @pl.when(jnp.logical_not(first))
        def _():
            upper = lax.broadcasted_iota(jnp.int32, part_k.shape, 1) >= HD
            dk_ref[rows, :] = jnp.where(upper, part_k, dk_ref[rows, :])
            dv_ref[rows, :] = jnp.where(upper, part_v, dv_ref[rows, :])

        return 0

    lax.fori_loop(0, n, step, 0)
    for i in range(n):
        pair = jnp.concatenate([grad_q[i, :HD, :block], grad_q[i, HD:, block:]], axis=0)
        dq_ref[i * block : (i + 1) * block, :] = pair.T.astype(bf16)


def attend_backward(qkv, grads, mixed, lse, block):
    length, width = qkv.shape
    kv = width // (4 * HD)
    n = length // block
    spec = lambda at: pl.BlockSpec((length, 2 * HD), at)
    at_q = lambda j: (0, j)
    at_half = lambda j: (0, j // 2)
    return pl.pallas_call(
        functools.partial(attend_bwd_kernel, block),
        grid=(kv,),
        in_specs=[
            spec(at_q),
            spec(lambda j: (0, kv + j // 2)),
            spec(lambda j: (0, kv + kv // 2 + j // 2)),
            spec(at_q),
            spec(at_q),
            pl.BlockSpec((1, n, 1, 2 * block), lambda j: (j, 0, 0, 0)),
        ],
        out_specs=[spec(at_q), spec(at_half), spec(at_half)],
        out_shape=[
            jax.ShapeDtypeStruct((length, width // 2), bf16),
            jax.ShapeDtypeStruct((length, width // 4), bf16),
            jax.ShapeDtypeStruct((length, width // 4), bf16),
        ],
        scratch_shapes=[
            pltpu.VMEM((n, 2 * block, 2 * HD), bf16),
            pltpu.VMEM((n, 2 * block, 2 * HD), bf16),
            pltpu.VMEM((n, 1, 2 * block), f32),
            pltpu.VMEM((length, 2 * HD), bf16),
            pltpu.VMEM((length, 2 * HD), bf16),
            pltpu.VMEM((n, 2 * HD, 2 * block), f32),
        ],
        cost_estimate=pl.CostEstimate(
            flops=20 * length * length * 2 * HD * kv,
            transcendentals=length * length * kv,
            bytes_accessed=6 * length * width,
        ),
        name="attend_backward",
    )(qkv, qkv, qkv, grads, mixed, lse)


def ffn_kernel(
    shards, z_ref, h_ref, ht_ref, gy_ref, own_g, own_u, own_d, far_g, far_u, far_d,
    out_in, grad_in, out_ref, grad_ref, mine, theirs, down,
):
    t = pl.program_id(0)
    z = z_ref[0]
    even = z_ref[1] == 0
    rows = own_g.shape[0]
    piece = rows // SPLIT
    unit = own_g.shape[1]
    lanes = down.shape[1] // SPLIT
    blocks = unit // piece

    @pl.when(t == 0)
    def _():
        out_ref[...] = out_in[...]
        grad_ref[...] = grad_in[...]
        down[...] = own_d[...]

    @pl.when(t > 0)
    def _():
        for d in range(SPLIT):
            for k in range(blocks):
                down[k * piece : (k + 1) * piece, d * lanes : (d + 1) * lanes] = far_d[
                    d, 0, 0, :, k * lanes : (k + 1) * lanes
                ]

    def shard_of(r):
        return lax.rem(z + shards - r, shards)

    def columns(r):
        return pl.ds(pl.multiple_of(shard_of(r) * rows, rows), rows)

    def weight(own, far, r):
        return own[...] if r == 0 else far[:, r - 1, 0].reshape(rows, unit)

    gate = up = None
    for r in range(shards):
        left = h_ref[:, columns(r)]
        part_g, part_u = dot(left, weight(own_g, far_g, r)), dot(left, weight(own_u, far_u, r))
        gate, up = (part_g, part_u) if r == 0 else (gate + part_g, up + part_u)
    grad_inner = dot(gy_ref[...], down[...], NT)
    sigma = jax.nn.sigmoid(gate)
    active = gate * sigma
    inner = (active * up).astype(bf16)
    grad_g = (grad_inner * up * sigma * (1.0 + gate * (1.0 - sigma))).astype(bf16)
    grad_u = (grad_inner * active).astype(bf16)
    out_ref[...] += dot(inner, down[...])
    seg = pl.ds(pl.multiple_of(shard_of(t) * unit, unit), unit)

    def keep(term, r, at):
        term = term.astype(bf16).reshape(SPLIT // 2, 2, piece, unit)
        mine[:, r, at : at + piece, seg] = jnp.where(even, term[:, 0], term[:, 1])
        theirs[:, r, at : at + piece, seg] = jnp.where(even, term[:, 1], term[:, 0])

    for r in range(shards):
        grad_ref[:, columns(r)] += dot(grad_g, weight(own_g, far_g, r), NT) + dot(
            grad_u, weight(own_u, far_u, r), NT
        )
        left = ht_ref[columns(r), :]
        keep(dot(left, grad_g), r, 0)
        keep(dot(left, grad_u), r, piece)
    term = dot(inner, gy_ref[...], TN).astype(bf16)
    for d in range(0, SPLIT, 2):
        for k in range(blocks):
            rows_k = slice(k * piece, (k + 1) * piece)
            first = term[rows_k, d * lanes : (d + 1) * lanes]
            second = term[rows_k, (d + 1) * lanes : (d + 2) * lanes]
            to = (d // 2, t, slice(2 * piece, 3 * piece), slice(k * lanes, (k + 1) * lanes))
            mine[to] = jnp.where(even, first, second)
            theirs[to] = jnp.where(even, second, first)


def ffn_chunk(c, z, hidden, hidden_t, grad_y, w_gate, w_up, w_down, far, out_in, grad_in):
    rows, width = hidden.shape
    shards = width // w_gate.shape[0]
    depth = w_gate.shape[0]
    unit = w_down.shape[0] // CHUNKS
    piece = depth // SPLIT
    far = far.reshape(SPLIT, shards - 1, 3, piece, shards * unit)
    seg = lambda t, z_ref: lax.rem(z_ref[0] + shards - t, shards)
    whole = lambda shape: pl.BlockSpec(shape, lambda t, z_ref: (0,) * len(shape))
    own = pl.BlockSpec((depth, unit), lambda t, z_ref: (0, seg(t, z_ref) * CHUNKS + c))
    gathered = lambda kind: pl.BlockSpec(
        (SPLIT, shards - 1, 1, piece, unit), lambda t, z_ref: (0, 0, kind, 0, seg(t, z_ref))
    )
    return pl.pallas_call(
        functools.partial(ffn_kernel, shards),
        grid_spec=pltpu.PrefetchScalarGridSpec(
            num_scalar_prefetch=1,
            grid=(shards,),
            in_specs=[
                whole((rows, width)),
                whole((width, rows)),
                whole((rows, width)),
                own,
                own,
                pl.BlockSpec((unit, width), lambda t, z_ref: (c, 0)),
                gathered(0),
                gathered(1),
                pl.BlockSpec(
                    (SPLIT, 1, 1, piece, shards * unit),
                    lambda t, z_ref: (0, jnp.maximum(t - 1, 0), 2, 0, 0),
                ),
                whole((rows, width)),
                whole((rows, width)),
            ],
            out_specs=[
                whole((rows, width)),
                whole((rows, width)),
                whole((SPLIT // 2, shards, 3 * piece, shards * unit)),
                whole((SPLIT // 2, shards, 3 * piece, shards * unit)),
            ],
            scratch_shapes=[pltpu.VMEM((unit, width), bf16)],
        ),
        out_shape=[
            jax.ShapeDtypeStruct((rows, width), f32),
            jax.ShapeDtypeStruct((rows, width), f32),
            jax.ShapeDtypeStruct((SPLIT // 2, shards, 3 * piece, shards * unit), bf16),
            jax.ShapeDtypeStruct((SPLIT // 2, shards, 3 * piece, shards * unit), bf16),
        ],
        cost_estimate=pl.CostEstimate(
            flops=18 * rows * width * shards * unit,
            transcendentals=rows * shards * unit,
            bytes_accessed=12 * width * shards * unit + 20 * rows * width,
        ),
        name="ffn_chunk",
    )(z, hidden, hidden_t, grad_y, w_gate, w_up, w_down, far, far, far, out_in, grad_in)


def unpack_kernel(*refs):
    sources, (gate_ref, up_ref, down_ref) = refs[:-3], refs[-3:]
    c = pl.program_id(0)
    piece = sources[0].shape[1] // 3
    lanes = down_ref.shape[1] // SPLIT
    blocks = down_ref.shape[0] // piece
    for index, ref in enumerate(sources):

        @pl.when(c == index)
        def _(ref=ref):
            gate_ref[...] = ref[:, 0:piece, :].astype(f32).reshape(gate_ref.shape)
            up_ref[...] = ref[:, piece : 2 * piece, :].astype(f32).reshape(up_ref.shape)
            for d in range(SPLIT):
                for k in range(blocks):
                    down_ref[k * piece : (k + 1) * piece, d * lanes : (d + 1) * lanes] = ref[
                        d, 2 * piece :, k * lanes : (k + 1) * lanes
                    ].astype(f32)


def unpack_ffn(sources, depth, shards, unit, width):
    piece = depth // SPLIT
    blocks = shards * unit // (width // SPLIT) // shards
    return pl.pallas_call(
        unpack_kernel,
        grid=(CHUNKS, shards),
        in_specs=[
            pl.BlockSpec((SPLIT, 3 * piece, unit), lambda c, s, i=i: (0, 0, jnp.where(c == i, s, jnp.where(c < i, 0, shards - 1))))
            for i in range(CHUNKS)
        ],
        out_specs=[
            pl.BlockSpec((depth, unit), lambda c, s: (0, s * CHUNKS + c)),
            pl.BlockSpec((depth, unit), lambda c, s: (0, s * CHUNKS + c)),
            pl.BlockSpec((blocks * piece, width), lambda c, s: (c * shards + s, 0)),
        ],
        out_shape=[
            jax.ShapeDtypeStruct((depth, shards * CHUNKS * unit), f32),
            jax.ShapeDtypeStruct((depth, shards * CHUNKS * unit), f32),
            jax.ShapeDtypeStruct((CHUNKS * unit, width), f32),
        ],
        name="unpack_ffn",
    )(*sources)


class Axes:
    def __init__(self, mesh):
        self.n_dp = mesh.shape["dp"]
        self.n_seq = mesh.shape["seq"]
        self.groups = None
        self.across = None
        if self.n_dp > SPLIT:
            self.groups = [[g + i for i in range(SPLIT)] for g in range(0, self.n_dp, SPLIT)]
            self.across = [list(range(i, self.n_dp, SPLIT)) for i in range(SPLIT)]

    def member(self):
        return lax.rem(lax.axis_index("dp"), SPLIT)

    def shift(self, x, r):
        n = self.n_seq
        return lax.ppermute(x, "seq", [(i, (i + r) % n) for i in range(n)])

    def from_others(self, x):
        return [self.shift(x, r) for r in range(1, self.n_seq)]

    def gather(self, x):
        return lax.all_gather(x, "dp", axis=0, tiled=True, axis_index_groups=self.groups)

    def swap(self, x, bit):
        return lax.ppermute(x, "dp", [(i, i ^ bit) for i in range(self.n_dp)])

    def halves(self, terms):
        terms = terms.reshape(SPLIT // 2, 2, *terms.shape[1:])
        parity = lax.rem(lax.axis_index("dp"), 2)
        pick = lambda i: lax.dynamic_index_in_dim(terms, i, axis=1, keepdims=False)
        return pick(parity), pick(1 - parity)


def after(x, *others):
    return lax.optimization_barrier((x, *others))[0]


class Reduction:
    def __init__(self, axes, mine, theirs):
        self.axes = axes
        member = axes.member()
        self.x = lax.rem(lax.div(member, 2), 2)
        self.y = lax.div(member, 4)
        self.mine = mine.reshape(2, 2, *mine.shape[1:])
        self.state = (axes.swap(theirs, 1),)

    def then(self, *others):
        self.state = lax.optimization_barrier((*self.state, *others))[: len(self.state)]

    def _sum(self, y, x, low, *more):
        def cut(arr):
            shards = arr.shape[2] // 2
            start = [y if y is not None else 0, x if x is not None else 0, 0 if low else shards]
            size = [1 if y is not None else 2, 1 if x is not None else 2, shards]
            rest = arr.ndim - 3
            part = lax.dynamic_slice(arr, start + [0] * rest, size + list(arr.shape[3:]))
            drop = tuple(i for i, at in enumerate((y, x)) if at is not None)
            return lax.squeeze(part, drop).astype(f32)

        total = cut(self.mine) + cut(self.recv)
        for arr in more:
            total = total + arr.astype(f32)
        return total

    def first(self):
        (recv,) = self.state
        self.recv = recv.reshape(self.mine.shape)
        to_x = self._sum(None, 1 - self.x, True).astype(bf16)
        to_y = self._sum(1 - self.y, None, False).astype(bf16)
        self.state = (self.axes.swap(to_x, 2), self.axes.swap(to_y, 4))
        return self

    def second(self):
        self.got_x, self.got_y = self.state
        pick = lambda arr, i: lax.dynamic_index_in_dim(arr, i, axis=0, keepdims=False)
        to_y = self._sum(1 - self.y, self.x, True, pick(self.got_x, 1 - self.y)).astype(bf16)
        to_x = self._sum(self.y, 1 - self.x, False, pick(self.got_y, 1 - self.x)).astype(bf16)
        self.state = (self.axes.swap(to_y, 4), self.axes.swap(to_x, 2))
        return self

    def third(self):
        got_y, got_x = self.state
        pick = lambda arr, i: lax.dynamic_index_in_dim(arr, i, axis=0, keepdims=False)
        low = self._sum(self.y, self.x, True, pick(self.got_x, self.y), got_y)
        high = self._sum(self.y, self.x, False, pick(self.got_y, self.x), got_x)
        half = low.shape[0]
        part = lambda r: (low if r < half else high)[r % half]
        n = 2 * half
        self.own = part(0)
        self.state = tuple(self.axes.shift(part(r).astype(bf16), -r) for r in range(1, n))
        return self

    def last(self):
        total = self.own
        for arr in self.state:
            total = total + arr.astype(f32)
        total = total.astype(bf16)
        if self.axes.across:
            total = lax.psum(total, "dp", axis_index_groups=self.axes.across)
        return total


def per_device(
    axes, tokens, lengths, cotangent, w_query, w_key, w_value, w_out, w_gate, w_up, w_down,
    gain_attn, gain_ffn, gain_query, gain_key,
):
    slots, local, width = tokens.shape
    assert slots == 1
    shards = axes.n_seq
    depth = width // shards
    piece = depth // SPLIT
    z = lax.axis_index("seq")
    member = axes.member()
    heads = H // shards
    kv_heads = KV // shards
    unit = w_down.shape[0] // CHUNKS
    lanes = width // SPLIT

    packed = jnp.concatenate([w_query, w_key, w_value, w_out], axis=1)
    packed = lax.dynamic_slice_in_dim(packed, member * piece, piece, axis=0)
    gains = jnp.concatenate([gain_attn, gain_ffn, gain_query, gain_key])
    gains = jnp.pad(gains, (0, piece * 128 - gains.shape[0])).reshape(piece, 128)
    packed = jnp.concatenate([packed, gains], axis=1)
    near = [packed] + axes.from_others(packed)
    gains = [x[:, -128:].reshape(-1) for x in near]
    attn_w = axes.gather(jnp.stack([x[:, :-128] for x in near]))
    attn_w = attn_w.reshape(SPLIT, shards, piece, -1).transpose(1, 0, 2, 3).reshape(width, -1)
    w_qkv, w_o = attn_w[:, : -width], attn_w[:, -width:]

    mine_g = lax.dynamic_slice_in_dim(w_gate, member * piece, piece, axis=0)
    mine_u = lax.dynamic_slice_in_dim(w_up, member * piece, piece, axis=0)
    mine_d = lax.dynamic_slice_in_dim(w_down, member * lanes, lanes, axis=1)
    mine_g = mine_g.reshape(piece, shards, CHUNKS, unit)
    mine_u = mine_u.reshape(piece, shards, CHUNKS, unit)
    own_parts = []
    for c in range(CHUNKS):
        part_d = mine_d[c * unit : (c + 1) * unit].reshape(unit // piece, piece, lanes)
        own = jnp.concatenate(
            [
                mine_g[:, :, c].reshape(piece, shards * unit),
                mine_u[:, :, c].reshape(piece, shards * unit),
                part_d.transpose(1, 0, 2).reshape(piece, shards * unit),
            ],
            axis=0,
        )
        own_parts.append(own)

    def cross(c, *others):
        return jnp.stack(axes.from_others(after(own_parts[c], *others) if others else own_parts[c]))


    def relative(x):
        parts = [
            lax.dynamic_slice_in_dim(x, lax.rem(z + shards - r, shards) * depth, depth, axis=1)
            for r in range(shards)
        ]
        return jnp.concatenate(parts, axis=1)

    def absolute(x):
        return relative_back(x)

    def relative_back(x):
        parts = [
            lax.dynamic_slice_in_dim(x, lax.rem(z + shards - r, shards) * depth, depth, axis=1)
            for r in range(shards)
        ]
        return jnp.concatenate(parts, axis=1)

    def gathered_gain(start, size):
        parts = jnp.stack([g[start : start + size] for g in gains])
        order = lax.rem(z + shards - jnp.arange(shards), shards)
        hot = (order[:, None] == jnp.arange(shards)[None, :]).astype(f32)
        return jnp.sum(hot[:, :, None] * parts.astype(f32)[:, None, :], axis=0).reshape(-1)

    head = HD // shards
    gain1 = gathered_gain(0, depth)
    gain2 = gathered_gain(depth, depth)
    gainq = gathered_gain(2 * depth, head)
    gaink = gathered_gain(2 * depth + head, head)

    positions = z * local + jnp.arange(local, dtype=jnp.int32)
    cosine, sine = tables(positions, HD)
    valid = (positions < lengths[0])[:, None]
    inputs = tokens[0].astype(f32)
    scale1 = rms_scale(inputs)
    normed1 = inputs * scale1
    hidden1 = relative((normed1 * gain1).astype(bf16))
    raw = dot(hidden1, w_qkv)
    query_raw = raw[:, : H * HD].reshape(local, H, HD)
    key_raw = raw[:, H * HD : (H + KV) * HD].reshape(local, KV, HD)
    value = raw[:, (H + KV) * HD :].astype(bf16)
    q_scale = rms_scale(query_raw)
    q_hat = query_raw * q_scale
    k_scale = rms_scale(key_raw)
    k_hat = key_raw * k_scale
    query = rotary(q_hat * gainq, cosine, sine).astype(bf16)
    key = rotary(k_hat * gaink, cosine, sine).astype(bf16)

    def by_head(x, count):
        return x.reshape(local, shards, count * HD).transpose(1, 0, 2)

    def exchange(x):
        return lax.all_to_all(x, "seq", split_axis=0, concat_axis=0, tiled=True)

    send = jnp.concatenate(
        [by_head(query, heads), by_head(key, kv_heads), by_head(value, kv_heads)], axis=2
    )
    far = [axes.gather(after(cross(0), send))]
    qkv = exchange(send).reshape(shards * local, -1)
    block = 512
    mixed_heads, lse = attend_forward(qkv, block)
    far.append(axes.gather(after(cross(1, qkv), mixed_heads)))
    mixed = exchange(mixed_heads.reshape(shards, local, heads * HD))
    mixed = mixed.transpose(1, 0, 2).reshape(local, H * HD)
    mixed_rel = relative(mixed)
    resid = inputs + dot(mixed_rel, w_o)
    scale2 = rms_scale(resid)
    normed2 = resid * scale2
    hidden2 = (normed2 * gain2).astype(bf16)
    hidden2_t = hidden2.T
    far.append(axes.gather(after(cross(2, mixed), hidden2)))
    grad_y = jnp.where(valid, cotangent[0], jnp.zeros((), bf16))

    where = jnp.stack([z, lax.rem(member, 2)]).astype(jnp.int32)
    result, grad_hidden2 = resid, jnp.zeros_like(resid)
    sums = []

    def chunk(c, result, grad_hidden2):
        result, grad_hidden2, mine, theirs = ffn_chunk(
            c, where, hidden2, hidden2_t, grad_y, w_gate, w_up, w_down, far[c], result, grad_hidden2
        )
        sums.append(Reduction(axes, mine, theirs))
        return result, grad_hidden2

    result, grad_hidden2 = chunk(0, result, grad_hidden2)
    result, grad_hidden2 = chunk(1, result, grad_hidden2)
    sums[0].then(result)
    result = after(result, *sums[0].state)
    sums[0].first()
    result, grad_hidden2 = chunk(2, result, grad_hidden2)
    output = jnp.where(valid, result, 0.0).astype(bf16)[None]
    sums[0].then(grad_hidden2)
    sums[1].then(grad_hidden2)
    grad_hidden2 = after(grad_hidden2, *sums[1].state, *sums[0].state)
    sums[1].first()
    sums[0].second()

    term_gain2 = jnp.sum(grad_hidden2 * normed2, axis=0)
    grad_resid = grad_y.astype(f32) + norm_back(grad_hidden2 * gain2, normed2, scale2)
    grad_branch = grad_resid.astype(bf16)

    def by_piece(term):
        return term.reshape(shards, SPLIT, piece, -1).transpose(1, 0, 2, 3)

    term_out = by_piece(dot(mixed_rel, grad_branch, TN).astype(bf16))
    sums.append(Reduction(axes, *axes.halves(term_out)))
    grad_mixed = absolute(dot(grad_branch, w_o, NT).astype(bf16))
    grad_heads = exchange(by_head(grad_mixed, heads)).reshape(shards * local, -1)
    grad_heads = after(grad_heads, *sums[2].state, *sums[1].state, *sums[0].state, *sums[3].state)
    for i in range(4):
        sums[i].then(grad_heads)
    sums[2].first()
    sums[3].first()
    sums[1].second()
    sums[0].third()
    back_q, back_k, back_v = attend_backward(qkv, grad_heads, mixed_heads, lse, block)
    back = jnp.concatenate([back_q, back_k, back_v], axis=1).reshape(shards, local, -1)
    back = after(back, *sums[2].state, *sums[1].state, *sums[0].state, *sums[3].state)
    for i in range(4):
        sums[i].then(back)
    pieces = [axes.gather(sums[0].last()[None])]
    sums[2].second()
    sums[3].second()
    back = exchange(back)
    back = after(back, *sums[2].state, *sums[3].state)
    sums[2].then(back)
    sums[3].then(back)
    sums[1].third()
    sums[2].third()
    sums[3].third()

    def joined(start, count):
        part = back[:, :, start * HD : (start + count) * HD]
        return part.transpose(1, 0, 2).reshape(local, shards * count * HD)

    back_q = joined(0, heads).astype(f32).reshape(local, H, HD)
    back_k = joined(heads, kv_heads).astype(f32).reshape(local, KV, HD)
    back_v = joined(heads + kv_heads, kv_heads)
    grad_qhat = rotary_back(back_q, cosine, sine)
    term_gainq = jnp.sum(grad_qhat * q_hat, axis=(0, 1))
    grad_qraw = norm_back(grad_qhat * gainq, q_hat, q_scale).reshape(local, H * HD).astype(bf16)
    grad_khat = rotary_back(back_k, cosine, sine)
    term_gaink = jnp.sum(grad_khat * k_hat, axis=(0, 1))
    grad_kraw = norm_back(grad_khat * gaink, k_hat, k_scale).reshape(local, KV * HD).astype(bf16)
    grad_raw = jnp.concatenate([grad_qraw, grad_kraw, back_v], axis=1)
    term_qkv = dot(hidden1, grad_raw, TN).astype(bf16)
    grad_hidden1 = absolute(dot(grad_raw, w_qkv, NT))
    term_gain1 = jnp.sum(grad_hidden1 * normed1, axis=0)
    grad_tokens = (grad_resid + norm_back(grad_hidden1 * gain1, normed1, scale1))[None]

    parts = [
        term_gain1.reshape(shards, depth),
        term_gain2.reshape(shards, depth),
        term_gainq.reshape(shards, head),
        term_gaink.reshape(shards, head),
    ]
    parts = jnp.concatenate(parts, axis=1)
    order = lax.rem(z + shards - jnp.arange(shards), shards)
    hot = (order[:, None] == jnp.arange(shards)[None, :]).astype(f32)
    parts = jnp.sum(hot[:, :, None] * parts[None], axis=1)
    each = parts.shape[1] // SPLIT
    parts = parts.reshape(shards, SPLIT, each).transpose(1, 0, 2)
    parts = jnp.pad(parts, ((0, 0), (0, 0), (0, piece * 128 - each)))
    parts = parts.reshape(SPLIT, shards, piece, 128).astype(bf16)
    term_qkv = jnp.concatenate([by_piece(term_qkv), parts], axis=3)
    term_qkv = after(term_qkv, *sums[1].state, *sums[2].state, *sums[3].state)
    for i in range(1, 4):
        sums[i].then(term_qkv)
    pieces += [axes.gather(sums[1].last()[None]), axes.gather(sums[2].last()[None])]
    grad_out = axes.gather(sums[3].last()).astype(f32)
    grad_gate, grad_up, grad_down = unpack_ffn(pieces, depth, shards, unit, width)
    tail = Reduction(axes, *axes.halves(term_qkv)).first().second().third()
    whole = axes.gather(tail.last()).astype(f32)
    grad_query = whole[:, : H * HD]
    grad_key = whole[:, H * HD : (H + KV) * HD]
    grad_value = whole[:, (H + KV) * HD : (H + 2 * KV) * HD]
    sums = whole[:, -128:].reshape(SPLIT, -1)[:, :each].reshape(-1)
    return (
        output,
        grad_tokens,
        grad_query,
        grad_key,
        grad_value,
        grad_out,
        grad_gate,
        grad_up,
        grad_down,
        sums[:depth],
        sums[depth : 2 * depth],
        sums[2 * depth : 2 * depth + head],
        sums[2 * depth + head :],
    )


def solution(mesh):
    rows = P("seq", None)
    whole = P("dp", "seq", None)
    return jax.shard_map(
        functools.partial(per_device, Axes(mesh)),
        mesh=mesh,
        in_specs=(whole, P("dp"), whole) + (rows,) * 7 + (P("seq"),) * 4,
        out_specs=(whole, whole) + (rows,) * 7 + (P("seq"),) * 4,
        check_vma=False,
    )
```

time: 1830 us -> 788 us (0.43)
  waiting for transfers between devices: 1060 us -> 275 us
  matrix products: 338 us -> 16.7 us
  Pallas kernels: 0 us -> 160 us
  blocking collectives: 85.6 us -> 10.5 us
  starting transfers between devices: 37.5 us -> 80.6 us
  local copies, waits for them, and re-layouts: 142 us -> 106 us
  other arithmetic: 143 us -> 115 us
    reduce_scatter x7 -> x0, waiting for transfers between devices: 503 us -> none  [the longest x1 165 us: per_device(): lax.psum_scatter(term_up.astype(jnp.bfloat16), 'seq', scatter_dimension=0...]
    all_gather x7 -> x8, waiting for transfers between devices: 415 us -> 16.6 us  [gather(): lax.all_gather(x, 'dp', axis=0, tiled=True, axis_index_groups=self.groups)]
    dot_general x45 -> x6, matrix products: 338 us -> 16.7 us  [dot(): return lax.dot_general(left, right, dims, preferred_element_type=f32)]
    ppermute x0 -> x52, waiting for transfers between devices: none -> 167 us  [the longest x25 85.4 us: swap(): return lax.ppermute(x, 'dp', [(i, i ^ bit) for i in range(self.n_dp)])]
    pallas_call x0 -> x6, Pallas kernels: none -> 160 us  [the longest x3 93.9 us: ffn_chunk(): pl.pallas_call(functools.partial(ffn_kernel, shards), grid_spec=pltpu.Pre...]
    unnamed x8 -> x1, other arithmetic: 68.2 us -> 0.01 us
    ppermute x0 -> x52, starting transfers between devices: none -> 61.4 us  [the longest x27 39.7 us: shift(): return lax.ppermute(x, 'seq', [(i, (i + r) % n) for i in range(n)])]
    psum x1 -> x0, waiting for transfers between devices: 61.3 us -> none  [per_device(): lax.psum(shards[0].astype(jnp.bfloat16), 'dp').astype(jnp.float32)]
  transfers between devices with their start and end apart: 23 -> 64, of which waited for: 15 -> 21; matrix products, arithmetic and copies ran while one was open for 30% -> 24% of each run, Pallas kernels for 0% -> 20%
where the time goes in v1:
time: 788 us; the launch traced here: 781 us
  waiting for transfers between devices  275 us (35%)
  Pallas kernels  160 us (20%)
  other arithmetic  115 us (15%)
  local copies, waits for them, and re-layouts  106 us (13%)
  starting transfers between devices  80.6 us (10%)
  between operations  16.9 us (2%)
  matrix products  16.7 us (2%)
  blocking collectives  10.5 us (1%)
    pallas_call x3, Pallas kernels, ffn_chunk(): pl.pallas_call(functools.partial(ffn_kernel, shards), grid_spec=pltpu.Pre...  93.9 us
    all_to_all x4, waiting for transfers between devices, exchange(): return lax.all_to_all(x, 'seq', split_axis=0, concat_axis=0, tiled=True)  91 us
    ppermute x25, waiting for transfers between devices, swap(): return lax.ppermute(x, 'dp', [(i, i ^ bit) for i in range(self.n_dp)])  85.4 us
    ppermute x27, waiting for transfers between devices, shift(): return lax.ppermute(x, 'seq', [(i, (i + r) % n) for i in range(n)])  81.9 us
    ppermute x27, starting transfers between devices, shift(): return lax.ppermute(x, 'seq', [(i, (i + r) % n) for i in range(n)])  39.7 us
    pallas_call x1, Pallas kernels, attend_backward(): pl.pallas_call(functools.partial(attend_bwd_kernel, block), grid=(kv,), i...  37.5 us
    ppermute x25, starting transfers between devices, swap(): return lax.ppermute(x, 'dp', [(i, i ^ bit) for i in range(self.n_dp)])  21.7 us
    unnamed x205, local copies, waits for them, and re-layouts  20.5 us
  transfers between devices with their start and end apart: 64, of which 21 were waited for; matrix products, arithmetic and copies ran while one was open for 24% of the time, Pallas kernels for 20%

profile of v1, /device:TPU:0, one launch (start us, length us, event | category | flops | bytes accessed | tf_op | source)
XLA Modules:
  0.0 780.9 jit_solution(8288033129573347513)
XLA Ops:
  9.0 5.1 collective-permute-start.2
  15.1 4.5 collective-permute-done.2
  19.6 11.8 %collective-permute-done.1 = bf16[32,3200]{1,0:T(8,128)(2,1)S(1)} collective-permute-done((bf16[32,3200]{1,0:T(8,128)(2,1)S(1)}, bf16[32,3200]{1,0:T(8,128)(2,1)S(1)}, u32[]{:S(2)}, u32[]{:S(2)}) %collective-permute-start.1) | collective-permute-done | bytes 204832 | tf_op jit(solution)/shard_map/ppermute | solution.py:431
  54.2 16.5 %collective-permute-done.10 = bf16[96,1536]{1,0:T(8,128)(2,1)S(1)} collective-permute-done((bf16[96,1536]{1,0:T(8,128)(2,1)}, bf16[96,1536]{1,0:T(8,128)(2,1)S(1)}, u32[]{:S(2)}, u32[]{:S(2)}) %collective-permute-start.10) | collective-permute-done | bytes 294944 | tf_op jit(solution)/shard_map/ppermute | solution.py:431
  71.7 6.9 all-gather.12.cloned.1.call-done
  78.6 3.2 copy.142
  100.8 4.6 all-to-all-start
  109.0 45.2 %all-to-all-done = bf16[4,512,512]{1,2,0:T(8,128)(2,1)} async-done(((bf16[4,512,512]{1,2,0:T(8,128)(2,1)}), bf16[4,512,512]{1,2,0:T(8,128)(2,1)}, u32[]{:S(2)}, u32[]{:S(2)}) %all-to-all-start) | async-done | bytes 2097184 | tf_op jit(solution)/shard_map/all_to_all | solution.py:618
  154.3 4.1 copy.148
  160.5 16.5 %attend_forward.1 = (bf16[2048,256]{1,0:T(8,128)(2,1)}, f32[2,4,1,1024]{3,2,1,0:T(1,128)}) custom-call(bf16[2048,512]{1,0:T(8,128)(2,1)} %bitcast.564, bf16[2048,512]{1,0:T(8,128)(2,1)} %bitcast.565, bf16[2048,512]{1,0:T(8,128)(2,1)} %bitcast.566), custom_call_target="tpu_custom_call" | custom-call | flops 8589934592 | bytes 3145728 | tf_op jit(solution)/shard_map/attend_forward/pallas_call | solution.py:114
  176.9 7.0 collective-permute-done.7
  188.4 4.7 all-to-all-start.1
  196.9 21.9 %all-to-all-done.1 = bf16[4,512,256]{1,2,0:T(8,128)(2,1)} async-done(((bf16[4,512,256]{1,2,0:T(8,128)(2,1)}), bf16[4,512,256]{1,2,0:T(8,128)(2,1)}, u32[]{:S(2)}, u32[]{:S(2)}) %all-to-all-start.1) | async-done | bytes 1048608 | tf_op jit(solution)/shard_map/all_to_all | solution.py:618
  222.1 3.3 multiply_reduce_fusion.3
  228.8 15.5 %collective-permute-done.4 = bf16[96,1536]{1,0:T(8,128)(2,1)S(1)} collective-permute-done((bf16[96,1536]{1,0:T(8,128)(2,1)}, bf16[96,1536]{1,0:T(8,128)(2,1)S(1)}, u32[]{:S(2)}, u32[]{:S(2)}) %collective-permute-start.4) | collective-permute-done | bytes 294944 | tf_op jit(solution)/shard_map/ppermute | solution.py:431
  254.3 31.2 %ffn_chunk.3 = (f32[512,1024]{1,0:T(8,128)}, f32[512,1024]{1,0:T(8,128)}, bf16[4,4,96,1536]{3,2,1,0:T(8,128)(2,1)}, bf16[4,4,96,1536]{3,2,1,0:T(8,128)(2,1)}) custom-call(s32[2]{0:T(128)} %pad_add_fusion.z_ref, bf16[512,1024]{1,0:T(8,128)(2,1)} %multiply_convert_fusion.1.h_ref, bf16[1024,512]{1,0:T(8,128)(2,1)} %copy.155.ht_ref, ...), custom_call_target="tpu_custom_call" | custom-call | flops 14495514624 | bytes 29360128 | tf_op jit(solution)/shard_map/ffn_chunk/pallas_call | solution.py:329
  285.6 31.3 %ffn_chunk.4 = (f32[512,1024]{1,0:T(8,128)}, f32[512,1024]{1,0:T(8,128)}, bf16[4,4,96,1536]{3,2,1,0:T(8,128)(2,1)}, bf16[4,4,96,1536]{3,2,1,0:T(8,128)(2,1)}) custom-call(s32[2]{0:T(128)} %pad_add_fusion.z_ref, bf16[512,1024]{1,0:T(8,128)(2,1)} %multiply_convert_fusion.1.h_ref, bf16[1024,512]{1,0:T(8,128)(2,1)} %copy.155.ht_ref, ...), custom_call_target="tpu_custom_call" | custom-call | flops 14495514624 | bytes 29360128 | tf_op jit(solution)/shard_map/ffn_chunk/pallas_call | solution.py:329
  317.3 2.9 fusion.30
  321.7 3.0 fusion.31
  325.5 31.3 %ffn_chunk.5 = (f32[512,1024]{1,0:T(8,128)}, f32[512,1024]{1,0:T(8,128)}, bf16[4,4,96,1536]{3,2,1,0:T(8,128)(2,1)}, bf16[4,4,96,1536]{3,2,1,0:T(8,128)(2,1)}) custom-call(s32[2]{0:T(128)} %pad_add_fusion.z_ref, bf16[512,1024]{1,0:T(8,128)(2,1)} %multiply_convert_fusion.1.h_ref, bf16[1024,512]{1,0:T(8,128)(2,1)} %copy.155.ht_ref, ...), custom_call_target="tpu_custom_call" | custom-call | flops 14495514624 | bytes 29360128 | tf_op jit(solution)/shard_map/ffn_chunk/pallas_call | solution.py:329
  356.9 3.5 fusion.49
  363.0 3.7 fusion.27
  368.0 4.8 all-to-all-start.2
  383.2 34.1 %collective-permute-done.20 = bf16[2,96,1536]{2,1,0:T(8,128)(2,1)S(1)} collective-permute-done((bf16[2,96,1536]{2,1,0:T(8,128)(2,1)S(1)}, bf16[2,96,1536]{2,1,0:T(8,128)(2,1)S(1)}, u32[]{:S(2)}, u32[]{:S(2)}) %collective-permute-start.20) | collective-permute-done | bytes 589856 | tf_op jit(solution)/shard_map/ppermute | solution.py:440
  418.5 2.9 fusion.34
  421.4 3.0 fusion.35
  424.4 2.8 fusion.45
  427.3 3.8 collective-permute-start.26
  434.9 3.4 fusion.47
  438.3 26.3 %collective-permute-done.29 = bf16[2,2,32,1024]{3,2,1,0:T(8,128)(2,1)S(1)} collective-permute-done((bf16[2,2,32,1024]{3,2,1,0:T(8,128)(2,1)S(1)}, bf16[2,2,32,1024]{3,2,1,0:T(8,128)(2,1)S(1)}, u32[]{:S(2)}, u32[]{:S(2)}) %collective-permute-start.29) | collective-permute-done | bytes 262176 | tf_op jit(solution)/shard_map/ppermute | solution.py:440
  469.0 37.5 %attend_backward.1 = (bf16[2048,256]{1,0:T(8,128)(2,1)}, bf16[2048,128]{1,0:T(8,128)(2,1)}, bf16[2048,128]{1,0:T(8,128)(2,1)}) custom-call(bf16[2048,512]{1,0:T(8,128)(2,1)} %bitcast.567, bf16[2048,512]{1,0:T(8,128)(2,1)} %bitcast.568, bf16[2048,512]{1,0:T(8,128)(2,1)} %bitcast.569, bf16[2048,256]{1,0:T(8,128)(2,1)} %bitcast.70.g_ref, ...), custom_call_target="tpu_custom_call" | custom-call | flops 21474836480 | bytes 6291456 | tf_op jit(solution)/shard_map/attend_backward/pallas_call | solution.py:209
  506.5 3.1 pad_maximum_fusion.2
  509.6 4.1 copy.159
  513.7 4.5 all-to-all-start.3
  520.8 3.0 copy.161
  526.5 2.9 copy.165
  529.3 3.5 fusion.42
  538.8 3.7 fusion.40
  544.3 3.7 collective-permute-start.35
  553.6 23.8 %all-to-all-done.3 = bf16[4,512,512]{1,2,0:T(8,128)(2,1)} async-done(((bf16[4,512,512]{1,2,0:T(8,128)(2,1)}), bf16[4,512,512]{1,2,0:T(8,128)(2,1)}, u32[]{:S(2)}, u32[]{:S(2)}) %all-to-all-start.3) | async-done | bytes 2097184 | tf_op jit(solution)/shard_map/all_to_all | solution.py:618
  580.0 2.8 slice_convert_fusion.1
  603.9 2.9 copy.164
  606.8 2.9 copy.162
  609.7 2.9 copy.178
  612.6 3.8 multiply_convert_fusion.2
  617.3 5.4 multiply_convert_fusion
  629.4 3.7 fusion.20
  637.4 4.8 collective-permute-start.41
  642.2 3.7 convolution_convert_fusion
  646.0 2.9 fusion.37
  651.2 2.9 collective-permute-start.42
  654.2 2.6 pad_maximum_fusion
  656.8 19.0 %collective-permute-done.42 = bf16[32,1024]{1,0:T(8,128)(2,1)S(1)} collective-permute-done((bf16[32,1024]{1,0:T(8,128)(2,1)S(1)}, bf16[32,1024]{1,0:T(8,128)(2,1)S(1)}, u32[]{:S(2)}, u32[]{:S(2)}) %collective-permute-start.42) | collective-permute-done | bytes 65568 | tf_op jit(solution)/shard_map/ppermute | solution.py:431
  678.0 2.8 constant_dynamic-slice_fusion.2
  681.3 4.1 collective-permute-done.44
  691.3 12.1 %collective-permute-done.48 = bf16[2,2,32,2176]{3,2,1,0:T(8,128)(2,1)} collective-permute-done((bf16[2,2,32,2176]{3,2,1,0:T(8,128)(2,1)S(1)}, bf16[2,2,32,2176]{3,2,1,0:T(8,128)(2,1)}, u32[]{:S(2)}, u32[]{:S(2)}) %collective-permute-start.48) | collective-permute-done | bytes 557088 | tf_op jit(solution)/shard_map/ppermute | solution.py:440
  709.7 5.0 collective-permute-done.49
  721.8 3.7 collective-permute-done.51
  725.6 3.0 collective-permute-done.50
  729.4 2.9 fusion.56
  732.3 3.0 fusion.13
  735.3 10.5 %all_gather.32 = bf16[256,1024]{1,0:T(8,128)(2,1)S(1)} all-gather(bf16[32,1024]{1,0:T(8,128)(2,1)S(1)} %fusion.101), channel_id=1, replica_groups=mesh['dp'=8,'seq'=4] {'dp'}, dimensions={0}, use_global_device_ids=true | all-gather | bytes 589824 | tf_op jit(solution)/shard_map/all_gather | solution.py:437
  746.9 11.8 %unpack_ffn.1 = (f32[256,4608]{1,0:T(8,128)}, f32[256,4608]{1,0:T(8,128)}, f32[1152,1024]{1,0:T(8,128)}) custom-call(bf16[8,96,1536]{2,1,0:T(8,128)(2,1)} %bitcast.554, bf16[8,96,1536]{2,1,0:T(8,128)(2,1)} %bitcast.555, bf16[8,96,1536]{2,1,0:T(8,128)(2,1)} %bitcast.556), custom_call_target="tpu_custom_call" | custom-call | tf_op jit(solution)/shard_map/unpack_ffn/pallas_call | solution.py:395
  758.7 9.7 %all-gather.20.cloned.1.call-done = bf16[256,2176]{1,0:T(8,128)(2,1)} async-done(((bf16[32,2176]{1,0:T(8,128)(2,1)}), bf16[256,2176]{1,0:T(8,128)(2,1)}) %all-gather.20.cloned.1.call-update) | async-done | bytes 1114128 | tf_op jit(solution)/shard_map/all_gather | solution.py:437
  (484 shorter events, 186.2 us)
Async XLA Ops:
  7.2 71.4 %all-gather.12.cloned.1.call-start = ((), (), s32[]{:S(2)}) async-start(), calls=%async_computation.4 | async-start | bytes 7077888 | tf_op jit(solution)/shard_map/all_gather | solution.py:437
  9.0 10.6 %collective-permute-start.2 = (bf16[32,3200]{1,0:T(8,128)(2,1)S(1)}, bf16[32,3200]{1,0:T(8,128)(2,1)S(1)}, u32[]{:S(2)}, u32[]{:S(2)}) collective-permute-start(bf16[32,3200]{1,0:T(8,128)(2,1)S(1)} %pad_maximum_fusion.18), channel_id=1, source_target_pairs={{0,3},{1,0},{2,1},{3,2},{4,7},{5,4},{6,5},{7,6},{8,11},{9,8},{10,9... | collective-permute-start | bytes 614408 | tf_op jit(solution)/shard_map/ppermute | solution.py:431
  14.1 17.4 %collective-permute-start.1 = (bf16[32,3200]{1,0:T(8,128)(2,1)S(1)}, bf16[32,3200]{1,0:T(8,128)(2,1)S(1)}, u32[]{:S(2)}, u32[]{:S(2)}) collective-permute-start(bf16[32,3200]{1,0:T(8,128)(2,1)S(1)} %pad_maximum_fusion.18), channel_id=1, source_target_pairs={{0,2},{1,3},{2,0},{3,1},{4,6},{5,7},{6,4},{7,5},{8,10},{9,11},{10,... | collective-permute-start | bytes 614408 | tf_op jit(solution)/shard_map/ppermute | solution.py:431
  14.1 17.4 %collective-permute-start = (bf16[32,3200]{1,0:T(8,128)(2,1)S(1)}, bf16[32,3200]{1,0:T(8,128)(2,1)S(1)}, u32[]{:S(2)}, u32[]{:S(2)}) collective-permute-start(bf16[32,3200]{1,0:T(8,128)(2,1)S(1)} %pad_maximum_fusion.18), channel_id=1, source_target_pairs={{0,1},{1,2},{2,3},{3,0},{4,5},{5,6},{6,7},{7,4},{8,9},{9,10},{10,1... | collective-permute-start | bytes 614408 | tf_op jit(solution)/shard_map/ppermute | solution.py:431
  32.5 220.2 %all-gather.18.cloned.1.call-start = ((), (), s32[]{:S(2)}) async-start(), calls=%async_computation.7 | async-start | bytes 7962624 | tf_op jit(solution)/shard_map/all_gather | solution.py:437
  42.4 11.7 %collective-permute-start.11 = (bf16[96,1536]{1,0:T(8,128)(2,1)}, bf16[96,1536]{1,0:T(8,128)(2,1)S(1)}, u32[]{:S(2)}, u32[]{:S(2)}) collective-permute-start(bf16[96,1536]{1,0:T(8,128)(2,1)} %bitcast_dynamic-update-slice_fusion), channel_id=1, source_target_pairs={{0,3},{1,0},{2,1},{3,2},{4,7},{5,4},{6,5},{7,6},{8,11},{9,8},{10,9... | collective-permute-start | bytes 884744 | tf_op jit(solution)/shard_map/ppermute | solution.py:431
  42.6 28.1 %collective-permute-start.10 = (bf16[96,1536]{1,0:T(8,128)(2,1)}, bf16[96,1536]{1,0:T(8,128)(2,1)S(1)}, u32[]{:S(2)}, u32[]{:S(2)}) collective-permute-start(bf16[96,1536]{1,0:T(8,128)(2,1)} %bitcast_dynamic-update-slice_fusion), channel_id=1, source_target_pairs={{0,2},{1,3},{2,0},{3,1},{4,6},{5,7},{6,4},{7,5},{8,10},{9,11},{10,... | collective-permute-start | bytes 884744 | tf_op jit(solution)/shard_map/ppermute | solution.py:431
  45.2 25.5 %collective-permute-start.9 = (bf16[96,1536]{1,0:T(8,128)(2,1)}, bf16[96,1536]{1,0:T(8,128)(2,1)S(1)}, u32[]{:S(2)}, u32[]{:S(2)}) collective-permute-start(bf16[96,1536]{1,0:T(8,128)(2,1)} %bitcast_dynamic-update-slice_fusion), channel_id=1, source_target_pairs={{0,1},{1,2},{2,3},{3,0},{4,5},{5,6},{6,7},{7,4},{8,9},{9,10},{10,1... | collective-permute-start | bytes 884744 | tf_op jit(solution)/shard_map/ppermute | solution.py:431
  100.8 53.4 %all-to-all-start = ((bf16[4,512,512]{1,2,0:T(8,128)(2,1)}), bf16[4,512,512]{1,2,0:T(8,128)(2,1)}, u32[]{:S(2)}, u32[]{:S(2)}) async-start(bf16[4,512,512]{1,2,0:T(8,128)(2,1)} %pad_maximum_fusion.1), calls=%async_computation | async-start | bytes 4194304 | tf_op jit(solution)/shard_map/all_to_all | solution.py:618
  105.5 180.1 %all-gather.16.cloned.1.call-start = ((), (), s32[]{:S(2)}) async-start(), calls=%async_computation.6 | async-start | bytes 7962624 | tf_op jit(solution)/shard_map/all_gather | solution.py:437
  158.4 18.5 %collective-permute-start.8 = (bf16[96,1536]{1,0:T(8,128)(2,1)}, bf16[96,1536]{1,0:T(8,128)(2,1)}, u32[]{:S(2)}, u32[]{:S(2)}) collective-permute-start(bf16[96,1536]{1,0:T(8,128)(2,1)} %pad_maximum_fusion.17), channel_id=1, source_target_pairs={{0,3},{1,0},{2,1},{3,2},{4,7},{5,4},{6,5},{7,6},{8,11},{9,8},{10,9... | collective-permute-start | bytes 884744 | tf_op jit(solution)/shard_map/ppermute | solution.py:431
  159.9 24.0 %collective-permute-start.7 = (bf16[96,1536]{1,0:T(8,128)(2,1)}, bf16[96,1536]{1,0:T(8,128)(2,1)}, u32[]{:S(2)}, u32[]{:S(2)}) collective-permute-start(bf16[96,1536]{1,0:T(8,128)(2,1)} %pad_maximum_fusion.17), channel_id=1, source_target_pairs={{0,2},{1,3},{2,0},{3,1},{4,6},{5,7},{6,4},{7,5},{8,10},{9,11},{10,... | collective-permute-start | bytes 884744 | tf_op jit(solution)/shard_map/ppermute | solution.py:431
  159.9 24.0 %collective-permute-start.6 = (bf16[96,1536]{1,0:T(8,128)(2,1)}, bf16[96,1536]{1,0:T(8,128)(2,1)}, u32[]{:S(2)}, u32[]{:S(2)}) collective-permute-start(bf16[96,1536]{1,0:T(8,128)(2,1)} %pad_maximum_fusion.17), channel_id=1, source_target_pairs={{0,1},{1,2},{2,3},{3,0},{4,5},{5,6},{6,7},{7,4},{8,9},{9,10},{10,1... | collective-permute-start | bytes 884744 | tf_op jit(solution)/shard_map/ppermute | solution.py:431
  188.4 30.4 %all-to-all-start.1 = ((bf16[4,512,256]{1,2,0:T(8,128)(2,1)}), bf16[4,512,256]{1,2,0:T(8,128)(2,1)}, u32[]{:S(2)}, u32[]{:S(2)}) async-start(bf16[4,512,256]{1,2,0:T(8,128)(2,1)} %copy.149), calls=%async_computation.1 | async-start | bytes 2097152 | tf_op jit(solution)/shard_map/all_to_all | solution.py:618
  193.1 132.4 %all-gather.14.cloned.1.call-start = ((), (), s32[]{:S(2)}) async-start(), calls=%async_computation.5 | async-start | bytes 7962624 | tf_op jit(solution)/shard_map/all_gather | solution.py:437
  218.8 10.0 %collective-permute-start.5 = (bf16[96,1536]{1,0:T(8,128)(2,1)}, bf16[96,1536]{1,0:T(8,128)(2,1)S(1)}, u32[]{:S(2)}, u32[]{:S(2)}) collective-permute-start(bf16[96,1536]{1,0:T(8,128)(2,1)} %pad_maximum_fusion.16), channel_id=1, source_target_pairs={{0,3},{1,0},{2,1},{3,2},{4,7},{5,4},{6,5},{7,6},{8,11},{9,8},{10,9... | collective-permute-start | bytes 884744 | tf_op jit(solution)/shard_map/ppermute | solution.py:431
  219.7 24.7 %collective-permute-start.4 = (bf16[96,1536]{1,0:T(8,128)(2,1)}, bf16[96,1536]{1,0:T(8,128)(2,1)S(1)}, u32[]{:S(2)}, u32[]{:S(2)}) collective-permute-start(bf16[96,1536]{1,0:T(8,128)(2,1)} %pad_maximum_fusion.16), channel_id=1, source_target_pairs={{0,2},{1,3},{2,0},{3,1},{4,6},{5,7},{6,4},{7,5},{8,10},{9,11},{10,... | collective-permute-start | bytes 884744 | tf_op jit(solution)/shard_map/ppermute | solution.py:431
  219.7 24.7 %collective-permute-start.3 = (bf16[96,1536]{1,0:T(8,128)(2,1)}, bf16[96,1536]{1,0:T(8,128)(2,1)S(1)}, u32[]{:S(2)}, u32[]{:S(2)}) collective-permute-start(bf16[96,1536]{1,0:T(8,128)(2,1)} %pad_maximum_fusion.16), channel_id=1, source_target_pairs={{0,1},{1,2},{2,3},{3,0},{4,5},{5,6},{6,7},{7,4},{8,9},{9,10},{10,1... | collective-permute-start | bytes 884744 | tf_op jit(solution)/shard_map/ppermute | solution.py:431
  285.5 31.8 %collective-permute-start.12 = (bf16[4,4,96,1536]{3,2,1,0:T(8,128)(2,1)}, bf16[4,4,96,1536]{3,2,1,0:T(8,128)(2,1)}, u32[]{:S(2)}, u32[]{:S(2)}) collective-permute-start(bf16[4,4,96,1536]{3,2,1,0:T(8,128)(2,1)} %get-tuple-element.85), channel_id=1, source_target_pairs={{0,4},{4,0},{8,12},{12,8},{16,20},{20,16},{24,28},{28,24},{1,5},{5... | collective-permute-start | bytes 14155784 | tf_op jit(solution)/shard_map/ppermute | solution.py:440
  316.9 44.8 %collective-permute-start.13 = (bf16[4,4,96,1536]{3,2,1,0:T(8,128)(2,1)}, bf16[4,4,96,1536]{3,2,1,0:T(8,128)(2,1)}, u32[]{:S(2)}, u32[]{:S(2)}) collective-permute-start(bf16[4,4,96,1536]{3,2,1,0:T(8,128)(2,1)} %get-tuple-element.91), channel_id=1, source_target_pairs={{0,4},{4,0},{8,12},{12,8},{16,20},{20,16},{24,28},{28,24},{1,5},{5... | collective-permute-start | bytes 14155784 | tf_op jit(solution)/shard_map/ppermute | solution.py:440
  320.2 36.6 %collective-permute-start.14 = (bf16[2,2,96,1536]{3,2,1,0:T(8,128)(2,1)}, bf16[2,2,96,1536]{3,2,1,0:T(8,128)(2,1)}, u32[]{:S(2)}, u32[]{:S(2)}) collective-permute-start(bf16[2,2,96,1536]{3,2,1,0:T(8,128)(2,1)} %fusion.30), channel_id=1, source_target_pairs={{0,8},{4,12},{8,0},{12,4},{16,24},{20,28},{24,16},{28,20},{1,9},{5... | collective-permute-start | bytes 3538952 | tf_op jit(solution)/shard_map/ppermute | solution.py:440
  324.7 32.2 %collective-permute-start.15 = (bf16[2,2,96,1536]{3,2,1,0:T(8,128)(2,1)}, bf16[2,2,96,1536]{3,2,1,0:T(8,128)(2,1)}, u32[]{:S(2)}, u32[]{:S(2)}) collective-permute-start(bf16[2,2,96,1536]{3,2,1,0:T(8,128)(2,1)} %fusion.31), channel_id=1, source_target_pairs={{0,16},{4,20},{8,24},{12,28},{16,0},{20,4},{24,8},{28,12},{1,17},{... | collective-permute-start | bytes 3538952 | tf_op jit(solution)/shard_map/ppermute | solution.py:440
  356.8 61.6 %collective-permute-start.16 = (bf16[4,4,96,1536]{3,2,1,0:T(8,128)(2,1)}, bf16[4,4,96,1536]{3,2,1,0:T(8,128)(2,1)}, u32[]{:S(2)}, u32[]{:S(2)}) collective-permute-start(bf16[4,4,96,1536]{3,2,1,0:T(8,128)(2,1)} %get-tuple-element.97), channel_id=1, source_target_pairs={{0,4},{4,0},{8,12},{12,8},{16,20},{20,16},{24,28},{28,24},{1,5},{5... | collective-permute-start | bytes 14155784 | tf_op jit(solution)/shard_map/ppermute | solution.py:440
  360.5 19.8 %collective-permute-start.19 = (bf16[2,96,1536]{2,1,0:T(8,128)(2,1)}, bf16[2,96,1536]{2,1,0:T(8,128)(2,1)}, u32[]{:S(2)}, u32[]{:S(2)}) collective-permute-start(bf16[2,96,1536]{2,1,0:T(8,128)(2,1)} %get-tuple-element.164), channel_id=1, source_target_pairs={{0,16},{4,20},{8,24},{12,28},{16,0},{20,4},{24,8},{28,12},{1,17},{... | collective-permute-start | bytes 1769480 | tf_op jit(solution)/shard_map/ppermute | solution.py:440
  368.0 50.4 %all-to-all-start.2 = ((bf16[4,512,256]{2,1,0:T(8,128)(2,1)}), bf16[4,512,256]{2,1,0:T(8,128)(2,1)}, u32[]{:S(2)}, u32[]{:S(2)}) async-start(bf16[4,512,256]{2,1,0:T(8,128)(2,1)} %bitcast.547), calls=%async_computation.2 | async-start | bytes 2097152 | tf_op jit(solution)/shard_map/all_to_all | solution.py:618
  376.8 40.5 %collective-permute-start.17 = (bf16[2,2,96,1536]{3,2,1,0:T(8,128)(2,1)S(1)}, bf16[2,2,96,1536]{3,2,1,0:T(8,128)(2,1)}, u32[]{:S(2)}, u32[]{:S(2)}) collective-permute-start(bf16[2,2,96,1536]{3,2,1,0:T(8,128)(2,1)S(1)} %fusion.32), channel_id=1, source_target_pairs={{0,8},{4,12},{8,0},{12,4},{16,24},{20,28},{24,16},{28,20},{1,9},{5... | collective-permute-start | bytes 3538952 | tf_op jit(solution)/shard_map/ppermute | solution.py:440
  377.4 41.0 %collective-permute-start.18 = (bf16[2,2,96,1536]{3,2,1,0:T(8,128)(2,1)S(1)}, bf16[2,2,96,1536]{3,2,1,0:T(8,128)(2,1)}, u32[]{:S(2)}, u32[]{:S(2)}) collective-permute-start(bf16[2,2,96,1536]{3,2,1,0:T(8,128)(2,1)S(1)} %fusion.33), channel_id=1, source_target_pairs={{0,16},{4,20},{8,24},{12,28},{16,0},{20,4},{24,8},{28,12},{1,17},{... | collective-permute-start | bytes 3538952 | tf_op jit(solution)/shard_map/ppermute | solution.py:440
  380.2 37.1 %collective-permute-start.21 = (bf16[4,4,32,1024]{3,2,1,0:T(8,128)(2,1)S(1)}, bf16[4,4,32,1024]{3,2,1,0:T(8,128)(2,1)S(1)}, u32[]{:S(2)}, u32[]{:S(2)}) collective-permute-start(bf16[4,4,32,1024]{3,2,1,0:T(8,128)(2,1)S(1)} %bitcast.574), channel_id=1, source_target_pairs={{0,4},{4,0},{8,12},{12,8},{16,20},{20,16},{24,28},{28,24},{1,5},{5... | collective-permute-start | bytes 3145736 | tf_op jit(solution)/shard_map/ppermute | solution.py:440
  381.1 36.2 %collective-permute-start.20 = (bf16[2,96,1536]{2,1,0:T(8,128)(2,1)S(1)}, bf16[2,96,1536]{2,1,0:T(8,128)(2,1)S(1)}, u32[]{:S(2)}, u32[]{:S(2)}) collective-permute-start(bf16[2,96,1536]{2,1,0:T(8,128)(2,1)S(1)} %copy-done.44), channel_id=1, source_target_pairs={{0,8},{4,12},{8,0},{12,4},{16,24},{20,28},{24,16},{28,20},{1,9},{5... | collective-permute-start | bytes 1769480 | tf_op jit(solution)/shard_map/ppermute | solution.py:440
  427.3 39.4 %collective-permute-start.26 = (bf16[96,1536]{1,0:T(8,128)(2,1)S(1)}, bf16[96,1536]{1,0:T(8,128)(2,1)}, u32[]{:S(2)}, u32[]{:S(2)}) collective-permute-start(bf16[96,1536]{1,0:T(8,128)(2,1)S(1)} %fusion.80), channel_id=1, source_target_pairs={{0,3},{1,0},{2,1},{3,2},{4,7},{5,4},{6,5},{7,6},{8,11},{9,8},{10,9... | collective-permute-start | bytes 884744 | tf_op jit(solution)/shard_map/ppermute | solution.py:431
  431.9 35.4 %collective-permute-start.27 = (bf16[96,1536]{1,0:T(8,128)(2,1)S(1)}, bf16[96,1536]{1,0:T(8,128)(2,1)}, u32[]{:S(2)}, u32[]{:S(2)}) collective-permute-start(bf16[96,1536]{1,0:T(8,128)(2,1)S(1)} %get-tuple-element.217), channel_id=1, source_target_pairs={{0,2},{1,3},{2,0},{3,1},{4,6},{5,7},{6,4},{7,5},{8,10},{9,11},{10,... | collective-permute-start | bytes 884744 | tf_op jit(solution)/shard_map/ppermute | solution.py:431
  432.0 77.5 %collective-permute-start.22 = (bf16[2,2,96,1536]{3,2,1,0:T(8,128)(2,1)}, bf16[2,2,96,1536]{3,2,1,0:T(8,128)(2,1)}, u32[]{:S(2)}, u32[]{:S(2)}) collective-permute-start(bf16[2,2,96,1536]{3,2,1,0:T(8,128)(2,1)} %fusion.34), channel_id=1, source_target_pairs={{0,8},{4,12},{8,0},{12,4},{16,24},{20,28},{24,16},{28,20},{1,9},{5... | collective-permute-start | bytes 3538952 | tf_op jit(solution)/shard_map/ppermute | solution.py:440
  432.6 32.0 %collective-permute-start.29 = (bf16[2,2,32,1024]{3,2,1,0:T(8,128)(2,1)S(1)}, bf16[2,2,32,1024]{3,2,1,0:T(8,128)(2,1)S(1)}, u32[]{:S(2)}, u32[]{:S(2)}) collective-permute-start(bf16[2,2,32,1024]{3,2,1,0:T(8,128)(2,1)S(1)} %fusion.87), channel_id=1, source_target_pairs={{0,8},{4,12},{8,0},{12,4},{16,24},{20,28},{24,16},{28,20},{1,9},{5... | collective-permute-start | bytes 786440 | tf_op jit(solution)/shard_map/ppermute | solution.py:440
  434.1 31.7 %collective-permute-start.30 = (bf16[2,2,32,1024]{3,2,1,0:T(8,128)(2,1)S(1)}, bf16[2,2,32,1024]{3,2,1,0:T(8,128)(2,1)S(1)}, u32[]{:S(2)}, u32[]{:S(2)}) collective-permute-start(bf16[2,2,32,1024]{3,2,1,0:T(8,128)(2,1)S(1)} %fusion.88), channel_id=1, source_target_pairs={{0,16},{4,20},{8,24},{12,28},{16,0},{20,4},{24,8},{28,12},{1,17},{... | collective-permute-start | bytes 786440 | tf_op jit(solution)/shard_map/ppermute | solution.py:440
  464.7 44.9 %collective-permute-start.23 = (bf16[2,2,96,1536]{3,2,1,0:T(8,128)(2,1)}, bf16[2,2,96,1536]{3,2,1,0:T(8,128)(2,1)}, u32[]{:S(2)}, u32[]{:S(2)}) collective-permute-start(bf16[2,2,96,1536]{3,2,1,0:T(8,128)(2,1)} %fusion.35), channel_id=1, source_target_pairs={{0,16},{4,20},{8,24},{12,28},{16,0},{20,4},{24,8},{28,12},{1,17},{... | collective-permute-start | bytes 3538952 | tf_op jit(solution)/shard_map/ppermute | solution.py:440
  465.8 43.8 %collective-permute-start.24 = (bf16[2,96,1536]{2,1,0:T(8,128)(2,1)}, bf16[2,96,1536]{2,1,0:T(8,128)(2,1)}, u32[]{:S(2)}, u32[]{:S(2)}) collective-permute-start(bf16[2,96,1536]{2,1,0:T(8,128)(2,1)} %get-tuple-element.162), channel_id=1, source_target_pairs={{0,16},{4,20},{8,24},{12,28},{16,0},{20,4},{24,8},{28,12},{1,17},{... | collective-permute-start | bytes 1769480 | tf_op jit(solution)/shard_map/ppermute | solution.py:440
  466.7 42.9 %collective-permute-start.25 = (bf16[2,96,1536]{2,1,0:T(8,128)(2,1)}, bf16[2,96,1536]{2,1,0:T(8,128)(2,1)}, u32[]{:S(2)}, u32[]{:S(2)}) collective-permute-start(bf16[2,96,1536]{2,1,0:T(8,128)(2,1)} %get-tuple-element.161), channel_id=1, source_target_pairs={{0,8},{4,12},{8,0},{12,4},{16,24},{20,28},{24,16},{28,20},{1,9},{5... | collective-permute-start | bytes 1769480 | tf_op jit(solution)/shard_map/ppermute | solution.py:440
  467.3 42.3 %collective-permute-start.28 = (bf16[96,1536]{1,0:T(8,128)(2,1)}, bf16[96,1536]{1,0:T(8,128)(2,1)}, u32[]{:S(2)}, u32[]{:S(2)}) collective-permute-start(bf16[96,1536]{1,0:T(8,128)(2,1)} %get-tuple-element.216), channel_id=1, source_target_pairs={{0,1},{1,2},{2,3},{3,0},{4,5},{5,6},{6,7},{7,4},{8,9},{9,10},{10,1... | collective-permute-start | bytes 884744 | tf_op jit(solution)/shard_map/ppermute | solution.py:431
  513.7 63.7 %all-to-all-start.3 = ((bf16[4,512,512]{1,2,0:T(8,128)(2,1)}), bf16[4,512,512]{1,2,0:T(8,128)(2,1)}, u32[]{:S(2)}, u32[]{:S(2)}) async-start(bf16[4,512,512]{1,2,0:T(8,128)(2,1)} %copy.159), calls=%async_computation.3 | async-start | bytes 4194304 | tf_op jit(solution)/shard_map/all_to_all | solution.py:618
  518.2 228.7 %all-gather.22.cloned.1.call-start = ((), (), s32[]{:S(2)}) async-start(), calls=%async_computation.9 | async-start | bytes 2654208 | tf_op jit(solution)/shard_map/all_gather | solution.py:437
  532.8 20.8 %collective-permute-start.31 = (bf16[2,96,1536]{2,1,0:T(8,128)(2,1)}, bf16[2,96,1536]{2,1,0:T(8,128)(2,1)}, u32[]{:S(2)}, u32[]{:S(2)}) collective-permute-start(bf16[2,96,1536]{2,1,0:T(8,128)(2,1)} %get-tuple-element.158), channel_id=1, source_target_pairs={{0,16},{4,20},{8,24},{12,28},{16,0},{20,4},{24,8},{28,12},{1,17},{... | collective-permute-start | bytes 1769480 | tf_op jit(solution)/shard_map/ppermute | solution.py:440
  533.9 19.7 %collective-permute-start.32 = (bf16[2,96,1536]{2,1,0:T(8,128)(2,1)}, bf16[2,96,1536]{2,1,0:T(8,128)(2,1)}, u32[]{:S(2)}, u32[]{:S(2)}) collective-permute-start(bf16[2,96,1536]{2,1,0:T(8,128)(2,1)} %get-tuple-element.157), channel_id=1, source_target_pairs={{0,8},{4,12},{8,0},{12,4},{16,24},{20,28},{24,16},{28,20},{1,9},{5... | collective-permute-start | bytes 1769480 | tf_op jit(solution)/shard_map/ppermute | solution.py:440
  537.4 14.6 %collective-permute-start.33 = (bf16[2,32,1024]{2,1,0:T(8,128)(2,1)}, bf16[2,32,1024]{2,1,0:T(8,128)(2,1)}, u32[]{:S(2)}, u32[]{:S(2)}) collective-permute-start(bf16[2,32,1024]{2,1,0:T(8,128)(2,1)} %get-tuple-element.187), channel_id=1, source_target_pairs={{0,16},{4,20},{8,24},{12,28},{16,0},{20,4},{24,8},{28,12},{1,17},{... | collective-permute-start | bytes 393224 | tf_op jit(solution)/shard_map/ppermute | solution.py:440
  538.3 13.8 %collective-permute-start.34 = (bf16[2,32,1024]{2,1,0:T(8,128)(2,1)}, bf16[2,32,1024]{2,1,0:T(8,128)(2,1)}, u32[]{:S(2)}, u32[]{:S(2)}) collective-permute-start(bf16[2,32,1024]{2,1,0:T(8,128)(2,1)} %get-tuple-element.186), channel_id=1, source_target_pairs={{0,8},{4,12},{8,0},{12,4},{16,24},{20,28},{24,16},{28,20},{1,9},{5... | collective-permute-start | bytes 393224 | tf_op jit(solution)/shard_map/ppermute | solution.py:440
  544.3 104.9 %collective-permute-start.35 = (bf16[96,1536]{1,0:T(8,128)(2,1)}, bf16[96,1536]{1,0:T(8,128)(2,1)}, u32[]{:S(2)}, u32[]{:S(2)}) collective-permute-start(bf16[96,1536]{1,0:T(8,128)(2,1)} %fusion.81), channel_id=1, source_target_pairs={{0,3},{1,0},{2,1},{3,2},{4,7},{5,4},{6,5},{7,6},{8,11},{9,8},{10,9... | collective-permute-start | bytes 884744 | tf_op jit(solution)/shard_map/ppermute | solution.py:431
  552.0 195.0 %all-gather.24.cloned.1.call-start = ((), (), s32[]{:S(2)}) async-start(), calls=%async_computation.10 | async-start | bytes 2654208 | tf_op jit(solution)/shard_map/all_gather | solution.py:437
  552.0 97.2 %collective-permute-start.36 = (bf16[96,1536]{1,0:T(8,128)(2,1)}, bf16[96,1536]{1,0:T(8,128)(2,1)}, u32[]{:S(2)}, u32[]{:S(2)}) collective-permute-start(bf16[96,1536]{1,0:T(8,128)(2,1)} %get-tuple-element.215), channel_id=1, source_target_pairs={{0,2},{1,3},{2,0},{3,1},{4,6},{5,7},{6,4},{7,5},{8,10},{9,11},{10,... | collective-permute-start | bytes 884744 | tf_op jit(solution)/shard_map/ppermute | solution.py:431
  552.1 99.1 %collective-permute-start.37 = (bf16[96,1536]{1,0:T(8,128)(2,1)}, bf16[96,1536]{1,0:T(8,128)(2,1)}, u32[]{:S(2)}, u32[]{:S(2)}) collective-permute-start(bf16[96,1536]{1,0:T(8,128)(2,1)} %get-tuple-element.214), channel_id=1, source_target_pairs={{0,1},{1,2},{2,3},{3,0},{4,5},{5,6},{6,7},{7,4},{8,9},{9,10},{10,1... | collective-permute-start | bytes 884744 | tf_op jit(solution)/shard_map/ppermute | solution.py:431
  637.4 16.7 %collective-permute-start.41 = (bf16[32,1024]{1,0:T(8,128)(2,1)S(1)}, bf16[32,1024]{1,0:T(8,128)(2,1)S(1)}, u32[]{:S(2)}, u32[]{:S(2)}) collective-permute-start(bf16[32,1024]{1,0:T(8,128)(2,1)S(1)} %fusion.104), channel_id=1, source_target_pairs={{0,3},{1,0},{2,1},{3,2},{4,7},{5,4},{6,5},{7,6},{8,11},{9,8},{10,9... | collective-permute-start | bytes 196616 | tf_op jit(solution)/shard_map/ppermute | solution.py:431
  649.1 26.7 %collective-permute-start.38 = (bf16[96,1536]{1,0:T(8,128)(2,1)S(1)}, bf16[96,1536]{1,0:T(8,128)(2,1)S(1)}, u32[]{:S(2)}, u32[]{:S(2)}) collective-permute-start(bf16[96,1536]{1,0:T(8,128)(2,1)S(1)} %fusion.82), channel_id=1, source_target_pairs={{0,3},{1,0},{2,1},{3,2},{4,7},{5,4},{6,5},{7,6},{8,11},{9,8},{10,9... | collective-permute-start | bytes 884744 | tf_op jit(solution)/shard_map/ppermute | solution.py:431
  649.2 26.6 %collective-permute-start.39 = (bf16[96,1536]{1,0:T(8,128)(2,1)S(1)}, bf16[96,1536]{1,0:T(8,128)(2,1)S(1)}, u32[]{:S(2)}, u32[]{:S(2)}) collective-permute-start(bf16[96,1536]{1,0:T(8,128)(2,1)S(1)} %get-tuple-element.213), channel_id=1, source_target_pairs={{0,2},{1,3},{2,0},{3,1},{4,6},{5,7},{6,4},{7,5},{8,10},{9,11},{10,... | collective-permute-start | bytes 884744 | tf_op jit(solution)/shard_map/ppermute | solution.py:431
  649.3 26.6 %collective-permute-start.40 = (bf16[96,1536]{1,0:T(8,128)(2,1)S(1)}, bf16[96,1536]{1,0:T(8,128)(2,1)}, u32[]{:S(2)}, u32[]{:S(2)}) collective-permute-start(bf16[96,1536]{1,0:T(8,128)(2,1)S(1)} %get-tuple-element.212), channel_id=1, source_target_pairs={{0,1},{1,2},{2,3},{3,0},{4,5},{5,6},{6,7},{7,4},{8,9},{9,10},{10,1... | collective-permute-start | bytes 884744 | tf_op jit(solution)/shard_map/ppermute | solution.py:431
  651.2 24.6 %collective-permute-start.42 = (bf16[32,1024]{1,0:T(8,128)(2,1)S(1)}, bf16[32,1024]{1,0:T(8,128)(2,1)S(1)}, u32[]{:S(2)}, u32[]{:S(2)}) collective-permute-start(bf16[32,1024]{1,0:T(8,128)(2,1)S(1)} %get-tuple-element.227), channel_id=1, source_target_pairs={{0,2},{1,3},{2,0},{3,1},{4,6},{5,7},{6,4},{7,5},{8,10},{9,11},{10,... | collective-permute-start | bytes 196616 | tf_op jit(solution)/shard_map/ppermute | solution.py:431
  654.1 21.7 %collective-permute-start.43 = (bf16[32,1024]{1,0:T(8,128)(2,1)S(1)}, bf16[32,1024]{1,0:T(8,128)(2,1)S(1)}, u32[]{:S(2)}, u32[]{:S(2)}) collective-permute-start(bf16[32,1024]{1,0:T(8,128)(2,1)S(1)} %get-tuple-element.226), channel_id=1, source_target_pairs={{0,1},{1,2},{2,3},{3,0},{4,5},{5,6},{6,7},{7,4},{8,9},{9,10},{10,1... | collective-permute-start | bytes 196616 | tf_op jit(solution)/shard_map/ppermute | solution.py:431
  678.0 69.0 %all-gather.26.cloned.1.call-start = ((), (), s32[]{:S(2)}) async-start(), calls=%async_computation.11 | async-start | bytes 2654208 | tf_op jit(solution)/shard_map/all_gather | solution.py:437
  681.0 4.4 collective-permute-start.44
  685.6 17.8 %collective-permute-start.48 = (bf16[2,2,32,2176]{3,2,1,0:T(8,128)(2,1)S(1)}, bf16[2,2,32,2176]{3,2,1,0:T(8,128)(2,1)}, u32[]{:S(2)}, u32[]{:S(2)}) collective-permute-start(bf16[2,2,32,2176]{3,2,1,0:T(8,128)(2,1)S(1)} %fusion.71), channel_id=1, source_target_pairs={{0,16},{4,20},{8,24},{12,28},{16,0},{20,4},{24,8},{28,12},{1,17},{... | collective-permute-start | bytes 1671176 | tf_op jit(solution)/shard_map/ppermute | solution.py:440
  687.7 17.8 %collective-permute-start.45 = (bf16[2,2,32,2176]{3,2,1,0:T(8,128)(2,1)}, bf16[2,2,32,2176]{3,2,1,0:T(8,128)(2,1)}, u32[]{:S(2)}, u32[]{:S(2)}) collective-permute-start(bf16[2,2,32,2176]{3,2,1,0:T(8,128)(2,1)} %fusion.70), channel_id=1, source_target_pairs={{0,8},{4,12},{8,0},{12,4},{16,24},{20,28},{24,16},{28,20},{1,9},{5... | collective-permute-start | bytes 1671176 | tf_op jit(solution)/shard_map/ppermute | solution.py:440
  691.3 77.2 %all-gather.20.cloned.1.call-start = ((), (), s32[]{:S(2)}) async-start(), calls=%async_computation.8 | async-start | bytes 1253376 | tf_op jit(solution)/shard_map/all_gather | solution.py:437
  707.1 7.5 collective-permute-start.49
  709.7 6.5 collective-permute-start.46
  717.9 7.7 collective-permute-start.51
  718.0 10.7 %collective-permute-start.50 = (bf16[32,2176]{1,0:T(8,128)(2,1)S(1)}, bf16[32,2176]{1,0:T(8,128)(2,1)S(1)}, u32[]{:S(2)}, u32[]{:S(2)}) collective-permute-start(bf16[32,2176]{1,0:T(8,128)(2,1)S(1)} %get-tuple-element.218), channel_id=1, source_target_pairs={{0,2},{1,3},{2,0},{3,1},{4,6},{5,7},{6,4},{7,5},{8,10},{9,11},{10,... | collective-permute-start | bytes 417800 | tf_op jit(solution)/shard_map/ppermute | solution.py:431
  719.7 8.9 %collective-permute-start.47 = (bf16[32,2176]{1,0:T(8,128)(2,1)S(1)}, bf16[32,2176]{1,0:T(8,128)(2,1)S(1)}, u32[]{:S(2)}, u32[]{:S(2)}) collective-permute-start(bf16[32,2176]{1,0:T(8,128)(2,1)S(1)} %fusion.97), channel_id=1, source_target_pairs={{0,3},{1,0},{2,1},{3,2},{4,7},{5,4},{6,5},{7,6},{8,11},{9,8},{10,9... | collective-permute-start | bytes 417800 | tf_op jit(solution)/shard_map/ppermute | solution.py:431
  (93 other events, 695.7 us)
Sparse Core Ops, SparseCore 0:
  32.6 45.9 all-gather.11
  101.0 48.8 all-gather.17
  186.2 48.9 all-gather.15
  245.5 49.0 all-gather.13
  552.1 26.8 all-gather.21
  678.1 32.7 all-gather.23
  713.4 29.6 all-gather.25
  745.0 23.4 all-gather.19

commit v2 on v1

v2 whole, which is shorter than its diff:
```python
import functools
import math

import jax
import jax.numpy as jnp
from jax import lax
from jax.experimental import pallas as pl
from jax.experimental.pallas import tpu as pltpu
from jax.sharding import PartitionSpec as P

H = 16
KV = 8
HD = 64
EPS = 1e-05
ROPE_BASE = 1000000.0
LOG2E = math.log2(math.e)
SPLIT = 8
CHUNKS = 3

f32 = jnp.float32
bf16 = jnp.bfloat16
NN = (((1,), (0,)), ((), ()))
NT = (((1,), (1,)), ((), ()))
TN = (((0,), (0,)), ((), ()))


def dot(left, right, dims=NN):
    return lax.dot_general(left, right, dims, preferred_element_type=f32)


def rms_scale(values):
    return lax.rsqrt(jnp.mean(values * values, axis=-1, keepdims=True) + EPS)


def norm_back(grads, normed, scale):
    return scale * (grads - normed * jnp.mean(grads * normed, axis=-1, keepdims=True))


def tables(positions):
    half = HD // 2
    freq = ROPE_BASE ** (-(jnp.arange(half, dtype=f32) * 2.0 / HD))
    angle = positions.astype(f32)[:, None] * freq[None, :]
    cosine, sine = jnp.cos(angle), jnp.sin(angle)
    return jnp.tile(cosine, (1, 4)), jnp.concatenate([-sine, sine, -sine, sine], axis=1)


def lanes_of(x):
    return lax.broadcasted_iota(jnp.int32, x.shape, 1)


def pair_mean(x):
    row = lax.broadcasted_iota(jnp.int32, (2 * HD, 2 * HD), 0)
    same = (row < HD) == (lax.broadcasted_iota(jnp.int32, (2 * HD, 2 * HD), 1) < HD)
    ones = jnp.where(same, 1.0 / HD, 0.0).astype(bf16)
    high = x.astype(bf16)
    return dot(high, ones) + dot((x - high.astype(f32)).astype(bf16), ones)


def other_half(x):
    low = lax.rem(lanes_of(x), HD) < HD // 2
    return jnp.where(low, pltpu.roll(x, 3 * HD // 2, 1), pltpu.roll(x, HD // 2, 1))


def pair_half(x, first):
    lane = lax.broadcasted_iota(jnp.int32, x.shape, 1)
    rolled = pltpu.roll(x.astype(f32), HD, 1).astype(x.dtype)
    return jnp.where((lane < HD) == first, x, rolled)


def stack_pair(x):
    lane = lax.broadcasted_iota(jnp.int32, x.shape, 1)
    zero = jnp.zeros_like(x)
    return jnp.concatenate([jnp.where(lane < HD, x, zero), jnp.where(lane < HD, zero, x)], axis=0)


def causal(probs, block):
    key = lax.broadcasted_iota(jnp.int32, probs.shape, 0)
    query = lax.broadcasted_iota(jnp.int32, probs.shape, 1)
    query = jnp.where(query >= block, query - block, query)
    return jnp.where(key <= query, probs, 0.0)


def attend_fwd_kernel(block, q_ref, k_ref, v_ref, o_ref, lse_ref, keys, values):
    first = pl.program_id(0) % 2 == 0
    i = pl.program_id(1)

    @pl.when(i == 0)
    def _():
        keys[...] = pair_half(k_ref[...], first)
        values[...] = pair_half(v_ref[...], first)

    queries = stack_pair(q_ref[...])

    def tile(t, diagonal):
        rows = pl.ds(t * block, block)
        probs = jnp.exp2(dot(keys[rows, :], queries, NT) * (HD**-0.5 * LOG2E))
        if diagonal:
            probs = causal(probs, block)
        return dot(values[rows, :], probs.astype(bf16), TN), jnp.sum(probs, axis=0, keepdims=True)

    def body(t, carry):
        part, total = tile(t, False)
        return carry[0] + part, carry[1] + total

    mixed, total = lax.fori_loop(0, i, body, tile(i, True))
    mixed = mixed * (1.0 / total)
    pair = jnp.concatenate([mixed[:HD, :block], mixed[HD:, block:]], axis=0)
    o_ref[...] = pair.T.astype(bf16)
    lse_ref[0, 0] = jnp.log2(total)


def attend_forward(qkv, block):
    length, width = qkv.shape
    kv = width // (4 * HD)
    n = length // block
    key_at = lambda j, i: (0, kv + j // 2)
    value_at = lambda j, i: (0, kv + kv // 2 + j // 2)
    return pl.pallas_call(
        functools.partial(attend_fwd_kernel, block),
        grid=(kv, n),
        in_specs=[
            pl.BlockSpec((block, 2 * HD), lambda j, i: (i, j)),
            pl.BlockSpec((length, 2 * HD), key_at),
            pl.BlockSpec((length, 2 * HD), value_at),
        ],
        out_specs=[
            pl.BlockSpec((block, 2 * HD), lambda j, i: (i, j)),
            pl.BlockSpec((1, 1, 1, 2 * block), lambda j, i: (j, i, 0, 0)),
        ],
        out_shape=[
            jax.ShapeDtypeStruct((length, width // 2), bf16),
            jax.ShapeDtypeStruct((kv, n, 1, 2 * block), f32),
        ],
        scratch_shapes=[pltpu.VMEM((length, 2 * HD), bf16), pltpu.VMEM((length, 2 * HD), bf16)],
        cost_estimate=pl.CostEstimate(
            flops=8 * length * length * 2 * HD * kv,
            transcendentals=length * length * kv,
            bytes_accessed=3 * length * width,
        ),
        name="attend_forward",
    )(qkv, qkv, qkv)


def attend_bwd_kernel(
    block, kv, q_ref, k_ref, v_ref, g_ref, o_ref, lse_ref, back_ref,
    queries, grads, delta, keys, values, grad_q,
):
    j = pl.program_id(0)
    first = j % 2 == 0
    n = q_ref.shape[0] // block
    at_k = pl.ds(pl.multiple_of((kv + j // 2) * 2 * HD, 2 * HD), 2 * HD)
    at_v = pl.ds(pl.multiple_of((kv + kv // 2 + j // 2) * 2 * HD, 2 * HD), 2 * HD)
    keys[...] = pair_half(k_ref[...], first)
    values[...] = pair_half(v_ref[...], first)
    for i in range(n):
        rows = slice(i * block, (i + 1) * block)
        g = g_ref[rows, :]
        queries[i] = stack_pair(q_ref[rows, :])
        grads[i] = stack_pair(g)
        both = (g.astype(f32) * o_ref[rows, :].astype(f32)).T
        delta[i] = jnp.concatenate(
            [jnp.sum(both[:HD], axis=0, keepdims=True), jnp.sum(both[HD:], axis=0, keepdims=True)],
            axis=1,
        )
        grad_q[i] = jnp.zeros(grad_q.shape[1:], f32)

    def tile(key, value, key_t, i, diagonal):
        query, grad = queries[i], grads[i]
        probs = jnp.exp2(dot(key, query, NT) * (HD**-0.5 * LOG2E) - lse_ref[0, i])
        if diagonal:
            probs = causal(probs, block)
        grad_probs = dot(value, grad, NT)
        grad_scores = (probs * (grad_probs - delta[i]) * HD**-0.5).astype(bf16)
        grad_q[i] += dot(key_t, grad_scores)
        return dot(grad_scores, query), dot(probs.astype(bf16), grad)

    def step(t, _):
        rows = pl.ds(t * block, block)
        key, value = keys[rows, :], values[rows, :]
        key_t = key.astype(f32).T.astype(bf16)

        def body(i, carry):
            part_k, part_v = tile(key, value, key_t, i, False)
            return carry[0] + part_k, carry[1] + part_v

        part_k, part_v = lax.fori_loop(t + 1, n, body, tile(key, value, key_t, t, True))
        part_k = (part_k + pltpu.roll(part_k, HD, 1)).astype(bf16)
        part_v = (part_v + pltpu.roll(part_v, HD, 1)).astype(bf16)

        @pl.when(first)
        def _():
            back_ref[rows, at_k] = part_k
            back_ref[rows, at_v] = part_v

        @pl.when(jnp.logical_not(first))
        def _():
            upper = lax.broadcasted_iota(jnp.int32, part_k.shape, 1) >= HD
            back_ref[rows, at_k] = jnp.where(upper, part_k, back_ref[rows, at_k])
            back_ref[rows, at_v] = jnp.where(upper, part_v, back_ref[rows, at_v])

        return 0

    lax.fori_loop(0, n, step, 0)
    for i in range(n):
        pair = jnp.concatenate([grad_q[i, :HD, :block], grad_q[i, HD:, block:]], axis=0)
        at_q = pl.ds(pl.multiple_of(j * 2 * HD, 2 * HD), 2 * HD)
        back_ref[i * block : (i + 1) * block, at_q] = pair.T.astype(bf16)


def attend_backward(qkv, grads, mixed, lse, block):
    length, width = qkv.shape
    kv = width // (4 * HD)
    n = length // block
    spec = lambda at: pl.BlockSpec((length, 2 * HD), at)
    at_q = lambda j: (0, j)
    return pl.pallas_call(
        functools.partial(attend_bwd_kernel, block, kv),
        grid=(kv,),
        in_specs=[
            spec(at_q),
            spec(lambda j: (0, kv + j // 2)),
            spec(lambda j: (0, kv + kv // 2 + j // 2)),
            spec(at_q),
            spec(at_q),
            pl.BlockSpec((1, n, 1, 2 * block), lambda j: (j, 0, 0, 0)),
        ],
        out_specs=pl.BlockSpec((length, width), lambda j: (0, 0)),
        out_shape=jax.ShapeDtypeStruct((length, width), bf16),
        scratch_shapes=[
            pltpu.VMEM((n, 2 * block, 2 * HD), bf16),
            pltpu.VMEM((n, 2 * block, 2 * HD), bf16),
            pltpu.VMEM((n, 1, 2 * block), f32),
            pltpu.VMEM((length, 2 * HD), bf16),
            pltpu.VMEM((length, 2 * HD), bf16),
            pltpu.VMEM((n, 2 * HD, 2 * block), f32),
        ],
        cost_estimate=pl.CostEstimate(
            flops=20 * length * length * 2 * HD * kv,
            transcendentals=length * length * kv,
            bytes_accessed=6 * length * width,
        ),
        name="attend_backward",
    )(qkv, qkv, qkv, grads, mixed, lse)


def ffn_kernel(
    shards, begins, z_ref, h_ref, ht_ref, gy_ref, own_g, own_u, own_d, far_g, far_u, far_d,
    out_in, grad_in, out_ref, grad_ref, *refs,
):
    terms, down = refs[:-1], refs[-1]
    t = pl.program_id(0)
    z = z_ref[0]
    even = z_ref[1] == 0
    rows = own_g.shape[0]
    piece = rows // SPLIT
    unit = own_g.shape[1]
    lanes = down.shape[1] // SPLIT
    blocks = unit // piece

    @pl.when(t == 0)
    def _():
        out_ref[...] = out_in[...]
        grad_ref[...] = jnp.zeros_like(grad_ref) if begins else grad_in[...]
        down[...] = own_d[...]

    @pl.when(t > 0)
    def _():
        for d in range(SPLIT):
            for k in range(blocks):
                down[k * piece : (k + 1) * piece, d * lanes : (d + 1) * lanes] = far_d[
                    d, 0, 0, :, k * lanes : (k + 1) * lanes
                ]

    def shard_of(r):
        return lax.rem(z + shards - r, shards)

    def columns(r):
        return pl.ds(pl.multiple_of(shard_of(r) * rows, rows), rows)

    def weight(own, far, r):
        return own[...] if r == 0 else far[:, r - 1, 0].reshape(rows, unit)

    gate = up = None
    for r in range(shards):
        left = h_ref[:, columns(r)]
        part_g, part_u = dot(left, weight(own_g, far_g, r)), dot(left, weight(own_u, far_u, r))
        gate, up = (part_g, part_u) if r == 0 else (gate + part_g, up + part_u)
    grad_inner = dot(gy_ref[...], down[...], NT)
    sigma = jax.nn.sigmoid(gate)
    active = gate * sigma
    inner = (active * up).astype(bf16)
    grad_g = (grad_inner * up * sigma * (1.0 + gate * (1.0 - sigma))).astype(bf16)
    grad_u = (grad_inner * active).astype(bf16)
    out_ref[...] += dot(inner, down[...])
    seg = pl.ds(pl.multiple_of(shard_of(t) * unit, unit), unit)

    def keep(term, r, at):
        term = term.astype(bf16)
        if len(terms) == 1:
            terms[0][:, r, at : at + piece, seg] = term.reshape(SPLIT, piece, unit)
            return
        mine, theirs = terms
        term = term.reshape(SPLIT // 2, 2, piece, unit)
        mine[:, r, at : at + piece, seg] = jnp.where(even, term[:, 0], term[:, 1])
        theirs[:, r, at : at + piece, seg] = jnp.where(even, term[:, 1], term[:, 0])

    for r in range(shards):
        grad_ref[:, columns(r)] += dot(grad_g, weight(own_g, far_g, r), NT) + dot(
            grad_u, weight(own_u, far_u, r), NT
        )
        left = ht_ref[columns(r), :]
        keep(dot(left, grad_g), r, 0)
        keep(dot(left, grad_u), r, piece)
    term = dot(inner, gy_ref[...], TN).astype(bf16)
    for d in range(SPLIT):
        for k in range(blocks):
            part = term[k * piece : (k + 1) * piece, d * lanes : (d + 1) * lanes]
            to = (t, slice(2 * piece, 3 * piece), slice(k * lanes, (k + 1) * lanes))
            if len(terms) == 1:
                terms[0][(d, *to)] = part
            elif d % 2 == 0:
                even_part = part
            else:
                even_part = term[k * piece : (k + 1) * piece, (d - 1) * lanes : d * lanes]
                terms[0][(d // 2, *to)] = jnp.where(even, even_part, part)
                terms[1][(d // 2, *to)] = jnp.where(even, part, even_part)


def ffn_chunk(c, kind, parted, z, hidden, hidden_t, grad_y, w_gate, w_up, w_down, far, out_in, grad_in):
    rows, width = hidden.shape
    shards = width // w_gate.shape[0]
    depth = w_gate.shape[0]
    unit = w_down.shape[0] // CHUNKS
    piece = depth // SPLIT
    far = far.reshape(SPLIT, shards - 1, -1, piece, shards * unit)
    terms = (SPLIT // 2 if parted else SPLIT, shards, 3 * piece, shards * unit)
    n_terms = 2 if parted else 1
    seg = lambda t, z_ref: lax.rem(z_ref[0] + shards - t, shards)
    whole = lambda shape: pl.BlockSpec(shape, lambda t, z_ref: (0,) * len(shape))
    own = pl.BlockSpec((depth, unit), lambda t, z_ref: (0, seg(t, z_ref) * CHUNKS + c))
    gathered = lambda at: pl.BlockSpec(
        (SPLIT, shards - 1, 1, piece, unit), lambda t, z_ref: (0, 0, at, 0, seg(t, z_ref))
    )
    return pl.pallas_call(
        functools.partial(ffn_kernel, shards, c == 0),
        grid_spec=pltpu.PrefetchScalarGridSpec(
            num_scalar_prefetch=1,
            grid=(shards,),
            in_specs=[
                whole((rows, width)),
                whole((width, rows)),
                whole((rows, width)),
                own,
                own,
                pl.BlockSpec((unit, width), lambda t, z_ref: (c, 0)),
                gathered(kind),
                gathered(kind + 1),
                pl.BlockSpec(
                    (SPLIT, 1, 1, piece, shards * unit),
                    lambda t, z_ref: (0, jnp.maximum(t - 1, 0), kind + 2, 0, 0),
                ),
                whole((rows, width)),
                whole((rows, width)),
            ],
            out_specs=[
                whole((rows, width)),
                whole((rows, width)),
            ]
            + [whole(terms)] * n_terms,
            scratch_shapes=[pltpu.VMEM((unit, width), bf16)],
        ),
        out_shape=[
            jax.ShapeDtypeStruct((rows, width), f32),
            jax.ShapeDtypeStruct((rows, width), f32),
        ]
        + [jax.ShapeDtypeStruct(terms, bf16)] * n_terms,
        cost_estimate=pl.CostEstimate(
            flops=18 * rows * width * shards * unit,
            transcendentals=rows * shards * unit,
            bytes_accessed=12 * width * shards * unit + 20 * rows * width,
        ),
        name="ffn_chunk",
    )(z, hidden, hidden_t, grad_y, w_gate, w_up, w_down, far, far, far, out_in, grad_in)


def pack_kernel(m_ref, gate, up, down, out, first_ref, last_ref):
    piece, width = out.shape
    unit = down.shape[0] // CHUNKS
    shards = gate.shape[1] // down.shape[0]
    lanes = down.shape[1]
    for c in range(CHUNKS):
        ref = last_ref if c == CHUNKS - 1 else first_ref
        at = 0 if c == CHUNKS - 1 else 3 * piece * c
        for s in range(shards):
            source = slice((s * CHUNKS + c) * unit, (s * CHUNKS + c + 1) * unit)
            ref[at : at + piece, s * unit : (s + 1) * unit] = gate[:, source]
            ref[at + piece : at + 2 * piece, s * unit : (s + 1) * unit] = up[:, source]
        for k in range(unit // piece):
            rows = slice(c * unit + k * piece, c * unit + (k + 1) * piece)
            ref[at + 2 * piece : at + 3 * piece, k * lanes : (k + 1) * lanes] = down[rows, :]
    at = 3 * piece * (CHUNKS - 1)
    first_ref[at:, :width] = out[...]
    first_ref[at:, width:] = jnp.zeros_like(first_ref[at:, width:])


def pack(member, w_gate, w_up, w_down, w_out):
    depth, width = w_out.shape
    piece = depth // SPLIT
    lanes = width // SPLIT
    line = w_gate.shape[1] // CHUNKS
    rows = lambda w: pl.BlockSpec((piece, w.shape[1]), lambda i, m_ref: (m_ref[0], 0))
    outs = [((3 * CHUNKS - 2) * piece, line), (3 * piece, line)]
    return pl.pallas_call(
        pack_kernel,
        grid_spec=pltpu.PrefetchScalarGridSpec(
            num_scalar_prefetch=1,
            grid=(1,),
            in_specs=[
                rows(w_gate),
                rows(w_up),
                pl.BlockSpec((w_down.shape[0], lanes), lambda i, m_ref: (0, m_ref[0])),
                rows(w_out),
            ],
            out_specs=[pl.BlockSpec(shape, lambda i, m_ref: (0, 0)) for shape in outs],
        ),
        out_shape=[jax.ShapeDtypeStruct(shape, bf16) for shape in outs],
        name="pack",
    )(member.reshape(1), w_gate, w_up, w_down, w_out)


def unpack_kernel(source, *refs):
    gate_ref, up_ref, down_ref = refs[-3:]
    piece = source.shape[2]
    lanes = down_ref.shape[1] // SPLIT
    blocks = down_ref.shape[0] // piece
    gate_ref[...] = source[:, 0].astype(f32).reshape(gate_ref.shape)
    up_ref[...] = source[:, 1].astype(f32).reshape(up_ref.shape)
    for d in range(SPLIT):
        for k in range(blocks):
            down_ref[k * piece : (k + 1) * piece, d * lanes : (d + 1) * lanes] = source[
                d, 2, :, k * lanes : (k + 1) * lanes
            ].astype(f32)


def unpack_ffn(source, first, count, before, depth, shards, unit, width):
    piece = depth // SPLIT
    source = source.reshape(SPLIT, -1, piece, shards * unit)
    rows = unit // shards
    columns = pl.BlockSpec((depth, unit), lambda c, s: (0, s * CHUNKS + first + c))
    return pl.pallas_call(
        unpack_kernel,
        grid=(count, shards),
        in_specs=[pl.BlockSpec((SPLIT, 3, piece, unit), lambda c, s: (0, c, 0, s))]
        + [pl.BlockSpec(memory_space=pl.ANY)] * len(before),
        out_specs=[
            columns,
            columns,
            pl.BlockSpec((rows, width), lambda c, s: ((first + c) * shards + s, 0)),
        ],
        out_shape=[
            jax.ShapeDtypeStruct((depth, shards * CHUNKS * unit), f32),
            jax.ShapeDtypeStruct((depth, shards * CHUNKS * unit), f32),
            jax.ShapeDtypeStruct((CHUNKS * unit, width), f32),
        ],
        input_output_aliases={i + 1: i for i in range(len(before))},
        name="unpack_ffn",
    )(source, *before)


def shard_at(z, r, shards):
    return lax.rem(z + shards - r, shards)


def part_of(z, r, shards, size):
    return pl.ds(pl.multiple_of(shard_at(z, r, shards) * size, size), size)


def joined(own, far, r):
    return own[...] if r == 0 else far[:, r - 1].reshape(own.shape)


def qkv_fwd_kernel(
    shards, z_ref, h_ref, cos_ref, sin_ref, gain_q, gain_k, *refs
):
    own, far, (send_ref, raw_ref) = refs[:3], refs[3:6], refs[6:]
    z = z_ref[0]
    depth = own[0].shape[0]
    total = [None] * 3
    for r in range(shards):
        left = h_ref[:, part_of(z, r, shards, depth)]
        for i in range(3):
            part = dot(left, joined(own[i], far[i], r))
            total[i] = part if r == 0 else total[i] + part
    cosine, sine = cos_ref[...], sin_ref[...]
    at = 0
    for values, gain in ((total[0], gain_q), (total[1], gain_k)):
        for i in range(0, values.shape[1], 2 * HD):
            pair = values[:, i : i + 2 * HD]
            raw_ref[:, at : at + 2 * HD] = pair
            scaled = pair * lax.rsqrt(pair_mean(pair * pair) + EPS) * gain[...]
            rotated = scaled * cosine + other_half(scaled) * sine
            send_ref[:, at : at + 2 * HD] = rotated.astype(bf16)
            at += 2 * HD
    send_ref[:, at:] = total[2].astype(bf16)


def projection_specs(shards, depth, piece, columns):
    sizes = [n // shards for n in columns]
    own = [pl.BlockSpec((depth, n), lambda s, z_ref: (0, s)) for n in sizes]
    starts = [sum(columns[:i]) // sizes[i] for i in range(3)]
    far = [
        pl.BlockSpec(
            (SPLIT, shards - 1, piece, n), lambda s, z_ref, start=start: (0, 0, 0, start + s)
        )
        for n, start in zip(sizes, starts)
    ]
    return own + far


def qkv_forward(z, hidden, cosine, sine, gain_q, gain_k, weights, far):
    local, width = hidden.shape
    depth = weights[0].shape[0]
    shards = width // depth
    columns = [w.shape[1] for w in weights]
    each = sum(columns) // shards
    raw = each - columns[2] // shards
    whole = lambda x: pl.BlockSpec(x.shape, lambda s, z_ref: (0,) * x.ndim)
    return pl.pallas_call(
        functools.partial(qkv_fwd_kernel, shards),
        grid_spec=pltpu.PrefetchScalarGridSpec(
            num_scalar_prefetch=1,
            grid=(shards,),
            in_specs=[whole(x) for x in (hidden, cosine, sine, gain_q, gain_k)]
            + projection_specs(shards, depth, far.shape[2], columns),
            out_specs=[
                pl.BlockSpec((local, each), lambda s, z_ref: (s, 0)),
                pl.BlockSpec((local, raw), lambda s, z_ref: (s, 0)),
            ],
        ),
        out_shape=[
            jax.ShapeDtypeStruct((shards * local, each), bf16),
            jax.ShapeDtypeStruct((shards * local, raw), f32),
        ],
        cost_estimate=pl.CostEstimate(
            flops=2 * local * width * sum(columns),
            transcendentals=0,
            bytes_accessed=2 * width * sum(columns) + 8 * local * sum(columns),
        ),
        name="qkv_forward",
    )(z, hidden, cosine, sine, gain_q, gain_k, *weights, far, far, far)


def qkv_bwd_kernel(
    shards, z_ref, ht_ref, cos_ref, sin_ref, gain_q, gain_k, back_ref, raw_ref, *refs
):
    own, far, (grad_ref, mine, theirs, sum_q, sum_k, grads) = refs[:3], refs[3:6], refs[6:]
    z = z_ref[0]
    even = z_ref[1] == 0
    depth = own[0].shape[0]
    piece = depth // SPLIT

    @pl.when(pl.program_id(0) == 0)
    def _():
        grad_ref[...] = jnp.zeros_like(grad_ref)
        sum_q[...] = jnp.zeros_like(sum_q)
        sum_k[...] = jnp.zeros_like(sum_k)

    cosine, sine = cos_ref[...], sin_ref[...]
    at = 0
    for size, gain, total in ((own[0].shape[1], gain_q, sum_q), (own[1].shape[1], gain_k, sum_k)):
        for _ in range(0, size, 2 * HD):
            pair = raw_ref[:, at : at + 2 * HD]
            scale = lax.rsqrt(pair_mean(pair * pair) + EPS)
            hat = pair * scale
            grad = back_ref[:, at : at + 2 * HD].astype(f32)
            grad = grad * cosine + other_half(grad * sine)
            total[...] += jnp.sum(grad * hat, axis=0, keepdims=True)
            grad = grad * gain[...]
            grads[:, at : at + 2 * HD] = (scale * (grad - hat * pair_mean(grad * hat))).astype(bf16)
            at += 2 * HD
    grads[:, at:] = back_ref[:, at:]
    ends = (0, own[0].shape[1], at, grads.shape[1])
    for r in range(shards):
        part = None
        for i in range(3):
            one = dot(grads[:, ends[i] : ends[i + 1]], joined(own[i], far[i], r), NT)
            part = one if i == 0 else part + one
        grad_ref[:, part_of(z, r, shards, depth)] += part
        term = dot(ht_ref[part_of(z, r, shards, depth), :], grads[...]).astype(bf16)
        term = term.reshape(SPLIT // 2, 2, piece, term.shape[1])
        mine[:, r] = jnp.where(even, term[:, 0], term[:, 1])
        theirs[:, r] = jnp.where(even, term[:, 1], term[:, 0])


def qkv_backward(z, hidden_t, cosine, sine, gain_q, gain_k, back, raw, weights, far, extra):
    width, local = hidden_t.shape
    depth = weights[0].shape[0]
    shards = width // depth
    piece = depth // SPLIT
    columns = [w.shape[1] for w in weights]
    each = back.shape[1]
    whole = lambda shape: pl.BlockSpec(shape, lambda s, z_ref: (0,) * len(shape))
    rows = lambda x: pl.BlockSpec((local, x.shape[1]), lambda s, z_ref: (s, 0))
    terms = jax.ShapeDtypeStruct((SPLIT // 2, shards, piece, shards * each + extra), bf16)
    at_terms = pl.BlockSpec((SPLIT // 2, shards, piece, each), lambda s, z_ref: (0, 0, 0, s))
    return pl.pallas_call(
        functools.partial(qkv_bwd_kernel, shards),
        grid_spec=pltpu.PrefetchScalarGridSpec(
            num_scalar_prefetch=1,
            grid=(shards,),
            in_specs=[whole(x.shape) for x in (hidden_t, cosine, sine, gain_q, gain_k)]
            + [rows(back), rows(raw)]
            + projection_specs(shards, depth, piece, columns),
            out_specs=[whole((local, width)), at_terms, at_terms, whole((1, 2 * HD)), whole((1, 2 * HD))],
            scratch_shapes=[pltpu.VMEM((local, each), bf16)],
        ),
        out_shape=[
            jax.ShapeDtypeStruct((local, width), f32),
            terms,
            terms,
            jax.ShapeDtypeStruct((1, 2 * HD), f32),
            jax.ShapeDtypeStruct((1, 2 * HD), f32),
        ],
        cost_estimate=pl.CostEstimate(
            flops=4 * local * width * sum(columns),
            transcendentals=0,
            bytes_accessed=4 * width * sum(columns) + 8 * local * sum(columns),
        ),
        name="qkv_backward",
    )(z, hidden_t, cosine, sine, gain_q, gain_k, back, raw, *weights, far, far, far)


def unpack_qkv_kernel(source, q_ref, k_ref, v_ref):
    at = 0
    for ref in (q_ref, k_ref, v_ref):
        ref[...] = source[:, at : at + ref.shape[1]].astype(f32)
        at += ref.shape[1]


def unpack_qkv(source, shards, columns):
    depth = source.shape[0]
    each = [n // shards for n in columns]
    return pl.pallas_call(
        unpack_qkv_kernel,
        grid=(shards,),
        in_specs=[pl.BlockSpec((depth, sum(each)), lambda s: (0, s))],
        out_specs=[pl.BlockSpec((depth, n), lambda s: (0, s)) for n in each],
        out_shape=[jax.ShapeDtypeStruct((depth, n), f32) for n in columns],
        name="unpack_qkv",
    )(source)


def out_fwd_kernel(shards, z_ref, mixed, tokens, gain, own, far, resid_ref, scale_ref, h_ref, ht_ref):
    z = z_ref[0]
    local = tokens.shape[0]
    resid = tokens[...].astype(f32)
    for r in range(shards):
        weight = own[...] if r == 0 else far[:, r - 1, 0].reshape(own.shape)
        resid = resid + dot(mixed[part_of(z, r, shards, local), :], weight)
    scale = rms_scale(resid)
    hidden = resid * scale * gain[...]
    resid_ref[...] = resid
    scale_ref[...] = scale
    h_ref[...] = hidden.astype(bf16)
    ht_ref[...] = hidden.T.astype(bf16)


def far_out_spec(far, width):
    size = (SPLIT, far.shape[1], 1, far.shape[3], width)
    return pl.BlockSpec(size, lambda i, z_ref: (0, 0, far.shape[2] - 1, 0, 0))


def out_forward(z, mixed, tokens, gain, w_out, far):
    local, width = tokens.shape
    shards = mixed.shape[0] // local
    piece = w_out.shape[0] // SPLIT
    far = far.reshape(SPLIT, shards - 1, -1, piece, far.shape[-1])
    whole = lambda shape: pl.BlockSpec(shape, lambda i, z_ref: (0,) * len(shape))
    outs = [((local, width), f32), ((local, 1), f32), ((local, width), bf16), ((width, local), bf16)]
    return pl.pallas_call(
        functools.partial(out_fwd_kernel, shards),
        grid_spec=pltpu.PrefetchScalarGridSpec(
            num_scalar_prefetch=1,
            grid=(1,),
            in_specs=[whole(x.shape) for x in (mixed, tokens, gain, w_out)]
            + [far_out_spec(far, width)],
            out_specs=[whole(shape) for shape, _ in outs],
        ),
        out_shape=[jax.ShapeDtypeStruct(*out) for out in outs],
        cost_estimate=pl.CostEstimate(
            flops=2 * local * width * width, transcendentals=0, bytes_accessed=14 * local * width
        ),
        name="out_forward",
    )(z, mixed, tokens, gain, w_out, far)


def out_bwd_kernel(
    shards, z_ref, grad, grad_y, resid, scale_ref, gain, own, far, grad_resid, sum_ref, branch, send
):
    z = z_ref[0]
    local = grad.shape[0]
    scale = scale_ref[...]
    normed = resid[...] * scale
    sum_ref[...] = jnp.sum(grad[...] * normed, axis=0, keepdims=True)
    total = grad_y[...].astype(f32) + norm_back(grad[...] * gain[...], normed, scale)
    grad_resid[...] = total
    low = total.astype(bf16)
    branch[...] = low
    for r in range(shards):
        weight = own[...] if r == 0 else far[:, r - 1, 0].reshape(own.shape)
        send[part_of(z, r, shards, local), :] = dot(low, weight, NT).astype(bf16)


def out_backward(z, grad, grad_y, resid, scale, gain, w_out, far):
    local, width = grad.shape
    depth = w_out.shape[0]
    shards = width // depth
    piece = depth // SPLIT
    far = far.reshape(SPLIT, shards - 1, -1, piece, far.shape[-1])
    whole = lambda shape: pl.BlockSpec(shape, lambda i, z_ref: (0,) * len(shape))
    outs = [((local, width), f32), ((1, width), f32), ((local, width), bf16), ((shards * local, depth), bf16)]
    return pl.pallas_call(
        functools.partial(out_bwd_kernel, shards),
        grid_spec=pltpu.PrefetchScalarGridSpec(
            num_scalar_prefetch=1,
            grid=(1,),
            in_specs=[whole(x.shape) for x in (grad, grad_y, resid, scale, gain, w_out)]
            + [far_out_spec(far, width)],
            out_specs=[whole(shape) for shape, _ in outs],
        ),
        out_shape=[jax.ShapeDtypeStruct(*out) for out in outs],
        cost_estimate=pl.CostEstimate(
            flops=2 * local * width * width, transcendentals=0, bytes_accessed=20 * local * width
        ),
        name="out_backward",
    )(z, grad, grad_y, resid, scale, gain, w_out, far)


def out_terms_kernel(shards, z_ref, mixed, branch, terms):
    term = dot(mixed[...], branch[...], TN).astype(bf16)
    terms[:, 0] = term.reshape(terms.shape[0], terms.shape[2], terms.shape[3])


def out_terms(z, mixed, branch):
    local, width = branch.shape
    shards = mixed.shape[0] // local
    depth = mixed.shape[1]
    piece = depth // SPLIT
    return pl.pallas_call(
        functools.partial(out_terms_kernel, shards),
        grid_spec=pltpu.PrefetchScalarGridSpec(
            num_scalar_prefetch=1,
            grid=(shards,),
            in_specs=[
                pl.BlockSpec((local, depth), lambda r, z_ref: (shard_at(z_ref[0], r, shards), 0)),
                pl.BlockSpec((local, width), lambda r, z_ref: (0, 0)),
            ],
            out_specs=pl.BlockSpec((SPLIT, 1, piece, width), lambda r, z_ref: (0, r, 0, 0)),
        ),
        out_shape=jax.ShapeDtypeStruct((SPLIT, shards, piece, width), bf16),
        cost_estimate=pl.CostEstimate(
            flops=2 * local * width * width, transcendentals=0, bytes_accessed=8 * local * width
        ),
        name="out_terms",
    )(z, mixed, branch)


class Axes:
    def __init__(self, mesh):
        self.n_dp = mesh.shape["dp"]
        self.n_seq = mesh.shape["seq"]
        self.groups = None
        self.across = None
        if self.n_dp > SPLIT:
            self.groups = [[g + i for i in range(SPLIT)] for g in range(0, self.n_dp, SPLIT)]
            self.across = [list(range(i, self.n_dp, SPLIT)) for i in range(SPLIT)]

    def member(self):
        return lax.rem(lax.axis_index("dp"), SPLIT)

    def shift(self, x, r):
        n = self.n_seq
        return lax.ppermute(x, "seq", [(i, (i + r) % n) for i in range(n)])

    def from_others(self, x):
        return [self.shift(x, r) for r in range(1, self.n_seq)]

    def passed_on(self, x):
        n = self.n_seq
        z = lax.axis_index("seq")
        up = down = x
        below, above = [], []
        for step in range(1, n):
            up = lax.ppermute(up, "seq", [(i, i + 1) for i in range(step - 1, n - 1)])
            down = lax.ppermute(down, "seq", [(i + 1, i) for i in range(n - step)])
            below.append(up)
            above.append(down)
        return [jnp.where(z >= r, below[r - 1], above[n - r - 1]) for r in range(1, n)]

    def gather(self, x):
        return lax.all_gather(x, "dp", axis=0, tiled=True, axis_index_groups=self.groups)

    def scatter(self, terms):
        flat = terms.reshape(SPLIT * terms.shape[1], *terms.shape[2:])
        return lax.psum_scatter(
            flat, "dp", scatter_dimension=0, tiled=True, axis_index_groups=self.groups
        )

    def over_groups(self, x):
        return lax.psum(x, "dp", axis_index_groups=self.across) if self.across else x

    def swap(self, x, bit):
        return lax.ppermute(x, "dp", [(i, i ^ bit) for i in range(self.n_dp)])


def after(x, *others):
    return lax.optimization_barrier((x, *others))[0]


class Reduction:
    def __init__(self, axes, mine, theirs):
        self.axes = axes
        member = axes.member()
        self.x = lax.rem(lax.div(member, 2), 2)
        self.y = lax.div(member, 4)
        self.mine = mine.reshape(2, 2, *mine.shape[1:])
        self.state = (axes.swap(theirs, 1),)

    def then(self, *others):
        self.state = lax.optimization_barrier((*self.state, *others))[: len(self.state)]

    def _sum(self, y, x, low, *more):
        def cut(arr):
            shards = arr.shape[2] // 2
            start = [y if y is not None else 0, x if x is not None else 0, 0 if low else shards]
            size = [1 if y is not None else 2, 1 if x is not None else 2, shards]
            rest = arr.ndim - 3
            part = lax.dynamic_slice(arr, start + [0] * rest, size + list(arr.shape[3:]))
            drop = tuple(i for i, at in enumerate((y, x)) if at is not None)
            return lax.squeeze(part, drop).astype(f32)

        total = cut(self.mine) + cut(self.recv)
        for arr in more:
            total = total + arr.astype(f32)
        return total

    def first(self):
        (recv,) = self.state
        self.recv = recv.reshape(self.mine.shape)
        to_x = self._sum(None, 1 - self.x, True).astype(bf16)
        to_y = self._sum(1 - self.y, None, False).astype(bf16)
        self.sent = (to_x, to_y)
        self.state = (self.axes.swap(to_x, 2), self.axes.swap(to_y, 4))
        return self

    def second(self):
        self.got_x, self.got_y = self.state
        pick = lambda arr, i: lax.dynamic_index_in_dim(arr, i, axis=0, keepdims=False)
        to_y = self._sum(1 - self.y, self.x, True, pick(self.got_x, 1 - self.y)).astype(bf16)
        to_x = self._sum(self.y, 1 - self.x, False, pick(self.got_y, 1 - self.x)).astype(bf16)
        self.sent = (to_x, to_y)
        self.state = (self.axes.swap(to_y, 4), self.axes.swap(to_x, 2))
        return self

    def third(self):
        got_y, got_x = self.state
        pick = lambda arr, i: lax.dynamic_index_in_dim(arr, i, axis=0, keepdims=False)
        low = self._sum(self.y, self.x, True, pick(self.got_x, self.y), got_y)
        high = self._sum(self.y, self.x, False, pick(self.got_y, self.x), got_x)
        return jnp.concatenate([low, high], axis=0).astype(bf16)


def per_device(
    axes, tokens, lengths, cotangent, w_query, w_key, w_value, w_out, w_gate, w_up, w_down,
    gain_attn, gain_ffn, gain_query, gain_key,
):
    slots, local, width = tokens.shape
    assert slots == 1
    shards = axes.n_seq
    depth = width // shards
    piece = depth // SPLIT
    z = lax.axis_index("seq")
    member = axes.member()
    unit = w_down.shape[0] // CHUNKS
    lanes = width // SPLIT
    head = HD // shards
    weights = (w_query, w_key, w_value)
    columns = [w.shape[1] for w in weights]
    where = jnp.stack([z, lax.rem(member, 2)]).astype(jnp.int32)
    mine = lambda x: lax.dynamic_slice_in_dim(x, member * piece, piece, axis=0)

    def by_owner(parts):
        pick = lambda i: lax.dynamic_index_in_dim(parts, lax.rem(z + shards - i, shards), 0)
        return jnp.concatenate([pick(i) for i in range(shards)], axis=0)

    def total(parts):
        return axes.over_groups(jnp.sum(parts.astype(f32), axis=0).astype(bf16))

    gains = jnp.concatenate([gain_attn, gain_ffn, gain_query, gain_key])
    gains = jnp.pad(gains, (0, piece * 128 - gains.shape[0])).reshape(piece, 128)
    packed = jnp.concatenate([mine(w_query), mine(w_key), mine(w_value), gains], axis=1)
    near = axes.from_others(packed)
    far_qkv = axes.gather(jnp.stack([x[:, :-128] for x in near]))
    far_qkv = far_qkv.reshape(SPLIT, shards - 1, piece, -1)
    gains = jnp.stack([x[:, -128:].reshape(-1) for x in [packed] + near])
    order = lax.rem(z + shards - jnp.arange(shards), shards)
    hot = (order[:, None] == jnp.arange(shards)[None, :]).astype(f32)
    gains = jnp.sum(hot[:, :, None] * gains.astype(f32)[:, None, :], axis=0)

    def gathered_gain(start, size):
        return gains[:, start : start + size].reshape(1, -1)

    gain1 = gathered_gain(0, depth)
    gain2 = gathered_gain(depth, depth)
    gain_q = jnp.tile(gathered_gain(2 * depth, head), (1, 2))
    gain_k = jnp.tile(gathered_gain(2 * depth + head, head), (1, 2))

    first_chunks, last_chunk = pack(member, w_gate, w_up, w_down, w_out)

    def stack_after(parts, *others):
        return jnp.stack([after(x, *others) for x in parts])

    positions = z * local + jnp.arange(local, dtype=jnp.int32)
    cosine, sine = tables(positions)
    valid = (positions < lengths[0])[:, None]
    grad_y = jnp.where(valid, cotangent[0], jnp.zeros((), bf16))
    inputs = tokens[0].astype(f32)
    scale1 = rms_scale(inputs)
    hidden1 = (inputs * scale1 * gain1).astype(bf16)
    hidden1_t = hidden1.T

    def exchange(x):
        return lax.all_to_all(x, "seq", split_axis=0, concat_axis=0, tiled=True)

    crossed = axes.passed_on(after(first_chunks, *near))
    send, raw = qkv_forward(where, hidden1, cosine, sine, gain_q, gain_k, weights, far_qkv)
    far = axes.gather(stack_after(crossed, send))
    qkv = exchange(send)
    crossed = axes.from_others(after(last_chunk, qkv))
    block = 512
    mixed_heads, lse = attend_forward(qkv, block)
    mixed = exchange(after(mixed_heads, *crossed))
    crossed = stack_after(crossed, mixed_heads)
    far_last = axes.gather(crossed)
    resid, scale2, hidden2, hidden2_t = out_forward(where, mixed, tokens[0], gain2, w_out, far)
    hidden2 = after(hidden2, crossed)

    result, grad_hidden2 = resid, resid

    def chunk(c, result, grad_hidden2):
        last = c == CHUNKS - 1
        source, kind = (far_last, 0) if last else (far, 3 * c)
        return ffn_chunk(
            c, kind, last, where, hidden2, hidden2_t, grad_y, w_gate, w_up, w_down, source,
            result, grad_hidden2,
        )

    result, grad_hidden2, terms0 = chunk(0, result, grad_hidden2)
    sum0 = axes.scatter(terms0)
    result, grad_hidden2, terms1 = chunk(1, result, grad_hidden2)
    sum1 = axes.scatter(terms1)
    result, grad_hidden2, *terms2 = chunk(2, result, grad_hidden2)
    sum2 = Reduction(axes, *terms2)

    grad_resid, term_gain2, branch, send = out_backward(
        where, grad_hidden2, grad_y, resid, scale2, gain2, w_out, far
    )
    grad_heads = exchange(send)
    terms_out = out_terms(where, mixed, after(branch, send))
    sum_out = axes.scatter(terms_out)
    sum2.then(terms_out)
    sum2.first()
    parts0 = by_owner(after(sum0, grad_heads))
    grad_heads = after(grad_heads, terms_out, *sum2.sent, parts0)
    parts0 = exchange(parts0)
    back = attend_backward(qkv, grad_heads, mixed_heads, lse, block)
    back_rows = exchange(after(back, parts0))
    sum2.then(back)
    sum2.second()
    piece0 = total(after(parts0, back))
    parts1 = by_owner(after(sum1, back))
    parts2 = by_owner(sum2.third())
    back_rows = after(back_rows, *sum2.sent, piece0, parts1, parts2)
    piece0 = axes.gather(piece0[None])
    parts1 = exchange(after(parts1, back_rows))
    parts2 = exchange(after(parts2, back_rows))
    grad_hidden1, terms, other, sum_q, sum_k = qkv_backward(
        where, hidden1_t, cosine, sine, gain_q, gain_k, back_rows, raw, weights, far_qkv, 128
    )
    piece1 = axes.gather(total(after(parts1, grad_hidden1))[None])
    normed1 = inputs * scale1
    term_gain1 = jnp.sum(grad_hidden1 * normed1, axis=0)
    grad_tokens = (grad_resid + norm_back(grad_hidden1 * gain1, normed1, scale1))[None]

    parts = [
        term_gain1.reshape(shards, depth),
        term_gain2.reshape(shards, depth),
        (sum_q[0, :HD] + sum_q[0, HD:]).reshape(shards, head),
        (sum_k[0, :HD] + sum_k[0, HD:]).reshape(shards, head),
    ]
    parts = jnp.concatenate(parts, axis=1)
    parts = jnp.sum(hot[:, :, None] * parts[None], axis=1)
    each = parts.shape[1] // SPLIT
    parts = parts.reshape(shards, SPLIT, each).transpose(1, 0, 2)
    parts = jnp.pad(parts, ((0, 0), (0, 0), (0, piece * 128 - each)))
    parts = parts.reshape(SPLIT // 2, 2, shards, piece, 128).astype(bf16)
    parity = lax.rem(member, 2)
    pick = lambda i: lax.dynamic_index_in_dim(parts, i, axis=1, keepdims=False)
    start = (0, 0, 0, terms.shape[3] - 128)
    terms = lax.dynamic_update_slice(terms, pick(parity), start)
    other = lax.dynamic_update_slice(other, pick(1 - parity), start)
    tail = Reduction(axes, terms, other).first()
    parts2 = after(parts2, *tail.sent)
    piece2 = axes.gather(total(parts2)[None])
    tail.second()
    tail = by_owner(jnp.concatenate([tail.third(), sum_out], axis=2))
    whole = axes.gather(total(exchange(tail)))
    grads = unpack_ffn(piece0, 0, 1, (), depth, shards, unit, width)
    grads = unpack_ffn(piece1, 1, 1, grads, depth, shards, unit, width)
    grads = unpack_ffn(piece2, 2, 1, grads, depth, shards, unit, width)
    grad_gate, grad_up, grad_down = grads
    output = jnp.where(valid, result, 0.0).astype(bf16)[None]
    grad_out = whole[:, -width:].astype(f32)
    grad_query, grad_key, grad_value = unpack_qkv(whole, shards, columns)
    sums = whole[:, sum(columns) : sum(columns) + 128].astype(f32).reshape(SPLIT, -1)[:, :each].reshape(-1)
    return (
        output,
        grad_tokens,
        grad_query,
        grad_key,
        grad_value,
        grad_out,
        grad_gate,
        grad_up,
        grad_down,
        sums[:depth],
        sums[depth : 2 * depth],
        sums[2 * depth : 2 * depth + head],
        sums[2 * depth + head :],
    )


def solution(mesh):
    rows = P("seq", None)
    whole = P("dp", "seq", None)
    return jax.shard_map(
        functools.partial(per_device, Axes(mesh)),
        mesh=mesh,
        in_specs=(whole, P("dp"), whole) + (rows,) * 7 + (P("seq"),) * 4,
        out_specs=(whole, whole) + (rows,) * 7 + (P("seq"),) * 4,
        check_vma=False,
    )
```

time: 788 us -> 614 us (0.78)
  waiting for transfers between devices: 275 us -> 168 us
  local copies, waits for them, and re-layouts: 106 us -> 25.4 us
  blocking collectives: 10.5 us -> 73.3 us
  other arithmetic: 115 us -> 57.1 us
  Pallas kernels: 160 us -> 212 us
  starting transfers between devices: 80.6 us -> 54.2 us
  matrix products: 16.7 us -> 0 us
    all_to_all x0 -> x2, blocking collectives: none -> 73.3 us  [exchange(): return lax.all_to_all(x, 'seq', split_axis=0, concat_axis=0, tiled=True)]
    ppermute x27 -> x6, waiting for transfers between devices: 81.9 us -> 17.3 us  [shift(): return lax.ppermute(x, 'seq', [(i, (i + r) % n) for i in range(n)])]
    pallas_call x5 -> x14, Pallas kernels: 143 us -> 195 us  [the longest x3 93.6 us: ffn_chunk(): pl.pallas_call(functools.partial(ffn_kernel, shards, c == 0), grid_spec=p...]
    all_to_all x4 -> x6, waiting for transfers between devices: 91 us -> 47.5 us  [exchange(): return lax.all_to_all(x, 'seq', split_axis=0, concat_axis=0, tiled=True)]
    ppermute x0 -> x6, waiting for transfers between devices: none -> 35.9 us  [the longest x3 34.5 us: passed_on(): down = lax.ppermute(down, 'seq', [(i + 1, i) for i in range(n - step)])]
    ppermute x27 -> x6, starting transfers between devices: 39.7 us -> 8.15 us  [shift(): return lax.ppermute(x, 'seq', [(i, (i + r) % n) for i in range(n)])]
    convert_element_type x21 -> x6, other arithmetic: 37.9 us -> 7.11 us  [the longest x2 4.54 us: second(): self._sum(1 - self.y, self.x, True, pick(self.got_x, 1 - self.y))]
    mul x22 -> x0, local copies, waits for them, and re-layouts: 21.4 us -> none  [the longest x4 8.15 us: norm_back(): normed * jnp.mean(grads * normed, axis=-1, keepdims=True)]
  transfers between devices with their start and end apart: 64 -> 38, of which waited for: 21 -> 17; matrix products, arithmetic and copies ran while one was open for 24% -> 12% of each run, Pallas kernels for 20% -> 33%
where the time goes in v2:
time: 614 us; the launch traced here: 605 us
  Pallas kernels  212 us (35%)
  waiting for transfers between devices  168 us (27%)
  blocking collectives  73.3 us (12%)
  other arithmetic  57.1 us (9%)
  starting transfers between devices  54.2 us (9%)
  local copies, waits for them, and re-layouts  25.4 us (4%)
  between operations  15.9 us (3%)
    pallas_call x3, Pallas kernels, ffn_chunk(): pl.pallas_call(functools.partial(ffn_kernel, shards, c == 0), grid_spec=p...  93.6 us
    all_to_all x2, blocking collectives, exchange(): return lax.all_to_all(x, 'seq', split_axis=0, concat_axis=0, tiled=True)  73.3 us
    ppermute x10, waiting for transfers between devices, swap(): return lax.ppermute(x, 'dp', [(i, i ^ bit) for i in range(self.n_dp)])  66.2 us
    all_to_all x6, waiting for transfers between devices, exchange(): return lax.all_to_all(x, 'seq', split_axis=0, concat_axis=0, tiled=True)  47.5 us
    pallas_call x1, Pallas kernels, attend_backward(): pl.pallas_call(functools.partial(attend_bwd_kernel, block, kv), grid=(kv,...  38.8 us
    ppermute x3, waiting for transfers between devices, passed_on(): down = lax.ppermute(down, 'seq', [(i + 1, i) for i in range(n - step)])  34.5 us
    all_to_all x6, starting transfers between devices, exchange(): return lax.all_to_all(x, 'seq', split_axis=0, concat_axis=0, tiled=True)  24.6 us
    ppermute x6, waiting for transfers between devices, shift(): return lax.ppermute(x, 'seq', [(i, (i + r) % n) for i in range(n)])  17.3 us
  transfers between devices with their start and end apart: 38, of which 17 were waited for; matrix products, arithmetic and copies ran while one was open for 12% of the time, Pallas kernels for 33%

profile of v2, /device:TPU:0, one launch (start us, length us, event | category | flops | bytes accessed | tf_op | source)
XLA Modules:
  0.0 605.3 jit_solution(16407056732738974807)
XLA Ops:
  9.7 5.1 collective-permute-start.2
  15.9 3.1 collective-permute-done.2
  19.0 7.7 %collective-permute-done.1 = bf16[32,2176]{1,0:T(8,128)(2,1)S(1)} collective-permute-done((bf16[32,2176]{1,0:T(8,128)(2,1)S(1)}, bf16[32,2176]{1,0:T(8,128)(2,1)S(1)}, u32[]{:S(2)}, u32[]{:S(2)}) %collective-permute-start.1) | collective-permute-done | bytes 139296 | tf_op jit(solution)/shard_map/ppermute | solution.py:783
  28.2 2.2 pack.1
  35.8 4.6 collective-permute-start.6
  41.2 10.5 %collective-permute-done.7 = bf16[224,1536]{1,0:T(8,128)(2,1)S(1)} collective-permute-done((bf16[224,1536]{1,0:T(8,128)(2,1)}, bf16[224,1536]{1,0:T(8,128)(2,1)S(1)}, u32[]{:S(2)}, u32[]{:S(2)}) %collective-permute-start.7) | collective-permute-done | bytes 688160 | tf_op jit(solution)/shard_map/ppermute | solution.py:795
  54.6 1.5 collective-permute-start.10
  57.6 11.9 %collective-permute-done.8 = bf16[224,1536]{1,0:T(8,128)(2,1)} collective-permute-done((bf16[224,1536]{1,0:T(8,128)(2,1)S(1)}, bf16[224,1536]{1,0:T(8,128)(2,1)}, u32[]{:S(2)}, u32[]{:S(2)}) %collective-permute-start.8) | collective-permute-done | bytes 688160 | tf_op jit(solution)/shard_map/ppermute | solution.py:795
  74.4 12.1 %collective-permute-done.9 = bf16[224,1536]{1,0:T(8,128)(2,1)} collective-permute-done((bf16[224,1536]{1,0:T(8,128)(2,1)}, bf16[224,1536]{1,0:T(8,128)(2,1)}, u32[]{:S(2)}, u32[]{:S(2)}) %collective-permute-start.9) | collective-permute-done | bytes 688160 | tf_op jit(solution)/shard_map/ppermute | solution.py:795
  87.8 10.3 %qkv_forward.1 = (bf16[2048,512]{1,0:T(8,128)(2,1)}, f32[2048,384]{1,0:T(8,128)}) custom-call(s32[2]{0:T(128)} %pad_add_fusion.z_ref, bf16[512,1024]{1,0:T(8,128)(2,1)} %copy.79.h_ref, f32[512,128]{1,0:T(8,128)} %copy.80.cos_ref, f32[512,128]{1,0:T(8,128)} %pad_maximum_fusion.8.sin_ref, f32[1,128]{1,0:T(1,128)} %tile.33.gain_q, f32[1,128]{1,0:T(1,128)} %tile.36.gain_k, ...), custom_call_target="tpu_custom_call" | custom-call | flops 2147483648 | bytes 12582912 | tf_op jit(solution)/shard_map/qkv_forward/pallas_call | solution.py:528
  98.1 1.5 pad_maximum_fusion
  99.7 51.8 %all_to_all.66 = bf16[4,512,512]{2,1,0:T(8,128)(2,1)} all-to-all(bf16[4,512,512]{2,1,0:T(8,128)(2,1)} %bitcast.186), channel_id=1, replica_groups=mesh['dp'=8,'seq'=4] {'seq'}, dimensions={0} | all-to-all | bytes 4194304 | tf_op jit(solution)/shard_map/all_to_all | solution.py:933
  153.5 16.5 %attend_forward.1 = (bf16[2048,256]{1,0:T(8,128)(2,1)}, f32[2,4,1,1024]{3,2,1,0:T(1,128)}) custom-call(bf16[2048,512]{1,0:T(8,128)(2,1)} %bitcast.179, bf16[2048,512]{1,0:T(8,128)(2,1)} %bitcast.180, bf16[2048,512]{1,0:T(8,128)(2,1)} %bitcast.181), custom_call_target="tpu_custom_call" | custom-call | flops 8589934592 | bytes 3145728 | tf_op jit(solution)/shard_map/attend_forward/pallas_call | solution.py:118
  170.0 6.5 %collective-permute-done.4 = bf16[96,1536]{1,0:T(8,128)(2,1)S(1)} collective-permute-done((bf16[96,1536]{1,0:T(8,128)(2,1)S(1)}, bf16[96,1536]{1,0:T(8,128)(2,1)S(1)}, u32[]{:S(2)}, u32[]{:S(2)}) %collective-permute-start.4) | collective-permute-done | bytes 294944 | tf_op jit(solution)/shard_map/ppermute | solution.py:783
  177.5 3.5 all-to-all-start.1
  184.1 22.0 %all-to-all-done.1 = bf16[4,512,256]{2,1,0:T(8,128)(2,1)S(1)} async-done(((bf16[4,512,256]{2,1,0:T(8,128)(2,1)}), bf16[4,512,256]{2,1,0:T(8,128)(2,1)S(1)}, u32[]{:S(2)}, u32[]{:S(2)}) %all-to-all-start.1) | async-done | bytes 1048608 | tf_op jit(solution)/shard_map/all_to_all | solution.py:933
  207.1 6.3 %out_forward.1 = (f32[512,1024]{1,0:T(8,128)}, f32[512,1]{1,0:T(8,128)}, bf16[512,1024]{1,0:T(8,128)(2,1)}, bf16[1024,512]{1,0:T(8,128)(2,1)}) custom-call(s32[2]{0:T(128)} %pad_add_fusion.z_ref, bf16[2048,256]{1,0:T(8,128)(2,1)} %bitcast.157, bf16[512,1024]{1,0:T(8,128)(2,1)} %bitcast.167, f32[1,1024]{1,0:T(1,128)} %bitcast.202, bf16[256,1024]{1,0:T(8,128)(2,1)} %own.3, ...), custom_call_target="tpu_custom_call" | custom-call | flops 1073741824 | bytes 7340032 | tf_op jit(solution)/shard_map/out_forward/pallas_call | solution.py:680
  213.3 31.4 %ffn_chunk.3 = (f32[512,1024]{1,0:T(8,128)}, f32[512,1024]{1,0:T(8,128)}, bf16[8,4,96,1536]{3,2,1,0:T(8,128)(2,1)}) custom-call(s32[2]{0:T(128)} %pad_add_fusion.z_ref, bf16[512,1024]{1,0:T(8,128)(2,1)} %get-tuple-element.92.h_ref, bf16[1024,512]{1,0:T(8,128)(2,1)} %get-tuple-element.93.ht_ref, bf16[512,1024]{1,0:T(8,128)(2,1)} %bitcast_select_fusion.gy_ref.grad_y, ...), custom_call_target="tpu_custom_call" | custom-call | flops 14495514624 | bytes 29360128 | tf_op jit(solution)/shard_map/ffn_chunk/pallas_call | solution.py:344
  245.0 30.6 %ffn_chunk.4 = (f32[512,1024]{1,0:T(8,128)}, f32[512,1024]{1,0:T(8,128)}, bf16[8,4,96,1536]{3,2,1,0:T(8,128)(2,1)}) custom-call(s32[2]{0:T(128)} %pad_add_fusion.z_ref, bf16[512,1024]{1,0:T(8,128)(2,1)} %get-tuple-element.92.h_ref, bf16[1024,512]{1,0:T(8,128)(2,1)} %get-tuple-element.93.ht_ref, bf16[512,1024]{1,0:T(8,128)(2,1)} %bitcast_select_fusion.gy_ref.grad_y, ...), custom_call_target="tpu_custom_call" | custom-call | flops 14495514624 | bytes 29360128 | tf_op jit(solution)/shard_map/ffn_chunk/pallas_call | solution.py:344
  275.6 31.6 %ffn_chunk.5 = (f32[512,1024]{1,0:T(8,128)}, f32[512,1024]{1,0:T(8,128)}, bf16[4,4,96,1536]{3,2,1,0:T(8,128)(2,1)}, bf16[4,4,96,1536]{3,2,1,0:T(8,128)(2,1)}) custom-call(s32[2]{0:T(128)} %pad_add_fusion.z_ref, bf16[512,1024]{1,0:T(8,128)(2,1)} %get-tuple-element.92.h_ref, bf16[1024,512]{1,0:T(8,128)(2,1)} %get-tuple-element.93.ht_ref, ...), custom_call_target="tpu_custom_call" | custom-call | flops 14495514624 | bytes 29360128 | tf_op jit(solution)/shard_map/ffn_chunk/pallas_call | solution.py:344
  307.2 7.2 %out_backward.1 = (f32[512,1024]{1,0:T(8,128)}, f32[1,1024]{1,0:T(1,128)}, bf16[512,1024]{1,0:T(8,128)(2,1)}, bf16[2048,256]{1,0:T(8,128)(2,1)}) custom-call(s32[2]{0:T(128)} %pad_add_fusion.z_ref, f32[512,1024]{1,0:T(8,128)} %get-tuple-element.100.grad, bf16[512,1024]{1,0:T(8,128)(2,1)} %bitcast_select_fusion.gy_ref.grad_y, ...), custom_call_target="tpu_custom_call" | custom-call | flops 1073741824 | bytes 10485760 | tf_op jit(solution)/shard_map/out_backward/pallas_call | solution.py:722
  314.4 3.5 all-to-all-start.2
  318.2 5.6 out_terms.1
  323.9 2.9 fusion.13
  326.8 2.9 fusion.12
  329.7 14.8 %all-to-all-done.2 = bf16[4,512,256]{2,1,0:T(8,128)(2,1)S(1)} async-done(((bf16[4,512,256]{2,1,0:T(8,128)(2,1)}), bf16[4,512,256]{2,1,0:T(8,128)(2,1)S(1)}, u32[]{:S(2)}, u32[]{:S(2)}) %all-to-all-start.2) | async-done | bytes 1048608 | tf_op jit(solution)/shard_map/all_to_all | solution.py:933
  344.6 1.7 constant_dynamic-slice_fusion.13
  347.5 3.5 all-to-all-start.3
  351.0 38.8 %attend_backward.1 = bf16[2048,512]{1,0:T(8,128)(2,1)} custom-call(bf16[2048,512]{1,0:T(8,128)(2,1)} %bitcast.182, bf16[2048,512]{1,0:T(8,128)(2,1)} %bitcast.183, bf16[2048,512]{1,0:T(8,128)(2,1)} %bitcast.184, bf16[2048,256]{1,0:T(8,128)(2,1)} %bitcast.189, bf16[2048,256]{1,0:T(8,128)(2,1)} %get-tuple-element.82.o_ref, ...), custom_call_target="tpu_custom_call" | custom-call | flops 21474836480 | bytes 6291456 | tf_op jit(solution)/shard_map/attend_backward/pallas_call | solution.py:216
  390.9 5.0 all-to-all-start.4
  395.9 1.5 collective-permute-start.13
  397.4 1.5 collective-permute-start.14
  398.9 2.2 reduce_sum.95
  401.2 24.7 %collective-permute-done.13 = bf16[2,2,96,1536]{3,2,1,0:T(8,128)(2,1)} collective-permute-done((bf16[2,2,96,1536]{3,2,1,0:T(8,128)(2,1)}, bf16[2,2,96,1536]{3,2,1,0:T(8,128)(2,1)}, u32[]{:S(2)}, u32[]{:S(2)}) %collective-permute-start.13) | collective-permute-done | bytes 1179680 | tf_op jit(solution)/shard_map/ppermute | solution.py:813
  425.9 3.4 fusion.18
  429.3 1.5 collective-permute-start.15
  433.8 14.7 %collective-permute-done.15 = bf16[2,96,1536]{2,1,0:T(8,128)(2,1)} collective-permute-done((bf16[2,96,1536]{2,1,0:T(8,128)(2,1)}, bf16[2,96,1536]{2,1,0:T(8,128)(2,1)}, u32[]{:S(2)}, u32[]{:S(2)}) %collective-permute-start.15) | collective-permute-done | bytes 589856 | tf_op jit(solution)/shard_map/ppermute | solution.py:813
  448.5 2.9 fusion.15
  453.1 4.7 all-to-all-start.7
  460.6 14.8 %qkv_backward.1 = (f32[512,1024]{1,0:T(8,128)}, bf16[4,4,32,2176]{3,2,1,0:T(8,128)(2,1)}, bf16[4,4,32,2176]{3,2,1,0:T(8,128)(2,1)}, f32[1,128]{1,0:T(1,128)}, f32[1,128]{1,0:T(1,128)}) custom-call(s32[2]{0:T(128)} %pad_add_fusion.z_ref, bf16[1024,512]{1,0:T(8,128)(2,1)} %fusion.48.ht_ref, f32[512,128]{1,0:T(8,128)} %copy.80.cos_ref, ...), custom_call_target="tpu_custom_call" | custom-call | flops 4294967296 | bytes 16777216 | tf_op jit(solution)/shard_map/qkv_backward/pallas_call | solution.py:606
  477.1 1.9 copy.83
  480.0 6.1 %all-to-all-done.7 = bf16[4,96,1536]{2,1,0:T(8,128)(2,1)} async-done(((bf16[4,96,1536]{2,1,0:T(8,128)(2,1)}), bf16[4,96,1536]{2,1,0:T(8,128)(2,1)}, u32[]{:S(2)}, u32[]{:S(2)}) %all-to-all-start.7) | async-done | bytes 1179680 | tf_op jit(solution)/shard_map/all_to_all | solution.py:933
  486.1 2.2 reduce_sum.101
  489.1 4.3 all-to-all-start.6
  494.1 1.4 fusion.21
  497.0 2.2 fusion.22
  499.8 15.2 %collective-permute-done.18 = bf16[2,2,32,2176]{3,2,1,0:T(8,128)(2,1)S(1)} collective-permute-done((bf16[2,2,32,2176]{3,2,1,0:T(8,128)(2,1)S(1)}, bf16[2,2,32,2176]{3,2,1,0:T(8,128)(2,1)S(1)}, u32[]{:S(2)}, u32[]{:S(2)}) %collective-permute-start.18) | collective-permute-done | bytes 557088 | tf_op jit(solution)/shard_map/ppermute | solution.py:813
  517.0 1.5 collective-permute-start.19
  518.5 4.5 all-to-all-done.6
  523.0 2.2 reduce_sum.100
  526.6 1.7 fusion.28
  528.9 10.3 %collective-permute-done.21 = bf16[2,32,2176]{2,1,0:T(8,128)(2,1)S(1)} collective-permute-done((bf16[2,32,2176]{2,1,0:T(8,128)(2,1)S(1)}, bf16[2,32,2176]{2,1,0:T(8,128)(2,1)S(1)}, u32[]{:S(2)}, u32[]{:S(2)}) %collective-permute-start.21) | collective-permute-done | bytes 278560 | tf_op jit(solution)/shard_map/ppermute | solution.py:813
  539.2 2.0 fusion.25
  542.5 21.5 %all_to_all.67 = bf16[4,32,3200]{2,1,0:T(8,128)(2,1)} all-to-all(bf16[4,32,3200]{2,1,0:T(8,128)(2,1)S(1)} %pad_maximum_fusion.6), channel_id=1, replica_groups=mesh['dp'=8,'seq'=4] {'seq'}, dimensions={0} | all-to-all | bytes 1638400 | tf_op jit(solution)/shard_map/all_to_all | solution.py:933
  564.0 2.0 reduce_sum.99
  566.0 2.9 copy.84
  568.9 2.9 fusion.20
  571.8 1.8 fusion.9
  573.6 2.9 copy.88
  576.5 4.3 unpack_ffn.3
  580.8 4.3 unpack_ffn.4
  585.1 4.3 unpack_ffn.5
  592.4 2.1 slice_convert_fusion
  594.5 3.5 unpack_qkv.1
  (176 shorter events, 52.7 us)
Async XLA Ops:
  7.2 20.4 %copy-start.4 = (bf16[1,512,1024]{2,1,0:T(8,128)(2,1)S(1)}, bf16[1,512,1024]{2,1,0:T(8,128)(2,1)}, u32[]{:S(2)}) copy-start(bf16[1,512,1024]{2,1,0:T(8,128)(2,1)} %param.14) | copy-start | bytes 3145732
  7.2 80.6 %all-gather.11.cloned.1.call-start = ((), (), s32[]{:S(2)}) async-start(), calls=%async_computation.11 | async-start | bytes 3538944 | tf_op jit(solution)/shard_map/all_gather | solution.py:801
  9.7 9.2 %collective-permute-start.2 = (bf16[32,2176]{1,0:T(8,128)(2,1)S(1)}, bf16[32,2176]{1,0:T(8,128)(2,1)S(1)}, u32[]{:S(2)}, u32[]{:S(2)}) collective-permute-start(bf16[32,2176]{1,0:T(8,128)(2,1)S(1)} %pad_maximum_fusion.9), channel_id=1, source_target_pairs={{0,3},{1,0},{2,1},{3,2},{4,7},{5,4},{6,5},{7,6},{8,11},{9,8},{10,9... | collective-permute-start | bytes 417800 | tf_op jit(solution)/shard_map/ppermute | solution.py:783
  14.9 11.8 %collective-permute-start.1 = (bf16[32,2176]{1,0:T(8,128)(2,1)S(1)}, bf16[32,2176]{1,0:T(8,128)(2,1)S(1)}, u32[]{:S(2)}, u32[]{:S(2)}) collective-permute-start(bf16[32,2176]{1,0:T(8,128)(2,1)S(1)} %pad_maximum_fusion.9), channel_id=1, source_target_pairs={{0,2},{1,3},{2,0},{3,1},{4,6},{5,7},{6,4},{7,5},{8,10},{9,11},{10,... | collective-permute-start | bytes 417800 | tf_op jit(solution)/shard_map/ppermute | solution.py:783
  14.9 11.8 %collective-permute-start = (bf16[32,2176]{1,0:T(8,128)(2,1)S(1)}, bf16[32,2176]{1,0:T(8,128)(2,1)S(1)}, u32[]{:S(2)}, u32[]{:S(2)}) collective-permute-start(bf16[32,2176]{1,0:T(8,128)(2,1)S(1)} %pad_maximum_fusion.9), channel_id=1, source_target_pairs={{0,1},{1,2},{2,3},{3,0},{4,5},{5,6},{6,7},{7,4},{8,9},{9,10},{10,1... | collective-permute-start | bytes 417800 | tf_op jit(solution)/shard_map/ppermute | solution.py:783
  26.7 0.9 copy-start.10
  27.5 178.6 %all-gather.13.cloned.1.call-start = ((), (), s32[]{:S(2)}) async-start(), calls=%async_computation.12 | async-start | bytes 18579456 | tf_op jit(solution)/shard_map/all_gather | solution.py:801
  28.2 2.3 copy-start.12
  28.2 2.3 copy-start.13
  28.2 2.3 copy-start.14
  28.2 2.3 copy-start.15
  32.9 18.8 %collective-permute-start.7 = (bf16[224,1536]{1,0:T(8,128)(2,1)}, bf16[224,1536]{1,0:T(8,128)(2,1)S(1)}, u32[]{:S(2)}, u32[]{:S(2)}) collective-permute-start(bf16[224,1536]{1,0:T(8,128)(2,1)} %get-tuple-element.84), channel_id=1, source_target_pairs={{1,0},{2,1},{3,2},{5,4},{6,5},{7,6},{9,8},{10,9},{11,10},{13,12},{... | collective-permute-start | bytes 2064392 | tf_op jit(solution)/shard_map/ppermute | solution.py:795
  35.8 18.8 %collective-permute-start.6 = (bf16[224,1536]{1,0:T(8,128)(2,1)}, bf16[224,1536]{1,0:T(8,128)(2,1)S(1)}, u32[]{:S(2)}, u32[]{:S(2)}) collective-permute-start(bf16[224,1536]{1,0:T(8,128)(2,1)} %get-tuple-element.84), channel_id=1, source_target_pairs={{0,1},{1,2},{2,3},{4,5},{5,6},{6,7},{8,9},{9,10},{10,11},{12,13},{... | collective-permute-start | bytes 2064392 | tf_op jit(solution)/shard_map/ppermute | solution.py:794
  51.7 19.1 %copy-start.7 = (bf16[224,1536]{1,0:T(8,128)(2,1)}, bf16[224,1536]{1,0:T(8,128)(2,1)S(1)}, u32[]{:S(2)}) copy-start(bf16[224,1536]{1,0:T(8,128)(2,1)S(1)} %collective-permute-done.7) | copy-start | bytes 2064388
  51.7 17.8 %collective-permute-start.8 = (bf16[224,1536]{1,0:T(8,128)(2,1)S(1)}, bf16[224,1536]{1,0:T(8,128)(2,1)}, u32[]{:S(2)}, u32[]{:S(2)}) collective-permute-start(bf16[224,1536]{1,0:T(8,128)(2,1)S(1)} %collective-permute-done.7), channel_id=1, source_target_pairs={{1,0},{2,1},{5,4},{6,5},{9,8},{10,9},{13,12},{14,13},{17,16},{18,1... | collective-permute-start | bytes 2064392 | tf_op jit(solution)/shard_map/ppermute | solution.py:795
  54.6 17.8 %collective-permute-start.10 = (bf16[224,1536]{1,0:T(8,128)(2,1)S(1)}, bf16[224,1536]{1,0:T(8,128)(2,1)}, u32[]{:S(2)}, u32[]{:S(2)}) collective-permute-start(bf16[224,1536]{1,0:T(8,128)(2,1)S(1)} %collective-permute-done.6), channel_id=1, source_target_pairs={{1,2},{2,3},{5,6},{6,7},{9,10},{10,11},{13,14},{14,15},{17,18},{18... | collective-permute-start | bytes 2064392 | tf_op jit(solution)/shard_map/ppermute | solution.py:794
  69.5 17.0 %collective-permute-start.9 = (bf16[224,1536]{1,0:T(8,128)(2,1)}, bf16[224,1536]{1,0:T(8,128)(2,1)}, u32[]{:S(2)}, u32[]{:S(2)}) collective-permute-start(bf16[224,1536]{1,0:T(8,128)(2,1)} %collective-permute-done.8), channel_id=1, source_target_pairs={{1,0},{5,4},{9,8},{13,12},{17,16},{21,20},{25,24},{29,28}} | collective-permute-start | bytes 2064392 | tf_op jit(solution)/shard_map/ppermute | solution.py:795
  72.4 15.3 %copy-start.8 = (bf16[224,1536]{1,0:T(8,128)(2,1)S(1)}, bf16[224,1536]{1,0:T(8,128)(2,1)}, u32[]{:S(2)}) copy-start(bf16[224,1536]{1,0:T(8,128)(2,1)} %copy-done.7) | copy-start | bytes 2064388
  72.4 15.3 %collective-permute-start.11 = (bf16[224,1536]{1,0:T(8,128)(2,1)}, bf16[224,1536]{1,0:T(8,128)(2,1)S(1)}, u32[]{:S(2)}, u32[]{:S(2)}) collective-permute-start(bf16[224,1536]{1,0:T(8,128)(2,1)} %collective-permute-done.10), channel_id=1, source_target_pairs={{2,3},{6,7},{10,11},{14,15},{18,19},{22,23},{26,27},{30,31}} | collective-permute-start | bytes 2064392 | tf_op jit(solution)/shard_map/ppermute | solution.py:794
  99.6 176.0 %all-gather.15.cloned.1.call-start = ((), (), s32[]{:S(2)}) async-start(), calls=%async_computation.13 | async-start | bytes 7962624 | tf_op jit(solution)/shard_map/all_gather | solution.py:801
  99.7 51.8 %copy-start.16 = (bf16[96,1536]{1,0:T(8,128)(2,1)S(1)}, bf16[96,1536]{1,0:T(8,128)(2,1)}, u32[]{:S(2)}) copy-start(bf16[96,1536]{1,0:T(8,128)(2,1)} %get-tuple-element.81) | copy-start | bytes 884740
  151.5 18.5 %collective-permute-start.5 = (bf16[96,1536]{1,0:T(8,128)(2,1)S(1)}, bf16[96,1536]{1,0:T(8,128)(2,1)S(1)}, u32[]{:S(2)}, u32[]{:S(2)}) collective-permute-start(bf16[96,1536]{1,0:T(8,128)(2,1)S(1)} %copy-done.16), channel_id=1, source_target_pairs={{0,3},{1,0},{2,1},{3,2},{4,7},{5,4},{6,5},{7,6},{8,11},{9,8},{10,9... | collective-permute-start | bytes 884744 | tf_op jit(solution)/shard_map/ppermute | solution.py:783
  152.8 23.7 %collective-permute-start.4 = (bf16[96,1536]{1,0:T(8,128)(2,1)S(1)}, bf16[96,1536]{1,0:T(8,128)(2,1)S(1)}, u32[]{:S(2)}, u32[]{:S(2)}) collective-permute-start(bf16[96,1536]{1,0:T(8,128)(2,1)S(1)} %copy-done.16), channel_id=1, source_target_pairs={{0,2},{1,3},{2,0},{3,1},{4,6},{5,7},{6,4},{7,5},{8,10},{9,11},{10,... | collective-permute-start | bytes 884744 | tf_op jit(solution)/shard_map/ppermute | solution.py:783
  153.0 23.5 %collective-permute-start.3 = (bf16[96,1536]{1,0:T(8,128)(2,1)S(1)}, bf16[96,1536]{1,0:T(8,128)(2,1)S(1)}, u32[]{:S(2)}, u32[]{:S(2)}) collective-permute-start(bf16[96,1536]{1,0:T(8,128)(2,1)S(1)} %copy-done.16), channel_id=1, source_target_pairs={{0,1},{1,2},{2,3},{3,0},{4,5},{5,6},{6,7},{7,4},{8,9},{9,10},{10,1... | collective-permute-start | bytes 884744 | tf_op jit(solution)/shard_map/ppermute | solution.py:783
  176.5 5.8 copy-start.5
  177.5 28.6 %all-to-all-start.1 = ((bf16[4,512,256]{2,1,0:T(8,128)(2,1)}), bf16[4,512,256]{2,1,0:T(8,128)(2,1)S(1)}, u32[]{:S(2)}, u32[]{:S(2)}) async-start(bf16[4,512,256]{2,1,0:T(8,128)(2,1)} %bitcast.188), calls=%async_computation.1 | async-start | bytes 2097152 | tf_op jit(solution)/shard_map/all_to_all | solution.py:933
  181.1 163.5 %reduce-scatter.4.cloned.1.call-start = ((), (), s32[]{:S(2)}) async-start(), calls=%async_computation.14 | async-start | bytes 10616832 | tf_op jit(solution)/shard_map/reduce_scatter | solution.py:805
  206.1 1.0 copy-start
  244.8 186.5 %reduce-scatter.6.cloned.1.call-start = ((), (), s32[]{:S(2)}) async-start(), calls=%async_computation.15 | async-start | bytes 10616832 | tf_op jit(solution)/shard_map/reduce_scatter | solution.py:805
  307.2 16.7 %collective-permute-start.12 = (bf16[4,4,96,1536]{3,2,1,0:T(8,128)(2,1)}, bf16[4,4,96,1536]{3,2,1,0:T(8,128)(2,1)}, u32[]{:S(2)}, u32[]{:S(2)}) collective-permute-start(bf16[4,4,96,1536]{3,2,1,0:T(8,128)(2,1)} %get-tuple-element.107), channel_id=1, source_target_pairs={{0,4},{4,0},{8,12},{12,8},{16,20},{20,16},{24,28},{28,24},{1,5},{5... | collective-permute-start | bytes 14155784 | tf_op jit(solution)/shard_map/ppermute | solution.py:813
  314.4 30.2 %all-to-all-start.2 = ((bf16[4,512,256]{2,1,0:T(8,128)(2,1)}), bf16[4,512,256]{2,1,0:T(8,128)(2,1)S(1)}, u32[]{:S(2)}, u32[]{:S(2)}) async-start(bf16[4,512,256]{2,1,0:T(8,128)(2,1)} %bitcast.190), calls=%async_computation.2 | async-start | bytes 2097152 | tf_op jit(solution)/shard_map/all_to_all | solution.py:933
  317.9 223.2 %reduce-scatter.8.cloned.1.call-start = ((), (), s32[]{:S(2)}) async-start(), calls=%async_computation.16 | async-start | bytes 2359296 | tf_op jit(solution)/shard_map/reduce_scatter | solution.py:805
  344.5 2.9 copy-start.6
  347.5 42.3 %all-to-all-start.3 = ((bf16[4,96,1536]{2,1,0:T(8,128)(2,1)}), bf16[4,96,1536]{2,1,0:T(8,128)(2,1)S(1)}, u32[]{:S(2)}, u32[]{:S(2)}) async-start(bf16[4,96,1536]{2,1,0:T(8,128)(2,1)} %pad_maximum_fusion.1), calls=%async_computation.4 | async-start | bytes 2359296 | tf_op jit(solution)/shard_map/all_to_all | solution.py:933
  389.8 1.1 copy-start.3
  390.9 62.2 %all-to-all-start.4 = ((bf16[4,512,512]{2,1,0:T(8,128)(2,1)}), bf16[4,512,512]{2,1,0:T(8,128)(2,1)S(1)}, u32[]{:S(2)}, u32[]{:S(2)}) async-start(bf16[4,512,512]{2,1,0:T(8,128)(2,1)} %bitcast.185), calls=%async_computation.5 | async-start | bytes 4194304 | tf_op jit(solution)/shard_map/all_to_all | solution.py:933
  395.9 180.6 %all-gather.23.cloned.1.call-start = ((), (), s32[]{:S(2)}) async-start(), calls=%async_computation.20 | async-start | bytes 2654208 | tf_op jit(solution)/shard_map/all_gather | solution.py:801
  395.9 30.0 %collective-permute-start.13 = (bf16[2,2,96,1536]{3,2,1,0:T(8,128)(2,1)}, bf16[2,2,96,1536]{3,2,1,0:T(8,128)(2,1)}, u32[]{:S(2)}, u32[]{:S(2)}) collective-permute-start(bf16[2,2,96,1536]{3,2,1,0:T(8,128)(2,1)} %fusion.12), channel_id=1, source_target_pairs={{0,8},{4,12},{8,0},{12,4},{16,24},{20,28},{24,16},{28,20},{1,9},{5... | collective-permute-start | bytes 3538952 | tf_op jit(solution)/shard_map/ppermute | solution.py:813
  397.4 28.5 %collective-permute-start.14 = (bf16[2,2,96,1536]{3,2,1,0:T(8,128)(2,1)}, bf16[2,2,96,1536]{3,2,1,0:T(8,128)(2,1)}, u32[]{:S(2)}, u32[]{:S(2)}) collective-permute-start(bf16[2,2,96,1536]{3,2,1,0:T(8,128)(2,1)} %fusion.13), channel_id=1, source_target_pairs={{0,16},{4,20},{8,24},{12,28},{16,0},{20,4},{24,8},{28,12},{1,17},{... | collective-permute-start | bytes 3538952 | tf_op jit(solution)/shard_map/ppermute | solution.py:813
  429.3 19.2 %collective-permute-start.15 = (bf16[2,96,1536]{2,1,0:T(8,128)(2,1)}, bf16[2,96,1536]{2,1,0:T(8,128)(2,1)}, u32[]{:S(2)}, u32[]{:S(2)}) collective-permute-start(bf16[2,96,1536]{2,1,0:T(8,128)(2,1)} %get-tuple-element.212), channel_id=1, source_target_pairs={{0,16},{4,20},{8,24},{12,28},{16,0},{20,4},{24,8},{28,12},{1,17},{... | collective-permute-start | bytes 1769480 | tf_op jit(solution)/shard_map/ppermute | solution.py:813
  430.8 17.7 %collective-permute-start.16 = (bf16[2,96,1536]{2,1,0:T(8,128)(2,1)}, bf16[2,96,1536]{2,1,0:T(8,128)(2,1)}, u32[]{:S(2)}, u32[]{:S(2)}) collective-permute-start(bf16[2,96,1536]{2,1,0:T(8,128)(2,1)} %get-tuple-element.213), channel_id=1, source_target_pairs={{0,8},{4,12},{8,0},{12,4},{16,24},{20,28},{24,16},{28,20},{1,9},{5... | collective-permute-start | bytes 1769480 | tf_op jit(solution)/shard_map/ppermute | solution.py:813
  453.1 6.3 %copy-start.2 = (bf16[4,512,512]{2,1,0:T(8,128)(2,1)}, bf16[4,512,512]{2,1,0:T(8,128)(2,1)S(1)}, u32[]{:S(2)}) copy-start(bf16[4,512,512]{2,1,0:T(8,128)(2,1)S(1)} %all-to-all-done.4) | copy-start | bytes 6291460
  453.1 6.8 %copy-start.11 = (f32[1,1024]{1,0:T(1,128)S(1)}, f32[1,1024]{1,0:T(1,128)}, u32[]{:S(2)}) copy-start(f32[1,1024]{1,0:T(1,128)} %get-tuple-element.123) | copy-start | bytes 12292
  453.1 33.0 %all-to-all-start.7 = ((bf16[4,96,1536]{2,1,0:T(8,128)(2,1)}), bf16[4,96,1536]{2,1,0:T(8,128)(2,1)}, u32[]{:S(2)}, u32[]{:S(2)}) async-start(bf16[4,96,1536]{2,1,0:T(8,128)(2,1)} %pad_maximum_fusion.2), calls=%async_computation.10 | async-start | bytes 2359296 | tf_op jit(solution)/shard_map/all_to_all | solution.py:933
  457.8 123.0 %all-gather.21.cloned.1.call-start = ((), (), s32[]{:S(2)}) async-start(), calls=%async_computation.19 | async-start | bytes 2654208 | tf_op jit(solution)/shard_map/all_gather | solution.py:801
  489.1 5.0 collective-permute-start.17
  489.1 33.8 %all-to-all-start.6 = ((bf16[4,96,1536]{2,1,0:T(8,128)(2,1)}), bf16[4,96,1536]{2,1,0:T(8,128)(2,1)}, u32[]{:S(2)}, u32[]{:S(2)}) async-start(bf16[4,96,1536]{2,1,0:T(8,128)(2,1)} %pad_maximum_fusion.3), calls=%async_computation.9 | async-start | bytes 2359296 | tf_op jit(solution)/shard_map/all_to_all | solution.py:933
  493.4 91.7 %all-gather.19.cloned.1.call-start = ((), (), s32[]{:S(2)}) async-start(), calls=%async_computation.18 | async-start | bytes 2654208 | tf_op jit(solution)/shard_map/all_gather | solution.py:801
  495.6 19.4 %collective-permute-start.18 = (bf16[2,2,32,2176]{3,2,1,0:T(8,128)(2,1)S(1)}, bf16[2,2,32,2176]{3,2,1,0:T(8,128)(2,1)S(1)}, u32[]{:S(2)}, u32[]{:S(2)}) collective-permute-start(bf16[2,2,32,2176]{3,2,1,0:T(8,128)(2,1)S(1)} %fusion.21), channel_id=1, source_target_pairs={{0,8},{4,12},{8,0},{12,4},{16,24},{20,28},{24,16},{28,20},{1,9},{5... | collective-permute-start | bytes 1671176 | tf_op jit(solution)/shard_map/ppermute | solution.py:813
  499.2 26.1 %collective-permute-start.20 = (bf16[2,2,32,2176]{3,2,1,0:T(8,128)(2,1)}, bf16[2,2,32,2176]{3,2,1,0:T(8,128)(2,1)}, u32[]{:S(2)}, u32[]{:S(2)}) collective-permute-start(bf16[2,2,32,2176]{3,2,1,0:T(8,128)(2,1)} %fusion.22), channel_id=1, source_target_pairs={{0,16},{4,20},{8,24},{12,28},{16,0},{20,4},{24,8},{28,12},{1,17},{... | collective-permute-start | bytes 1671176 | tf_op jit(solution)/shard_map/ppermute | solution.py:813
  515.0 0.8 copy-start.9
  517.0 9.6 %collective-permute-start.19 = (bf16[2,32,2176]{2,1,0:T(8,128)(2,1)S(1)}, bf16[2,32,2176]{2,1,0:T(8,128)(2,1)}, u32[]{:S(2)}, u32[]{:S(2)}) collective-permute-start(bf16[2,32,2176]{2,1,0:T(8,128)(2,1)S(1)} %fusion.26), channel_id=1, source_target_pairs={{0,16},{4,20},{8,24},{12,28},{16,0},{20,4},{24,8},{28,12},{1,17},{... | collective-permute-start | bytes 835592 | tf_op jit(solution)/shard_map/ppermute | solution.py:813
  525.2 65.0 %all-gather.17.cloned.1.call-start = ((), (), s32[]{:S(2)}) async-start(), calls=%async_computation.17 | async-start | bytes 1843200 | tf_op jit(solution)/shard_map/all_gather | solution.py:801
  528.3 10.9 %collective-permute-start.21 = (bf16[2,32,2176]{2,1,0:T(8,128)(2,1)S(1)}, bf16[2,32,2176]{2,1,0:T(8,128)(2,1)S(1)}, u32[]{:S(2)}, u32[]{:S(2)}) collective-permute-start(bf16[2,32,2176]{2,1,0:T(8,128)(2,1)S(1)} %get-tuple-element.215), channel_id=1, source_target_pairs={{0,8},{4,12},{8,0},{12,4},{16,24},{20,28},{24,16},{28,20},{1,9},{5... | collective-permute-start | bytes 835592 | tf_op jit(solution)/shard_map/ppermute | solution.py:813
  568.9 2.9 copy-start.1
Sparse Core Ops, SparseCore 0:
  27.7 32.6 all-gather.10
  99.8 91.8 all-gather.12
  193.5 48.8 all-gather.14
  245.7 76.4 reduce-scatter.3
  325.6 78.5 reduce-scatter.5
  407.3 44.8 reduce-scatter.7
  454.2 28.9 all-gather.22
  488.5 34.2 all-gather.20
  525.4 29.9 all-gather.18
  566.1 24.1 all-gather.16

commit v3 on v2

--- a/solution.py
+++ b/solution.py
@@ -142,14 +142,11 @@
 
 
 def attend_bwd_kernel(
-    block, kv, q_ref, k_ref, v_ref, g_ref, o_ref, lse_ref, back_ref,
+    block, j, q_ref, k_ref, v_ref, g_ref, o_ref, lse_ref, back_ref,
     queries, grads, delta, keys, values, grad_q,
 ):
-    j = pl.program_id(0)
     first = j % 2 == 0
     n = q_ref.shape[0] // block
-    at_k = pl.ds(pl.multiple_of((kv + j // 2) * 2 * HD, 2 * HD), 2 * HD)
-    at_v = pl.ds(pl.multiple_of((kv + kv // 2 + j // 2) * 2 * HD, 2 * HD), 2 * HD)
     keys[...] = pair_half(k_ref[...], first)
     values[...] = pair_half(v_ref[...], first)
     for i in range(n):
@@ -184,48 +181,36 @@
             return carry[0] + part_k, carry[1] + part_v
 
         part_k, part_v = lax.fori_loop(t + 1, n, body, tile(key, value, key_t, t, True))
-        part_k = (part_k + pltpu.roll(part_k, HD, 1)).astype(bf16)
-        part_v = (part_v + pltpu.roll(part_v, HD, 1)).astype(bf16)
-
-        @pl.when(first)
-        def _():
-            back_ref[rows, at_k] = part_k
-            back_ref[rows, at_v] = part_v
-
-        @pl.when(jnp.logical_not(first))
-        def _():
-            upper = lax.broadcasted_iota(jnp.int32, part_k.shape, 1) >= HD
-            back_ref[rows, at_k] = jnp.where(upper, part_k, back_ref[rows, at_k])
-            back_ref[rows, at_v] = jnp.where(upper, part_v, back_ref[rows, at_v])
-
+        part_k = part_k + pltpu.roll(part_k, HD, 1)
+        part_v = part_v + pltpu.roll(part_v, HD, 1)
+        both = jnp.where(lanes_of(part_k) < HD, part_k, part_v)
+        back_ref[rows, 2 * HD :] = both.astype(bf16)
         return 0
 
     lax.fori_loop(0, n, step, 0)
     for i in range(n):
         pair = jnp.concatenate([grad_q[i, :HD, :block], grad_q[i, HD:, block:]], axis=0)
-        at_q = pl.ds(pl.multiple_of(j * 2 * HD, 2 * HD), 2 * HD)
-        back_ref[i * block : (i + 1) * block, at_q] = pair.T.astype(bf16)
-
-
-def attend_backward(qkv, grads, mixed, lse, block):
+        back_ref[i * block : (i + 1) * block, : 2 * HD] = pair.T.astype(bf16)
+
+
+def attend_backward(qkv, grads, mixed, lse, block, j):
     length, width = qkv.shape
     kv = width // (4 * HD)
     n = length // block
-    spec = lambda at: pl.BlockSpec((length, 2 * HD), at)
-    at_q = lambda j: (0, j)
+    column = lambda c: pl.BlockSpec((length, 2 * HD), lambda i: (0, c))
     return pl.pallas_call(
-        functools.partial(attend_bwd_kernel, block, kv),
-        grid=(kv,),
+        functools.partial(attend_bwd_kernel, block, j),
+        grid=(1,),
         in_specs=[
-            spec(at_q),
-            spec(lambda j: (0, kv + j // 2)),
-            spec(lambda j: (0, kv + kv // 2 + j // 2)),
-            spec(at_q),
-            spec(at_q),
-            pl.BlockSpec((1, n, 1, 2 * block), lambda j: (j, 0, 0, 0)),
+            column(j),
+            column(kv + j // 2),
+            column(kv + kv // 2 + j // 2),
+            column(j),
+            column(j),
+            pl.BlockSpec((1, n, 1, 2 * block), lambda i: (j, 0, 0, 0)),
         ],
-        out_specs=pl.BlockSpec((length, width), lambda j: (0, 0)),
-        out_shape=jax.ShapeDtypeStruct((length, width), bf16),
+        out_specs=pl.BlockSpec((length, 4 * HD), lambda i: (0, 0)),
+        out_shape=jax.ShapeDtypeStruct((length, 4 * HD), bf16),
         scratch_shapes=[
             pltpu.VMEM((n, 2 * block, 2 * HD), bf16),
             pltpu.VMEM((n, 2 * block, 2 * HD), bf16),
@@ -235,9 +220,9 @@
             pltpu.VMEM((n, 2 * HD, 2 * block), f32),
         ],
         cost_estimate=pl.CostEstimate(
-            flops=20 * length * length * 2 * HD * kv,
-            transcendentals=length * length * kv,
-            bytes_accessed=6 * length * width,
+            flops=20 * length * length * 2 * HD,
+            transcendentals=length * length,
+            bytes_accessed=6 * length * 4 * HD,
         ),
         name="attend_backward",
     )(qkv, qkv, qkv, grads, mixed, lse)
@@ -245,9 +230,9 @@
 
 def ffn_kernel(
     shards, begins, z_ref, h_ref, ht_ref, gy_ref, own_g, own_u, own_d, far_g, far_u, far_d,
-    out_in, grad_in, out_ref, grad_ref, *refs,
+    out_in, grad_in, valid, out_ref, grad_ref, *refs,
 ):
-    terms, down = refs[:-1], refs[-1]
+    terms, (down, total) = refs[:-2], refs[-2:]
     t = pl.program_id(0)
     z = z_ref[0]
     even = z_ref[1] == 0
@@ -259,7 +244,7 @@
 
     @pl.when(t == 0)
     def _():
-        out_ref[...] = out_in[...]
+        total[...] = out_in[...]
         grad_ref[...] = jnp.zeros_like(grad_ref) if begins else grad_in[...]
         down[...] = own_d[...]
 
@@ -274,43 +259,46 @@
     def shard_of(r):
         return lax.rem(z + shards - r, shards)
 
-    def columns(r):
-        return pl.ds(pl.multiple_of(shard_of(r) * rows, rows), rows)
-
-    def weight(own, far, r):
-        return own[...] if r == 0 else far[:, r - 1, 0].reshape(rows, unit)
-
-    gate = up = None
-    for r in range(shards):
-        left = h_ref[:, columns(r)]
-        part_g, part_u = dot(left, weight(own_g, far_g, r)), dot(left, weight(own_u, far_u, r))
-        gate, up = (part_g, part_u) if r == 0 else (gate + part_g, up + part_u)
+    def weight(own, far):
+        parts = [own[...]]
+        for r in range(1, shards):
+            parts.append(far[:, r - 1, 0].reshape(rows, unit))
+        return jnp.concatenate(parts, axis=0)
+
+    weight_g, weight_u = weight(own_g, far_g), weight(own_u, far_u)
+    gate, up = dot(h_ref[...], weight_g), dot(h_ref[...], weight_u)
     grad_inner = dot(gy_ref[...], down[...], NT)
     sigma = jax.nn.sigmoid(gate)
     active = gate * sigma
     inner = (active * up).astype(bf16)
     grad_g = (grad_inner * up * sigma * (1.0 + gate * (1.0 - sigma))).astype(bf16)
     grad_u = (grad_inner * active).astype(bf16)
-    out_ref[...] += dot(inner, down[...])
+    total[...] += dot(inner, down[...])
+    grad_ref[...] += dot(grad_g, weight_g, NT) + dot(grad_u, weight_u, NT)
     seg = pl.ds(pl.multiple_of(shard_of(t) * unit, unit), unit)
 
-    def keep(term, r, at):
+    def keep(term, at):
         term = term.astype(bf16)
-        if len(terms) == 1:
-            terms[0][:, r, at : at + piece, seg] = term.reshape(SPLIT, piece, unit)
-            return
-        mine, theirs = terms
-        term = term.reshape(SPLIT // 2, 2, piece, unit)
-        mine[:, r, at : at + piece, seg] = jnp.where(even, term[:, 0], term[:, 1])
-        theirs[:, r, at : at + piece, seg] = jnp.where(even, term[:, 1], term[:, 0])
-
-    for r in range(shards):
-        grad_ref[:, columns(r)] += dot(grad_g, weight(own_g, far_g, r), NT) + dot(
-            grad_u, weight(own_u, far_u, r), NT
-        )
-        left = ht_ref[columns(r), :]
-        keep(dot(left, grad_g), r, 0)
-        keep(dot(left, grad_u), r, piece)
+        for r in range(shards):
+            part = term[r * rows : (r + 1) * rows]
+            if len(terms) == 1:
+                terms[0][:, r, at : at + piece, seg] = part.reshape(SPLIT, piece, unit)
+                continue
+            part = part.reshape(SPLIT // 2, 2, piece, unit)
+            mine, theirs = terms
+            mine[:, r, at : at + piece, seg] = jnp.where(even, part[:, 0], part[:, 1])
+            theirs[:, r, at : at + piece, seg] = jnp.where(even, part[:, 1], part[:, 0])
+
+    keep(dot(ht_ref[...], grad_g), 0)
+    keep(dot(ht_ref[...], grad_u), piece)
+
+    @pl.when(t == shards - 1)
+    def _():
+        out = total[...]
+        if out_ref.dtype == bf16:
+            out = jnp.where(valid[...] > 0, out, 0.0).astype(bf16)
+        out_ref[...] = out
+
     term = dot(inner, gy_ref[...], TN).astype(bf16)
     for d in range(SPLIT):
         for k in range(blocks):
@@ -326,21 +314,25 @@
                 terms[1][(d // 2, *to)] = jnp.where(even, part, even_part)
 
 
-def ffn_chunk(c, kind, parted, z, hidden, hidden_t, grad_y, w_gate, w_up, w_down, far, out_in, grad_in):
+def ffn_chunk(
+    c, kind, parted, z, hidden, hidden_t, grad_y, w_gate, w_up, w_down, far, out_in, grad_in, valid
+):
     rows, width = hidden.shape
     shards = width // w_gate.shape[0]
     depth = w_gate.shape[0]
     unit = w_down.shape[0] // CHUNKS
     piece = depth // SPLIT
-    far = far.reshape(SPLIT, shards - 1, -1, piece, shards * unit)
+    n_far = shards - 1
+    far = far.reshape(SPLIT, n_far, -1, piece, shards * unit)
     terms = (SPLIT // 2 if parted else SPLIT, shards, 3 * piece, shards * unit)
     n_terms = 2 if parted else 1
     seg = lambda t, z_ref: lax.rem(z_ref[0] + shards - t, shards)
     whole = lambda shape: pl.BlockSpec(shape, lambda t, z_ref: (0,) * len(shape))
     own = pl.BlockSpec((depth, unit), lambda t, z_ref: (0, seg(t, z_ref) * CHUNKS + c))
     gathered = lambda at: pl.BlockSpec(
-        (SPLIT, shards - 1, 1, piece, unit), lambda t, z_ref: (0, 0, at, 0, seg(t, z_ref))
+        (SPLIT, n_far, 1, piece, unit), lambda t, z_ref: (0, 0, at, 0, seg(t, z_ref))
     )
+    source = lambda t, z_ref: jnp.maximum(t - 1, 0)
     return pl.pallas_call(
         functools.partial(ffn_kernel, shards, c == 0),
         grid_spec=pltpu.PrefetchScalarGridSpec(
@@ -357,20 +349,21 @@
                 gathered(kind + 1),
                 pl.BlockSpec(
                     (SPLIT, 1, 1, piece, shards * unit),
-                    lambda t, z_ref: (0, jnp.maximum(t - 1, 0), kind + 2, 0, 0),
+                    lambda t, z_ref: (0, source(t, z_ref), kind + 2, 0, 0),
                 ),
                 whole((rows, width)),
                 whole((rows, width)),
+                whole((rows, 1)),
             ],
             out_specs=[
                 whole((rows, width)),
                 whole((rows, width)),
             ]
             + [whole(terms)] * n_terms,
-            scratch_shapes=[pltpu.VMEM((unit, width), bf16)],
+            scratch_shapes=[pltpu.VMEM((unit, width), bf16), pltpu.VMEM((rows, width), f32)],
         ),
         out_shape=[
-            jax.ShapeDtypeStruct((rows, width), f32),
+            jax.ShapeDtypeStruct((rows, width), bf16 if c == CHUNKS - 1 else f32),
             jax.ShapeDtypeStruct((rows, width), f32),
         ]
         + [jax.ShapeDtypeStruct(terms, bf16)] * n_terms,
@@ -380,7 +373,7 @@
             bytes_accessed=12 * width * shards * unit + 20 * rows * width,
         ),
         name="ffn_chunk",
-    )(z, hidden, hidden_t, grad_y, w_gate, w_up, w_down, far, far, far, out_in, grad_in)
+    )(z, hidden, hidden_t, grad_y, w_gate, w_up, w_down, far, far, far, out_in, grad_in, valid)
 
 
 def pack_kernel(m_ref, gate, up, down, out, first_ref, last_ref):
@@ -551,9 +544,12 @@
 
 
 def qkv_bwd_kernel(
-    shards, z_ref, ht_ref, cos_ref, sin_ref, gain_q, gain_k, back_ref, raw_ref, *refs
+    shards, heads, z_ref, ht_ref, cos_ref, sin_ref, gain_q, gain_k,
+    tokens, scale_ref, gain_1, resid, raw_ref, *refs,
 ):
-    own, far, (grad_ref, mine, theirs, sum_q, sum_k, grads) = refs[:3], refs[3:6], refs[6:]
+    back, refs = refs[:heads], refs[heads:]
+    own, far, refs = refs[:3], refs[3:6], refs[6:]
+    tokens_ref, mine, theirs, sum_q, sum_k, sum_1, grads, grad_ref = refs
     z = z_ref[0]
     even = z_ref[1] == 0
     depth = own[0].shape[0]
@@ -567,18 +563,25 @@
 
     cosine, sine = cos_ref[...], sin_ref[...]
     at = 0
-    for size, gain, total in ((own[0].shape[1], gain_q, sum_q), (own[1].shape[1], gain_k, sum_k)):
-        for _ in range(0, size, 2 * HD):
+    halves = [ref[:, 2 * HD :] for ref in back]
+    swapped = [pltpu.roll(half.astype(f32), HD, 1).astype(bf16) for half in halves]
+    low = lanes_of(halves[0]) < HD
+    arrived = [[ref[:, : 2 * HD] for ref in back]]
+    arrived.append([jnp.where(low, halves[i], swapped[i + 1]) for i in range(0, heads, 2)])
+    arrived.append([jnp.where(low, swapped[i], halves[i + 1]) for i in range(0, heads, 2)])
+    for pairs, gain, total in ((arrived[0], gain_q, sum_q), (arrived[1], gain_k, sum_k)):
+        for grad in pairs:
             pair = raw_ref[:, at : at + 2 * HD]
             scale = lax.rsqrt(pair_mean(pair * pair) + EPS)
             hat = pair * scale
-            grad = back_ref[:, at : at + 2 * HD].astype(f32)
+            grad = grad.astype(f32)
             grad = grad * cosine + other_half(grad * sine)
             total[...] += jnp.sum(grad * hat, axis=0, keepdims=True)
             grad = grad * gain[...]
             grads[:, at : at + 2 * HD] = (scale * (grad - hat * pair_mean(grad * hat))).astype(bf16)
             at += 2 * HD
-    grads[:, at:] = back_ref[:, at:]
+    for i, pair in enumerate(arrived[2]):
+        grads[:, at + i * 2 * HD : at + (i + 1) * 2 * HD] = pair
     ends = (0, own[0].shape[1], at, grads.shape[1])
     for r in range(shards):
         part = None
@@ -591,63 +594,83 @@
         mine[:, r] = jnp.where(even, term[:, 0], term[:, 1])
         theirs[:, r] = jnp.where(even, term[:, 1], term[:, 0])
 
-
-def qkv_backward(z, hidden_t, cosine, sine, gain_q, gain_k, back, raw, weights, far, extra):
+    @pl.when(pl.program_id(0) == shards - 1)
+    def _():
+        scale = scale_ref[...]
+        normed = tokens[...].astype(f32) * scale
+        grad = grad_ref[...]
+        sum_1[...] = jnp.sum(grad * normed, axis=0, keepdims=True)
+        tokens_ref[...] = resid[...] + norm_back(grad * gain_1[...], normed, scale)
+
+
+def qkv_backward(z, hidden_t, tables_gains, first_norm, back, raw, weights, far, extra):
     width, local = hidden_t.shape
     depth = weights[0].shape[0]
     shards = width // depth
     piece = depth // SPLIT
     columns = [w.shape[1] for w in weights]
-    each = back.shape[1]
+    each = sum(columns) // shards
     whole = lambda shape: pl.BlockSpec(shape, lambda s, z_ref: (0,) * len(shape))
     rows = lambda x: pl.BlockSpec((local, x.shape[1]), lambda s, z_ref: (s, 0))
     terms = jax.ShapeDtypeStruct((SPLIT // 2, shards, piece, shards * each + extra), bf16)
     at_terms = pl.BlockSpec((SPLIT // 2, shards, piece, each), lambda s, z_ref: (0, 0, 0, s))
     return pl.pallas_call(
-        functools.partial(qkv_bwd_kernel, shards),
+        functools.partial(qkv_bwd_kernel, shards, len(back)),
         grid_spec=pltpu.PrefetchScalarGridSpec(
             num_scalar_prefetch=1,
             grid=(shards,),
-            in_specs=[whole(x.shape) for x in (hidden_t, cosine, sine, gain_q, gain_k)]
-            + [rows(back), rows(raw)]
+            in_specs=[whole(x.shape) for x in (hidden_t, *tables_gains, *first_norm)]
+            + [rows(x) for x in (raw, *back)]
             + projection_specs(shards, depth, piece, columns),
-            out_specs=[whole((local, width)), at_terms, at_terms, whole((1, 2 * HD)), whole((1, 2 * HD))],
-            scratch_shapes=[pltpu.VMEM((local, each), bf16)],
+            out_specs=[whole((local, width)), at_terms, at_terms]
+            + [whole((1, n)) for n in (2 * HD, 2 * HD, width)],
+            scratch_shapes=[pltpu.VMEM((local, each), bf16), pltpu.VMEM((local, width), f32)],
         ),
         out_shape=[
             jax.ShapeDtypeStruct((local, width), f32),
             terms,
             terms,
-            jax.ShapeDtypeStruct((1, 2 * HD), f32),
-            jax.ShapeDtypeStruct((1, 2 * HD), f32),
-        ],
+        ]
+        + [jax.ShapeDtypeStruct((1, n), f32) for n in (2 * HD, 2 * HD, width)],
         cost_estimate=pl.CostEstimate(
             flops=4 * local * width * sum(columns),
             transcendentals=0,
             bytes_accessed=4 * width * sum(columns) + 8 * local * sum(columns),
         ),
         name="qkv_backward",
-    )(z, hidden_t, cosine, sine, gain_q, gain_k, back, raw, *weights, far, far, far)
-
-
-def unpack_qkv_kernel(source, q_ref, k_ref, v_ref):
-    at = 0
-    for ref in (q_ref, k_ref, v_ref):
-        ref[...] = source[:, at : at + ref.shape[1]].astype(f32)
-        at += ref.shape[1]
-
-
-def unpack_qkv(source, shards, columns):
-    depth = source.shape[0]
-    each = [n // shards for n in columns]
+    )(z, hidden_t, *tables_gains, *first_norm, raw, *back, *weights, far, far, far)
+
+
+def unpack_qkv_kernel(shards, m_ref, even, odd, *refs):
+    piece = even.shape[1]
+    for b in range(SPLIT):
+        source = (odd if b % 2 else even)[b // 2].astype(f32)
+        rows = pl.ds(pl.multiple_of(jnp.bitwise_xor(m_ref[0], b) * piece, piece), piece)
+        at = 0
+        for s in range(shards):
+            for ref in refs[:3]:
+                n = ref.shape[1] // shards
+                ref[rows, s * n : (s + 1) * n] = source[:, at : at + n]
+                at += n
+        for ref in refs[3:]:
+            ref[rows, :] = source[:, at : at + ref.shape[1]]
+            at += ref.shape[1]
+
+
+def unpack_qkv(member, even, odd, shards, columns):
+    piece = even.shape[1]
+    whole = lambda shape: pl.BlockSpec(shape, lambda i, m_ref: (0,) * len(shape))
     return pl.pallas_call(
-        unpack_qkv_kernel,
-        grid=(shards,),
-        in_specs=[pl.BlockSpec((depth, sum(each)), lambda s: (0, s))],
-        out_specs=[pl.BlockSpec((depth, n), lambda s: (0, s)) for n in each],
-        out_shape=[jax.ShapeDtypeStruct((depth, n), f32) for n in columns],
+        functools.partial(unpack_qkv_kernel, shards),
+        grid_spec=pltpu.PrefetchScalarGridSpec(
+            num_scalar_prefetch=1,
+            grid=(1,),
+            in_specs=[whole(even.shape), whole(odd.shape)],
+            out_specs=[whole((SPLIT * piece, n)) for n in columns],
+        ),
+        out_shape=[jax.ShapeDtypeStruct((SPLIT * piece, n), f32) for n in columns],
         name="unpack_qkv",
-    )(source)
+    )(member.reshape(1), even, odd)
 
 
 def out_fwd_kernel(shards, z_ref, mixed, tokens, gain, own, far, resid_ref, scale_ref, h_ref, ht_ref):
@@ -661,8 +684,13 @@
     hidden = resid * scale * gain[...]
     resid_ref[...] = resid
     scale_ref[...] = scale
-    h_ref[...] = hidden.astype(bf16)
-    ht_ref[...] = hidden.T.astype(bf16)
+    turned = hidden.T.astype(bf16)
+    low = hidden.astype(bf16)
+    depth = own.shape[0]
+    for s in range(shards):
+        at = part_of(z, s, shards, depth)
+        h_ref[:, at] = low[:, s * depth : (s + 1) * depth]
+        ht_ref[at, :] = turned[s * depth : (s + 1) * depth]
 
 
 def far_out_spec(far, width):
@@ -701,8 +729,11 @@
     local = grad.shape[0]
     scale = scale_ref[...]
     normed = resid[...] * scale
-    sum_ref[...] = jnp.sum(grad[...] * normed, axis=0, keepdims=True)
-    total = grad_y[...].astype(f32) + norm_back(grad[...] * gain[...], normed, scale)
+    depth = own.shape[0]
+    parts = [grad[:, part_of(z, s, shards, depth)] for s in range(shards)]
+    come = jnp.concatenate(parts, axis=1)
+    sum_ref[...] = jnp.sum(come * normed, axis=0, keepdims=True)
+    total = grad_y[...].astype(f32) + norm_back(come * gain[...], normed, scale)
     grad_resid[...] = total
     low = total.astype(bf16)
     branch[...] = low
@@ -785,9 +816,8 @@
     def from_others(self, x):
         return [self.shift(x, r) for r in range(1, self.n_seq)]
 
-    def passed_on(self, x):
+    def pass_on(self, x):
         n = self.n_seq
-        z = lax.axis_index("seq")
         up = down = x
         below, above = [], []
         for step in range(1, n):
@@ -795,7 +825,23 @@
             down = lax.ppermute(down, "seq", [(i + 1, i) for i in range(n - step)])
             below.append(up)
             above.append(down)
-        return [jnp.where(z >= r, below[r - 1], above[n - r - 1]) for r in range(1, n)]
+        return below + above
+
+    def either(self, came):
+        n = self.n_seq
+        z = lax.axis_index("seq")
+        return [jnp.where(z >= r, came[r - 1], came[2 * n - 2 - r]) for r in range(1, n)]
+
+    def gather_all(self, x):
+        if self.groups:
+            x = self.gather(lax.all_gather(x, "seq")[None])
+        else:
+            x = lax.all_gather(x, ("dp", "seq"))
+        return x.reshape(SPLIT, self.n_seq, *x.shape[-2:])
+
+    def gather_near(self, x):
+        even = jnp.stack([x] + [self.swap(x, bit) for bit in (2, 4, 6)])
+        return even, self.swap(even, 1)
 
     def gather(self, x):
         return lax.all_gather(x, "dp", axis=0, tiled=True, axis_index_groups=self.groups)
@@ -850,7 +896,10 @@
         to_x = self._sum(None, 1 - self.x, True).astype(bf16)
         to_y = self._sum(1 - self.y, None, False).astype(bf16)
         self.sent = (to_x, to_y)
-        self.state = (self.axes.swap(to_x, 2), self.axes.swap(to_y, 4))
+        return self
+
+    def send_first(self):
+        self.state = (self.axes.swap(self.sent[0], 2), self.axes.swap(self.sent[1], 4))
         return self
 
     def second(self):
@@ -859,7 +908,10 @@
         to_y = self._sum(1 - self.y, self.x, True, pick(self.got_x, 1 - self.y)).astype(bf16)
         to_x = self._sum(self.y, 1 - self.x, False, pick(self.got_y, 1 - self.x)).astype(bf16)
         self.sent = (to_x, to_y)
-        self.state = (self.axes.swap(to_y, 4), self.axes.swap(to_x, 2))
+        return self
+
+    def send_second(self):
+        self.state = (self.axes.swap(self.sent[1], 4), self.axes.swap(self.sent[0], 2))
         return self
 
     def third(self):
@@ -889,6 +941,18 @@
     where = jnp.stack([z, lax.rem(member, 2)]).astype(jnp.int32)
     mine = lambda x: lax.dynamic_slice_in_dim(x, member * piece, piece, axis=0)
 
+    def cut(parts):
+        return lax.optimization_barrier(tuple(parts[r] for r in range(shards)))
+
+    def cross_back(parts):
+        return tuple(axes.shift(parts[r], -r) for r in range(1, shards))
+
+    def add(own, others):
+        own = own.astype(f32)
+        for arr in others:
+            own = own + arr.astype(f32)
+        return axes.over_groups(own.astype(bf16))
+
     def by_owner(parts):
         pick = lambda i: lax.dynamic_index_in_dim(parts, lax.rem(z + shards - i, shards), 0)
         return jnp.concatenate([pick(i) for i in range(shards)], axis=0)
@@ -932,18 +996,18 @@
     def exchange(x):
         return lax.all_to_all(x, "seq", split_axis=0, concat_axis=0, tiled=True)
 
-    crossed = axes.passed_on(after(first_chunks, *near))
+    crossed = axes.pass_on(after(first_chunks, *near))
     send, raw = qkv_forward(where, hidden1, cosine, sine, gain_q, gain_k, weights, far_qkv)
-    far = axes.gather(stack_after(crossed, send))
+    far = axes.gather(jnp.stack(axes.either([after(x, send) for x in crossed])))
     qkv = exchange(send)
     crossed = axes.from_others(after(last_chunk, qkv))
     block = 512
     mixed_heads, lse = attend_forward(qkv, block)
     mixed = exchange(after(mixed_heads, *crossed))
-    crossed = stack_after(crossed, mixed_heads)
+    crossed = jnp.stack([after(x, mixed_heads) for x in crossed])
     far_last = axes.gather(crossed)
+    mixed = after(mixed, crossed)
     resid, scale2, hidden2, hidden2_t = out_forward(where, mixed, tokens[0], gain2, w_out, far)
-    hidden2 = after(hidden2, crossed)
 
     result, grad_hidden2 = resid, resid
 
@@ -952,45 +1016,44 @@
         source, kind = (far_last, 0) if last else (far, 3 * c)
         return ffn_chunk(
             c, kind, last, where, hidden2, hidden2_t, grad_y, w_gate, w_up, w_down, source,
-            result, grad_hidden2,
+            result, grad_hidden2, valid.astype(f32),
         )
 
-    result, grad_hidden2, terms0 = chunk(0, result, grad_hidden2)
-    sum0 = axes.scatter(terms0)
-    result, grad_hidden2, terms1 = chunk(1, result, grad_hidden2)
-    sum1 = axes.scatter(terms1)
-    result, grad_hidden2, *terms2 = chunk(2, result, grad_hidden2)
-    sum2 = Reduction(axes, *terms2)
+    result, grad_hidden2, terms = chunk(0, result, grad_hidden2)
+    sum0 = axes.scatter(terms)
+    result, grad_hidden2, terms = chunk(1, result, grad_hidden2)
+    sum1 = axes.scatter(terms)
+    output, grad_hidden2, *terms = chunk(2, result, grad_hidden2)
+    sum2 = Reduction(axes, *terms)
 
     grad_resid, term_gain2, branch, send = out_backward(
         where, grad_hidden2, grad_y, resid, scale2, gain2, w_out, far
     )
     grad_heads = exchange(send)
     terms_out = out_terms(where, mixed, after(branch, send))
-    sum_out = axes.scatter(terms_out)
     sum2.then(terms_out)
-    sum2.first()
-    parts0 = by_owner(after(sum0, grad_heads))
-    grad_heads = after(grad_heads, terms_out, *sum2.sent, parts0)
-    parts0 = exchange(parts0)
-    back = attend_backward(qkv, grad_heads, mixed_heads, lse, block)
-    back_rows = exchange(after(back, parts0))
+    sum2.first().send_first()
+    parts0 = cut(after(sum0, grad_heads))
+    grad_heads = after(grad_heads, terms_out, *sum2.sent, *parts0)
+    others0 = cross_back(parts0)
+    back = attend_backward(qkv, grad_heads, mixed_heads, lse, block, 0)
+    back_rows = [exchange(back)]
+    for j in range(1, KV // shards):
+        piece0 = add(parts0[0], after(others0, back))
+        grad_heads = after(grad_heads, piece0)
+        back = attend_backward(qkv, grad_heads, mixed_heads, lse, block, j)
+        back_rows.append(exchange(after(back, back_rows[-1])))
     sum2.then(back)
-    sum2.second()
-    piece0 = total(after(parts0, back))
+    sum2.second().send_second()
     parts1 = by_owner(after(sum1, back))
-    parts2 = by_owner(sum2.third())
-    back_rows = after(back_rows, *sum2.sent, piece0, parts1, parts2)
+    back_rows[-1] = after(back_rows[-1], parts1, *sum2.sent)
+    sum_out = axes.scatter(after(terms_out, piece0))
     piece0 = axes.gather(piece0[None])
-    parts1 = exchange(after(parts1, back_rows))
-    parts2 = exchange(after(parts2, back_rows))
-    grad_hidden1, terms, other, sum_q, sum_k = qkv_backward(
-        where, hidden1_t, cosine, sine, gain_q, gain_k, back_rows, raw, weights, far_qkv, 128
+    parts1 = exchange(after(parts1, back_rows[-1]))
+    grad_tokens, terms, other, sum_q, sum_k, term_gain1 = qkv_backward(
+        where, hidden1_t, (cosine, sine, gain_q, gain_k), (tokens[0], scale1, gain1, grad_resid),
+        back_rows, raw, weights, far_qkv, 128,
     )
-    piece1 = axes.gather(total(after(parts1, grad_hidden1))[None])
-    normed1 = inputs * scale1
-    term_gain1 = jnp.sum(grad_hidden1 * normed1, axis=0)
-    grad_tokens = (grad_resid + norm_back(grad_hidden1 * gain1, normed1, scale1))[None]
 
     parts = [
         term_gain1.reshape(shards, depth),
@@ -1009,23 +1072,27 @@
     start = (0, 0, 0, terms.shape[3] - 128)
     terms = lax.dynamic_update_slice(terms, pick(parity), start)
     other = lax.dynamic_update_slice(other, pick(1 - parity), start)
-    tail = Reduction(axes, terms, other).first()
-    parts2 = after(parts2, *tail.sent)
-    piece2 = axes.gather(total(parts2)[None])
-    tail.second()
+    tail = Reduction(axes, terms, after(other, parts1, *sum2.state))
+    parts2 = by_owner(sum2.third())
+    tail.then(parts2)
+    parts2 = exchange(parts2)
+    tail.first().send_first()
+    piece1 = total(after(parts1, *tail.sent))
+    tail.second().send_second()
+    tail.then(parts2)
     tail = by_owner(jnp.concatenate([tail.third(), sum_out], axis=2))
-    whole = axes.gather(total(exchange(tail)))
-    grads = unpack_ffn(piece0, 0, 1, (), depth, shards, unit, width)
-    grads = unpack_ffn(piece1, 1, 1, grads, depth, shards, unit, width)
-    grads = unpack_ffn(piece2, 2, 1, grads, depth, shards, unit, width)
+    late = axes.gather(jnp.concatenate([piece1, total(after(parts2, tail))], axis=0)[None])
+    grads = unpack_ffn(after(piece0, tail), 0, 1, (), depth, shards, unit, width)
+    even, odd = axes.gather_near(after(total(exchange(tail)), *grads))
+    grads = unpack_ffn(late, 1, 2, grads, depth, shards, unit, width)
     grad_gate, grad_up, grad_down = grads
-    output = jnp.where(valid, result, 0.0).astype(bf16)[None]
-    grad_out = whole[:, -width:].astype(f32)
-    grad_query, grad_key, grad_value = unpack_qkv(whole, shards, columns)
-    sums = whole[:, sum(columns) : sum(columns) + 128].astype(f32).reshape(SPLIT, -1)[:, :each].reshape(-1)
+    grad_query, grad_key, grad_value, sums, grad_out = unpack_qkv(
+        member, even, odd, shards, columns + [128, width]
+    )
+    sums = sums.reshape(SPLIT, -1)[:, :each].reshape(-1)
     return (
-        output,
-        grad_tokens,
+        output[None],
+        grad_tokens[None],
         grad_query,
         grad_key,
         grad_value,

time: 614 us -> 576 us (0.938)
  blocking collectives: 73.3 us -> 52.7 us
  waiting for transfers between devices: 168 us -> 149 us
  other arithmetic: 57.1 us -> 43.4 us
  starting transfers between devices: 54.2 us -> 67.2 us
    ppermute x10 -> x14, waiting for transfers between devices: 66.2 us -> 39.8 us  [swap(): return lax.ppermute(x, 'dp', [(i, i ^ bit) for i in range(self.n_dp)])]
    all_to_all x2 -> x1, blocking collectives: 73.3 us -> 52.7 us  [exchange(): return lax.all_to_all(x, 'seq', split_axis=0, concat_axis=0, tiled=True)]
    ppermute x6, waiting for transfers between devices: 35.9 us -> 26.8 us  [the longest x3 26.8 us: pass_on(): down = lax.ppermute(down, 'seq', [(i + 1, i) for i in range(n - step)])]
    all_to_all x6 -> x7, waiting for transfers between devices: 47.5 us -> 56.4 us  [exchange(): return lax.all_to_all(x, 'seq', split_axis=0, concat_axis=0, tiled=True)]
    reduce_scatter x3, waiting for transfers between devices: 0.01 us -> 8.85 us  [scatter(): lax.psum_scatter(flat, 'dp', scatter_dimension=0, tiled=True, axis_index_...]
    reduce_sum x4 -> x3, other arithmetic: 8.7 us -> 0.53 us  [total(): return axes.over_groups(jnp.sum(parts.astype(f32), axis=0).astype(bf16))]
    all_to_all x6 -> x7, starting transfers between devices: 24.6 us -> 31.4 us  [exchange(): return lax.all_to_all(x, 'seq', split_axis=0, concat_axis=0, tiled=True)]
    ppermute x10 -> x14, starting transfers between devices: 9.21 us -> 12.9 us  [swap(): return lax.ppermute(x, 'dp', [(i, i ^ bit) for i in range(self.n_dp)])]
  transfers between devices with their start and end apart: 38 -> 44, of which waited for: 17 -> 22; matrix products, arithmetic and copies ran while one was open for 12% -> 10% of each run, Pallas kernels for 33% -> 37%
where the time goes in v3:
time: 576 us; the launch traced here: 565 us
  Pallas kernels  217 us (38%)
  waiting for transfers between devices  149 us (26%)
  starting transfers between devices  67.2 us (12%)
  blocking collectives  52.7 us (9%)
  other arithmetic  43.4 us (8%)
  local copies, waits for them, and re-layouts  20.9 us (4%)
  between operations  15.6 us (3%)
    pallas_call x3, Pallas kernels, ffn_chunk(): pl.pallas_call(functools.partial(ffn_kernel, shards, c == 0), grid_spec=p...  95.6 us
    all_to_all x7, waiting for transfers between devices, exchange(): return lax.all_to_all(x, 'seq', split_axis=0, concat_axis=0, tiled=True)  56.4 us
    all_to_all x1, blocking collectives, exchange(): return lax.all_to_all(x, 'seq', split_axis=0, concat_axis=0, tiled=True)  52.7 us
    pallas_call x2, Pallas kernels, attend_backward(): pl.pallas_call(functools.partial(attend_bwd_kernel, block, j), grid=(1,),...  40.2 us
    ppermute x14, waiting for transfers between devices, swap(): return lax.ppermute(x, 'dp', [(i, i ^ bit) for i in range(self.n_dp)])  39.8 us
    all_to_all x7, starting transfers between devices, exchange(): return lax.all_to_all(x, 'seq', split_axis=0, concat_axis=0, tiled=True)  31.4 us
    ppermute x3, waiting for transfers between devices, pass_on(): down = lax.ppermute(down, 'seq', [(i + 1, i) for i in range(n - step)])  26.8 us
    ppermute x9, waiting for transfers between devices, shift(): return lax.ppermute(x, 'seq', [(i, (i + r) % n) for i in range(n)])  17.3 us
  transfers between devices with their start and end apart: 44, of which 22 were waited for; matrix products, arithmetic and copies ran while one was open for 10% of the time, Pallas kernels for 37%

profile of v3, /device:TPU:0, one launch (start us, length us, event | category | flops | bytes accessed | tf_op | source)
XLA Modules:
  0.0 565.5 jit_solution(5937762515109500971)
XLA Ops:
  9.7 5.1 collective-permute-start.2
  15.8 3.1 collective-permute-done.2
  18.9 7.7 %collective-permute-done.1 = bf16[32,2176]{1,0:T(8,128)(2,1)S(1)} collective-permute-done((bf16[32,2176]{1,0:T(8,128)(2,1)S(1)}, bf16[32,2176]{1,0:T(8,128)(2,1)S(1)}, u32[]{:S(2)}, u32[]{:S(2)}) %collective-permute-start.1) | collective-permute-done | bytes 139296 | tf_op jit(solution)/shard_map/ppermute | solution.py:814
  27.6 2.2 pack.1
  33.6 4.6 collective-permute-start.6
  39.8 11.3 %collective-permute-done.7 = bf16[224,1536]{1,0:T(8,128)(2,1)S(1)} collective-permute-done((bf16[224,1536]{1,0:T(8,128)(2,1)}, bf16[224,1536]{1,0:T(8,128)(2,1)S(1)}, u32[]{:S(2)}, u32[]{:S(2)}) %collective-permute-start.7) | collective-permute-done | bytes 688160 | tf_op jit(solution)/shard_map/ppermute | solution.py:825
  52.4 1.5 collective-permute-start.10
  55.7 13.1 %collective-permute-done.8 = bf16[224,1536]{1,0:T(8,128)(2,1)S(1)} collective-permute-done((bf16[224,1536]{1,0:T(8,128)(2,1)S(1)}, bf16[224,1536]{1,0:T(8,128)(2,1)S(1)}, u32[]{:S(2)}, u32[]{:S(2)}) %collective-permute-start.8) | collective-permute-done | bytes 688160 | tf_op jit(solution)/shard_map/ppermute | solution.py:825
  70.0 1.5 collective-permute-start.11
  72.8 10.2 %qkv_forward.1 = (bf16[2048,512]{1,0:T(8,128)(2,1)}, f32[2048,384]{1,0:T(8,128)}) custom-call(s32[2]{0:T(128)} %pad_add_fusion.z_ref, bf16[512,1024]{1,0:T(8,128)(2,1)} %fusion.2.h_ref, f32[512,128]{1,0:T(8,128)} %copy.54.cos_ref, f32[512,128]{1,0:T(8,128)} %pad_maximum_fusion.9.sin_ref, f32[1,128]{1,0:T(1,128)} %tile.33.gain_q, f32[1,128]{1,0:T(1,128)} %tile.36.gain_k, ...), custom_call_target="tpu_custom_call" | custom-call | flops 2147483648 | bytes 12582912 | tf_op jit(solution)/shard_map/qkv_forward/pallas_call | solution.py:521
  83.1 2.5 collective-permute-done.9
  86.9 1.5 pad_maximum_fusion
  89.3 52.7 %all_to_all.73 = bf16[4,512,512]{2,1,0:T(8,128)(2,1)} all-to-all(bf16[4,512,512]{2,1,0:T(8,128)(2,1)S(1)} %bitcast.202), channel_id=1, replica_groups=mesh['dp'=8,'seq'=4] {'seq'}, dimensions={0} | all-to-all | bytes 4194304 | tf_op jit(solution)/shard_map/all_to_all | solution.py:997
  144.0 16.5 %attend_forward.1 = (bf16[2048,256]{1,0:T(8,128)(2,1)}, f32[2,4,1,1024]{3,2,1,0:T(1,128)}) custom-call(bf16[2048,512]{1,0:T(8,128)(2,1)} %bitcast.193, bf16[2048,512]{1,0:T(8,128)(2,1)} %bitcast.194, bf16[2048,512]{1,0:T(8,128)(2,1)} %bitcast.195), custom_call_target="tpu_custom_call" | custom-call | flops 8589934592 | bytes 3145728 | tf_op jit(solution)/shard_map/attend_forward/pallas_call | solution.py:118
  160.5 6.5 %collective-permute-done.4 = bf16[96,1536]{1,0:T(8,128)(2,1)S(1)} collective-permute-done((bf16[96,1536]{1,0:T(8,128)(2,1)S(1)}, bf16[96,1536]{1,0:T(8,128)(2,1)S(1)}, u32[]{:S(2)}, u32[]{:S(2)}) %collective-permute-start.4) | collective-permute-done | bytes 294944 | tf_op jit(solution)/shard_map/ppermute | solution.py:814
  168.0 3.7 all-to-all-start.1
  175.0 21.6 %all-to-all-done.1 = bf16[4,512,256]{2,1,0:T(8,128)(2,1)S(1)} async-done(((bf16[4,512,256]{2,1,0:T(8,128)(2,1)}), bf16[4,512,256]{2,1,0:T(8,128)(2,1)S(1)}, u32[]{:S(2)}, u32[]{:S(2)}) %all-to-all-start.1) | async-done | bytes 1048608 | tf_op jit(solution)/shard_map/all_to_all | solution.py:997
  197.6 6.6 %out_forward.1 = (f32[512,1024]{1,0:T(8,128)}, f32[512,1]{1,0:T(8,128)}, bf16[512,1024]{1,0:T(8,128)(2,1)}, bf16[1024,512]{1,0:T(8,128)(2,1)}) custom-call(s32[2]{0:T(128)} %pad_add_fusion.z_ref, bf16[2048,256]{1,0:T(8,128)(2,1)} %bitcast.176, bf16[512,1024]{1,0:T(8,128)(2,1)} %bitcast.174, f32[1,1024]{1,0:T(1,128)} %bitcast.222, bf16[256,1024]{1,0:T(8,128)(2,1)} %own.3, ...), custom_call_target="tpu_custom_call" | custom-call | flops 1073741824 | bytes 7340032 | tf_op jit(solution)/shard_map/out_forward/pallas_call | solution.py:708
  204.3 32.1 %ffn_chunk.3 = (f32[512,1024]{1,0:T(8,128)}, f32[512,1024]{1,0:T(8,128)}, bf16[8,4,96,1536]{3,2,1,0:T(8,128)(2,1)}) custom-call(s32[2]{0:T(128)} %pad_add_fusion.z_ref, bf16[512,1024]{1,0:T(8,128)(2,1)} %get-tuple-element.111.h_ref, bf16[1024,512]{1,0:T(8,128)(2,1)} %get-tuple-element.112.ht_ref, bf16[512,1024]{1,0:T(8,128)(2,1)} %bitcast_select_fusion.gy_ref.grad_y, ...), custom_call_target="tpu_custom_call" | custom-call | flops 14495514624 | bytes 29360128 | tf_op jit(solution)/shard_map/ffn_chunk/pallas_call | solution.py:336
  236.8 31.7 %ffn_chunk.4 = (f32[512,1024]{1,0:T(8,128)}, f32[512,1024]{1,0:T(8,128)}, bf16[8,4,96,1536]{3,2,1,0:T(8,128)(2,1)}) custom-call(s32[2]{0:T(128)} %pad_add_fusion.z_ref, bf16[512,1024]{1,0:T(8,128)(2,1)} %get-tuple-element.111.h_ref, bf16[1024,512]{1,0:T(8,128)(2,1)} %get-tuple-element.112.ht_ref, bf16[512,1024]{1,0:T(8,128)(2,1)} %bitcast_select_fusion.gy_ref.grad_y, ...), custom_call_target="tpu_custom_call" | custom-call | flops 14495514624 | bytes 29360128 | tf_op jit(solution)/shard_map/ffn_chunk/pallas_call | solution.py:336
  268.5 31.9 %ffn_chunk.5 = (bf16[512,1024]{1,0:T(8,128)(2,1)}, f32[512,1024]{1,0:T(8,128)}, bf16[4,4,96,1536]{3,2,1,0:T(8,128)(2,1)}, bf16[4,4,96,1536]{3,2,1,0:T(8,128)(2,1)}) custom-call(s32[2]{0:T(128)} %pad_add_fusion.z_ref, bf16[512,1024]{1,0:T(8,128)(2,1)} %get-tuple-element.111.h_ref, bf16[1024,512]{1,0:T(8,128)(2,1)} %get-tuple-element.112.ht_ref, ...), custom_call_target="tpu_custom_call" | custom-call | flops 14495514624 | bytes 29360128 | tf_op jit(solution)/shard_map/ffn_chunk/pallas_call | solution.py:336
  300.5 7.3 %out_backward.1 = (f32[512,1024]{1,0:T(8,128)}, f32[1,1024]{1,0:T(1,128)}, bf16[512,1024]{1,0:T(8,128)(2,1)}, bf16[2048,256]{1,0:T(8,128)(2,1)}) custom-call(s32[2]{0:T(128)} %pad_add_fusion.z_ref, f32[512,1024]{1,0:T(8,128)} %get-tuple-element.119.grad, bf16[512,1024]{1,0:T(8,128)(2,1)} %bitcast_select_fusion.gy_ref.grad_y, ...), custom_call_target="tpu_custom_call" | custom-call | flops 1073741824 | bytes 10485760 | tf_op jit(solution)/shard_map/out_backward/pallas_call | solution.py:753
  307.8 3.7 all-to-all-start.2
  311.5 5.5 out_terms.1
  317.0 2.9 fusion.4
  319.9 3.0 fusion.3
  322.9 15.2 %all-to-all-done.2 = bf16[4,512,256]{2,1,0:T(8,128)(2,1)S(1)} async-done(((bf16[4,512,256]{2,1,0:T(8,128)(2,1)}), bf16[4,512,256]{2,1,0:T(8,128)(2,1)S(1)}, u32[]{:S(2)}, u32[]{:S(2)}) %all-to-all-start.2) | async-done | bytes 1048608 | tf_op jit(solution)/shard_map/all_to_all | solution.py:997
  338.1 1.7 slice_bitcast_fusion
  339.8 1.5 collective-permute-start.13
  341.9 20.3 %attend_backward.2 = bf16[2048,256]{1,0:T(8,128)(2,1)} custom-call(bf16[2048,512]{1,0:T(8,128)(2,1)} %bitcast.196, bf16[2048,512]{1,0:T(8,128)(2,1)} %bitcast.197, bf16[2048,512]{1,0:T(8,128)(2,1)} %bitcast.198, bf16[2048,256]{1,0:T(8,128)(2,1)} %bitcast.205, bf16[2048,256]{1,0:T(8,128)(2,1)} %get-tuple-element.98.o_ref, ...), custom_call_target="tpu_custom_call" | custom-call | flops 10737418240 | bytes 3145728 | tf_op jit(solution)/shard_map/attend_backward/pallas_call | solution.py:201
  362.2 4.9 all-to-all-start.3
  367.0 1.5 collective-permute-start.16
  368.5 1.5 collective-permute-start.17
  370.0 2.0 add_convert_fusion.4
  372.0 20.0 %attend_backward.3 = bf16[2048,256]{1,0:T(8,128)(2,1)} custom-call(bf16[2048,512]{1,0:T(8,128)(2,1)} %bitcast.199, bf16[2048,512]{1,0:T(8,128)(2,1)} %bitcast.200, bf16[2048,512]{1,0:T(8,128)(2,1)} %bitcast.201, bf16[2048,256]{1,0:T(8,128)(2,1)} %bitcast.206, bf16[2048,256]{1,0:T(8,128)(2,1)} %get-tuple-element.98.o_ref, ...), custom_call_target="tpu_custom_call" | custom-call | flops 10737418240 | bytes 3145728 | tf_op jit(solution)/shard_map/attend_backward/pallas_call | solution.py:201
  392.0 5.1 all-to-all-start.4
  397.1 8.8 %reduce-scatter.6.cloned.1.call-done = bf16[4,96,1536]{2,1,0:T(8,128)(2,1)} async-done(((bf16[32,96,1536]{2,1,0:T(8,128)(2,1)}), bf16[4,96,1536]{2,1,0:T(8,128)(2,1)}) %reduce-scatter.6.cloned.1.call-update) | async-done | bytes 1179664 | tf_op jit(solution)/shard_map/reduce_scatter | solution.py:851
  406.0 1.3 collective-permute-done.16
  407.4 1.6 constant_dynamic-slice_fusion.9
  410.3 3.2 fusion.9
  413.5 7.1 %all-to-all-done.4 = bf16[4,512,256]{2,1,0:T(8,128)(2,1)S(1)} async-done(((bf16[4,512,256]{2,1,0:T(8,128)(2,1)}), bf16[4,512,256]{2,1,0:T(8,128)(2,1)S(1)}, u32[]{:S(2)}, u32[]{:S(2)}) %all-to-all-start.4) | async-done | bytes 1048608 | tf_op jit(solution)/shard_map/all_to_all | solution.py:997
  421.6 3.5 all-to-all-start.5
  430.9 1.5 collective-permute-start.19
  432.4 16.8 %qkv_backward.1 = (f32[512,1024]{1,0:T(8,128)}, bf16[4,4,32,2176]{3,2,1,0:T(8,128)(2,1)}, bf16[4,4,32,2176]{3,2,1,0:T(8,128)(2,1)}, f32[1,128]{1,0:T(1,128)}, f32[1,128]{1,0:T(1,128)}, /*index=5*/f32[1,1024]{1,0:T(1,128)}) custom-call(s32[2]{0:T(128)} %pad_add_fusion.z_ref, bf16[1024,512]{1,0:T(8,128)(2,1)} %copy.55.ht_ref, f32[512,128]{1,0:T(8,128)} %copy.54.cos_ref, ...), custom_call_target="tpu_custom_call" | custom-call | flops 4294967296 | bytes 16777216 | tf_op jit(solution)/shard_map/qkv_backward/pallas_call | solution.py:617
  456.1 2.4 fusion.6
  460.1 5.1 all-to-all-start.6
  465.9 1.4 fusion.12
  467.3 1.4 fusion.11
  470.2 17.7 %collective-permute-done.21 = bf16[2,2,32,2176]{3,2,1,0:T(8,128)(2,1)S(1)} collective-permute-done((bf16[2,2,32,2176]{3,2,1,0:T(8,128)(2,1)S(1)}, bf16[2,2,32,2176]{3,2,1,0:T(8,128)(2,1)S(1)}, u32[]{:S(2)}, u32[]{:S(2)}) %collective-permute-start.21) | collective-permute-done | bytes 557088 | tf_op jit(solution)/shard_map/ppermute | solution.py:859
  488.8 2.4 fusion.15
  491.2 1.6 collective-permute-start.24
  494.5 3.5 collective-permute-done.24
  497.9 1.7 collective-permute-done.22
  499.6 1.7 fusion.18
  504.5 5.4 all-to-all-start.7
  509.9 4.5 unpack_ffn.2
  514.3 11.4 %all-to-all-done.7 = bf16[4,32,3200]{2,1,0:T(8,128)(2,1)S(1)} async-done(((bf16[4,32,3200]{2,1,0:T(8,128)(2,1)}), bf16[4,32,3200]{2,1,0:T(8,128)(2,1)S(1)}, u32[]{:S(2)}, u32[]{:S(2)}) %all-to-all-start.7) | async-done | bytes 819232 | tf_op jit(solution)/shard_map/all_to_all | solution.py:997
  525.9 2.2 collective-permute-start.27
  529.5 5.7 %collective-permute-done.27 = bf16[32,3200]{1,0:T(8,128)(2,1)S(1)} collective-permute-done((bf16[32,3200]{1,0:T(8,128)(2,1)S(1)}, bf16[32,3200]{1,0:T(8,128)(2,1)S(1)}, u32[]{:S(2)}, u32[]{:S(2)}) %collective-permute-start.27) | collective-permute-done | bytes 204832 | tf_op jit(solution)/shard_map/ppermute | solution.py:859
  535.2 4.0 collective-permute-done.26
  539.2 2.6 collective-permute-done.25
  542.0 2.3 collective-permute-done.28.odd
  545.2 3.3 unpack_qkv.1
  550.7 7.7 %unpack_ffn.3 = (f32[256,4608]{1,0:T(8,128)}, f32[256,4608]{1,0:T(8,128)}, f32[1152,1024]{1,0:T(8,128)}) custom-call(bf16[8,6,32,1536]{3,2,1,0:T(8,128)(2,1)} %bitcast.185, f32[256,4608]{1,0:T(8,128)} %get-tuple-element.161.refs_0_, f32[256,4608]{1,0:T(8,128)} %get-tuple-element.162.refs_1_, ...), custom_call_target="tpu_custom_call", output_to_operand_aliasing={{0}: (1, {}), {1}: (2, {}), {2}: (3, {})} | custom-call | tf_op jit(solution)/shard_map/unpack_ffn/pallas_call | solution.py:443
  (185 shorter events, 54.6 us)
Async XLA Ops:
  7.2 65.6 %all-gather.8.cloned.1.call-start = ((), (), s32[]{:S(2)}) async-start(), calls=%async_computation.11 | async-start | bytes 3538944 | tf_op jit(solution)/shard_map/all_gather | solution.py:847
  9.7 9.2 %collective-permute-start.2 = (bf16[32,2176]{1,0:T(8,128)(2,1)S(1)}, bf16[32,2176]{1,0:T(8,128)(2,1)S(1)}, u32[]{:S(2)}, u32[]{:S(2)}) collective-permute-start(bf16[32,2176]{1,0:T(8,128)(2,1)S(1)} %pad_maximum_fusion.10), channel_id=1, source_target_pairs={{0,3},{1,0},{2,1},{3,2},{4,7},{5,4},{6,5},{7,6},{8,11},{9,8},{10,9... | collective-permute-start | bytes 417800 | tf_op jit(solution)/shard_map/ppermute | solution.py:814
  14.8 11.8 %collective-permute-start.1 = (bf16[32,2176]{1,0:T(8,128)(2,1)S(1)}, bf16[32,2176]{1,0:T(8,128)(2,1)S(1)}, u32[]{:S(2)}, u32[]{:S(2)}) collective-permute-start(bf16[32,2176]{1,0:T(8,128)(2,1)S(1)} %pad_maximum_fusion.10), channel_id=1, source_target_pairs={{0,2},{1,3},{2,0},{3,1},{4,6},{5,7},{6,4},{7,5},{8,10},{9,11},{10,... | collective-permute-start | bytes 417800 | tf_op jit(solution)/shard_map/ppermute | solution.py:814
  14.8 11.8 %collective-permute-start = (bf16[32,2176]{1,0:T(8,128)(2,1)S(1)}, bf16[32,2176]{1,0:T(8,128)(2,1)S(1)}, u32[]{:S(2)}, u32[]{:S(2)}) collective-permute-start(bf16[32,2176]{1,0:T(8,128)(2,1)S(1)} %pad_maximum_fusion.10), channel_id=1, source_target_pairs={{0,1},{1,2},{2,3},{3,0},{4,5},{5,6},{6,7},{7,4},{8,9},{9,10},{10,1... | collective-permute-start | bytes 417800 | tf_op jit(solution)/shard_map/ppermute | solution.py:814
  27.4 169.2 %all-gather.10.cloned.1.call-start = ((), (), s32[]{:S(2)}) async-start(), calls=%async_computation.12 | async-start | bytes 18579456 | tf_op jit(solution)/shard_map/all_gather | solution.py:847
  27.5 2.3 copy-start.15
  27.5 2.3 copy-start.16
  27.5 2.3 copy-start.17
  27.5 2.3 copy-start.18
  29.8 2.2 copy-start
  32.3 18.8 %collective-permute-start.7 = (bf16[224,1536]{1,0:T(8,128)(2,1)}, bf16[224,1536]{1,0:T(8,128)(2,1)S(1)}, u32[]{:S(2)}, u32[]{:S(2)}) collective-permute-start(bf16[224,1536]{1,0:T(8,128)(2,1)} %get-tuple-element.104), channel_id=1, source_target_pairs={{1,0},{2,1},{3,2},{5,4},{6,5},{7,6},{9,8},{10,9},{11,10},{13,12},{... | collective-permute-start | bytes 2064392 | tf_op jit(solution)/shard_map/ppermute | solution.py:825
  33.6 18.8 %collective-permute-start.6 = (bf16[224,1536]{1,0:T(8,128)(2,1)}, bf16[224,1536]{1,0:T(8,128)(2,1)S(1)}, u32[]{:S(2)}, u32[]{:S(2)}) collective-permute-start(bf16[224,1536]{1,0:T(8,128)(2,1)} %get-tuple-element.104), channel_id=1, source_target_pairs={{0,1},{1,2},{2,3},{4,5},{5,6},{6,7},{8,9},{9,10},{10,11},{12,13},{... | collective-permute-start | bytes 2064392 | tf_op jit(solution)/shard_map/ppermute | solution.py:824
  51.1 17.7 %collective-permute-start.8 = (bf16[224,1536]{1,0:T(8,128)(2,1)S(1)}, bf16[224,1536]{1,0:T(8,128)(2,1)S(1)}, u32[]{:S(2)}, u32[]{:S(2)}) collective-permute-start(bf16[224,1536]{1,0:T(8,128)(2,1)S(1)} %collective-permute-done.7), channel_id=1, source_target_pairs={{1,0},{2,1},{5,4},{6,5},{9,8},{10,9},{13,12},{14,13},{17,16},{18,1... | collective-permute-start | bytes 2064392 | tf_op jit(solution)/shard_map/ppermute | solution.py:825
  52.4 17.6 %collective-permute-start.10 = (bf16[224,1536]{1,0:T(8,128)(2,1)S(1)}, bf16[224,1536]{1,0:T(8,128)(2,1)}, u32[]{:S(2)}, u32[]{:S(2)}) collective-permute-start(bf16[224,1536]{1,0:T(8,128)(2,1)S(1)} %collective-permute-done.6), channel_id=1, source_target_pairs={{1,2},{2,3},{5,6},{6,7},{9,10},{10,11},{13,14},{14,15},{17,18},{18... | collective-permute-start | bytes 2064392 | tf_op jit(solution)/shard_map/ppermute | solution.py:824
  68.7 16.8 %collective-permute-start.9 = (bf16[224,1536]{1,0:T(8,128)(2,1)S(1)}, bf16[224,1536]{1,0:T(8,128)(2,1)}, u32[]{:S(2)}, u32[]{:S(2)}) collective-permute-start(bf16[224,1536]{1,0:T(8,128)(2,1)S(1)} %collective-permute-done.8), channel_id=1, source_target_pairs={{1,0},{5,4},{9,8},{13,12},{17,16},{21,20},{25,24},{29,28}} | collective-permute-start | bytes 2064392 | tf_op jit(solution)/shard_map/ppermute | solution.py:825
  70.0 13.1 %collective-permute-start.11 = (bf16[224,1536]{1,0:T(8,128)(2,1)}, bf16[224,1536]{1,0:T(8,128)(2,1)}, u32[]{:S(2)}, u32[]{:S(2)}) collective-permute-start(bf16[224,1536]{1,0:T(8,128)(2,1)} %collective-permute-done.10), channel_id=1, source_target_pairs={{2,3},{6,7},{10,11},{14,15},{18,19},{22,23},{26,27},{30,31}} | collective-permute-start | bytes 2064392 | tf_op jit(solution)/shard_map/ppermute | solution.py:824
  86.9 2.3 copy-start.6
  88.5 180.0 %all-gather.12.cloned.1.call-start = ((), (), s32[]{:S(2)}) async-start(), calls=%async_computation.13 | async-start | bytes 7962624 | tf_op jit(solution)/shard_map/all_gather | solution.py:847
  89.3 52.7 %copy-start.19 = (bf16[96,1536]{1,0:T(8,128)(2,1)S(1)}, bf16[96,1536]{1,0:T(8,128)(2,1)}, u32[]{:S(2)}) copy-start(bf16[96,1536]{1,0:T(8,128)(2,1)} %get-tuple-element.97) | copy-start | bytes 884740
  142.0 18.5 %collective-permute-start.5 = (bf16[96,1536]{1,0:T(8,128)(2,1)S(1)}, bf16[96,1536]{1,0:T(8,128)(2,1)S(1)}, u32[]{:S(2)}, u32[]{:S(2)}) collective-permute-start(bf16[96,1536]{1,0:T(8,128)(2,1)S(1)} %copy-done.19), channel_id=1, source_target_pairs={{0,3},{1,0},{2,1},{3,2},{4,7},{5,4},{6,5},{7,6},{8,11},{9,8},{10,9... | collective-permute-start | bytes 884744 | tf_op jit(solution)/shard_map/ppermute | solution.py:814
  143.2 23.7 %collective-permute-start.4 = (bf16[96,1536]{1,0:T(8,128)(2,1)S(1)}, bf16[96,1536]{1,0:T(8,128)(2,1)S(1)}, u32[]{:S(2)}, u32[]{:S(2)}) collective-permute-start(bf16[96,1536]{1,0:T(8,128)(2,1)S(1)} %copy-done.19), channel_id=1, source_target_pairs={{0,2},{1,3},{2,0},{3,1},{4,6},{5,7},{6,4},{7,5},{8,10},{9,11},{10,... | collective-permute-start | bytes 884744 | tf_op jit(solution)/shard_map/ppermute | solution.py:814
  143.4 23.5 %collective-permute-start.3 = (bf16[96,1536]{1,0:T(8,128)(2,1)S(1)}, bf16[96,1536]{1,0:T(8,128)(2,1)S(1)}, u32[]{:S(2)}, u32[]{:S(2)}) collective-permute-start(bf16[96,1536]{1,0:T(8,128)(2,1)S(1)} %copy-done.19), channel_id=1, source_target_pairs={{0,1},{1,2},{2,3},{3,0},{4,5},{5,6},{6,7},{7,4},{8,9},{9,10},{10,1... | collective-permute-start | bytes 884744 | tf_op jit(solution)/shard_map/ppermute | solution.py:814
  167.9 5.4 copy-start.9
  168.0 28.7 %all-to-all-start.1 = ((bf16[4,512,256]{2,1,0:T(8,128)(2,1)}), bf16[4,512,256]{2,1,0:T(8,128)(2,1)S(1)}, u32[]{:S(2)}, u32[]{:S(2)}) async-start(bf16[4,512,256]{2,1,0:T(8,128)(2,1)} %bitcast.12), calls=%async_computation.1 | async-start | bytes 2097152 | tf_op jit(solution)/shard_map/all_to_all | solution.py:997
  171.6 166.4 %reduce-scatter.4.cloned.1.call-start = ((), (), s32[]{:S(2)}) async-start(), calls=%async_computation.14 | async-start | bytes 10616832 | tf_op jit(solution)/shard_map/reduce_scatter | solution.py:851
  196.7 1.0 copy-start.2
  236.3 169.6 %reduce-scatter.6.cloned.1.call-start = ((), (), s32[]{:S(2)}) async-start(), calls=%async_computation.15 | async-start | bytes 10616832 | tf_op jit(solution)/shard_map/reduce_scatter | solution.py:851
  300.4 16.6 %collective-permute-start.12 = (bf16[4,4,96,1536]{3,2,1,0:T(8,128)(2,1)}, bf16[4,4,96,1536]{3,2,1,0:T(8,128)(2,1)}, u32[]{:S(2)}, u32[]{:S(2)}) collective-permute-start(bf16[4,4,96,1536]{3,2,1,0:T(8,128)(2,1)} %get-tuple-element.127), channel_id=1, source_target_pairs={{0,4},{4,0},{8,12},{12,8},{16,20},{20,16},{24,28},{28,24},{1,5},{5... | collective-permute-start | bytes 14155784 | tf_op jit(solution)/shard_map/ppermute | solution.py:859
  307.8 30.3 %all-to-all-start.2 = ((bf16[4,512,256]{2,1,0:T(8,128)(2,1)}), bf16[4,512,256]{2,1,0:T(8,128)(2,1)S(1)}, u32[]{:S(2)}, u32[]{:S(2)}) async-start(bf16[4,512,256]{2,1,0:T(8,128)(2,1)} %bitcast.207), calls=%async_computation.2 | async-start | bytes 2097152 | tf_op jit(solution)/shard_map/all_to_all | solution.py:997
  338.1 3.8 copy-start.10
  339.8 30.3 %collective-permute-start.13 = (bf16[96,1536]{1,0:T(8,128)(2,1)S(1)}, bf16[96,1536]{1,0:T(8,128)(2,1)}, u32[]{:S(2)}, u32[]{:S(2)}) collective-permute-start(bf16[96,1536]{1,0:T(8,128)(2,1)S(1)} %get-tuple-element.132), channel_id=1, source_target_pairs={{0,3},{1,0},{2,1},{3,2},{4,7},{5,4},{6,5},{7,6},{8,11},{9,8},{10,9... | collective-permute-start | bytes 884744 | tf_op jit(solution)/shard_map/ppermute | solution.py:814
  341.3 28.8 %collective-permute-start.14 = (bf16[96,1536]{1,0:T(8,128)(2,1)S(1)}, bf16[96,1536]{1,0:T(8,128)(2,1)}, u32[]{:S(2)}, u32[]{:S(2)}) collective-permute-start(bf16[96,1536]{1,0:T(8,128)(2,1)S(1)} %get-tuple-element.133), channel_id=1, source_target_pairs={{0,2},{1,3},{2,0},{3,1},{4,6},{5,7},{6,4},{7,5},{8,10},{9,11},{10,... | collective-permute-start | bytes 884744 | tf_op jit(solution)/shard_map/ppermute | solution.py:814
  341.3 28.8 %collective-permute-start.15 = (bf16[96,1536]{1,0:T(8,128)(2,1)S(1)}, bf16[96,1536]{1,0:T(8,128)(2,1)}, u32[]{:S(2)}, u32[]{:S(2)}) collective-permute-start(bf16[96,1536]{1,0:T(8,128)(2,1)S(1)} %get-tuple-element.134), channel_id=1, source_target_pairs={{0,1},{1,2},{2,3},{3,0},{4,5},{5,6},{6,7},{7,4},{8,9},{9,10},{10,1... | collective-permute-start | bytes 884744 | tf_op jit(solution)/shard_map/ppermute | solution.py:814
  362.2 29.8 %all-to-all-start.3 = ((bf16[4,512,256]{2,1,0:T(8,128)(2,1)}), bf16[4,512,256]{2,1,0:T(8,128)(2,1)S(1)}, u32[]{:S(2)}, u32[]{:S(2)}) async-start(bf16[4,512,256]{2,1,0:T(8,128)(2,1)} %bitcast.208), calls=%async_computation.4 | async-start | bytes 2097152 | tf_op jit(solution)/shard_map/all_to_all | solution.py:997
  367.0 40.3 %collective-permute-start.16 = (bf16[2,2,96,1536]{3,2,1,0:T(8,128)(2,1)}, bf16[2,2,96,1536]{3,2,1,0:T(8,128)(2,1)S(1)}, u32[]{:S(2)}, u32[]{:S(2)}) collective-permute-start(bf16[2,2,96,1536]{3,2,1,0:T(8,128)(2,1)} %fusion.3), channel_id=1, source_target_pairs={{0,8},{4,12},{8,0},{12,4},{16,24},{20,28},{24,16},{28,20},{1,9},{5... | collective-permute-start | bytes 3538952 | tf_op jit(solution)/shard_map/ppermute | solution.py:859
  368.5 38.9 %collective-permute-start.17 = (bf16[2,2,96,1536]{3,2,1,0:T(8,128)(2,1)}, bf16[2,2,96,1536]{3,2,1,0:T(8,128)(2,1)}, u32[]{:S(2)}, u32[]{:S(2)}) collective-permute-start(bf16[2,2,96,1536]{3,2,1,0:T(8,128)(2,1)} %fusion.4), channel_id=1, source_target_pairs={{0,16},{4,20},{8,24},{12,28},{16,0},{20,4},{24,8},{28,12},{1,17},{... | collective-permute-start | bytes 3538952 | tf_op jit(solution)/shard_map/ppermute | solution.py:859
  392.0 14.0 %copy-start.3 = (bf16[4,512,256]{2,1,0:T(8,128)(2,1)}, bf16[4,512,256]{2,1,0:T(8,128)(2,1)S(1)}, u32[]{:S(2)}) copy-start(bf16[4,512,256]{2,1,0:T(8,128)(2,1)S(1)} %all-to-all-done.3) | copy-start | bytes 3145732
  392.0 28.6 %all-to-all-start.4 = ((bf16[4,512,256]{2,1,0:T(8,128)(2,1)}), bf16[4,512,256]{2,1,0:T(8,128)(2,1)S(1)}, u32[]{:S(2)}, u32[]{:S(2)}) async-start(bf16[4,512,256]{2,1,0:T(8,128)(2,1)} %bitcast.204), calls=%async_computation.5 | async-start | bytes 2097152 | tf_op jit(solution)/shard_map/all_to_all | solution.py:997
  397.1 104.1 %reduce-scatter.8.cloned.1.call-start = ((), (), s32[]{:S(2)}) async-start(), calls=%async_computation.16 | async-start | bytes 2359296 | tf_op jit(solution)/shard_map/reduce_scatter | solution.py:851
  407.3 2.9 copy-start.7
  413.5 13.3 %copy-start.1 = (bf16[1,512,1024]{2,1,0:T(8,128)(2,1)S(1)}, bf16[1,512,1024]{2,1,0:T(8,128)(2,1)}, u32[]{:S(2)}) copy-start(bf16[1,512,1024]{2,1,0:T(8,128)(2,1)} %param.14) | copy-start | bytes 3145732
  420.6 1.0 copy-start.4
  421.6 34.4 %all-to-all-start.5 = ((bf16[4,96,1536]{2,1,0:T(8,128)(2,1)}), bf16[4,96,1536]{2,1,0:T(8,128)(2,1)S(1)}, u32[]{:S(2)}, u32[]{:S(2)}) async-start(bf16[4,96,1536]{2,1,0:T(8,128)(2,1)} %pad_maximum_fusion.1), calls=%async_computation.7 | async-start | bytes 2359296 | tf_op jit(solution)/shard_map/all_to_all | solution.py:997
  425.1 84.8 %all-gather.14.cloned.1.call-start = ((), (), s32[]{:S(2)}) async-start(), calls=%async_computation.17 | async-start | bytes 2654208 | tf_op jit(solution)/shard_map/all_gather | solution.py:847
  426.8 2.2 copy-start.14
  429.7 26.3 %collective-permute-start.18 = (bf16[2,96,1536]{2,1,0:T(8,128)(2,1)}, bf16[2,96,1536]{2,1,0:T(8,128)(2,1)S(1)}, u32[]{:S(2)}, u32[]{:S(2)}) collective-permute-start(bf16[2,96,1536]{2,1,0:T(8,128)(2,1)} %get-tuple-element.177), channel_id=1, source_target_pairs={{0,16},{4,20},{8,24},{12,28},{16,0},{20,4},{24,8},{28,12},{1,17},{... | collective-permute-start | bytes 1769480 | tf_op jit(solution)/shard_map/ppermute | solution.py:859
  430.9 25.0 %collective-permute-start.19 = (bf16[2,96,1536]{2,1,0:T(8,128)(2,1)}, bf16[2,96,1536]{2,1,0:T(8,128)(2,1)S(1)}, u32[]{:S(2)}, u32[]{:S(2)}) collective-permute-start(bf16[2,96,1536]{2,1,0:T(8,128)(2,1)} %get-tuple-element.178), channel_id=1, source_target_pairs={{0,8},{4,12},{8,0},{12,4},{16,24},{20,28},{24,16},{28,20},{1,9},{5... | collective-permute-start | bytes 1769480 | tf_op jit(solution)/shard_map/ppermute | solution.py:859
  449.2 6.9 %copy-start.8 = (bf16[2,2,96,1536]{3,2,1,0:T(8,128)(2,1)S(1)}, bf16[2,2,96,1536]{3,2,1,0:T(8,128)(2,1)}, u32[]{:S(2)}) copy-start(bf16[2,2,96,1536]{3,2,1,0:T(8,128)(2,1)} %copy-done.7) | copy-start | bytes 3538948
  456.0 9.9 %collective-permute-start.20 = (bf16[4,4,32,2176]{3,2,1,0:T(8,128)(2,1)}, bf16[4,4,32,2176]{3,2,1,0:T(8,128)(2,1)}, u32[]{:S(2)}, u32[]{:S(2)}) collective-permute-start(bf16[4,4,32,2176]{3,2,1,0:T(8,128)(2,1)} %bitcast_dynamic-update-slice_fusion), channel_id=1, source_target_pairs={{0,4},{4,0},{8,12},{12,8},{16,20},{20,16},{24,28},{28,24},{1,5},{5... | collective-permute-start | bytes 6684680 | tf_op jit(solution)/shard_map/ppermute | solution.py:859
  460.1 5.1 copy-start.13
  460.1 34.3 %all-to-all-start.6 = ((bf16[4,96,1536]{2,1,0:T(8,128)(2,1)}), bf16[4,96,1536]{2,1,0:T(8,128)(2,1)S(1)}, u32[]{:S(2)}, u32[]{:S(2)}) async-start(bf16[4,96,1536]{2,1,0:T(8,128)(2,1)} %pad_maximum_fusion.2), calls=%async_computation.8 | async-start | bytes 2359296 | tf_op jit(solution)/shard_map/all_to_all | solution.py:997
  465.3 85.4 %all-gather.16.cloned.1.call-start = ((), (), s32[]{:S(2)}) async-start(), calls=%async_computation.18 | async-start | bytes 5308416 | tf_op jit(solution)/shard_map/all_gather | solution.py:847
  468.7 19.3 %collective-permute-start.21 = (bf16[2,2,32,2176]{3,2,1,0:T(8,128)(2,1)S(1)}, bf16[2,2,32,2176]{3,2,1,0:T(8,128)(2,1)S(1)}, u32[]{:S(2)}, u32[]{:S(2)}) collective-permute-start(bf16[2,2,32,2176]{3,2,1,0:T(8,128)(2,1)S(1)} %fusion.11), channel_id=1, source_target_pairs={{0,8},{4,12},{8,0},{12,4},{16,24},{20,28},{24,16},{28,20},{1,9},{5... | collective-permute-start | bytes 1671176 | tf_op jit(solution)/shard_map/ppermute | solution.py:859
  469.3 19.5 %collective-permute-start.23 = (bf16[2,2,32,2176]{3,2,1,0:T(8,128)(2,1)S(1)}, bf16[2,2,32,2176]{3,2,1,0:T(8,128)(2,1)S(1)}, u32[]{:S(2)}, u32[]{:S(2)}) collective-permute-start(bf16[2,2,32,2176]{3,2,1,0:T(8,128)(2,1)S(1)} %fusion.12), channel_id=1, source_target_pairs={{0,16},{4,20},{8,24},{12,28},{16,0},{20,4},{24,8},{28,12},{1,17},{... | collective-permute-start | bytes 1671176 | tf_op jit(solution)/shard_map/ppermute | solution.py:859
  488.7 4.0 copy-start.12
  491.2 6.8 %collective-permute-start.24 = (bf16[2,32,2176]{2,1,0:T(8,128)(2,1)}, bf16[2,32,2176]{2,1,0:T(8,128)(2,1)S(1)}, u32[]{:S(2)}, u32[]{:S(2)}) collective-permute-start(bf16[2,32,2176]{2,1,0:T(8,128)(2,1)} %get-tuple-element.181), channel_id=1, source_target_pairs={{0,8},{4,12},{8,0},{12,4},{16,24},{20,28},{24,16},{28,20},{1,9},{5... | collective-permute-start | bytes 835592 | tf_op jit(solution)/shard_map/ppermute | solution.py:859
  492.7 6.9 %collective-permute-start.22 = (bf16[2,32,2176]{2,1,0:T(8,128)(2,1)}, bf16[2,32,2176]{2,1,0:T(8,128)(2,1)}, u32[]{:S(2)}, u32[]{:S(2)}) collective-permute-start(bf16[2,32,2176]{2,1,0:T(8,128)(2,1)} %get-tuple-element.182), channel_id=1, source_target_pairs={{0,16},{4,20},{8,24},{12,28},{16,0},{20,4},{24,8},{28,12},{1,17},{... | collective-permute-start | bytes 835592 | tf_op jit(solution)/shard_map/ppermute | solution.py:859
  504.5 21.2 %all-to-all-start.7 = ((bf16[4,32,3200]{2,1,0:T(8,128)(2,1)}), bf16[4,32,3200]{2,1,0:T(8,128)(2,1)S(1)}, u32[]{:S(2)}, u32[]{:S(2)}) async-start(bf16[4,32,3200]{2,1,0:T(8,128)(2,1)} %pad_maximum_fusion.5), calls=%async_computation.10 | async-start | bytes 1638400 | tf_op jit(solution)/shard_map/all_to_all | solution.py:997
  525.9 9.3 %collective-permute-start.27 = (bf16[32,3200]{1,0:T(8,128)(2,1)S(1)}, bf16[32,3200]{1,0:T(8,128)(2,1)S(1)}, u32[]{:S(2)}, u32[]{:S(2)}) collective-permute-start(bf16[32,3200]{1,0:T(8,128)(2,1)S(1)} %reduce_sum.66), channel_id=1, source_target_pairs={{0,24},{4,28},{8,16},{12,20},{16,8},{20,12},{24,0},{28,4},{1,25},{... | collective-permute-start | bytes 614408 | tf_op jit(solution)/shard_map/ppermute | solution.py:859
  528.1 11.1 %collective-permute-start.26 = (bf16[32,3200]{1,0:T(8,128)(2,1)S(1)}, bf16[32,3200]{1,0:T(8,128)(2,1)S(1)}, u32[]{:S(2)}, u32[]{:S(2)}) collective-permute-start(bf16[32,3200]{1,0:T(8,128)(2,1)S(1)} %reduce_sum.66), channel_id=1, source_target_pairs={{0,16},{4,20},{8,24},{12,28},{16,0},{20,4},{24,8},{28,12},{1,17},{... | collective-permute-start | bytes 614408 | tf_op jit(solution)/shard_map/ppermute | solution.py:859
  528.2 13.5 %collective-permute-start.25 = (bf16[32,3200]{1,0:T(8,128)(2,1)S(1)}, bf16[32,3200]{1,0:T(8,128)(2,1)S(1)}, u32[]{:S(2)}, u32[]{:S(2)}) collective-permute-start(bf16[32,3200]{1,0:T(8,128)(2,1)S(1)} %reduce_sum.66), channel_id=1, source_target_pairs={{0,8},{4,12},{8,0},{12,4},{16,24},{20,28},{24,16},{28,20},{1,9},{5... | collective-permute-start | bytes 614408 | tf_op jit(solution)/shard_map/ppermute | solution.py:859
  541.9 2.4 copy-start.5
  541.9 2.4 collective-permute-start.28
  544.3 0.9 copy-start.11
Sparse Core Ops, SparseCore 0:
  27.6 32.6 all-gather.7
  88.6 92.9 all-gather.9
  184.1 48.8 all-gather.11
  236.5 76.2 reduce-scatter.3
  316.2 89.7 reduce-scatter.5
  409.1 46.4 reduce-scatter.7
  458.2 33.4 all-gather.13
  504.6 44.5 all-gather.15

commit v4 on v3

--- a/solution.py
+++ b/solution.py
@@ -460,6 +460,48 @@
     )(source, *before)
 
 
+def unpack_near_kernel(m_ref, even, odd, *refs):
+    gate_ref, up_ref, down_ref = refs[-3:]
+    piece = gate_ref.shape[0] // SPLIT
+    lanes = down_ref.shape[1] // SPLIT
+    blocks = down_ref.shape[0] // piece
+    for b in range(SPLIT):
+        source = (odd if b % 2 else even)[b // 2].astype(f32)
+        member = jnp.bitwise_xor(m_ref[0], b)
+        rows = pl.ds(pl.multiple_of(member * piece, piece), piece)
+        gate_ref[rows, :] = source[:piece]
+        up_ref[rows, :] = source[piece : 2 * piece]
+        columns = pl.ds(pl.multiple_of(member * lanes, lanes), lanes)
+        for k in range(blocks):
+            down_ref[k * piece : (k + 1) * piece, columns] = source[
+                2 * piece :, k * lanes : (k + 1) * lanes
+            ]
+
+
+def unpack_near(member, even, odd, chunk, before, shards):
+    gate, _, down = before
+    unit = gate.shape[1] // (shards * CHUNKS)
+    columns = pl.BlockSpec((gate.shape[0], unit), lambda s, m_ref: (0, s * CHUNKS + chunk))
+    source = pl.BlockSpec((SPLIT // 2, even.shape[1], unit), lambda s, m_ref: (0, 0, s))
+    rows = down.shape[0] // (CHUNKS * shards)
+    return pl.pallas_call(
+        unpack_near_kernel,
+        grid_spec=pltpu.PrefetchScalarGridSpec(
+            num_scalar_prefetch=1,
+            grid=(shards,),
+            in_specs=[source, source] + [pl.BlockSpec(memory_space=pl.ANY)] * 3,
+            out_specs=[
+                columns,
+                columns,
+                pl.BlockSpec((rows, down.shape[1]), lambda s, m_ref: (chunk * shards + s, 0)),
+            ],
+        ),
+        out_shape=[jax.ShapeDtypeStruct(x.shape, f32) for x in before],
+        input_output_aliases={3 + i: i for i in range(3)},
+        name="unpack_near",
+    )(member.reshape(1), even, odd, *before)
+
+
 def shard_at(z, r, shards):
     return lax.rem(z + shards - r, shards)
 
@@ -499,11 +541,12 @@
 
 def projection_specs(shards, depth, piece, columns):
     sizes = [n // shards for n in columns]
-    own = [pl.BlockSpec((depth, n), lambda s, z_ref: (0, s)) for n in sizes]
+    last = lambda s: jnp.minimum(s, shards - 1)
+    own = [pl.BlockSpec((depth, n), lambda s, z_ref: (0, last(s))) for n in sizes]
     starts = [sum(columns[:i]) // sizes[i] for i in range(3)]
     far = [
         pl.BlockSpec(
-            (SPLIT, shards - 1, piece, n), lambda s, z_ref, start=start: (0, 0, 0, start + s)
+            (SPLIT, shards - 1, piece, n), lambda s, z_ref, start=start: (0, 0, 0, start + last(s))
         )
         for n, start in zip(sizes, starts)
     ]
@@ -545,65 +588,85 @@
 
 def qkv_bwd_kernel(
     shards, heads, z_ref, ht_ref, cos_ref, sin_ref, gain_q, gain_k,
-    tokens, scale_ref, gain_1, resid, raw_ref, *refs,
+    tokens, scale_ref, gain_1, resid, sum_2, raw_ref, *refs,
 ):
     back, refs = refs[:heads], refs[heads:]
-    own, far, refs = refs[:3], refs[3:6], refs[6:]
-    tokens_ref, mine, theirs, sum_q, sum_k, sum_1, grads, grad_ref = refs
+    own, far, (tokens_ref, mine, theirs), refs = refs[:3], refs[3:6], refs[6:9], refs[9:]
+    sum_q, sum_k, grads, grad_ref = refs
+    step = pl.program_id(0)
     z = z_ref[0]
     even = z_ref[1] == 0
     depth = own[0].shape[0]
     piece = depth // SPLIT
 
-    @pl.when(pl.program_id(0) == 0)
+    @pl.when(step == 0)
     def _():
         grad_ref[...] = jnp.zeros_like(grad_ref)
         sum_q[...] = jnp.zeros_like(sum_q)
         sum_k[...] = jnp.zeros_like(sum_k)
 
-    cosine, sine = cos_ref[...], sin_ref[...]
-    at = 0
-    halves = [ref[:, 2 * HD :] for ref in back]
-    swapped = [pltpu.roll(half.astype(f32), HD, 1).astype(bf16) for half in halves]
-    low = lanes_of(halves[0]) < HD
-    arrived = [[ref[:, : 2 * HD] for ref in back]]
-    arrived.append([jnp.where(low, halves[i], swapped[i + 1]) for i in range(0, heads, 2)])
-    arrived.append([jnp.where(low, swapped[i], halves[i + 1]) for i in range(0, heads, 2)])
-    for pairs, gain, total in ((arrived[0], gain_q, sum_q), (arrived[1], gain_k, sum_k)):
-        for grad in pairs:
-            pair = raw_ref[:, at : at + 2 * HD]
-            scale = lax.rsqrt(pair_mean(pair * pair) + EPS)
-            hat = pair * scale
-            grad = grad.astype(f32)
-            grad = grad * cosine + other_half(grad * sine)
-            total[...] += jnp.sum(grad * hat, axis=0, keepdims=True)
-            grad = grad * gain[...]
-            grads[:, at : at + 2 * HD] = (scale * (grad - hat * pair_mean(grad * hat))).astype(bf16)
-            at += 2 * HD
-    for i, pair in enumerate(arrived[2]):
-        grads[:, at + i * 2 * HD : at + (i + 1) * 2 * HD] = pair
-    ends = (0, own[0].shape[1], at, grads.shape[1])
-    for r in range(shards):
-        part = None
-        for i in range(3):
-            one = dot(grads[:, ends[i] : ends[i + 1]], joined(own[i], far[i], r), NT)
-            part = one if i == 0 else part + one
-        grad_ref[:, part_of(z, r, shards, depth)] += part
-        term = dot(ht_ref[part_of(z, r, shards, depth), :], grads[...]).astype(bf16)
-        term = term.reshape(SPLIT // 2, 2, piece, term.shape[1])
-        mine[:, r] = jnp.where(even, term[:, 0], term[:, 1])
-        theirs[:, r] = jnp.where(even, term[:, 1], term[:, 0])
-
-    @pl.when(pl.program_id(0) == shards - 1)
+    @pl.when(step < shards)
+    def _():
+        cosine, sine = cos_ref[...], sin_ref[...]
+        at = 0
+        halves = [ref[:, 2 * HD :] for ref in back]
+        swapped = [pltpu.roll(half.astype(f32), HD, 1).astype(bf16) for half in halves]
+        low = lanes_of(halves[0]) < HD
+        arrived = [[ref[:, : 2 * HD] for ref in back]]
+        arrived.append([jnp.where(low, halves[i], swapped[i + 1]) for i in range(0, heads, 2)])
+        arrived.append([jnp.where(low, swapped[i], halves[i + 1]) for i in range(0, heads, 2)])
+        for pairs, gain, total in ((arrived[0], gain_q, sum_q), (arrived[1], gain_k, sum_k)):
+            for grad in pairs:
+                pair = raw_ref[:, at : at + 2 * HD]
+                scale = lax.rsqrt(pair_mean(pair * pair) + EPS)
+                hat = pair * scale
+                grad = grad.astype(f32)
+                grad = grad * cosine + other_half(grad * sine)
+                total[...] += jnp.sum(grad * hat, axis=0, keepdims=True)
+                grad = grad * gain[...]
+                grads[:, at : at + 2 * HD] = (scale * (grad - hat * pair_mean(grad * hat))).astype(bf16)
+                at += 2 * HD
+        for i, pair in enumerate(arrived[2]):
+            grads[:, at + i * 2 * HD : at + (i + 1) * 2 * HD] = pair
+        ends = (0, own[0].shape[1], at, grads.shape[1])
+        for r in range(shards):
+            part = None
+            for i in range(3):
+                one = dot(grads[:, ends[i] : ends[i + 1]], joined(own[i], far[i], r), NT)
+                part = one if i == 0 else part + one
+            grad_ref[:, part_of(z, r, shards, depth)] += part
+            term = dot(ht_ref[part_of(z, r, shards, depth), :], grads[...]).astype(bf16)
+            term = term.reshape(SPLIT // 2, 2, piece, term.shape[1])
+            mine[:, r] = jnp.where(even, term[:, 0], term[:, 1])
+            theirs[:, r] = jnp.where(even, term[:, 1], term[:, 0])
+
+    @pl.when(step == shards)
     def _():
         scale = scale_ref[...]
         normed = tokens[...].astype(f32) * scale
         grad = grad_ref[...]
-        sum_1[...] = jnp.sum(grad * normed, axis=0, keepdims=True)
+        sum_1 = jnp.sum(grad * normed, axis=0, keepdims=True)
         tokens_ref[...] = resid[...] + norm_back(grad * gain_1[...], normed, scale)
-
-
-def qkv_backward(z, hidden_t, tables_gains, first_norm, back, raw, weights, far, extra):
+        lanes = 2 * HD
+        empty = jnp.zeros((piece, mine.shape[3] - lanes), f32)
+        turn = [shard_at(z, r, shards) for r in range(shards)]
+        grad_ref[0:1, :] = sum_1
+        grad_ref[1:2, :] = sum_2[...]
+        for r in range(shards):
+            rows = []
+            for i in range(2):
+                for k in range(0, depth, lanes):
+                    at = pl.multiple_of(turn[r] * depth + k, lanes)
+                    rows.append(grad_ref[i : i + 1, pl.ds(at, lanes)])
+            rows += [sum_q[...], sum_k[...]]
+            rows.append(jnp.zeros((piece - len(rows), lanes), f32))
+            block = jnp.concatenate([jnp.concatenate(rows, axis=0), empty], axis=1).astype(bf16)
+            for d in range(SPLIT // 2):
+                mine[d, r] = block
+                theirs[d, r] = block
+
+
+def qkv_backward(z, hidden_t, tables_gains, first_norm, back, raw, weights, far):
     width, local = hidden_t.shape
     depth = weights[0].shape[0]
     shards = width // depth
@@ -611,27 +674,27 @@
     columns = [w.shape[1] for w in weights]
     each = sum(columns) // shards
     whole = lambda shape: pl.BlockSpec(shape, lambda s, z_ref: (0,) * len(shape))
-    rows = lambda x: pl.BlockSpec((local, x.shape[1]), lambda s, z_ref: (s, 0))
-    terms = jax.ShapeDtypeStruct((SPLIT // 2, shards, piece, shards * each + extra), bf16)
+    last = lambda s: jnp.minimum(s, shards - 1)
+    rows = lambda x: pl.BlockSpec((local, x.shape[1]), lambda s, z_ref: (last(s), 0))
+    terms = jax.ShapeDtypeStruct((SPLIT // 2, shards, piece, shards * each + 2 * HD), bf16)
     at_terms = pl.BlockSpec((SPLIT // 2, shards, piece, each), lambda s, z_ref: (0, 0, 0, s))
     return pl.pallas_call(
         functools.partial(qkv_bwd_kernel, shards, len(back)),
         grid_spec=pltpu.PrefetchScalarGridSpec(
             num_scalar_prefetch=1,
-            grid=(shards,),
+            grid=(shards + 1,),
             in_specs=[whole(x.shape) for x in (hidden_t, *tables_gains, *first_norm)]
             + [rows(x) for x in (raw, *back)]
             + projection_specs(shards, depth, piece, columns),
-            out_specs=[whole((local, width)), at_terms, at_terms]
-            + [whole((1, n)) for n in (2 * HD, 2 * HD, width)],
-            scratch_shapes=[pltpu.VMEM((local, each), bf16), pltpu.VMEM((local, width), f32)],
-        ),
-        out_shape=[
-            jax.ShapeDtypeStruct((local, width), f32),
-            terms,
-            terms,
-        ]
-        + [jax.ShapeDtypeStruct((1, n), f32) for n in (2 * HD, 2 * HD, width)],
+            out_specs=[whole((local, width)), at_terms, at_terms],
+            scratch_shapes=[
+                pltpu.VMEM((1, 2 * HD), f32),
+                pltpu.VMEM((1, 2 * HD), f32),
+                pltpu.VMEM((local, each), bf16),
+                pltpu.VMEM((local, width), f32),
+            ],
+        ),
+        out_shape=[jax.ShapeDtypeStruct((local, width), f32), terms, terms],
         cost_estimate=pl.CostEstimate(
             flops=4 * local * width * sum(columns),
             transcendentals=0,
@@ -643,6 +706,7 @@
 
 def unpack_qkv_kernel(shards, m_ref, even, odd, *refs):
     piece = even.shape[1]
+    out = refs[3]
     for b in range(SPLIT):
         source = (odd if b % 2 else even)[b // 2].astype(f32)
         rows = pl.ds(pl.multiple_of(jnp.bitwise_xor(m_ref[0], b) * piece, piece), piece)
@@ -652,13 +716,12 @@
                 n = ref.shape[1] // shards
                 ref[rows, s * n : (s + 1) * n] = source[:, at : at + n]
                 at += n
-        for ref in refs[3:]:
-            ref[rows, :] = source[:, at : at + ref.shape[1]]
-            at += ref.shape[1]
-
-
-def unpack_qkv(member, even, odd, shards, columns):
+        out[rows, :] = source[:, source.shape[1] - out.shape[1] :]
+
+
+def unpack_qkv(member, even, odd, shards, columns, width):
     piece = even.shape[1]
+    columns = columns + [width]
     whole = lambda shape: pl.BlockSpec(shape, lambda i, m_ref: (0,) * len(shape))
     return pl.pallas_call(
         functools.partial(unpack_qkv_kernel, shards),
@@ -839,8 +902,8 @@
             x = lax.all_gather(x, ("dp", "seq"))
         return x.reshape(SPLIT, self.n_seq, *x.shape[-2:])
 
-    def gather_near(self, x):
-        even = jnp.stack([x] + [self.swap(x, bit) for bit in (2, 4, 6)])
+    def gather_near(self, x, *others):
+        even = jnp.stack([after(y, *others) for y in [x] + [self.swap(x, bit) for bit in (2, 4, 6)]])
         return even, self.swap(even, 1)
 
     def gather(self, x):
@@ -1050,46 +1113,35 @@
     sum_out = axes.scatter(after(terms_out, piece0))
     piece0 = axes.gather(piece0[None])
     parts1 = exchange(after(parts1, back_rows[-1]))
-    grad_tokens, terms, other, sum_q, sum_k, term_gain1 = qkv_backward(
-        where, hidden1_t, (cosine, sine, gain_q, gain_k), (tokens[0], scale1, gain1, grad_resid),
-        back_rows, raw, weights, far_qkv, 128,
+    grad_tokens, terms, other = qkv_backward(
+        where, hidden1_t, (cosine, sine, gain_q, gain_k),
+        (tokens[0], scale1, gain1, grad_resid, term_gain2), back_rows, raw, weights, far_qkv,
     )
-
-    parts = [
-        term_gain1.reshape(shards, depth),
-        term_gain2.reshape(shards, depth),
-        (sum_q[0, :HD] + sum_q[0, HD:]).reshape(shards, head),
-        (sum_k[0, :HD] + sum_k[0, HD:]).reshape(shards, head),
-    ]
-    parts = jnp.concatenate(parts, axis=1)
-    parts = jnp.sum(hot[:, :, None] * parts[None], axis=1)
-    each = parts.shape[1] // SPLIT
-    parts = parts.reshape(shards, SPLIT, each).transpose(1, 0, 2)
-    parts = jnp.pad(parts, ((0, 0), (0, 0), (0, piece * 128 - each)))
-    parts = parts.reshape(SPLIT // 2, 2, shards, piece, 128).astype(bf16)
-    parity = lax.rem(member, 2)
-    pick = lambda i: lax.dynamic_index_in_dim(parts, i, axis=1, keepdims=False)
-    start = (0, 0, 0, terms.shape[3] - 128)
-    terms = lax.dynamic_update_slice(terms, pick(parity), start)
-    other = lax.dynamic_update_slice(other, pick(1 - parity), start)
     tail = Reduction(axes, terms, after(other, parts1, *sum2.state))
     parts2 = by_owner(sum2.third())
     tail.then(parts2)
     parts2 = exchange(parts2)
     tail.first().send_first()
-    piece1 = total(after(parts1, *tail.sent))
+    piece1 = axes.gather(total(after(parts1, *tail.sent))[None])
     tail.second().send_second()
     tail.then(parts2)
     tail = by_owner(jnp.concatenate([tail.third(), sum_out], axis=2))
-    late = axes.gather(jnp.concatenate([piece1, total(after(parts2, tail))], axis=0)[None])
+    late = total(after(parts2, tail))
     grads = unpack_ffn(after(piece0, tail), 0, 1, (), depth, shards, unit, width)
-    even, odd = axes.gather_near(after(total(exchange(tail)), *grads))
-    grads = unpack_ffn(late, 1, 2, grads, depth, shards, unit, width)
+    tail = total(after(exchange(tail), *grads))
+    even, odd = axes.gather_near(tail)
+    late = axes.gather_near(late, tail)
+    grads = unpack_ffn(piece1, 1, 1, grads, depth, shards, unit, width)
+    grads = unpack_near(member, *late, CHUNKS - 1, grads, shards)
     grad_gate, grad_up, grad_down = grads
-    grad_query, grad_key, grad_value, sums, grad_out = unpack_qkv(
-        member, even, odd, shards, columns + [128, width]
+    grad_query, grad_key, grad_value, grad_out = unpack_qkv(
+        member, even, odd, shards, columns, width
     )
-    sums = sums.reshape(SPLIT, -1)[:, :each].reshape(-1)
+    sums = even[0, :, sum(columns) : sum(columns) + 2 * HD].astype(f32)
+    n = depth // (2 * HD)
+    sum_1, sum_2 = sums[:n].reshape(depth), sums[n : 2 * n].reshape(depth)
+    heads = [sums[i, :HD] + sums[i, HD:] for i in (2 * n, 2 * n + 1)]
+    sum_q, sum_k = (lax.dynamic_slice_in_dim(x, z * head, head) for x in heads)
     return (
         output[None],
         grad_tokens[None],
@@ -1100,10 +1152,10 @@
         grad_gate,
         grad_up,
         grad_down,
-        sums[:depth],
-        sums[depth : 2 * depth],
-        sums[2 * depth : 2 * depth + head],
-        sums[2 * depth + head :],
+        sum_1,
+        sum_2,
+        sum_q,
+        sum_k,
     )
 
 

time: 576 us -> 566 us (0.983)
    ppermute x14 -> x18, waiting for transfers between devices: 39.8 us -> 32.3 us  [swap(): return lax.ppermute(x, 'dp', [(i, i ^ bit) for i in range(self.n_dp)])]
    ppermute x14 -> x18, starting transfers between devices: 12.9 us -> 17.7 us  [swap(): return lax.ppermute(x, 'dp', [(i, i ^ bit) for i in range(self.n_dp)])]
  transfers between devices with their start and end apart: 44 -> 48, of which waited for: 22 -> 24; matrix products, arithmetic and copies ran while one was open for 10% -> 8% of each run, Pallas kernels for 37% -> 38%
where the time goes in v4:
time: 566 us; the launch traced here: 559 us
  Pallas kernels  217 us (38%)
  waiting for transfers between devices  147 us (26%)
  starting transfers between devices  68.4 us (12%)
  blocking collectives  52.7 us (9%)
  other arithmetic  40.3 us (7%)
  local copies, waits for them, and re-layouts  17.6 us (3%)
  between operations  15.6 us (3%)
    pallas_call x3, Pallas kernels, ffn_chunk(): pl.pallas_call(functools.partial(ffn_kernel, shards, c == 0), grid_spec=p...  95.6 us
    all_to_all x7, waiting for transfers between devices, exchange(): return lax.all_to_all(x, 'seq', split_axis=0, concat_axis=0, tiled=True)  62 us
    all_to_all x1, blocking collectives, exchange(): return lax.all_to_all(x, 'seq', split_axis=0, concat_axis=0, tiled=True)  52.7 us
    pallas_call x2, Pallas kernels, attend_backward(): pl.pallas_call(functools.partial(attend_bwd_kernel, block, j), grid=(1,),...  40 us
    ppermute x18, waiting for transfers between devices, swap(): return lax.ppermute(x, 'dp', [(i, i ^ bit) for i in range(self.n_dp)])  32.3 us
    all_to_all x7, starting transfers between devices, exchange(): return lax.all_to_all(x, 'seq', split_axis=0, concat_axis=0, tiled=True)  27.9 us
    ppermute x3, waiting for transfers between devices, pass_on(): down = lax.ppermute(down, 'seq', [(i + 1, i) for i in range(n - step)])  26.8 us
    ppermute x18, starting transfers between devices, swap(): return lax.ppermute(x, 'dp', [(i, i ^ bit) for i in range(self.n_dp)])  17.7 us
  transfers between devices with their start and end apart: 48, of which 24 were waited for; matrix products, arithmetic and copies ran while one was open for 8% of the time, Pallas kernels for 38%

profile of v4, /device:TPU:0, one launch (start us, length us, event | category | flops | bytes accessed | tf_op | source)
XLA Modules:
  0.0 558.7 jit_solution(14199140836800638068)
XLA Ops:
  9.7 5.1 collective-permute-start.2
  15.8 3.1 collective-permute-done.2
  18.9 7.7 %collective-permute-done.1 = bf16[32,2176]{1,0:T(8,128)(2,1)S(1)} collective-permute-done((bf16[32,2176]{1,0:T(8,128)(2,1)S(1)}, bf16[32,2176]{1,0:T(8,128)(2,1)S(1)}, u32[]{:S(2)}, u32[]{:S(2)}) %collective-permute-start.1) | collective-permute-done | bytes 139296 | tf_op jit(solution)/shard_map/ppermute | solution.py:877
  27.6 2.2 pack.1
  33.6 4.6 collective-permute-start.6
  39.8 11.2 %collective-permute-done.7 = bf16[224,1536]{1,0:T(8,128)(2,1)S(1)} collective-permute-done((bf16[224,1536]{1,0:T(8,128)(2,1)}, bf16[224,1536]{1,0:T(8,128)(2,1)S(1)}, u32[]{:S(2)}, u32[]{:S(2)}) %collective-permute-start.7) | collective-permute-done | bytes 688160 | tf_op jit(solution)/shard_map/ppermute | solution.py:888
  52.4 1.5 collective-permute-start.10
  55.5 13.2 %collective-permute-done.8 = bf16[224,1536]{1,0:T(8,128)(2,1)S(1)} collective-permute-done((bf16[224,1536]{1,0:T(8,128)(2,1)S(1)}, bf16[224,1536]{1,0:T(8,128)(2,1)S(1)}, u32[]{:S(2)}, u32[]{:S(2)}) %collective-permute-start.8) | collective-permute-done | bytes 688160 | tf_op jit(solution)/shard_map/ppermute | solution.py:888
  70.0 1.5 collective-permute-start.11
  72.8 10.3 %qkv_forward.1 = (bf16[2048,512]{1,0:T(8,128)(2,1)}, f32[2048,384]{1,0:T(8,128)}) custom-call(s32[2]{0:T(128)} %pad_add_fusion.z_ref, bf16[512,1024]{1,0:T(8,128)(2,1)} %fusion.2.h_ref, f32[512,128]{1,0:T(8,128)} %copy.51.cos_ref, f32[512,128]{1,0:T(8,128)} %pad_maximum_fusion.9.sin_ref, f32[1,128]{1,0:T(1,128)} %tile.33.gain_q, f32[1,128]{1,0:T(1,128)} %tile.36.gain_k, ...), custom_call_target="tpu_custom_call" | custom-call | flops 2147483648 | bytes 12582912 | tf_op jit(solution)/shard_map/qkv_forward/pallas_call | solution.py:564
  83.1 2.4 collective-permute-done.9
  86.9 1.5 pad_maximum_fusion
  89.3 52.7 %all_to_all.73 = bf16[4,512,512]{2,1,0:T(8,128)(2,1)} all-to-all(bf16[4,512,512]{2,1,0:T(8,128)(2,1)S(1)} %bitcast.204), channel_id=1, replica_groups=mesh['dp'=8,'seq'=4] {'seq'}, dimensions={0} | all-to-all | bytes 4194304 | tf_op jit(solution)/shard_map/all_to_all | solution.py:1060
  144.0 16.5 %attend_forward.1 = (bf16[2048,256]{1,0:T(8,128)(2,1)}, f32[2,4,1,1024]{3,2,1,0:T(1,128)}) custom-call(bf16[2048,512]{1,0:T(8,128)(2,1)} %bitcast.195, bf16[2048,512]{1,0:T(8,128)(2,1)} %bitcast.196, bf16[2048,512]{1,0:T(8,128)(2,1)} %bitcast.197), custom_call_target="tpu_custom_call" | custom-call | flops 8589934592 | bytes 3145728 | tf_op jit(solution)/shard_map/attend_forward/pallas_call | solution.py:118
  160.5 6.5 %collective-permute-done.4 = bf16[96,1536]{1,0:T(8,128)(2,1)S(1)} collective-permute-done((bf16[96,1536]{1,0:T(8,128)(2,1)S(1)}, bf16[96,1536]{1,0:T(8,128)(2,1)S(1)}, u32[]{:S(2)}, u32[]{:S(2)}) %collective-permute-start.4) | collective-permute-done | bytes 294944 | tf_op jit(solution)/shard_map/ppermute | solution.py:877
  168.0 3.7 all-to-all-start.1
  175.1 21.6 %all-to-all-done.1 = bf16[4,512,256]{2,1,0:T(8,128)(2,1)S(1)} async-done(((bf16[4,512,256]{2,1,0:T(8,128)(2,1)}), bf16[4,512,256]{2,1,0:T(8,128)(2,1)S(1)}, u32[]{:S(2)}, u32[]{:S(2)}) %all-to-all-start.1) | async-done | bytes 1048608 | tf_op jit(solution)/shard_map/all_to_all | solution.py:1060
  197.6 6.7 %out_forward.1 = (f32[512,1024]{1,0:T(8,128)}, f32[512,1]{1,0:T(8,128)}, bf16[512,1024]{1,0:T(8,128)(2,1)}, bf16[1024,512]{1,0:T(8,128)(2,1)}) custom-call(s32[2]{0:T(128)} %pad_add_fusion.z_ref, bf16[2048,256]{1,0:T(8,128)(2,1)} %bitcast.178, bf16[512,1024]{1,0:T(8,128)(2,1)} %bitcast.176, f32[1,1024]{1,0:T(1,128)} %bitcast.228, bf16[256,1024]{1,0:T(8,128)(2,1)} %own.3, ...), custom_call_target="tpu_custom_call" | custom-call | flops 1073741824 | bytes 7340032 | tf_op jit(solution)/shard_map/out_forward/pallas_call | solution.py:771
  204.3 32.0 %ffn_chunk.3 = (f32[512,1024]{1,0:T(8,128)}, f32[512,1024]{1,0:T(8,128)}, bf16[8,4,96,1536]{3,2,1,0:T(8,128)(2,1)}) custom-call(s32[2]{0:T(128)} %pad_add_fusion.z_ref, bf16[512,1024]{1,0:T(8,128)(2,1)} %get-tuple-element.114.h_ref, bf16[1024,512]{1,0:T(8,128)(2,1)} %get-tuple-element.115.ht_ref, bf16[512,1024]{1,0:T(8,128)(2,1)} %bitcast_select_fusion.gy_ref.grad_y, ...), custom_call_target="tpu_custom_call" | custom-call | flops 14495514624 | bytes 29360128 | tf_op jit(solution)/shard_map/ffn_chunk/pallas_call | solution.py:336
  236.8 31.7 %ffn_chunk.4 = (f32[512,1024]{1,0:T(8,128)}, f32[512,1024]{1,0:T(8,128)}, bf16[8,4,96,1536]{3,2,1,0:T(8,128)(2,1)}) custom-call(s32[2]{0:T(128)} %pad_add_fusion.z_ref, bf16[512,1024]{1,0:T(8,128)(2,1)} %get-tuple-element.114.h_ref, bf16[1024,512]{1,0:T(8,128)(2,1)} %get-tuple-element.115.ht_ref, bf16[512,1024]{1,0:T(8,128)(2,1)} %bitcast_select_fusion.gy_ref.grad_y, ...), custom_call_target="tpu_custom_call" | custom-call | flops 14495514624 | bytes 29360128 | tf_op jit(solution)/shard_map/ffn_chunk/pallas_call | solution.py:336
  268.5 31.9 %ffn_chunk.5 = (bf16[512,1024]{1,0:T(8,128)(2,1)}, f32[512,1024]{1,0:T(8,128)}, bf16[4,4,96,1536]{3,2,1,0:T(8,128)(2,1)}, bf16[4,4,96,1536]{3,2,1,0:T(8,128)(2,1)}) custom-call(s32[2]{0:T(128)} %pad_add_fusion.z_ref, bf16[512,1024]{1,0:T(8,128)(2,1)} %get-tuple-element.114.h_ref, bf16[1024,512]{1,0:T(8,128)(2,1)} %get-tuple-element.115.ht_ref, ...), custom_call_target="tpu_custom_call" | custom-call | flops 14495514624 | bytes 29360128 | tf_op jit(solution)/shard_map/ffn_chunk/pallas_call | solution.py:336
  300.5 7.3 %out_backward.1 = (f32[512,1024]{1,0:T(8,128)}, f32[1,1024]{1,0:T(1,128)}, bf16[512,1024]{1,0:T(8,128)(2,1)}, bf16[2048,256]{1,0:T(8,128)(2,1)}) custom-call(s32[2]{0:T(128)} %pad_add_fusion.z_ref, f32[512,1024]{1,0:T(8,128)} %get-tuple-element.122.grad, bf16[512,1024]{1,0:T(8,128)(2,1)} %bitcast_select_fusion.gy_ref.grad_y, ...), custom_call_target="tpu_custom_call" | custom-call | flops 1073741824 | bytes 10485760 | tf_op jit(solution)/shard_map/out_backward/pallas_call | solution.py:816
  307.8 3.7 all-to-all-start.2
  311.5 5.6 %out_terms.1 = bf16[8,4,32,1024]{3,2,1,0:T(8,128)(2,1)} custom-call(s32[2]{0:T(128)} %pad_add_fusion.z_ref, bf16[2048,256]{1,0:T(8,128)(2,1)} %bitcast.179, bf16[512,1024]{1,0:T(8,128)(2,1)} %get-tuple-element.129.branch), custom_call_target="tpu_custom_call" | custom-call | flops 1073741824 | bytes 4194304 | tf_op jit(solution)/shard_map/out_terms/pallas_call | solution.py:843
  317.1 2.9 fusion.4
  320.0 3.1 fusion.3
  323.1 15.0 %all-to-all-done.2 = bf16[4,512,256]{2,1,0:T(8,128)(2,1)S(1)} async-done(((bf16[4,512,256]{2,1,0:T(8,128)(2,1)}), bf16[4,512,256]{2,1,0:T(8,128)(2,1)S(1)}, u32[]{:S(2)}, u32[]{:S(2)}) %all-to-all-start.2) | async-done | bytes 1048608 | tf_op jit(solution)/shard_map/all_to_all | solution.py:1060
  338.1 2.4 slice_bitcast_fusion
  340.5 1.5 collective-permute-start.13
  342.5 20.0 %attend_backward.2 = bf16[2048,256]{1,0:T(8,128)(2,1)} custom-call(bf16[2048,512]{1,0:T(8,128)(2,1)} %bitcast.198, bf16[2048,512]{1,0:T(8,128)(2,1)} %bitcast.199, bf16[2048,512]{1,0:T(8,128)(2,1)} %bitcast.200, bf16[2048,256]{1,0:T(8,128)(2,1)} %bitcast.208, bf16[2048,256]{1,0:T(8,128)(2,1)} %get-tuple-element.101.o_ref, ...), custom_call_target="tpu_custom_call" | custom-call | flops 10737418240 | bytes 3145728 | tf_op jit(solution)/shard_map/attend_backward/pallas_call | solution.py:201
  362.6 4.6 all-to-all-start.3
  367.2 1.5 collective-permute-start.16
  368.7 1.5 collective-permute-start.17
  370.2 2.0 add_convert_fusion.4
  372.3 20.0 %attend_backward.3 = bf16[2048,256]{1,0:T(8,128)(2,1)} custom-call(bf16[2048,512]{1,0:T(8,128)(2,1)} %bitcast.201, bf16[2048,512]{1,0:T(8,128)(2,1)} %bitcast.202, bf16[2048,512]{1,0:T(8,128)(2,1)} %bitcast.203, bf16[2048,256]{1,0:T(8,128)(2,1)} %bitcast.209, bf16[2048,256]{1,0:T(8,128)(2,1)} %get-tuple-element.101.o_ref, ...), custom_call_target="tpu_custom_call" | custom-call | flops 10737418240 | bytes 3145728 | tf_op jit(solution)/shard_map/attend_backward/pallas_call | solution.py:201
  392.8 4.5 all-to-all-start.4
  398.0 7.5 %reduce-scatter.6.cloned.1.call-done = bf16[4,96,1536]{2,1,0:T(8,128)(2,1)} async-done(((bf16[32,96,1536]{2,1,0:T(8,128)(2,1)}), bf16[4,96,1536]{2,1,0:T(8,128)(2,1)}) %reduce-scatter.6.cloned.1.call-update) | async-done | bytes 1179664 | tf_op jit(solution)/shard_map/reduce_scatter | solution.py:914
  405.5 1.9 collective-permute-done.16
  411.2 3.3 fusion.9
  414.5 7.3 %all-to-all-done.4 = bf16[4,512,256]{2,1,0:T(8,128)(2,1)S(1)} async-done(((bf16[4,512,256]{2,1,0:T(8,128)(2,1)}), bf16[4,512,256]{2,1,0:T(8,128)(2,1)S(1)}, u32[]{:S(2)}, u32[]{:S(2)}) %all-to-all-start.4) | async-done | bytes 1048608 | tf_op jit(solution)/shard_map/all_to_all | solution.py:1060
  422.9 3.5 all-to-all-start.5
  429.4 1.5 collective-permute-start.19
  432.5 17.0 %qkv_backward.1 = (f32[512,1024]{1,0:T(8,128)}, bf16[4,4,32,2176]{3,2,1,0:T(8,128)(2,1)}, bf16[4,4,32,2176]{3,2,1,0:T(8,128)(2,1)}) custom-call(s32[2]{0:T(128)} %pad_add_fusion.z_ref, bf16[1024,512]{1,0:T(8,128)(2,1)} %copy.52.ht_ref, f32[512,128]{1,0:T(8,128)} %copy.51.cos_ref, f32[512,128]{1,0:T(8,128)} %pad_maximum_fusion.9.sin_ref, ...), custom_call_target="tpu_custom_call" | custom-call | flops 4294967296 | bytes 16777216 | tf_op jit(solution)/shard_map/qkv_backward/pallas_call | solution.py:681
  449.5 4.9 all-to-all-done.5
  454.4 2.8 fusion.6
  458.8 3.5 all-to-all-start.6
  462.4 1.4 fusion.12
  463.8 1.4 fusion.11
  466.4 1.4 collective-permute-start.23
  467.9 16.4 %collective-permute-done.21 = bf16[2,2,32,2176]{3,2,1,0:T(8,128)(2,1)S(1)} collective-permute-done((bf16[2,2,32,2176]{3,2,1,0:T(8,128)(2,1)S(1)}, bf16[2,2,32,2176]{3,2,1,0:T(8,128)(2,1)S(1)}, u32[]{:S(2)}, u32[]{:S(2)}) %collective-permute-start.21) | collective-permute-done | bytes 557088 | tf_op jit(solution)/shard_map/ppermute | solution.py:922
  484.9 2.2 fusion.15
  490.2 1.6 all-to-all-done.6
  491.8 3.9 collective-permute-done.24
  496.8 1.7 fusion.18
  500.6 4.3 all-to-all-start.7
  505.1 1.7 collective-permute-start.31
  508.7 4.3 unpack_ffn.2
  513.0 11.0 %all-to-all-done.7 = bf16[4,32,3200]{2,1,0:T(8,128)(2,1)S(1)} async-done(((bf16[4,32,3200]{2,1,0:T(8,128)(2,1)}), bf16[4,32,3200]{2,1,0:T(8,128)(2,1)S(1)}, u32[]{:S(2)}, u32[]{:S(2)}) %all-to-all-start.7) | async-done | bytes 819232 | tf_op jit(solution)/shard_map/all_to_all | solution.py:1060
  524.1 2.4 collective-permute-start.27
  529.6 3.5 collective-permute-done.27
  533.1 2.5 collective-permute-done.26
  538.6 3.2 unpack_qkv.1
  541.9 4.3 unpack_ffn.3
  547.2 4.4 unpack_near.1
  (175 shorter events, 55.0 us)
Async XLA Ops:
  7.2 65.6 %all-gather.8.cloned.1.call-start = ((), (), s32[]{:S(2)}) async-start(), calls=%async_computation.11 | async-start | bytes 3538944 | tf_op jit(solution)/shard_map/all_gather | solution.py:910
  9.7 9.2 %collective-permute-start.2 = (bf16[32,2176]{1,0:T(8,128)(2,1)S(1)}, bf16[32,2176]{1,0:T(8,128)(2,1)S(1)}, u32[]{:S(2)}, u32[]{:S(2)}) collective-permute-start(bf16[32,2176]{1,0:T(8,128)(2,1)S(1)} %pad_maximum_fusion.10), channel_id=1, source_target_pairs={{0,3},{1,0},{2,1},{3,2},{4,7},{5,4},{6,5},{7,6},{8,11},{9,8},{10,9... | collective-permute-start | bytes 417800 | tf_op jit(solution)/shard_map/ppermute | solution.py:877
  14.8 11.8 %collective-permute-start.1 = (bf16[32,2176]{1,0:T(8,128)(2,1)S(1)}, bf16[32,2176]{1,0:T(8,128)(2,1)S(1)}, u32[]{:S(2)}, u32[]{:S(2)}) collective-permute-start(bf16[32,2176]{1,0:T(8,128)(2,1)S(1)} %pad_maximum_fusion.10), channel_id=1, source_target_pairs={{0,2},{1,3},{2,0},{3,1},{4,6},{5,7},{6,4},{7,5},{8,10},{9,11},{10,... | collective-permute-start | bytes 417800 | tf_op jit(solution)/shard_map/ppermute | solution.py:877
  14.8 11.8 %collective-permute-start = (bf16[32,2176]{1,0:T(8,128)(2,1)S(1)}, bf16[32,2176]{1,0:T(8,128)(2,1)S(1)}, u32[]{:S(2)}, u32[]{:S(2)}) collective-permute-start(bf16[32,2176]{1,0:T(8,128)(2,1)S(1)} %pad_maximum_fusion.10), channel_id=1, source_target_pairs={{0,1},{1,2},{2,3},{3,0},{4,5},{5,6},{6,7},{7,4},{8,9},{9,10},{10,1... | collective-permute-start | bytes 417800 | tf_op jit(solution)/shard_map/ppermute | solution.py:877
  27.4 169.2 %all-gather.10.cloned.1.call-start = ((), (), s32[]{:S(2)}) async-start(), calls=%async_computation.12 | async-start | bytes 18579456 | tf_op jit(solution)/shard_map/all_gather | solution.py:910
  27.5 2.3 copy-start.14
  27.5 2.3 copy-start.15
  27.5 2.3 copy-start.16
  27.5 2.3 copy-start.17
  29.8 2.2 copy-start
  32.3 18.8 %collective-permute-start.7 = (bf16[224,1536]{1,0:T(8,128)(2,1)}, bf16[224,1536]{1,0:T(8,128)(2,1)S(1)}, u32[]{:S(2)}, u32[]{:S(2)}) collective-permute-start(bf16[224,1536]{1,0:T(8,128)(2,1)} %get-tuple-element.107), channel_id=1, source_target_pairs={{1,0},{2,1},{3,2},{5,4},{6,5},{7,6},{9,8},{10,9},{11,10},{13,12},{... | collective-permute-start | bytes 2064392 | tf_op jit(solution)/shard_map/ppermute | solution.py:888
  33.6 18.8 %collective-permute-start.6 = (bf16[224,1536]{1,0:T(8,128)(2,1)}, bf16[224,1536]{1,0:T(8,128)(2,1)S(1)}, u32[]{:S(2)}, u32[]{:S(2)}) collective-permute-start(bf16[224,1536]{1,0:T(8,128)(2,1)} %get-tuple-element.107), channel_id=1, source_target_pairs={{0,1},{1,2},{2,3},{4,5},{5,6},{6,7},{8,9},{9,10},{10,11},{12,13},{... | collective-permute-start | bytes 2064392 | tf_op jit(solution)/shard_map/ppermute | solution.py:887
  51.1 17.7 %collective-permute-start.8 = (bf16[224,1536]{1,0:T(8,128)(2,1)S(1)}, bf16[224,1536]{1,0:T(8,128)(2,1)S(1)}, u32[]{:S(2)}, u32[]{:S(2)}) collective-permute-start(bf16[224,1536]{1,0:T(8,128)(2,1)S(1)} %collective-permute-done.7), channel_id=1, source_target_pairs={{1,0},{2,1},{5,4},{6,5},{9,8},{10,9},{13,12},{14,13},{17,16},{18,1... | collective-permute-start | bytes 2064392 | tf_op jit(solution)/shard_map/ppermute | solution.py:888
  52.4 17.6 %collective-permute-start.10 = (bf16[224,1536]{1,0:T(8,128)(2,1)S(1)}, bf16[224,1536]{1,0:T(8,128)(2,1)}, u32[]{:S(2)}, u32[]{:S(2)}) collective-permute-start(bf16[224,1536]{1,0:T(8,128)(2,1)S(1)} %collective-permute-done.6), channel_id=1, source_target_pairs={{1,2},{2,3},{5,6},{6,7},{9,10},{10,11},{13,14},{14,15},{17,18},{18... | collective-permute-start | bytes 2064392 | tf_op jit(solution)/shard_map/ppermute | solution.py:887
  68.7 16.8 %collective-permute-start.9 = (bf16[224,1536]{1,0:T(8,128)(2,1)S(1)}, bf16[224,1536]{1,0:T(8,128)(2,1)}, u32[]{:S(2)}, u32[]{:S(2)}) collective-permute-start(bf16[224,1536]{1,0:T(8,128)(2,1)S(1)} %collective-permute-done.8), channel_id=1, source_target_pairs={{1,0},{5,4},{9,8},{13,12},{17,16},{21,20},{25,24},{29,28}} | collective-permute-start | bytes 2064392 | tf_op jit(solution)/shard_map/ppermute | solution.py:888
  70.0 13.1 %collective-permute-start.11 = (bf16[224,1536]{1,0:T(8,128)(2,1)}, bf16[224,1536]{1,0:T(8,128)(2,1)}, u32[]{:S(2)}, u32[]{:S(2)}) collective-permute-start(bf16[224,1536]{1,0:T(8,128)(2,1)} %collective-permute-done.10), channel_id=1, source_target_pairs={{2,3},{6,7},{10,11},{14,15},{18,19},{22,23},{26,27},{30,31}} | collective-permute-start | bytes 2064392 | tf_op jit(solution)/shard_map/ppermute | solution.py:887
  86.9 2.3 copy-start.7
  88.5 180.0 %all-gather.12.cloned.1.call-start = ((), (), s32[]{:S(2)}) async-start(), calls=%async_computation.13 | async-start | bytes 7962624 | tf_op jit(solution)/shard_map/all_gather | solution.py:910
  89.3 52.7 %copy-start.18 = (bf16[96,1536]{1,0:T(8,128)(2,1)S(1)}, bf16[96,1536]{1,0:T(8,128)(2,1)}, u32[]{:S(2)}) copy-start(bf16[96,1536]{1,0:T(8,128)(2,1)} %get-tuple-element.100) | copy-start | bytes 884740
  142.0 18.5 %collective-permute-start.5 = (bf16[96,1536]{1,0:T(8,128)(2,1)S(1)}, bf16[96,1536]{1,0:T(8,128)(2,1)S(1)}, u32[]{:S(2)}, u32[]{:S(2)}) collective-permute-start(bf16[96,1536]{1,0:T(8,128)(2,1)S(1)} %copy-done.18), channel_id=1, source_target_pairs={{0,3},{1,0},{2,1},{3,2},{4,7},{5,4},{6,5},{7,6},{8,11},{9,8},{10,9... | collective-permute-start | bytes 884744 | tf_op jit(solution)/shard_map/ppermute | solution.py:877
  143.2 23.7 %collective-permute-start.4 = (bf16[96,1536]{1,0:T(8,128)(2,1)S(1)}, bf16[96,1536]{1,0:T(8,128)(2,1)S(1)}, u32[]{:S(2)}, u32[]{:S(2)}) collective-permute-start(bf16[96,1536]{1,0:T(8,128)(2,1)S(1)} %copy-done.18), channel_id=1, source_target_pairs={{0,2},{1,3},{2,0},{3,1},{4,6},{5,7},{6,4},{7,5},{8,10},{9,11},{10,... | collective-permute-start | bytes 884744 | tf_op jit(solution)/shard_map/ppermute | solution.py:877
  143.4 23.5 %collective-permute-start.3 = (bf16[96,1536]{1,0:T(8,128)(2,1)S(1)}, bf16[96,1536]{1,0:T(8,128)(2,1)S(1)}, u32[]{:S(2)}, u32[]{:S(2)}) collective-permute-start(bf16[96,1536]{1,0:T(8,128)(2,1)S(1)} %copy-done.18), channel_id=1, source_target_pairs={{0,1},{1,2},{2,3},{3,0},{4,5},{5,6},{6,7},{7,4},{8,9},{9,10},{10,1... | collective-permute-start | bytes 884744 | tf_op jit(solution)/shard_map/ppermute | solution.py:877
  168.0 5.3 copy-start.11
  168.0 28.7 %all-to-all-start.1 = ((bf16[4,512,256]{2,1,0:T(8,128)(2,1)}), bf16[4,512,256]{2,1,0:T(8,128)(2,1)S(1)}, u32[]{:S(2)}, u32[]{:S(2)}) async-start(bf16[4,512,256]{2,1,0:T(8,128)(2,1)} %bitcast.12), calls=%async_computation.1 | async-start | bytes 2097152 | tf_op jit(solution)/shard_map/all_to_all | solution.py:1060
  171.6 166.5 %reduce-scatter.4.cloned.1.call-start = ((), (), s32[]{:S(2)}) async-start(), calls=%async_computation.14 | async-start | bytes 10616832 | tf_op jit(solution)/shard_map/reduce_scatter | solution.py:914
  236.3 169.1 %reduce-scatter.6.cloned.1.call-start = ((), (), s32[]{:S(2)}) async-start(), calls=%async_computation.15 | async-start | bytes 10616832 | tf_op jit(solution)/shard_map/reduce_scatter | solution.py:914
  300.4 16.7 %collective-permute-start.12 = (bf16[4,4,96,1536]{3,2,1,0:T(8,128)(2,1)}, bf16[4,4,96,1536]{3,2,1,0:T(8,128)(2,1)}, u32[]{:S(2)}, u32[]{:S(2)}) collective-permute-start(bf16[4,4,96,1536]{3,2,1,0:T(8,128)(2,1)} %get-tuple-element.131), channel_id=1, source_target_pairs={{0,4},{4,0},{8,12},{12,8},{16,20},{20,16},{24,28},{28,24},{1,5},{5... | collective-permute-start | bytes 14155784 | tf_op jit(solution)/shard_map/ppermute | solution.py:922
  307.8 30.3 %all-to-all-start.2 = ((bf16[4,512,256]{2,1,0:T(8,128)(2,1)}), bf16[4,512,256]{2,1,0:T(8,128)(2,1)S(1)}, u32[]{:S(2)}, u32[]{:S(2)}) async-start(bf16[4,512,256]{2,1,0:T(8,128)(2,1)} %bitcast.210), calls=%async_computation.2 | async-start | bytes 2097152 | tf_op jit(solution)/shard_map/all_to_all | solution.py:1060
  338.1 2.4 copy-start.12
  340.5 29.7 %collective-permute-start.13 = (bf16[96,1536]{1,0:T(8,128)(2,1)}, bf16[96,1536]{1,0:T(8,128)(2,1)}, u32[]{:S(2)}, u32[]{:S(2)}) collective-permute-start(bf16[96,1536]{1,0:T(8,128)(2,1)} %get-tuple-element.136), channel_id=1, source_target_pairs={{0,3},{1,0},{2,1},{3,2},{4,7},{5,4},{6,5},{7,6},{8,11},{9,8},{10,9... | collective-permute-start | bytes 884744 | tf_op jit(solution)/shard_map/ppermute | solution.py:877
  342.0 28.3 %collective-permute-start.14 = (bf16[96,1536]{1,0:T(8,128)(2,1)S(1)}, bf16[96,1536]{1,0:T(8,128)(2,1)}, u32[]{:S(2)}, u32[]{:S(2)}) collective-permute-start(bf16[96,1536]{1,0:T(8,128)(2,1)S(1)} %get-tuple-element.137), channel_id=1, source_target_pairs={{0,2},{1,3},{2,0},{3,1},{4,6},{5,7},{6,4},{7,5},{8,10},{9,11},{10,... | collective-permute-start | bytes 884744 | tf_op jit(solution)/shard_map/ppermute | solution.py:877
  342.0 28.3 %collective-permute-start.15 = (bf16[96,1536]{1,0:T(8,128)(2,1)S(1)}, bf16[96,1536]{1,0:T(8,128)(2,1)}, u32[]{:S(2)}, u32[]{:S(2)}) collective-permute-start(bf16[96,1536]{1,0:T(8,128)(2,1)S(1)} %get-tuple-element.138), channel_id=1, source_target_pairs={{0,1},{1,2},{2,3},{3,0},{4,5},{5,6},{6,7},{7,4},{8,9},{9,10},{10,1... | collective-permute-start | bytes 884744 | tf_op jit(solution)/shard_map/ppermute | solution.py:877
  362.6 30.2 %all-to-all-start.3 = ((bf16[4,512,256]{2,1,0:T(8,128)(2,1)}), bf16[4,512,256]{2,1,0:T(8,128)(2,1)S(1)}, u32[]{:S(2)}, u32[]{:S(2)}) async-start(bf16[4,512,256]{2,1,0:T(8,128)(2,1)} %bitcast.211), calls=%async_computation.4 | async-start | bytes 2097152 | tf_op jit(solution)/shard_map/all_to_all | solution.py:1060
  367.2 40.2 %collective-permute-start.16 = (bf16[2,2,96,1536]{3,2,1,0:T(8,128)(2,1)}, bf16[2,2,96,1536]{3,2,1,0:T(8,128)(2,1)S(1)}, u32[]{:S(2)}, u32[]{:S(2)}) collective-permute-start(bf16[2,2,96,1536]{3,2,1,0:T(8,128)(2,1)} %fusion.3), channel_id=1, source_target_pairs={{0,8},{4,12},{8,0},{12,4},{16,24},{20,28},{24,16},{28,20},{1,9},{5... | collective-permute-start | bytes 3538952 | tf_op jit(solution)/shard_map/ppermute | solution.py:922
  368.7 40.1 %collective-permute-start.17 = (bf16[2,2,96,1536]{3,2,1,0:T(8,128)(2,1)}, bf16[2,2,96,1536]{3,2,1,0:T(8,128)(2,1)}, u32[]{:S(2)}, u32[]{:S(2)}) collective-permute-start(bf16[2,2,96,1536]{3,2,1,0:T(8,128)(2,1)} %fusion.4), channel_id=1, source_target_pairs={{0,16},{4,20},{8,24},{12,28},{16,0},{20,4},{24,8},{28,12},{1,17},{... | collective-permute-start | bytes 3538952 | tf_op jit(solution)/shard_map/ppermute | solution.py:922
  392.8 5.1 copy-start.4
  392.8 29.0 %all-to-all-start.4 = ((bf16[4,512,256]{2,1,0:T(8,128)(2,1)}), bf16[4,512,256]{2,1,0:T(8,128)(2,1)S(1)}, u32[]{:S(2)}, u32[]{:S(2)}) async-start(bf16[4,512,256]{2,1,0:T(8,128)(2,1)} %bitcast.207), calls=%async_computation.5 | async-start | bytes 2097152 | tf_op jit(solution)/shard_map/all_to_all | solution.py:1060
  397.4 101.1 %reduce-scatter.8.cloned.1.call-start = ((), (), s32[]{:S(2)}) async-start(), calls=%async_computation.16 | async-start | bytes 2359296 | tf_op jit(solution)/shard_map/reduce_scatter | solution.py:914
  407.4 3.9 copy-start.9
  421.9 9.0 %copy-start.1 = (bf16[1,512,1024]{2,1,0:T(8,128)(2,1)S(1)}, bf16[1,512,1024]{2,1,0:T(8,128)(2,1)}, u32[]{:S(2)}) copy-start(bf16[1,512,1024]{2,1,0:T(8,128)(2,1)} %param.14) | copy-start | bytes 3145732
  422.9 31.5 %all-to-all-start.5 = ((bf16[4,96,1536]{2,1,0:T(8,128)(2,1)}), bf16[4,96,1536]{2,1,0:T(8,128)(2,1)S(1)}, u32[]{:S(2)}, u32[]{:S(2)}) async-start(bf16[4,96,1536]{2,1,0:T(8,128)(2,1)} %pad_maximum_fusion.1), calls=%async_computation.7 | async-start | bytes 2359296 | tf_op jit(solution)/shard_map/all_to_all | solution.py:1060
  426.4 82.3 %all-gather.14.cloned.1.call-start = ((), (), s32[]{:S(2)}) async-start(), calls=%async_computation.17 | async-start | bytes 2654208 | tf_op jit(solution)/shard_map/all_gather | solution.py:910
  428.1 21.4 %collective-permute-start.18 = (bf16[2,96,1536]{2,1,0:T(8,128)(2,1)}, bf16[2,96,1536]{2,1,0:T(8,128)(2,1)}, u32[]{:S(2)}, u32[]{:S(2)}) collective-permute-start(bf16[2,96,1536]{2,1,0:T(8,128)(2,1)} %get-tuple-element.183), channel_id=1, source_target_pairs={{0,16},{4,20},{8,24},{12,28},{16,0},{20,4},{24,8},{28,12},{1,17},{... | collective-permute-start | bytes 1769480 | tf_op jit(solution)/shard_map/ppermute | solution.py:922
  429.4 20.1 %collective-permute-start.19 = (bf16[2,96,1536]{2,1,0:T(8,128)(2,1)}, bf16[2,96,1536]{2,1,0:T(8,128)(2,1)}, u32[]{:S(2)}, u32[]{:S(2)}) collective-permute-start(bf16[2,96,1536]{2,1,0:T(8,128)(2,1)} %get-tuple-element.184), channel_id=1, source_target_pairs={{0,8},{4,12},{8,0},{12,4},{16,24},{20,28},{24,16},{28,20},{1,9},{5... | collective-permute-start | bytes 1769480 | tf_op jit(solution)/shard_map/ppermute | solution.py:922
  432.5 21.9 %copy-start.10 = (bf16[2,2,96,1536]{3,2,1,0:T(8,128)(2,1)S(1)}, bf16[2,2,96,1536]{3,2,1,0:T(8,128)(2,1)}, u32[]{:S(2)}) copy-start(bf16[2,2,96,1536]{3,2,1,0:T(8,128)(2,1)} %copy-done.9) | copy-start | bytes 3538948
  454.4 8.0 %collective-permute-start.20 = (bf16[4,4,32,2176]{3,2,1,0:T(8,128)(2,1)}, bf16[4,4,32,2176]{3,2,1,0:T(8,128)(2,1)}, u32[]{:S(2)}, u32[]{:S(2)}) collective-permute-start(bf16[4,4,32,2176]{3,2,1,0:T(8,128)(2,1)} %get-tuple-element.155), channel_id=1, source_target_pairs={{0,4},{4,0},{8,12},{12,8},{16,20},{20,16},{24,28},{28,24},{1,5},{5... | collective-permute-start | bytes 6684680 | tf_op jit(solution)/shard_map/ppermute | solution.py:922
  458.8 33.0 %all-to-all-start.6 = ((bf16[4,96,1536]{2,1,0:T(8,128)(2,1)}), bf16[4,96,1536]{2,1,0:T(8,128)(2,1)S(1)}, u32[]{:S(2)}, u32[]{:S(2)}) async-start(bf16[4,96,1536]{2,1,0:T(8,128)(2,1)} %pad_maximum_fusion.2), calls=%async_computation.8 | async-start | bytes 2359296 | tf_op jit(solution)/shard_map/all_to_all | solution.py:1060
  462.4 79.5 %all-gather.16.cloned.1.call-start = ((), (), s32[]{:S(2)}) async-start(), calls=%async_computation.18 | async-start | bytes 2654208 | tf_op jit(solution)/shard_map/all_gather | solution.py:910
  465.2 19.1 %collective-permute-start.21 = (bf16[2,2,32,2176]{3,2,1,0:T(8,128)(2,1)S(1)}, bf16[2,2,32,2176]{3,2,1,0:T(8,128)(2,1)S(1)}, u32[]{:S(2)}, u32[]{:S(2)}) collective-permute-start(bf16[2,2,32,2176]{3,2,1,0:T(8,128)(2,1)S(1)} %fusion.11), channel_id=1, source_target_pairs={{0,8},{4,12},{8,0},{12,4},{16,24},{20,28},{24,16},{28,20},{1,9},{5... | collective-permute-start | bytes 1671176 | tf_op jit(solution)/shard_map/ppermute | solution.py:922
  466.4 18.5 %collective-permute-start.23 = (bf16[2,2,32,2176]{3,2,1,0:T(8,128)(2,1)S(1)}, bf16[2,2,32,2176]{3,2,1,0:T(8,128)(2,1)S(1)}, u32[]{:S(2)}, u32[]{:S(2)}) collective-permute-start(bf16[2,2,32,2176]{3,2,1,0:T(8,128)(2,1)S(1)} %fusion.12), channel_id=1, source_target_pairs={{0,16},{4,20},{8,24},{12,28},{16,0},{20,4},{24,8},{28,12},{1,17},{... | collective-permute-start | bytes 1671176 | tf_op jit(solution)/shard_map/ppermute | solution.py:922
  487.2 8.5 %collective-permute-start.24 = (bf16[2,32,2176]{2,1,0:T(8,128)(2,1)}, bf16[2,32,2176]{2,1,0:T(8,128)(2,1)}, u32[]{:S(2)}, u32[]{:S(2)}) collective-permute-start(bf16[2,32,2176]{2,1,0:T(8,128)(2,1)} %get-tuple-element.187), channel_id=1, source_target_pairs={{0,8},{4,12},{8,0},{12,4},{16,24},{20,28},{24,16},{28,20},{1,9},{5... | collective-permute-start | bytes 835592 | tf_op jit(solution)/shard_map/ppermute | solution.py:922
  488.5 8.3 %collective-permute-start.22 = (bf16[2,32,2176]{2,1,0:T(8,128)(2,1)}, bf16[2,32,2176]{2,1,0:T(8,128)(2,1)}, u32[]{:S(2)}, u32[]{:S(2)}) collective-permute-start(bf16[2,32,2176]{2,1,0:T(8,128)(2,1)} %get-tuple-element.188), channel_id=1, source_target_pairs={{0,16},{4,20},{8,24},{12,28},{16,0},{20,4},{24,8},{28,12},{1,17},{... | collective-permute-start | bytes 835592 | tf_op jit(solution)/shard_map/ppermute | solution.py:922
  500.6 23.4 %all-to-all-start.7 = ((bf16[4,32,3200]{2,1,0:T(8,128)(2,1)}), bf16[4,32,3200]{2,1,0:T(8,128)(2,1)S(1)}, u32[]{:S(2)}, u32[]{:S(2)}) async-start(bf16[4,32,3200]{2,1,0:T(8,128)(2,1)} %pad_maximum_fusion.6), calls=%async_computation.10 | async-start | bytes 1638400 | tf_op jit(solution)/shard_map/all_to_all | solution.py:1060
  505.1 21.4 %collective-permute-start.31 = (bf16[96,1536]{1,0:T(8,128)(2,1)S(1)}, bf16[96,1536]{1,0:T(8,128)(2,1)S(1)}, u32[]{:S(2)}, u32[]{:S(2)}) collective-permute-start(bf16[96,1536]{1,0:T(8,128)(2,1)S(1)} %reduce_sum.57), channel_id=1, source_target_pairs={{0,24},{4,28},{8,16},{12,20},{16,8},{20,12},{24,0},{28,4},{1,25},{... | collective-permute-start | bytes 884744 | tf_op jit(solution)/shard_map/ppermute | solution.py:922
  506.8 20.9 %collective-permute-start.30 = (bf16[96,1536]{1,0:T(8,128)(2,1)S(1)}, bf16[96,1536]{1,0:T(8,128)(2,1)S(1)}, u32[]{:S(2)}, u32[]{:S(2)}) collective-permute-start(bf16[96,1536]{1,0:T(8,128)(2,1)S(1)} %reduce_sum.57), channel_id=1, source_target_pairs={{0,16},{4,20},{8,24},{12,28},{16,0},{20,4},{24,8},{28,12},{1,17},{... | collective-permute-start | bytes 884744 | tf_op jit(solution)/shard_map/ppermute | solution.py:922
  507.4 20.2 %collective-permute-start.29 = (bf16[96,1536]{1,0:T(8,128)(2,1)S(1)}, bf16[96,1536]{1,0:T(8,128)(2,1)S(1)}, u32[]{:S(2)}, u32[]{:S(2)}) collective-permute-start(bf16[96,1536]{1,0:T(8,128)(2,1)S(1)} %reduce_sum.57), channel_id=1, source_target_pairs={{0,8},{4,12},{8,0},{12,4},{16,24},{20,28},{24,16},{28,20},{1,9},{5... | collective-permute-start | bytes 884744 | tf_op jit(solution)/shard_map/ppermute | solution.py:922
  524.1 9.0 %collective-permute-start.27 = (bf16[32,3200]{1,0:T(8,128)(2,1)S(1)}, bf16[32,3200]{1,0:T(8,128)(2,1)S(1)}, u32[]{:S(2)}, u32[]{:S(2)}) collective-permute-start(bf16[32,3200]{1,0:T(8,128)(2,1)S(1)} %reduce_sum.56), channel_id=1, source_target_pairs={{0,24},{4,28},{8,16},{12,20},{16,8},{20,12},{24,0},{28,4},{1,25},{... | collective-permute-start | bytes 614408 | tf_op jit(solution)/shard_map/ppermute | solution.py:922
  526.5 9.1 %collective-permute-start.26 = (bf16[32,3200]{1,0:T(8,128)(2,1)S(1)}, bf16[32,3200]{1,0:T(8,128)(2,1)S(1)}, u32[]{:S(2)}, u32[]{:S(2)}) collective-permute-start(bf16[32,3200]{1,0:T(8,128)(2,1)S(1)} %reduce_sum.56), channel_id=1, source_target_pairs={{0,16},{4,20},{8,24},{12,28},{16,0},{20,4},{24,8},{28,12},{1,17},{... | collective-permute-start | bytes 614408 | tf_op jit(solution)/shard_map/ppermute | solution.py:922
  526.5 9.4 %collective-permute-start.25 = (bf16[32,3200]{1,0:T(8,128)(2,1)S(1)}, bf16[32,3200]{1,0:T(8,128)(2,1)S(1)}, u32[]{:S(2)}, u32[]{:S(2)}) collective-permute-start(bf16[32,3200]{1,0:T(8,128)(2,1)S(1)} %reduce_sum.56), channel_id=1, source_target_pairs={{0,8},{4,12},{8,0},{12,4},{16,24},{20,28},{24,16},{28,20},{1,9},{5... | collective-permute-start | bytes 614408 | tf_op jit(solution)/shard_map/ppermute | solution.py:922
  529.5 12.4 %copy-start.3 = (bf16[4,96,1536]{2,1,0:T(8,128)(2,1)}, bf16[4,96,1536]{2,1,0:T(8,128)(2,1)S(1)}, u32[]{:S(2)}) copy-start(bf16[4,96,1536]{2,1,0:T(8,128)(2,1)S(1)} %pad_maximum_fusion.3.even) | copy-start | bytes 3538948
  529.5 16.7 %collective-permute-start.32 = (bf16[4,96,1536]{2,1,0:T(8,128)(2,1)S(1)}, bf16[4,96,1536]{2,1,0:T(8,128)(2,1)S(1)}, u32[]{:S(2)}, u32[]{:S(2)}) collective-permute-start(bf16[4,96,1536]{2,1,0:T(8,128)(2,1)S(1)} %pad_maximum_fusion.3.even), channel_id=1, source_target_pairs={{0,4},{4,0},{8,12},{12,8},{16,20},{20,16},{24,28},{28,24},{1,5},{5... | collective-permute-start | bytes 3538952 | tf_op jit(solution)/shard_map/ppermute | solution.py:922
  536.1 2.5 copy-start.6
  536.1 2.5 collective-permute-start.28
  546.2 1.0 copy-start.8
  (3 other events, 2.7 us)
Sparse Core Ops, SparseCore 0:
  27.6 32.6 all-gather.7
  88.6 92.9 all-gather.9
  184.1 48.8 all-gather.11
  236.5 76.3 reduce-scatter.3
  316.2 89.2 reduce-scatter.5
  408.6 46.7 reduce-scatter.7
  458.1 33.2 all-gather.13
  493.4 34.2 all-gather.15

commit v5 on v4

--- a/solution.py
+++ b/solution.py
@@ -859,6 +859,12 @@
     )(z, mixed, branch)
 
 
+def either_kernel(n, z_ref, *refs):
+    came, out = refs[:-1], refs[-1]
+    for r in range(1, n):
+        out[r - 1] = jnp.where(z_ref[0] >= r, came[r - 1][...], came[2 * n - 2 - r][...])
+
+
 class Axes:
     def __init__(self, mesh):
         self.n_dp = mesh.shape["dp"]
@@ -892,8 +898,20 @@
 
     def either(self, came):
         n = self.n_seq
-        z = lax.axis_index("seq")
-        return [jnp.where(z >= r, came[r - 1], came[2 * n - 2 - r]) for r in range(1, n)]
+        rows, width = came[0].shape
+        block = rows // (7 if rows % 7 == 0 else 1)
+        spec = pl.BlockSpec((block, width), lambda i, z_ref: (i, 0))
+        return pl.pallas_call(
+            functools.partial(either_kernel, n),
+            grid_spec=pltpu.PrefetchScalarGridSpec(
+                num_scalar_prefetch=1,
+                grid=(rows // block,),
+                in_specs=[spec] * len(came),
+                out_specs=pl.BlockSpec((n - 1, block, width), lambda i, z_ref: (0, i, 0)),
+            ),
+            out_shape=jax.ShapeDtypeStruct((n - 1, rows, width), came[0].dtype),
+            name="either",
+        )(lax.axis_index("seq").reshape(1), *came)
 
     def gather_all(self, x):
         if self.groups:
@@ -1027,6 +1045,8 @@
     gains = jnp.pad(gains, (0, piece * 128 - gains.shape[0])).reshape(piece, 128)
     packed = jnp.concatenate([mine(w_query), mine(w_key), mine(w_value), gains], axis=1)
     near = axes.from_others(packed)
+    first_chunks, last_chunk = pack(member, w_gate, w_up, w_down, w_out)
+    near = [after(x, first_chunks) for x in near]
     far_qkv = axes.gather(jnp.stack([x[:, :-128] for x in near]))
     far_qkv = far_qkv.reshape(SPLIT, shards - 1, piece, -1)
     gains = jnp.stack([x[:, -128:].reshape(-1) for x in [packed] + near])
@@ -1042,7 +1062,6 @@
     gain_q = jnp.tile(gathered_gain(2 * depth, head), (1, 2))
     gain_k = jnp.tile(gathered_gain(2 * depth + head, head), (1, 2))
 
-    first_chunks, last_chunk = pack(member, w_gate, w_up, w_down, w_out)
 
     def stack_after(parts, *others):
         return jnp.stack([after(x, *others) for x in parts])
@@ -1061,7 +1080,7 @@
 
     crossed = axes.pass_on(after(first_chunks, *near))
     send, raw = qkv_forward(where, hidden1, cosine, sine, gain_q, gain_k, weights, far_qkv)
-    far = axes.gather(jnp.stack(axes.either([after(x, send) for x in crossed])))
+    far = axes.gather(axes.either([after(x, send) for x in crossed]))
     qkv = exchange(send)
     crossed = axes.from_others(after(last_chunk, qkv))
     block = 512

time: 566 us -> 566 us (level)
  Pallas kernels: 217 us -> 224 us
    pallas_call x0 -> x1, Pallas kernels: none -> 5.88 us  [either(): pl.pallas_call(functools.partial(either_kernel, n), grid_spec=pltpu.Prefe...]
  transfers between devices with their start and end apart: 48 -> 48, of which waited for: 24 -> 23; matrix products, arithmetic and copies ran while one was open for 8% -> 8% of each run, Pallas kernels for 38% -> 38%
where the time goes in v5:
time: 566 us; the launch traced here: 557 us
  Pallas kernels  224 us (40%)
  waiting for transfers between devices  143 us (25%)
  starting transfers between devices  69.4 us (12%)
  blocking collectives  51.3 us (9%)
  other arithmetic  37.3 us (7%)
  local copies, waits for them, and re-layouts  16.9 us (3%)
  between operations  15.6 us (3%)
    pallas_call x3, Pallas kernels, ffn_chunk(): pl.pallas_call(functools.partial(ffn_kernel, shards, c == 0), grid_spec=p...  95.8 us
    all_to_all x7, waiting for transfers between devices, exchange(): return lax.all_to_all(x, 'seq', split_axis=0, concat_axis=0, tiled=True)  62.2 us
    all_to_all x1, blocking collectives, exchange(): return lax.all_to_all(x, 'seq', split_axis=0, concat_axis=0, tiled=True)  51.3 us
    pallas_call x2, Pallas kernels, attend_backward(): pl.pallas_call(functools.partial(attend_bwd_kernel, block, j), grid=(1,),...  40.2 us
    ppermute x18, waiting for transfers between devices, swap(): return lax.ppermute(x, 'dp', [(i, i ^ bit) for i in range(self.n_dp)])  30.5 us
    all_to_all x7, starting transfers between devices, exchange(): return lax.all_to_all(x, 'seq', split_axis=0, concat_axis=0, tiled=True)  29.1 us
    ppermute x3, waiting for transfers between devices, pass_on(): down = lax.ppermute(down, 'seq', [(i + 1, i) for i in range(n - step)])  26.8 us
    ppermute x18, starting transfers between devices, swap(): return lax.ppermute(x, 'dp', [(i, i ^ bit) for i in range(self.n_dp)])  17.5 us
  transfers between devices with their start and end apart: 48, of which 23 were waited for; matrix products, arithmetic and copies ran while one was open for 8% of the time, Pallas kernels for 38%

profile of v5, /device:TPU:0, one launch (start us, length us, event | category | flops | bytes accessed | tf_op | source)
XLA Modules:
  0.0 557.5 jit_solution(15978543846311018999)
XLA Ops:
  9.7 5.1 collective-permute-start.2
  15.8 2.2 pack.1
  18.9 7.7 %collective-permute-done.1 = bf16[32,2176]{1,0:T(8,128)(2,1)S(1)} collective-permute-done((bf16[32,2176]{1,0:T(8,128)(2,1)S(1)}, bf16[32,2176]{1,0:T(8,128)(2,1)S(1)}, u32[]{:S(2)}, u32[]{:S(2)}) %collective-permute-start.1) | collective-permute-done | bytes 139296 | tf_op jit(solution)/shard_map/ppermute | solution.py:883
  31.3 4.6 collective-permute-start.6
  37.6 11.2 %collective-permute-done.9.refs_3_ = bf16[224,1536]{1,0:T(8,128)(2,1)S(1)} collective-permute-done((bf16[224,1536]{1,0:T(8,128)(2,1)}, bf16[224,1536]{1,0:T(8,128)(2,1)S(1)}, u32[]{:S(2)}, u32[]{:S(2)}) %collective-permute-start.9) | collective-permute-done | bytes 688160 | tf_op jit(solution)/shard_map/ppermute | solution.py:894
  50.1 1.5 collective-permute-start.7
  53.3 13.2 %collective-permute-done.10.refs_4_ = bf16[224,1536]{1,0:T(8,128)(2,1)S(1)} collective-permute-done((bf16[224,1536]{1,0:T(8,128)(2,1)S(1)}, bf16[224,1536]{1,0:T(8,128)(2,1)S(1)}, u32[]{:S(2)}, u32[]{:S(2)}) %collective-permute-start.10) | collective-permute-done | bytes 688160 | tf_op jit(solution)/shard_map/ppermute | solution.py:894
  67.8 1.5 collective-permute-start.8
  70.6 10.3 %qkv_forward.1 = (bf16[2048,512]{1,0:T(8,128)(2,1)}, f32[2048,384]{1,0:T(8,128)}) custom-call(s32[2]{0:T(128)} %pad_add_fusion.z_ref, bf16[512,1024]{1,0:T(8,128)(2,1)} %fusion.2.h_ref, f32[512,128]{1,0:T(8,128)} %copy.51.cos_ref, f32[512,128]{1,0:T(8,128)} %pad_maximum_fusion.8.sin_ref, f32[1,128]{1,0:T(1,128)} %tile.33.gain_q, f32[1,128]{1,0:T(1,128)} %tile.36.gain_k, ...), custom_call_target="tpu_custom_call" | custom-call | flops 2147483648 | bytes 12582912 | tf_op jit(solution)/shard_map/qkv_forward/pallas_call | solution.py:564
  80.9 2.4 collective-permute-done.11.refs_5_
  83.3 5.9 %either.1 = bf16[3,224,1536]{2,1,0:T(8,128)(2,1)} custom-call(s32[1]{0:T(128)} %bitcast.z_ref, bf16[224,1536]{1,0:T(8,128)(2,1)} %copy-done.14, bf16[224,1536]{1,0:T(8,128)(2,1)} %collective-permute-done.7.refs_1_, bf16[224,1536]{1,0:T(8,128)(2,1)} %collective-permute-done.8.refs_2_, bf16[224,1536]{1,0:T(8,128)(2,1)} %copy-done.13, ...), custom_call_target="tpu_custom_call" | custom-call | tf_op jit(solution)/shard_map/either/pallas_call | solution.py:904
  89.3 51.3 %all_to_all.73 = bf16[4,512,512]{2,1,0:T(8,128)(2,1)} all-to-all(bf16[4,512,512]{2,1,0:T(8,128)(2,1)S(1)} %bitcast.198), channel_id=1, replica_groups=mesh['dp'=8,'seq'=4] {'seq'}, dimensions={0} | all-to-all | bytes 4194304 | tf_op jit(solution)/shard_map/all_to_all | solution.py:1079
  142.7 16.5 %attend_forward.1 = (bf16[2048,256]{1,0:T(8,128)(2,1)}, f32[2,4,1,1024]{3,2,1,0:T(1,128)}) custom-call(bf16[2048,512]{1,0:T(8,128)(2,1)} %bitcast.189, bf16[2048,512]{1,0:T(8,128)(2,1)} %bitcast.190, bf16[2048,512]{1,0:T(8,128)(2,1)} %bitcast.191), custom_call_target="tpu_custom_call" | custom-call | flops 8589934592 | bytes 3145728 | tf_op jit(solution)/shard_map/attend_forward/pallas_call | solution.py:118
  159.1 6.5 %collective-permute-done.4 = bf16[96,1536]{1,0:T(8,128)(2,1)S(1)} collective-permute-done((bf16[96,1536]{1,0:T(8,128)(2,1)S(1)}, bf16[96,1536]{1,0:T(8,128)(2,1)S(1)}, u32[]{:S(2)}, u32[]{:S(2)}) %collective-permute-start.4) | collective-permute-done | bytes 294944 | tf_op jit(solution)/shard_map/ppermute | solution.py:883
  166.6 3.7 all-to-all-start.1
  173.8 21.6 %all-to-all-done.1 = bf16[4,512,256]{2,1,0:T(8,128)(2,1)S(1)} async-done(((bf16[4,512,256]{2,1,0:T(8,128)(2,1)}), bf16[4,512,256]{2,1,0:T(8,128)(2,1)S(1)}, u32[]{:S(2)}, u32[]{:S(2)}) %all-to-all-start.1) | async-done | bytes 1048608 | tf_op jit(solution)/shard_map/all_to_all | solution.py:1079
  196.3 6.7 %out_forward.1 = (f32[512,1024]{1,0:T(8,128)}, f32[512,1]{1,0:T(8,128)}, bf16[512,1024]{1,0:T(8,128)(2,1)}, bf16[1024,512]{1,0:T(8,128)(2,1)}) custom-call(s32[2]{0:T(128)} %pad_add_fusion.z_ref, bf16[2048,256]{1,0:T(8,128)(2,1)} %bitcast.172, bf16[512,1024]{1,0:T(8,128)(2,1)} %bitcast.170, f32[1,1024]{1,0:T(1,128)} %bitcast.222, bf16[256,1024]{1,0:T(8,128)(2,1)} %own.3, ...), custom_call_target="tpu_custom_call" | custom-call | flops 1073741824 | bytes 7340032 | tf_op jit(solution)/shard_map/out_forward/pallas_call | solution.py:771
  203.0 32.1 %ffn_chunk.3 = (f32[512,1024]{1,0:T(8,128)}, f32[512,1024]{1,0:T(8,128)}, bf16[8,4,96,1536]{3,2,1,0:T(8,128)(2,1)}) custom-call(s32[2]{0:T(128)} %pad_add_fusion.z_ref, bf16[512,1024]{1,0:T(8,128)(2,1)} %get-tuple-element.120.h_ref, bf16[1024,512]{1,0:T(8,128)(2,1)} %get-tuple-element.121.ht_ref, bf16[512,1024]{1,0:T(8,128)(2,1)} %bitcast_select_fusion.gy_ref.grad_y, ...), custom_call_target="tpu_custom_call" | custom-call | flops 14495514624 | bytes 29360128 | tf_op jit(solution)/shard_map/ffn_chunk/pallas_call | solution.py:336
  235.5 31.7 %ffn_chunk.4 = (f32[512,1024]{1,0:T(8,128)}, f32[512,1024]{1,0:T(8,128)}, bf16[8,4,96,1536]{3,2,1,0:T(8,128)(2,1)}) custom-call(s32[2]{0:T(128)} %pad_add_fusion.z_ref, bf16[512,1024]{1,0:T(8,128)(2,1)} %get-tuple-element.120.h_ref, bf16[1024,512]{1,0:T(8,128)(2,1)} %get-tuple-element.121.ht_ref, bf16[512,1024]{1,0:T(8,128)(2,1)} %bitcast_select_fusion.gy_ref.grad_y, ...), custom_call_target="tpu_custom_call" | custom-call | flops 14495514624 | bytes 29360128 | tf_op jit(solution)/shard_map/ffn_chunk/pallas_call | solution.py:336
  267.3 32.1 %ffn_chunk.5 = (bf16[512,1024]{1,0:T(8,128)(2,1)}, f32[512,1024]{1,0:T(8,128)}, bf16[4,4,96,1536]{3,2,1,0:T(8,128)(2,1)}, bf16[4,4,96,1536]{3,2,1,0:T(8,128)(2,1)}) custom-call(s32[2]{0:T(128)} %pad_add_fusion.z_ref, bf16[512,1024]{1,0:T(8,128)(2,1)} %get-tuple-element.120.h_ref, bf16[1024,512]{1,0:T(8,128)(2,1)} %get-tuple-element.121.ht_ref, ...), custom_call_target="tpu_custom_call" | custom-call | flops 14495514624 | bytes 29360128 | tf_op jit(solution)/shard_map/ffn_chunk/pallas_call | solution.py:336
  299.3 7.3 %out_backward.1 = (f32[512,1024]{1,0:T(8,128)}, f32[1,1024]{1,0:T(1,128)}, bf16[512,1024]{1,0:T(8,128)(2,1)}, bf16[2048,256]{1,0:T(8,128)(2,1)}) custom-call(s32[2]{0:T(128)} %pad_add_fusion.z_ref, f32[512,1024]{1,0:T(8,128)} %get-tuple-element.128.grad, bf16[512,1024]{1,0:T(8,128)(2,1)} %bitcast_select_fusion.gy_ref.grad_y, ...), custom_call_target="tpu_custom_call" | custom-call | flops 1073741824 | bytes 10485760 | tf_op jit(solution)/shard_map/out_backward/pallas_call | solution.py:816
  306.6 3.7 all-to-all-start.2
  310.3 5.5 out_terms.1
  315.8 2.9 fusion.4
  318.8 2.9 fusion.3
  321.7 15.3 %all-to-all-done.2 = bf16[4,512,256]{2,1,0:T(8,128)(2,1)S(1)} async-done(((bf16[4,512,256]{2,1,0:T(8,128)(2,1)}), bf16[4,512,256]{2,1,0:T(8,128)(2,1)S(1)}, u32[]{:S(2)}, u32[]{:S(2)}) %all-to-all-start.2) | async-done | bytes 1048608 | tf_op jit(solution)/shard_map/all_to_all | solution.py:1079
  337.0 2.4 slice_bitcast_fusion
  339.4 1.5 collective-permute-start.13
  341.4 20.2 %attend_backward.2 = bf16[2048,256]{1,0:T(8,128)(2,1)} custom-call(bf16[2048,512]{1,0:T(8,128)(2,1)} %bitcast.192, bf16[2048,512]{1,0:T(8,128)(2,1)} %bitcast.193, bf16[2048,512]{1,0:T(8,128)(2,1)} %bitcast.194, bf16[2048,256]{1,0:T(8,128)(2,1)} %bitcast.202, bf16[2048,256]{1,0:T(8,128)(2,1)} %get-tuple-element.108.o_ref, ...), custom_call_target="tpu_custom_call" | custom-call | flops 10737418240 | bytes 3145728 | tf_op jit(solution)/shard_map/attend_backward/pallas_call | solution.py:201
  361.6 4.9 all-to-all-start.3
  366.5 1.5 collective-permute-start.16
  368.0 1.5 collective-permute-start.17
  369.5 2.0 add_convert_fusion.4
  371.5 20.0 %attend_backward.3 = bf16[2048,256]{1,0:T(8,128)(2,1)} custom-call(bf16[2048,512]{1,0:T(8,128)(2,1)} %bitcast.195, bf16[2048,512]{1,0:T(8,128)(2,1)} %bitcast.196, bf16[2048,512]{1,0:T(8,128)(2,1)} %bitcast.197, bf16[2048,256]{1,0:T(8,128)(2,1)} %bitcast.203, bf16[2048,256]{1,0:T(8,128)(2,1)} %get-tuple-element.108.o_ref, ...), custom_call_target="tpu_custom_call" | custom-call | flops 10737418240 | bytes 3145728 | tf_op jit(solution)/shard_map/attend_backward/pallas_call | solution.py:201
  391.5 5.1 all-to-all-start.4
  397.2 8.1 %reduce-scatter.6.cloned.1.call-done = bf16[4,96,1536]{2,1,0:T(8,128)(2,1)} async-done(((bf16[32,96,1536]{2,1,0:T(8,128)(2,1)}), bf16[4,96,1536]{2,1,0:T(8,128)(2,1)}) %reduce-scatter.6.cloned.1.call-update) | async-done | bytes 1179664 | tf_op jit(solution)/shard_map/reduce_scatter | solution.py:932
  405.3 1.5 collective-permute-done.16
  407.1 1.4 constant_dynamic-slice_fusion.9
  409.7 3.3 fusion.9
  413.0 7.1 %all-to-all-done.4 = bf16[4,512,256]{2,1,0:T(8,128)(2,1)S(1)} async-done(((bf16[4,512,256]{2,1,0:T(8,128)(2,1)}), bf16[4,512,256]{2,1,0:T(8,128)(2,1)S(1)}, u32[]{:S(2)}, u32[]{:S(2)}) %all-to-all-start.4) | async-done | bytes 1048608 | tf_op jit(solution)/shard_map/all_to_all | solution.py:1079
  421.1 3.5 all-to-all-start.5
  426.3 1.4 collective-permute-start.18
  430.5 17.0 %qkv_backward.1 = (f32[512,1024]{1,0:T(8,128)}, bf16[4,4,32,2176]{3,2,1,0:T(8,128)(2,1)}, bf16[4,4,32,2176]{3,2,1,0:T(8,128)(2,1)}) custom-call(s32[2]{0:T(128)} %pad_add_fusion.z_ref, bf16[1024,512]{1,0:T(8,128)(2,1)} %copy.52.ht_ref, f32[512,128]{1,0:T(8,128)} %copy.51.cos_ref, f32[512,128]{1,0:T(8,128)} %pad_maximum_fusion.8.sin_ref, ...), custom_call_target="tpu_custom_call" | custom-call | flops 4294967296 | bytes 16777216 | tf_op jit(solution)/shard_map/qkv_backward/pallas_call | solution.py:681
  447.7 4.9 all-to-all-done.5
  452.6 2.8 fusion.6
  457.0 3.5 all-to-all-start.6
  463.4 1.5 collective-permute-start.21
  466.0 15.6 %collective-permute-done.21 = bf16[2,2,32,2176]{3,2,1,0:T(8,128)(2,1)S(1)} collective-permute-done((bf16[2,2,32,2176]{3,2,1,0:T(8,128)(2,1)S(1)}, bf16[2,2,32,2176]{3,2,1,0:T(8,128)(2,1)S(1)}, u32[]{:S(2)}, u32[]{:S(2)}) %collective-permute-start.21) | collective-permute-done | bytes 557088 | tf_op jit(solution)/shard_map/ppermute | solution.py:940
  481.6 2.0 collective-permute-done.23
  483.7 2.2 fusion.15
  486.0 2.0 collective-permute-start.22
  490.0 4.6 collective-permute-done.24
  495.1 1.7 fusion.18
  498.9 4.7 all-to-all-start.7
  503.8 1.7 collective-permute-start.31
  507.4 4.3 unpack_ffn.2
  511.7 12.3 %all-to-all-done.7 = bf16[4,32,3200]{2,1,0:T(8,128)(2,1)S(1)} async-done(((bf16[4,32,3200]{2,1,0:T(8,128)(2,1)}), bf16[4,32,3200]{2,1,0:T(8,128)(2,1)S(1)}, u32[]{:S(2)}, u32[]{:S(2)}) %all-to-all-start.7) | async-done | bytes 819232 | tf_op jit(solution)/shard_map/all_to_all | solution.py:1079
  524.6 1.4 collective-permute-start.26
  526.0 1.6 collective-permute-start.25
  529.6 3.5 collective-permute-done.27
  533.1 1.7 collective-permute-done.26
  537.5 3.2 unpack_qkv.1
  540.7 4.3 unpack_ffn.3
  546.1 4.4 unpack_near.1
  (178 shorter events, 50.6 us)
Async XLA Ops:
  7.2 63.4 %all-gather.8.cloned.1.call-start = ((), (), s32[]{:S(2)}) async-start(), calls=%async_computation.11 | async-start | bytes 3538944 | tf_op jit(solution)/shard_map/all_gather | solution.py:928
  9.7 9.2 %collective-permute-start.2 = (bf16[32,2176]{1,0:T(8,128)(2,1)S(1)}, bf16[32,2176]{1,0:T(8,128)(2,1)S(1)}, u32[]{:S(2)}, u32[]{:S(2)}) collective-permute-start(bf16[32,2176]{1,0:T(8,128)(2,1)S(1)} %pad_maximum_fusion.9), channel_id=1, source_target_pairs={{0,3},{1,0},{2,1},{3,2},{4,7},{5,4},{6,5},{7,6},{8,11},{9,8},{10,9... | collective-permute-start | bytes 417800 | tf_op jit(solution)/shard_map/ppermute | solution.py:883
  14.8 11.8 %collective-permute-start.1 = (bf16[32,2176]{1,0:T(8,128)(2,1)S(1)}, bf16[32,2176]{1,0:T(8,128)(2,1)S(1)}, u32[]{:S(2)}, u32[]{:S(2)}) collective-permute-start(bf16[32,2176]{1,0:T(8,128)(2,1)S(1)} %pad_maximum_fusion.9), channel_id=1, source_target_pairs={{0,2},{1,3},{2,0},{3,1},{4,6},{5,7},{6,4},{7,5},{8,10},{9,11},{10,... | collective-permute-start | bytes 417800 | tf_op jit(solution)/shard_map/ppermute | solution.py:883
  14.8 11.8 %collective-permute-start = (bf16[32,2176]{1,0:T(8,128)(2,1)S(1)}, bf16[32,2176]{1,0:T(8,128)(2,1)S(1)}, u32[]{:S(2)}, u32[]{:S(2)}) collective-permute-start(bf16[32,2176]{1,0:T(8,128)(2,1)S(1)} %pad_maximum_fusion.9), channel_id=1, source_target_pairs={{0,1},{1,2},{2,3},{3,0},{4,5},{5,6},{6,7},{7,4},{8,9},{9,10},{10,1... | collective-permute-start | bytes 417800 | tf_op jit(solution)/shard_map/ppermute | solution.py:883
  18.0 9.6 %copy-start.17 = (bf16[16]{0:T(256)(128)(2,1)S(1)}, bf16[16]{0:T(256)(128)(2,1)}, u32[]{:S(2)}) copy-start(bf16[16]{0:T(256)(128)(2,1)} %param.27) | copy-start | bytes 100
  18.0 9.6 %copy-start.18 = (bf16[16]{0:T(256)(128)(2,1)S(1)}, bf16[16]{0:T(256)(128)(2,1)}, u32[]{:S(2)}) copy-start(bf16[16]{0:T(256)(128)(2,1)} %param.26) | copy-start | bytes 100
  18.0 9.6 %copy-start.19 = (bf16[256]{0:T(256)(128)(2,1)S(1)}, bf16[256]{0:T(256)(128)(2,1)}, u32[]{:S(2)}) copy-start(bf16[256]{0:T(256)(128)(2,1)} %param.25) | copy-start | bytes 1540
  18.0 9.6 %copy-start.20 = (bf16[256]{0:T(256)(128)(2,1)S(1)}, bf16[256]{0:T(256)(128)(2,1)}, u32[]{:S(2)}) copy-start(bf16[256]{0:T(256)(128)(2,1)} %param.24) | copy-start | bytes 1540
  27.5 167.9 %all-gather.10.cloned.1.call-start = ((), (), s32[]{:S(2)}) async-start(), calls=%async_computation.12 | async-start | bytes 18579456 | tf_op jit(solution)/shard_map/all_gather | solution.py:928
  30.0 18.8 %collective-permute-start.9 = (bf16[224,1536]{1,0:T(8,128)(2,1)}, bf16[224,1536]{1,0:T(8,128)(2,1)S(1)}, u32[]{:S(2)}, u32[]{:S(2)}) collective-permute-start(bf16[224,1536]{1,0:T(8,128)(2,1)} %get-tuple-element.113), channel_id=1, source_target_pairs={{1,0},{2,1},{3,2},{5,4},{6,5},{7,6},{9,8},{10,9},{11,10},{13,12},{... | collective-permute-start | bytes 2064392 | tf_op jit(solution)/shard_map/ppermute | solution.py:894
  31.3 18.8 %collective-permute-start.6 = (bf16[224,1536]{1,0:T(8,128)(2,1)}, bf16[224,1536]{1,0:T(8,128)(2,1)S(1)}, u32[]{:S(2)}, u32[]{:S(2)}) collective-permute-start(bf16[224,1536]{1,0:T(8,128)(2,1)} %get-tuple-element.113), channel_id=1, source_target_pairs={{0,1},{1,2},{2,3},{4,5},{5,6},{6,7},{8,9},{9,10},{10,11},{12,13},{... | collective-permute-start | bytes 2064392 | tf_op jit(solution)/shard_map/ppermute | solution.py:893
  48.8 21.8 %copy-start.13 = (bf16[224,1536]{1,0:T(8,128)(2,1)}, bf16[224,1536]{1,0:T(8,128)(2,1)S(1)}, u32[]{:S(2)}) copy-start(bf16[224,1536]{1,0:T(8,128)(2,1)S(1)} %collective-permute-done.9.refs_3_) | copy-start | bytes 2064388
  48.8 17.7 %collective-permute-start.10 = (bf16[224,1536]{1,0:T(8,128)(2,1)S(1)}, bf16[224,1536]{1,0:T(8,128)(2,1)S(1)}, u32[]{:S(2)}, u32[]{:S(2)}) collective-permute-start(bf16[224,1536]{1,0:T(8,128)(2,1)S(1)} %collective-permute-done.9.refs_3_), channel_id=1, source_target_pairs={{1,0},{2,1},{5,4},{6,5},{9,8},{10,9},{13,12},{14,13},{17,16},{18,1... | collective-permute-start | bytes 2064392 | tf_op jit(solution)/shard_map/ppermute | solution.py:894
  50.1 20.5 %copy-start.14 = (bf16[224,1536]{1,0:T(8,128)(2,1)}, bf16[224,1536]{1,0:T(8,128)(2,1)S(1)}, u32[]{:S(2)}) copy-start(bf16[224,1536]{1,0:T(8,128)(2,1)S(1)} %collective-permute-done.6.refs_0_) | copy-start | bytes 2064388
  50.1 17.6 %collective-permute-start.7 = (bf16[224,1536]{1,0:T(8,128)(2,1)S(1)}, bf16[224,1536]{1,0:T(8,128)(2,1)}, u32[]{:S(2)}, u32[]{:S(2)}) collective-permute-start(bf16[224,1536]{1,0:T(8,128)(2,1)S(1)} %collective-permute-done.6.refs_0_), channel_id=1, source_target_pairs={{1,2},{2,3},{5,6},{6,7},{9,10},{10,11},{13,14},{14,15},{17,18},{18... | collective-permute-start | bytes 2064392 | tf_op jit(solution)/shard_map/ppermute | solution.py:893
  66.5 14.4 %copy-start.15 = (bf16[224,1536]{1,0:T(8,128)(2,1)}, bf16[224,1536]{1,0:T(8,128)(2,1)S(1)}, u32[]{:S(2)}) copy-start(bf16[224,1536]{1,0:T(8,128)(2,1)S(1)} %collective-permute-done.10.refs_4_) | copy-start | bytes 2064388
  66.5 16.8 %collective-permute-start.11 = (bf16[224,1536]{1,0:T(8,128)(2,1)S(1)}, bf16[224,1536]{1,0:T(8,128)(2,1)}, u32[]{:S(2)}, u32[]{:S(2)}) collective-permute-start(bf16[224,1536]{1,0:T(8,128)(2,1)S(1)} %collective-permute-done.10.refs_4_), channel_id=1, source_target_pairs={{1,0},{5,4},{9,8},{13,12},{17,16},{21,20},{25,24},{29,28}} | collective-permute-start | bytes 2064392 | tf_op jit(solution)/shard_map/ppermute | solution.py:894
  67.8 15.5 %collective-permute-start.8 = (bf16[224,1536]{1,0:T(8,128)(2,1)}, bf16[224,1536]{1,0:T(8,128)(2,1)}, u32[]{:S(2)}, u32[]{:S(2)}) collective-permute-start(bf16[224,1536]{1,0:T(8,128)(2,1)} %collective-permute-done.7.refs_1_), channel_id=1, source_target_pairs={{2,3},{6,7},{10,11},{14,15},{18,19},{22,23},{26,27},{30,31}} | collective-permute-start | bytes 2064392 | tf_op jit(solution)/shard_map/ppermute | solution.py:893
  83.3 6.0 %copy-start.7 = (bf16[2048,512]{1,0:T(8,128)(2,1)S(1)}, bf16[2048,512]{1,0:T(8,128)(2,1)}, u32[]{:S(2)}) copy-start(bf16[2048,512]{1,0:T(8,128)(2,1)} %get-tuple-element.104) | copy-start | bytes 6291460
  89.2 178.0 %all-gather.12.cloned.1.call-start = ((), (), s32[]{:S(2)}) async-start(), calls=%async_computation.13 | async-start | bytes 7962624 | tf_op jit(solution)/shard_map/all_gather | solution.py:928
  89.3 51.3 %copy-start.21 = (bf16[96,1536]{1,0:T(8,128)(2,1)S(1)}, bf16[96,1536]{1,0:T(8,128)(2,1)}, u32[]{:S(2)}) copy-start(bf16[96,1536]{1,0:T(8,128)(2,1)} %get-tuple-element.107) | copy-start | bytes 884740
  140.6 18.5 %collective-permute-start.5 = (bf16[96,1536]{1,0:T(8,128)(2,1)S(1)}, bf16[96,1536]{1,0:T(8,128)(2,1)S(1)}, u32[]{:S(2)}, u32[]{:S(2)}) collective-permute-start(bf16[96,1536]{1,0:T(8,128)(2,1)S(1)} %copy-done.21), channel_id=1, source_target_pairs={{0,3},{1,0},{2,1},{3,2},{4,7},{5,4},{6,5},{7,6},{8,11},{9,8},{10,9... | collective-permute-start | bytes 884744 | tf_op jit(solution)/shard_map/ppermute | solution.py:883
  141.9 23.7 %collective-permute-start.4 = (bf16[96,1536]{1,0:T(8,128)(2,1)S(1)}, bf16[96,1536]{1,0:T(8,128)(2,1)S(1)}, u32[]{:S(2)}, u32[]{:S(2)}) collective-permute-start(bf16[96,1536]{1,0:T(8,128)(2,1)S(1)} %copy-done.21), channel_id=1, source_target_pairs={{0,2},{1,3},{2,0},{3,1},{4,6},{5,7},{6,4},{7,5},{8,10},{9,11},{10,... | collective-permute-start | bytes 884744 | tf_op jit(solution)/shard_map/ppermute | solution.py:883
  142.1 23.5 %collective-permute-start.3 = (bf16[96,1536]{1,0:T(8,128)(2,1)S(1)}, bf16[96,1536]{1,0:T(8,128)(2,1)S(1)}, u32[]{:S(2)}, u32[]{:S(2)}) collective-permute-start(bf16[96,1536]{1,0:T(8,128)(2,1)S(1)} %copy-done.21), channel_id=1, source_target_pairs={{0,1},{1,2},{2,3},{3,0},{4,5},{5,6},{6,7},{7,4},{8,9},{9,10},{10,1... | collective-permute-start | bytes 884744 | tf_op jit(solution)/shard_map/ppermute | solution.py:883
  166.6 5.3 copy-start.11
  166.6 28.7 %all-to-all-start.1 = ((bf16[4,512,256]{2,1,0:T(8,128)(2,1)}), bf16[4,512,256]{2,1,0:T(8,128)(2,1)S(1)}, u32[]{:S(2)}, u32[]{:S(2)}) async-start(bf16[4,512,256]{2,1,0:T(8,128)(2,1)} %bitcast.12), calls=%async_computation.1 | async-start | bytes 2097152 | tf_op jit(solution)/shard_map/all_to_all | solution.py:1079
  170.3 166.7 %reduce-scatter.4.cloned.1.call-start = ((), (), s32[]{:S(2)}) async-start(), calls=%async_computation.14 | async-start | bytes 10616832 | tf_op jit(solution)/shard_map/reduce_scatter | solution.py:932
  235.1 170.2 %reduce-scatter.6.cloned.1.call-start = ((), (), s32[]{:S(2)}) async-start(), calls=%async_computation.15 | async-start | bytes 10616832 | tf_op jit(solution)/shard_map/reduce_scatter | solution.py:932
  299.3 16.5 %collective-permute-start.12 = (bf16[4,4,96,1536]{3,2,1,0:T(8,128)(2,1)}, bf16[4,4,96,1536]{3,2,1,0:T(8,128)(2,1)}, u32[]{:S(2)}, u32[]{:S(2)}) collective-permute-start(bf16[4,4,96,1536]{3,2,1,0:T(8,128)(2,1)} %get-tuple-element.137), channel_id=1, source_target_pairs={{0,4},{4,0},{8,12},{12,8},{16,20},{20,16},{24,28},{28,24},{1,5},{5... | collective-permute-start | bytes 14155784 | tf_op jit(solution)/shard_map/ppermute | solution.py:940
  306.6 30.4 %all-to-all-start.2 = ((bf16[4,512,256]{2,1,0:T(8,128)(2,1)}), bf16[4,512,256]{2,1,0:T(8,128)(2,1)S(1)}, u32[]{:S(2)}, u32[]{:S(2)}) async-start(bf16[4,512,256]{2,1,0:T(8,128)(2,1)} %bitcast.204), calls=%async_computation.2 | async-start | bytes 2097152 | tf_op jit(solution)/shard_map/all_to_all | solution.py:1079
  339.4 30.1 %collective-permute-start.13 = (bf16[96,1536]{1,0:T(8,128)(2,1)}, bf16[96,1536]{1,0:T(8,128)(2,1)}, u32[]{:S(2)}, u32[]{:S(2)}) collective-permute-start(bf16[96,1536]{1,0:T(8,128)(2,1)} %get-tuple-element.142), channel_id=1, source_target_pairs={{0,3},{1,0},{2,1},{3,2},{4,7},{5,4},{6,5},{7,6},{8,11},{9,8},{10,9... | collective-permute-start | bytes 884744 | tf_op jit(solution)/shard_map/ppermute | solution.py:883
  340.8 28.6 %collective-permute-start.14 = (bf16[96,1536]{1,0:T(8,128)(2,1)S(1)}, bf16[96,1536]{1,0:T(8,128)(2,1)}, u32[]{:S(2)}, u32[]{:S(2)}) collective-permute-start(bf16[96,1536]{1,0:T(8,128)(2,1)S(1)} %get-tuple-element.143), channel_id=1, source_target_pairs={{0,2},{1,3},{2,0},{3,1},{4,6},{5,7},{6,4},{7,5},{8,10},{9,11},{10,... | collective-permute-start | bytes 884744 | tf_op jit(solution)/shard_map/ppermute | solution.py:883
  340.8 28.6 %collective-permute-start.15 = (bf16[96,1536]{1,0:T(8,128)(2,1)S(1)}, bf16[96,1536]{1,0:T(8,128)(2,1)}, u32[]{:S(2)}, u32[]{:S(2)}) collective-permute-start(bf16[96,1536]{1,0:T(8,128)(2,1)S(1)} %get-tuple-element.144), channel_id=1, source_target_pairs={{0,1},{1,2},{2,3},{3,0},{4,5},{5,6},{6,7},{7,4},{8,9},{9,10},{10,1... | collective-permute-start | bytes 884744 | tf_op jit(solution)/shard_map/ppermute | solution.py:883
  361.6 29.8 %all-to-all-start.3 = ((bf16[4,512,256]{2,1,0:T(8,128)(2,1)}), bf16[4,512,256]{2,1,0:T(8,128)(2,1)S(1)}, u32[]{:S(2)}, u32[]{:S(2)}) async-start(bf16[4,512,256]{2,1,0:T(8,128)(2,1)} %bitcast.205), calls=%async_computation.4 | async-start | bytes 2097152 | tf_op jit(solution)/shard_map/all_to_all | solution.py:1079
  366.5 40.3 %collective-permute-start.16 = (bf16[2,2,96,1536]{3,2,1,0:T(8,128)(2,1)}, bf16[2,2,96,1536]{3,2,1,0:T(8,128)(2,1)S(1)}, u32[]{:S(2)}, u32[]{:S(2)}) collective-permute-start(bf16[2,2,96,1536]{3,2,1,0:T(8,128)(2,1)} %fusion.3), channel_id=1, source_target_pairs={{0,8},{4,12},{8,0},{12,4},{16,24},{20,28},{24,16},{28,20},{1,9},{5... | collective-permute-start | bytes 3538952 | tf_op jit(solution)/shard_map/ppermute | solution.py:940
  368.0 39.1 %collective-permute-start.17 = (bf16[2,2,96,1536]{3,2,1,0:T(8,128)(2,1)}, bf16[2,2,96,1536]{3,2,1,0:T(8,128)(2,1)}, u32[]{:S(2)}, u32[]{:S(2)}) collective-permute-start(bf16[2,2,96,1536]{3,2,1,0:T(8,128)(2,1)} %fusion.4), channel_id=1, source_target_pairs={{0,16},{4,20},{8,24},{12,28},{16,0},{20,4},{24,8},{28,12},{1,17},{... | collective-permute-start | bytes 3538952 | tf_op jit(solution)/shard_map/ppermute | solution.py:940
  391.5 5.7 %copy-start.4 = (bf16[4,512,256]{2,1,0:T(8,128)(2,1)}, bf16[4,512,256]{2,1,0:T(8,128)(2,1)S(1)}, u32[]{:S(2)}) copy-start(bf16[4,512,256]{2,1,0:T(8,128)(2,1)S(1)} %all-to-all-done.3) | copy-start | bytes 3145732
  391.5 28.6 %all-to-all-start.4 = ((bf16[4,512,256]{2,1,0:T(8,128)(2,1)}), bf16[4,512,256]{2,1,0:T(8,128)(2,1)S(1)}, u32[]{:S(2)}, u32[]{:S(2)}) async-start(bf16[4,512,256]{2,1,0:T(8,128)(2,1)} %bitcast.201), calls=%async_computation.5 | async-start | bytes 2097152 | tf_op jit(solution)/shard_map/all_to_all | solution.py:1079
  396.6 100.2 %reduce-scatter.8.cloned.1.call-start = ((), (), s32[]{:S(2)}) async-start(), calls=%async_computation.16 | async-start | bytes 2359296 | tf_op jit(solution)/shard_map/reduce_scatter | solution.py:932
  406.8 2.9 copy-start.9
  420.1 8.8 %copy-start.1 = (bf16[1,512,1024]{2,1,0:T(8,128)(2,1)S(1)}, bf16[1,512,1024]{2,1,0:T(8,128)(2,1)}, u32[]{:S(2)}) copy-start(bf16[1,512,1024]{2,1,0:T(8,128)(2,1)} %param.14) | copy-start | bytes 3145732
  421.1 31.5 %all-to-all-start.5 = ((bf16[4,96,1536]{2,1,0:T(8,128)(2,1)}), bf16[4,96,1536]{2,1,0:T(8,128)(2,1)S(1)}, u32[]{:S(2)}, u32[]{:S(2)}) async-start(bf16[4,96,1536]{2,1,0:T(8,128)(2,1)} %pad_maximum_fusion), calls=%async_computation.7 | async-start | bytes 2359296 | tf_op jit(solution)/shard_map/all_to_all | solution.py:1079
  424.6 82.8 %all-gather.14.cloned.1.call-start = ((), (), s32[]{:S(2)}) async-start(), calls=%async_computation.17 | async-start | bytes 2654208 | tf_op jit(solution)/shard_map/all_gather | solution.py:928
  426.3 21.2 %collective-permute-start.18 = (bf16[2,96,1536]{2,1,0:T(8,128)(2,1)}, bf16[2,96,1536]{2,1,0:T(8,128)(2,1)}, u32[]{:S(2)}, u32[]{:S(2)}) collective-permute-start(bf16[2,96,1536]{2,1,0:T(8,128)(2,1)} %get-tuple-element.189), channel_id=1, source_target_pairs={{0,16},{4,20},{8,24},{12,28},{16,0},{20,4},{24,8},{28,12},{1,17},{... | collective-permute-start | bytes 1769480 | tf_op jit(solution)/shard_map/ppermute | solution.py:940
  427.7 19.9 %collective-permute-start.19 = (bf16[2,96,1536]{2,1,0:T(8,128)(2,1)}, bf16[2,96,1536]{2,1,0:T(8,128)(2,1)}, u32[]{:S(2)}, u32[]{:S(2)}) collective-permute-start(bf16[2,96,1536]{2,1,0:T(8,128)(2,1)} %get-tuple-element.190), channel_id=1, source_target_pairs={{0,8},{4,12},{8,0},{12,4},{16,24},{20,28},{24,16},{28,20},{1,9},{5... | collective-permute-start | bytes 1769480 | tf_op jit(solution)/shard_map/ppermute | solution.py:940
  430.5 22.1 %copy-start.10 = (bf16[2,2,96,1536]{3,2,1,0:T(8,128)(2,1)S(1)}, bf16[2,2,96,1536]{3,2,1,0:T(8,128)(2,1)}, u32[]{:S(2)}) copy-start(bf16[2,2,96,1536]{3,2,1,0:T(8,128)(2,1)} %copy-done.9) | copy-start | bytes 3538948
  452.6 8.0 %collective-permute-start.20 = (bf16[4,4,32,2176]{3,2,1,0:T(8,128)(2,1)}, bf16[4,4,32,2176]{3,2,1,0:T(8,128)(2,1)}, u32[]{:S(2)}, u32[]{:S(2)}) collective-permute-start(bf16[4,4,32,2176]{3,2,1,0:T(8,128)(2,1)} %get-tuple-element.161), channel_id=1, source_target_pairs={{0,4},{4,0},{8,12},{12,8},{16,20},{20,16},{24,28},{28,24},{1,5},{5... | collective-permute-start | bytes 6684680 | tf_op jit(solution)/shard_map/ppermute | solution.py:940
  457.0 33.0 %all-to-all-start.6 = ((bf16[4,96,1536]{2,1,0:T(8,128)(2,1)}), bf16[4,96,1536]{2,1,0:T(8,128)(2,1)S(1)}, u32[]{:S(2)}, u32[]{:S(2)}) async-start(bf16[4,96,1536]{2,1,0:T(8,128)(2,1)} %pad_maximum_fusion.1), calls=%async_computation.8 | async-start | bytes 2359296 | tf_op jit(solution)/shard_map/all_to_all | solution.py:1079
  460.6 80.1 %all-gather.16.cloned.1.call-start = ((), (), s32[]{:S(2)}) async-start(), calls=%async_computation.18 | async-start | bytes 2654208 | tf_op jit(solution)/shard_map/all_gather | solution.py:928
  463.4 18.3 %collective-permute-start.21 = (bf16[2,2,32,2176]{3,2,1,0:T(8,128)(2,1)S(1)}, bf16[2,2,32,2176]{3,2,1,0:T(8,128)(2,1)S(1)}, u32[]{:S(2)}, u32[]{:S(2)}) collective-permute-start(bf16[2,2,32,2176]{3,2,1,0:T(8,128)(2,1)S(1)} %fusion.11), channel_id=1, source_target_pairs={{0,8},{4,12},{8,0},{12,4},{16,24},{20,28},{24,16},{28,20},{1,9},{5... | collective-permute-start | bytes 1671176 | tf_op jit(solution)/shard_map/ppermute | solution.py:940
  464.8 18.8 %collective-permute-start.23 = (bf16[2,2,32,2176]{3,2,1,0:T(8,128)(2,1)S(1)}, bf16[2,2,32,2176]{3,2,1,0:T(8,128)(2,1)S(1)}, u32[]{:S(2)}, u32[]{:S(2)}) collective-permute-start(bf16[2,2,32,2176]{3,2,1,0:T(8,128)(2,1)S(1)} %fusion.12), channel_id=1, source_target_pairs={{0,16},{4,20},{8,24},{12,28},{16,0},{20,4},{24,8},{28,12},{1,17},{... | collective-permute-start | bytes 1671176 | tf_op jit(solution)/shard_map/ppermute | solution.py:940
  485.9 8.7 %collective-permute-start.24 = (bf16[2,32,2176]{2,1,0:T(8,128)(2,1)}, bf16[2,32,2176]{2,1,0:T(8,128)(2,1)}, u32[]{:S(2)}, u32[]{:S(2)}) collective-permute-start(bf16[2,32,2176]{2,1,0:T(8,128)(2,1)} %get-tuple-element.193), channel_id=1, source_target_pairs={{0,8},{4,12},{8,0},{12,4},{16,24},{20,28},{24,16},{28,20},{1,9},{5... | collective-permute-start | bytes 835592 | tf_op jit(solution)/shard_map/ppermute | solution.py:940
  486.0 9.2 %collective-permute-start.22 = (bf16[2,32,2176]{2,1,0:T(8,128)(2,1)}, bf16[2,32,2176]{2,1,0:T(8,128)(2,1)}, u32[]{:S(2)}, u32[]{:S(2)}) collective-permute-start(bf16[2,32,2176]{2,1,0:T(8,128)(2,1)} %get-tuple-element.194), channel_id=1, source_target_pairs={{0,16},{4,20},{8,24},{12,28},{16,0},{20,4},{24,8},{28,12},{1,17},{... | collective-permute-start | bytes 835592 | tf_op jit(solution)/shard_map/ppermute | solution.py:940
  498.9 25.0 %all-to-all-start.7 = ((bf16[4,32,3200]{2,1,0:T(8,128)(2,1)}), bf16[4,32,3200]{2,1,0:T(8,128)(2,1)S(1)}, u32[]{:S(2)}, u32[]{:S(2)}) async-start(bf16[4,32,3200]{2,1,0:T(8,128)(2,1)} %pad_maximum_fusion.5), calls=%async_computation.10 | async-start | bytes 1638400 | tf_op jit(solution)/shard_map/all_to_all | solution.py:1079
  503.8 22.2 %collective-permute-start.31 = (bf16[96,1536]{1,0:T(8,128)(2,1)S(1)}, bf16[96,1536]{1,0:T(8,128)(2,1)S(1)}, u32[]{:S(2)}, u32[]{:S(2)}) collective-permute-start(bf16[96,1536]{1,0:T(8,128)(2,1)S(1)} %reduce_sum.57), channel_id=1, source_target_pairs={{0,24},{4,28},{8,16},{12,20},{16,8},{20,12},{24,0},{28,4},{1,25},{... | collective-permute-start | bytes 884744 | tf_op jit(solution)/shard_map/ppermute | solution.py:940
  505.5 22.2 %collective-permute-start.30 = (bf16[96,1536]{1,0:T(8,128)(2,1)S(1)}, bf16[96,1536]{1,0:T(8,128)(2,1)S(1)}, u32[]{:S(2)}, u32[]{:S(2)}) collective-permute-start(bf16[96,1536]{1,0:T(8,128)(2,1)S(1)} %reduce_sum.57), channel_id=1, source_target_pairs={{0,16},{4,20},{8,24},{12,28},{16,0},{20,4},{24,8},{28,12},{1,17},{... | collective-permute-start | bytes 884744 | tf_op jit(solution)/shard_map/ppermute | solution.py:940
  506.2 21.5 %collective-permute-start.29 = (bf16[96,1536]{1,0:T(8,128)(2,1)S(1)}, bf16[96,1536]{1,0:T(8,128)(2,1)S(1)}, u32[]{:S(2)}, u32[]{:S(2)}) collective-permute-start(bf16[96,1536]{1,0:T(8,128)(2,1)S(1)} %reduce_sum.57), channel_id=1, source_target_pairs={{0,8},{4,12},{8,0},{12,4},{16,24},{20,28},{24,16},{28,20},{1,9},{5... | collective-permute-start | bytes 884744 | tf_op jit(solution)/shard_map/ppermute | solution.py:940
  524.1 9.0 %collective-permute-start.27 = (bf16[32,3200]{1,0:T(8,128)(2,1)S(1)}, bf16[32,3200]{1,0:T(8,128)(2,1)S(1)}, u32[]{:S(2)}, u32[]{:S(2)}) collective-permute-start(bf16[32,3200]{1,0:T(8,128)(2,1)S(1)} %reduce_sum.56), channel_id=1, source_target_pairs={{0,24},{4,28},{8,16},{12,20},{16,8},{20,12},{24,0},{28,4},{1,25},{... | collective-permute-start | bytes 614408 | tf_op jit(solution)/shard_map/ppermute | solution.py:940
  524.6 10.1 %collective-permute-start.26 = (bf16[32,3200]{1,0:T(8,128)(2,1)S(1)}, bf16[32,3200]{1,0:T(8,128)(2,1)S(1)}, u32[]{:S(2)}, u32[]{:S(2)}) collective-permute-start(bf16[32,3200]{1,0:T(8,128)(2,1)S(1)} %reduce_sum.56), channel_id=1, source_target_pairs={{0,16},{4,20},{8,24},{12,28},{16,0},{20,4},{24,8},{28,12},{1,17},{... | collective-permute-start | bytes 614408 | tf_op jit(solution)/shard_map/ppermute | solution.py:940
  526.0 8.8 %collective-permute-start.25 = (bf16[32,3200]{1,0:T(8,128)(2,1)S(1)}, bf16[32,3200]{1,0:T(8,128)(2,1)S(1)}, u32[]{:S(2)}, u32[]{:S(2)}) collective-permute-start(bf16[32,3200]{1,0:T(8,128)(2,1)S(1)} %reduce_sum.56), channel_id=1, source_target_pairs={{0,8},{4,12},{8,0},{12,4},{16,24},{20,28},{24,16},{28,20},{1,9},{5... | collective-permute-start | bytes 614408 | tf_op jit(solution)/shard_map/ppermute | solution.py:940
  529.5 11.2 %copy-start.3 = (bf16[4,96,1536]{2,1,0:T(8,128)(2,1)}, bf16[4,96,1536]{2,1,0:T(8,128)(2,1)S(1)}, u32[]{:S(2)}) copy-start(bf16[4,96,1536]{2,1,0:T(8,128)(2,1)S(1)} %pad_maximum_fusion.2.even) | copy-start | bytes 3538948
  529.5 15.5 %collective-permute-start.32 = (bf16[4,96,1536]{2,1,0:T(8,128)(2,1)S(1)}, bf16[4,96,1536]{2,1,0:T(8,128)(2,1)S(1)}, u32[]{:S(2)}, u32[]{:S(2)}) collective-permute-start(bf16[4,96,1536]{2,1,0:T(8,128)(2,1)S(1)} %pad_maximum_fusion.2.even), channel_id=1, source_target_pairs={{0,4},{4,0},{8,12},{12,8},{16,20},{20,16},{24,28},{28,24},{1,5},{5... | collective-permute-start | bytes 3538952 | tf_op jit(solution)/shard_map/ppermute | solution.py:940
  534.9 2.5 copy-start.6
  534.9 2.5 collective-permute-start.28
  (6 other events, 8.4 us)
Sparse Core Ops, SparseCore 0:
  27.6 32.6 all-gather.7
  89.4 91.6 all-gather.9
  183.5 48.8 all-gather.11
  235.8 76.4 reduce-scatter.3
  315.6 89.6 reduce-scatter.5
  408.4 46.8 reduce-scatter.7
  458.0 33.3 all-gather.13
  493.4 34.3 all-gather.15

commit v6 on v5

--- a/solution.py
+++ b/solution.py
@@ -1046,7 +1046,9 @@
     packed = jnp.concatenate([mine(w_query), mine(w_key), mine(w_value), gains], axis=1)
     near = axes.from_others(packed)
     first_chunks, last_chunk = pack(member, w_gate, w_up, w_down, w_out)
-    near = [after(x, first_chunks) for x in near]
+    positions = z * local + jnp.arange(local, dtype=jnp.int32)
+    cosine, sine = tables(positions)
+    near = [after(x, first_chunks, cosine, sine) for x in near]
     far_qkv = axes.gather(jnp.stack([x[:, :-128] for x in near]))
     far_qkv = far_qkv.reshape(SPLIT, shards - 1, piece, -1)
     gains = jnp.stack([x[:, -128:].reshape(-1) for x in [packed] + near])
@@ -1066,8 +1068,6 @@
     def stack_after(parts, *others):
         return jnp.stack([after(x, *others) for x in parts])
 
-    positions = z * local + jnp.arange(local, dtype=jnp.int32)
-    cosine, sine = tables(positions)
     valid = (positions < lengths[0])[:, None]
     grad_y = jnp.where(valid, cotangent[0], jnp.zeros((), bf16))
     inputs = tokens[0].astype(f32)

time: 566 us -> 564 us (level)
  transfers between devices with their start and end apart: 48 -> 48, of which waited for: 23 -> 22; matrix products, arithmetic and copies ran while one was open for 8% -> 8% of each run, Pallas kernels for 38% -> 38%
where the time goes in v6:
time: 564 us; the launch traced here: 556 us
  Pallas kernels  224 us (40%)
  waiting for transfers between devices  142 us (25%)
  starting transfers between devices  69.3 us (12%)
  blocking collectives  51.3 us (9%)
  other arithmetic  37.3 us (7%)
  local copies, waits for them, and re-layouts  16.9 us (3%)
  between operations  15.6 us (3%)
    pallas_call x3, Pallas kernels, ffn_chunk(): pl.pallas_call(functools.partial(ffn_kernel, shards, c == 0), grid_spec=p...  95.8 us
    all_to_all x7, waiting for transfers between devices, exchange(): return lax.all_to_all(x, 'seq', split_axis=0, concat_axis=0, tiled=True)  62.4 us
    all_to_all x1, blocking collectives, exchange(): return lax.all_to_all(x, 'seq', split_axis=0, concat_axis=0, tiled=True)  51.3 us
    pallas_call x2, Pallas kernels, attend_backward(): pl.pallas_call(functools.partial(attend_bwd_kernel, block, j), grid=(1,),...  40.2 us
    ppermute x18, waiting for transfers between devices, swap(): return lax.ppermute(x, 'dp', [(i, i ^ bit) for i in range(self.n_dp)])  30.4 us
    all_to_all x7, starting transfers between devices, exchange(): return lax.all_to_all(x, 'seq', split_axis=0, concat_axis=0, tiled=True)  29.1 us
    ppermute x3, waiting for transfers between devices, pass_on(): down = lax.ppermute(down, 'seq', [(i + 1, i) for i in range(n - step)])  27 us
    ppermute x18, starting transfers between devices, swap(): return lax.ppermute(x, 'dp', [(i, i ^ bit) for i in range(self.n_dp)])  17.4 us
  transfers between devices with their start and end apart: 48, of which 22 were waited for; matrix products, arithmetic and copies ran while one was open for 8% of the time, Pallas kernels for 38%

profile of v6, /device:TPU:0, one launch (start us, length us, event | category | flops | bytes accessed | tf_op | source)
XLA Modules:
  0.0 555.5 jit_solution(10687306108345517941)
XLA Ops:
  9.7 5.1 collective-permute-start.2
  16.9 2.2 pack.1
  20.2 6.4 %collective-permute-done.1 = bf16[32,2176]{1,0:T(8,128)(2,1)S(1)} collective-permute-done((bf16[32,2176]{1,0:T(8,128)(2,1)S(1)}, bf16[32,2176]{1,0:T(8,128)(2,1)S(1)}, u32[]{:S(2)}, u32[]{:S(2)}) %collective-permute-start.1) | collective-permute-done | bytes 139296 | tf_op jit(solution)/shard_map/ppermute | solution.py:883
  29.3 4.6 collective-permute-start.6
  35.4 11.4 %collective-permute-done.9.refs_3_ = bf16[224,1536]{1,0:T(8,128)(2,1)S(1)} collective-permute-done((bf16[224,1536]{1,0:T(8,128)(2,1)}, bf16[224,1536]{1,0:T(8,128)(2,1)S(1)}, u32[]{:S(2)}, u32[]{:S(2)}) %collective-permute-start.9) | collective-permute-done | bytes 688160 | tf_op jit(solution)/shard_map/ppermute | solution.py:894
  48.1 1.5 collective-permute-start.7
  51.3 13.2 %collective-permute-done.10.refs_4_ = bf16[224,1536]{1,0:T(8,128)(2,1)S(1)} collective-permute-done((bf16[224,1536]{1,0:T(8,128)(2,1)S(1)}, bf16[224,1536]{1,0:T(8,128)(2,1)S(1)}, u32[]{:S(2)}, u32[]{:S(2)}) %collective-permute-start.10) | collective-permute-done | bytes 688160 | tf_op jit(solution)/shard_map/ppermute | solution.py:894
  65.8 1.5 collective-permute-start.8
  68.6 10.3 %qkv_forward.1 = (bf16[2048,512]{1,0:T(8,128)(2,1)}, f32[2048,384]{1,0:T(8,128)}) custom-call(s32[2]{0:T(128)} %pad_add_fusion.z_ref, bf16[512,1024]{1,0:T(8,128)(2,1)} %fusion.2.h_ref, f32[512,128]{1,0:T(8,128)} %copy.51.cos_ref, f32[512,128]{1,0:T(8,128)} %pad_maximum_fusion.8.sin_ref, f32[1,128]{1,0:T(1,128)} %tile.33.gain_q, f32[1,128]{1,0:T(1,128)} %tile.36.gain_k, ...), custom_call_target="tpu_custom_call" | custom-call | flops 2147483648 | bytes 12582912 | tf_op jit(solution)/shard_map/qkv_forward/pallas_call | solution.py:564
  78.9 2.4 collective-permute-done.11.refs_5_
  81.3 5.9 %either.1 = bf16[3,224,1536]{2,1,0:T(8,128)(2,1)} custom-call(s32[1]{0:T(128)} %bitcast.z_ref, bf16[224,1536]{1,0:T(8,128)(2,1)} %copy-done.14, bf16[224,1536]{1,0:T(8,128)(2,1)} %collective-permute-done.7.refs_1_, bf16[224,1536]{1,0:T(8,128)(2,1)} %collective-permute-done.8.refs_2_, bf16[224,1536]{1,0:T(8,128)(2,1)} %copy-done.13, ...), custom_call_target="tpu_custom_call" | custom-call | tf_op jit(solution)/shard_map/either/pallas_call | solution.py:904
  87.3 51.3 %all_to_all.73 = bf16[4,512,512]{2,1,0:T(8,128)(2,1)} all-to-all(bf16[4,512,512]{2,1,0:T(8,128)(2,1)S(1)} %bitcast.198), channel_id=1, replica_groups=mesh['dp'=8,'seq'=4] {'seq'}, dimensions={0} | all-to-all | bytes 4194304 | tf_op jit(solution)/shard_map/all_to_all | solution.py:1079
  140.6 16.5 %attend_forward.1 = (bf16[2048,256]{1,0:T(8,128)(2,1)}, f32[2,4,1,1024]{3,2,1,0:T(1,128)}) custom-call(bf16[2048,512]{1,0:T(8,128)(2,1)} %bitcast.189, bf16[2048,512]{1,0:T(8,128)(2,1)} %bitcast.190, bf16[2048,512]{1,0:T(8,128)(2,1)} %bitcast.191), custom_call_target="tpu_custom_call" | custom-call | flops 8589934592 | bytes 3145728 | tf_op jit(solution)/shard_map/attend_forward/pallas_call | solution.py:118
  157.1 6.5 %collective-permute-done.4 = bf16[96,1536]{1,0:T(8,128)(2,1)S(1)} collective-permute-done((bf16[96,1536]{1,0:T(8,128)(2,1)S(1)}, bf16[96,1536]{1,0:T(8,128)(2,1)S(1)}, u32[]{:S(2)}, u32[]{:S(2)}) %collective-permute-start.4) | collective-permute-done | bytes 294944 | tf_op jit(solution)/shard_map/ppermute | solution.py:883
  164.6 3.7 all-to-all-start.1
  171.7 21.6 %all-to-all-done.1 = bf16[4,512,256]{2,1,0:T(8,128)(2,1)S(1)} async-done(((bf16[4,512,256]{2,1,0:T(8,128)(2,1)}), bf16[4,512,256]{2,1,0:T(8,128)(2,1)S(1)}, u32[]{:S(2)}, u32[]{:S(2)}) %all-to-all-start.1) | async-done | bytes 1048608 | tf_op jit(solution)/shard_map/all_to_all | solution.py:1079
  194.3 6.7 %out_forward.1 = (f32[512,1024]{1,0:T(8,128)}, f32[512,1]{1,0:T(8,128)}, bf16[512,1024]{1,0:T(8,128)(2,1)}, bf16[1024,512]{1,0:T(8,128)(2,1)}) custom-call(s32[2]{0:T(128)} %pad_add_fusion.z_ref, bf16[2048,256]{1,0:T(8,128)(2,1)} %bitcast.172, bf16[512,1024]{1,0:T(8,128)(2,1)} %bitcast.170, f32[1,1024]{1,0:T(1,128)} %bitcast.222, bf16[256,1024]{1,0:T(8,128)(2,1)} %own.3, ...), custom_call_target="tpu_custom_call" | custom-call | flops 1073741824 | bytes 7340032 | tf_op jit(solution)/shard_map/out_forward/pallas_call | solution.py:771
  200.9 32.1 %ffn_chunk.3 = (f32[512,1024]{1,0:T(8,128)}, f32[512,1024]{1,0:T(8,128)}, bf16[8,4,96,1536]{3,2,1,0:T(8,128)(2,1)}) custom-call(s32[2]{0:T(128)} %pad_add_fusion.z_ref, bf16[512,1024]{1,0:T(8,128)(2,1)} %get-tuple-element.120.h_ref, bf16[1024,512]{1,0:T(8,128)(2,1)} %get-tuple-element.121.ht_ref, bf16[512,1024]{1,0:T(8,128)(2,1)} %bitcast_select_fusion.gy_ref.grad_y, ...), custom_call_target="tpu_custom_call" | custom-call | flops 14495514624 | bytes 29360128 | tf_op jit(solution)/shard_map/ffn_chunk/pallas_call | solution.py:336
  233.5 31.7 %ffn_chunk.4 = (f32[512,1024]{1,0:T(8,128)}, f32[512,1024]{1,0:T(8,128)}, bf16[8,4,96,1536]{3,2,1,0:T(8,128)(2,1)}) custom-call(s32[2]{0:T(128)} %pad_add_fusion.z_ref, bf16[512,1024]{1,0:T(8,128)(2,1)} %get-tuple-element.120.h_ref, bf16[1024,512]{1,0:T(8,128)(2,1)} %get-tuple-element.121.ht_ref, bf16[512,1024]{1,0:T(8,128)(2,1)} %bitcast_select_fusion.gy_ref.grad_y, ...), custom_call_target="tpu_custom_call" | custom-call | flops 14495514624 | bytes 29360128 | tf_op jit(solution)/shard_map/ffn_chunk/pallas_call | solution.py:336
  265.2 32.1 %ffn_chunk.5 = (bf16[512,1024]{1,0:T(8,128)(2,1)}, f32[512,1024]{1,0:T(8,128)}, bf16[4,4,96,1536]{3,2,1,0:T(8,128)(2,1)}, bf16[4,4,96,1536]{3,2,1,0:T(8,128)(2,1)}) custom-call(s32[2]{0:T(128)} %pad_add_fusion.z_ref, bf16[512,1024]{1,0:T(8,128)(2,1)} %get-tuple-element.120.h_ref, bf16[1024,512]{1,0:T(8,128)(2,1)} %get-tuple-element.121.ht_ref, ...), custom_call_target="tpu_custom_call" | custom-call | flops 14495514624 | bytes 29360128 | tf_op jit(solution)/shard_map/ffn_chunk/pallas_call | solution.py:336
  297.3 7.3 %out_backward.1 = (f32[512,1024]{1,0:T(8,128)}, f32[1,1024]{1,0:T(1,128)}, bf16[512,1024]{1,0:T(8,128)(2,1)}, bf16[2048,256]{1,0:T(8,128)(2,1)}) custom-call(s32[2]{0:T(128)} %pad_add_fusion.z_ref, f32[512,1024]{1,0:T(8,128)} %get-tuple-element.128.grad, bf16[512,1024]{1,0:T(8,128)(2,1)} %bitcast_select_fusion.gy_ref.grad_y, ...), custom_call_target="tpu_custom_call" | custom-call | flops 1073741824 | bytes 10485760 | tf_op jit(solution)/shard_map/out_backward/pallas_call | solution.py:816
  304.6 3.7 all-to-all-start.2
  308.3 5.5 out_terms.1
  313.8 2.9 fusion.4
  316.7 2.9 fusion.3
  319.6 15.3 %all-to-all-done.2 = bf16[4,512,256]{2,1,0:T(8,128)(2,1)S(1)} async-done(((bf16[4,512,256]{2,1,0:T(8,128)(2,1)}), bf16[4,512,256]{2,1,0:T(8,128)(2,1)S(1)}, u32[]{:S(2)}, u32[]{:S(2)}) %all-to-all-start.2) | async-done | bytes 1048608 | tf_op jit(solution)/shard_map/all_to_all | solution.py:1079
  334.9 2.4 slice_bitcast_fusion
  337.4 1.5 collective-permute-start.13
  339.4 20.2 %attend_backward.2 = bf16[2048,256]{1,0:T(8,128)(2,1)} custom-call(bf16[2048,512]{1,0:T(8,128)(2,1)} %bitcast.192, bf16[2048,512]{1,0:T(8,128)(2,1)} %bitcast.193, bf16[2048,512]{1,0:T(8,128)(2,1)} %bitcast.194, bf16[2048,256]{1,0:T(8,128)(2,1)} %bitcast.202, bf16[2048,256]{1,0:T(8,128)(2,1)} %get-tuple-element.108.o_ref, ...), custom_call_target="tpu_custom_call" | custom-call | flops 10737418240 | bytes 3145728 | tf_op jit(solution)/shard_map/attend_backward/pallas_call | solution.py:201
  359.6 4.9 all-to-all-start.3
  364.5 1.5 collective-permute-start.16
  366.0 1.4 collective-permute-start.17
  367.4 2.0 add_convert_fusion.4
  369.4 20.0 %attend_backward.3 = bf16[2048,256]{1,0:T(8,128)(2,1)} custom-call(bf16[2048,512]{1,0:T(8,128)(2,1)} %bitcast.195, bf16[2048,512]{1,0:T(8,128)(2,1)} %bitcast.196, bf16[2048,512]{1,0:T(8,128)(2,1)} %bitcast.197, bf16[2048,256]{1,0:T(8,128)(2,1)} %bitcast.203, bf16[2048,256]{1,0:T(8,128)(2,1)} %get-tuple-element.108.o_ref, ...), custom_call_target="tpu_custom_call" | custom-call | flops 10737418240 | bytes 3145728 | tf_op jit(solution)/shard_map/attend_backward/pallas_call | solution.py:201
  389.4 5.1 all-to-all-start.4
  395.2 8.1 %reduce-scatter.6.cloned.1.call-done = bf16[4,96,1536]{2,1,0:T(8,128)(2,1)} async-done(((bf16[32,96,1536]{2,1,0:T(8,128)(2,1)}), bf16[4,96,1536]{2,1,0:T(8,128)(2,1)}) %reduce-scatter.6.cloned.1.call-update) | async-done | bytes 1179664 | tf_op jit(solution)/shard_map/reduce_scatter | solution.py:932
  403.3 1.5 collective-permute-done.16
  405.1 1.4 constant_dynamic-slice_fusion.9
  407.7 3.3 fusion.9
  411.0 7.1 %all-to-all-done.4 = bf16[4,512,256]{2,1,0:T(8,128)(2,1)S(1)} async-done(((bf16[4,512,256]{2,1,0:T(8,128)(2,1)}), bf16[4,512,256]{2,1,0:T(8,128)(2,1)S(1)}, u32[]{:S(2)}, u32[]{:S(2)}) %all-to-all-start.4) | async-done | bytes 1048608 | tf_op jit(solution)/shard_map/all_to_all | solution.py:1079
  419.0 3.5 all-to-all-start.5
  428.5 17.0 %qkv_backward.1 = (f32[512,1024]{1,0:T(8,128)}, bf16[4,4,32,2176]{3,2,1,0:T(8,128)(2,1)}, bf16[4,4,32,2176]{3,2,1,0:T(8,128)(2,1)}) custom-call(s32[2]{0:T(128)} %pad_add_fusion.z_ref, bf16[1024,512]{1,0:T(8,128)(2,1)} %copy.52.ht_ref, f32[512,128]{1,0:T(8,128)} %copy.51.cos_ref, f32[512,128]{1,0:T(8,128)} %pad_maximum_fusion.8.sin_ref, ...), custom_call_target="tpu_custom_call" | custom-call | flops 4294967296 | bytes 16777216 | tf_op jit(solution)/shard_map/qkv_backward/pallas_call | solution.py:681
  445.6 5.0 all-to-all-done.5
  450.6 2.8 fusion.6
  455.0 3.5 all-to-all-start.6
  458.6 1.4 fusion.12
  460.0 1.4 fusion.11
  461.3 1.4 collective-permute-start.21
  464.0 15.6 %collective-permute-done.21 = bf16[2,2,32,2176]{3,2,1,0:T(8,128)(2,1)S(1)} collective-permute-done((bf16[2,2,32,2176]{3,2,1,0:T(8,128)(2,1)S(1)}, bf16[2,2,32,2176]{3,2,1,0:T(8,128)(2,1)S(1)}, u32[]{:S(2)}, u32[]{:S(2)}) %collective-permute-start.21) | collective-permute-done | bytes 557088 | tf_op jit(solution)/shard_map/ppermute | solution.py:940
  479.6 2.0 collective-permute-done.23
  481.6 2.2 fusion.15
  483.9 1.9 collective-permute-start.22
  488.0 4.6 collective-permute-done.24
  493.1 1.7 fusion.18
  496.9 4.7 all-to-all-start.7
  501.8 1.7 collective-permute-start.31
  505.3 4.3 unpack_ffn.2
  509.7 12.3 %all-to-all-done.7 = bf16[4,32,3200]{2,1,0:T(8,128)(2,1)S(1)} async-done(((bf16[4,32,3200]{2,1,0:T(8,128)(2,1)}), bf16[4,32,3200]{2,1,0:T(8,128)(2,1)S(1)}, u32[]{:S(2)}, u32[]{:S(2)}) %all-to-all-start.7) | async-done | bytes 819232 | tf_op jit(solution)/shard_map/all_to_all | solution.py:1079
  524.0 1.7 collective-permute-start.25
  527.6 3.5 collective-permute-done.27
  531.1 1.8 collective-permute-done.26
  535.5 3.2 unpack_qkv.1
  538.8 4.3 unpack_ffn.3
  544.1 4.4 unpack_near.1
  (178 shorter events, 49.7 us)
Async XLA Ops:
  7.2 61.4 %all-gather.8.cloned.1.call-start = ((), (), s32[]{:S(2)}) async-start(), calls=%async_computation.11 | async-start | bytes 3538944 | tf_op jit(solution)/shard_map/all_gather | solution.py:928
  9.7 10.5 %collective-permute-start.2 = (bf16[32,2176]{1,0:T(8,128)(2,1)S(1)}, bf16[32,2176]{1,0:T(8,128)(2,1)S(1)}, u32[]{:S(2)}, u32[]{:S(2)}) collective-permute-start(bf16[32,2176]{1,0:T(8,128)(2,1)S(1)} %pad_maximum_fusion.9), channel_id=1, source_target_pairs={{0,3},{1,0},{2,1},{3,2},{4,7},{5,4},{6,5},{7,6},{8,11},{9,8},{10,9... | collective-permute-start | bytes 417800 | tf_op jit(solution)/shard_map/ppermute | solution.py:883
  14.8 11.8 %collective-permute-start.1 = (bf16[32,2176]{1,0:T(8,128)(2,1)S(1)}, bf16[32,2176]{1,0:T(8,128)(2,1)S(1)}, u32[]{:S(2)}, u32[]{:S(2)}) collective-permute-start(bf16[32,2176]{1,0:T(8,128)(2,1)S(1)} %pad_maximum_fusion.9), channel_id=1, source_target_pairs={{0,2},{1,3},{2,0},{3,1},{4,6},{5,7},{6,4},{7,5},{8,10},{9,11},{10,... | collective-permute-start | bytes 417800 | tf_op jit(solution)/shard_map/ppermute | solution.py:883
  14.8 11.8 %collective-permute-start = (bf16[32,2176]{1,0:T(8,128)(2,1)S(1)}, bf16[32,2176]{1,0:T(8,128)(2,1)S(1)}, u32[]{:S(2)}, u32[]{:S(2)}) collective-permute-start(bf16[32,2176]{1,0:T(8,128)(2,1)S(1)} %pad_maximum_fusion.9), channel_id=1, source_target_pairs={{0,1},{1,2},{2,3},{3,0},{4,5},{5,6},{6,7},{7,4},{8,9},{9,10},{10,1... | collective-permute-start | bytes 417800 | tf_op jit(solution)/shard_map/ppermute | solution.py:883
  20.1 7.4 %copy-start.17 = (bf16[16]{0:T(256)(128)(2,1)S(1)}, bf16[16]{0:T(256)(128)(2,1)}, u32[]{:S(2)}) copy-start(bf16[16]{0:T(256)(128)(2,1)} %param.27) | copy-start | bytes 100
  20.1 7.4 %copy-start.18 = (bf16[16]{0:T(256)(128)(2,1)S(1)}, bf16[16]{0:T(256)(128)(2,1)}, u32[]{:S(2)}) copy-start(bf16[16]{0:T(256)(128)(2,1)} %param.26) | copy-start | bytes 100
  20.1 7.5 %copy-start.19 = (bf16[256]{0:T(256)(128)(2,1)S(1)}, bf16[256]{0:T(256)(128)(2,1)}, u32[]{:S(2)}) copy-start(bf16[256]{0:T(256)(128)(2,1)} %param.25) | copy-start | bytes 1540
  20.1 7.5 %copy-start.20 = (bf16[256]{0:T(256)(128)(2,1)S(1)}, bf16[256]{0:T(256)(128)(2,1)}, u32[]{:S(2)}) copy-start(bf16[256]{0:T(256)(128)(2,1)} %param.24) | copy-start | bytes 1540
  20.1 7.5 %copy-start = (bf16[1,512,1024]{2,1,0:T(8,128)(2,1)S(1)}, bf16[1,512,1024]{2,1,0:T(8,128)(2,1)}, u32[]{:S(2)}) copy-start(bf16[1,512,1024]{2,1,0:T(8,128)(2,1)} %param.14) | copy-start | bytes 3145732
  27.5 165.9 %all-gather.10.cloned.1.call-start = ((), (), s32[]{:S(2)}) async-start(), calls=%async_computation.12 | async-start | bytes 18579456 | tf_op jit(solution)/shard_map/all_gather | solution.py:928
  28.0 18.8 %collective-permute-start.9 = (bf16[224,1536]{1,0:T(8,128)(2,1)}, bf16[224,1536]{1,0:T(8,128)(2,1)S(1)}, u32[]{:S(2)}, u32[]{:S(2)}) collective-permute-start(bf16[224,1536]{1,0:T(8,128)(2,1)} %get-tuple-element.113), channel_id=1, source_target_pairs={{1,0},{2,1},{3,2},{5,4},{6,5},{7,6},{9,8},{10,9},{11,10},{13,12},{... | collective-permute-start | bytes 2064392 | tf_op jit(solution)/shard_map/ppermute | solution.py:894
  29.3 18.8 %collective-permute-start.6 = (bf16[224,1536]{1,0:T(8,128)(2,1)}, bf16[224,1536]{1,0:T(8,128)(2,1)S(1)}, u32[]{:S(2)}, u32[]{:S(2)}) collective-permute-start(bf16[224,1536]{1,0:T(8,128)(2,1)} %get-tuple-element.113), channel_id=1, source_target_pairs={{0,1},{1,2},{2,3},{4,5},{5,6},{6,7},{8,9},{9,10},{10,11},{12,13},{... | collective-permute-start | bytes 2064392 | tf_op jit(solution)/shard_map/ppermute | solution.py:893
  46.8 21.8 %copy-start.13 = (bf16[224,1536]{1,0:T(8,128)(2,1)}, bf16[224,1536]{1,0:T(8,128)(2,1)S(1)}, u32[]{:S(2)}) copy-start(bf16[224,1536]{1,0:T(8,128)(2,1)S(1)} %collective-permute-done.9.refs_3_) | copy-start | bytes 2064388
  46.8 17.7 %collective-permute-start.10 = (bf16[224,1536]{1,0:T(8,128)(2,1)S(1)}, bf16[224,1536]{1,0:T(8,128)(2,1)S(1)}, u32[]{:S(2)}, u32[]{:S(2)}) collective-permute-start(bf16[224,1536]{1,0:T(8,128)(2,1)S(1)} %collective-permute-done.9.refs_3_), channel_id=1, source_target_pairs={{1,0},{2,1},{5,4},{6,5},{9,8},{10,9},{13,12},{14,13},{17,16},{18,1... | collective-permute-start | bytes 2064392 | tf_op jit(solution)/shard_map/ppermute | solution.py:894
  48.1 20.5 %copy-start.14 = (bf16[224,1536]{1,0:T(8,128)(2,1)}, bf16[224,1536]{1,0:T(8,128)(2,1)S(1)}, u32[]{:S(2)}) copy-start(bf16[224,1536]{1,0:T(8,128)(2,1)S(1)} %collective-permute-done.6.refs_0_) | copy-start | bytes 2064388
  48.1 17.6 %collective-permute-start.7 = (bf16[224,1536]{1,0:T(8,128)(2,1)S(1)}, bf16[224,1536]{1,0:T(8,128)(2,1)}, u32[]{:S(2)}, u32[]{:S(2)}) collective-permute-start(bf16[224,1536]{1,0:T(8,128)(2,1)S(1)} %collective-permute-done.6.refs_0_), channel_id=1, source_target_pairs={{1,2},{2,3},{5,6},{6,7},{9,10},{10,11},{13,14},{14,15},{17,18},{18... | collective-permute-start | bytes 2064392 | tf_op jit(solution)/shard_map/ppermute | solution.py:893
  64.5 14.4 %copy-start.15 = (bf16[224,1536]{1,0:T(8,128)(2,1)}, bf16[224,1536]{1,0:T(8,128)(2,1)S(1)}, u32[]{:S(2)}) copy-start(bf16[224,1536]{1,0:T(8,128)(2,1)S(1)} %collective-permute-done.10.refs_4_) | copy-start | bytes 2064388
  64.5 16.8 %collective-permute-start.11 = (bf16[224,1536]{1,0:T(8,128)(2,1)S(1)}, bf16[224,1536]{1,0:T(8,128)(2,1)}, u32[]{:S(2)}, u32[]{:S(2)}) collective-permute-start(bf16[224,1536]{1,0:T(8,128)(2,1)S(1)} %collective-permute-done.10.refs_4_), channel_id=1, source_target_pairs={{1,0},{5,4},{9,8},{13,12},{17,16},{21,20},{25,24},{29,28}} | collective-permute-start | bytes 2064392 | tf_op jit(solution)/shard_map/ppermute | solution.py:894
  65.8 15.5 %collective-permute-start.8 = (bf16[224,1536]{1,0:T(8,128)(2,1)}, bf16[224,1536]{1,0:T(8,128)(2,1)}, u32[]{:S(2)}, u32[]{:S(2)}) collective-permute-start(bf16[224,1536]{1,0:T(8,128)(2,1)} %collective-permute-done.7.refs_1_), channel_id=1, source_target_pairs={{2,3},{6,7},{10,11},{14,15},{18,19},{22,23},{26,27},{30,31}} | collective-permute-start | bytes 2064392 | tf_op jit(solution)/shard_map/ppermute | solution.py:893
  81.3 6.0 %copy-start.7 = (bf16[2048,512]{1,0:T(8,128)(2,1)S(1)}, bf16[2048,512]{1,0:T(8,128)(2,1)}, u32[]{:S(2)}) copy-start(bf16[2048,512]{1,0:T(8,128)(2,1)} %get-tuple-element.104) | copy-start | bytes 6291460
  87.2 178.0 %all-gather.12.cloned.1.call-start = ((), (), s32[]{:S(2)}) async-start(), calls=%async_computation.13 | async-start | bytes 7962624 | tf_op jit(solution)/shard_map/all_gather | solution.py:928
  87.3 51.3 %copy-start.21 = (bf16[96,1536]{1,0:T(8,128)(2,1)S(1)}, bf16[96,1536]{1,0:T(8,128)(2,1)}, u32[]{:S(2)}) copy-start(bf16[96,1536]{1,0:T(8,128)(2,1)} %get-tuple-element.107) | copy-start | bytes 884740
  138.6 18.5 %collective-permute-start.5 = (bf16[96,1536]{1,0:T(8,128)(2,1)S(1)}, bf16[96,1536]{1,0:T(8,128)(2,1)S(1)}, u32[]{:S(2)}, u32[]{:S(2)}) collective-permute-start(bf16[96,1536]{1,0:T(8,128)(2,1)S(1)} %copy-done.21), channel_id=1, source_target_pairs={{0,3},{1,0},{2,1},{3,2},{4,7},{5,4},{6,5},{7,6},{8,11},{9,8},{10,9... | collective-permute-start | bytes 884744 | tf_op jit(solution)/shard_map/ppermute | solution.py:883
  139.9 23.7 %collective-permute-start.4 = (bf16[96,1536]{1,0:T(8,128)(2,1)S(1)}, bf16[96,1536]{1,0:T(8,128)(2,1)S(1)}, u32[]{:S(2)}, u32[]{:S(2)}) collective-permute-start(bf16[96,1536]{1,0:T(8,128)(2,1)S(1)} %copy-done.21), channel_id=1, source_target_pairs={{0,2},{1,3},{2,0},{3,1},{4,6},{5,7},{6,4},{7,5},{8,10},{9,11},{10,... | collective-permute-start | bytes 884744 | tf_op jit(solution)/shard_map/ppermute | solution.py:883
  140.1 23.5 %collective-permute-start.3 = (bf16[96,1536]{1,0:T(8,128)(2,1)S(1)}, bf16[96,1536]{1,0:T(8,128)(2,1)S(1)}, u32[]{:S(2)}, u32[]{:S(2)}) collective-permute-start(bf16[96,1536]{1,0:T(8,128)(2,1)S(1)} %copy-done.21), channel_id=1, source_target_pairs={{0,1},{1,2},{2,3},{3,0},{4,5},{5,6},{6,7},{7,4},{8,9},{9,10},{10,1... | collective-permute-start | bytes 884744 | tf_op jit(solution)/shard_map/ppermute | solution.py:883
  164.6 5.3 copy-start.11
  164.6 28.7 %all-to-all-start.1 = ((bf16[4,512,256]{2,1,0:T(8,128)(2,1)}), bf16[4,512,256]{2,1,0:T(8,128)(2,1)S(1)}, u32[]{:S(2)}, u32[]{:S(2)}) async-start(bf16[4,512,256]{2,1,0:T(8,128)(2,1)} %bitcast.12), calls=%async_computation.1 | async-start | bytes 2097152 | tf_op jit(solution)/shard_map/all_to_all | solution.py:1079
  168.3 166.7 %reduce-scatter.4.cloned.1.call-start = ((), (), s32[]{:S(2)}) async-start(), calls=%async_computation.14 | async-start | bytes 10616832 | tf_op jit(solution)/shard_map/reduce_scatter | solution.py:932
  233.1 170.3 %reduce-scatter.6.cloned.1.call-start = ((), (), s32[]{:S(2)}) async-start(), calls=%async_computation.15 | async-start | bytes 10616832 | tf_op jit(solution)/shard_map/reduce_scatter | solution.py:932
  297.3 16.5 %collective-permute-start.12 = (bf16[4,4,96,1536]{3,2,1,0:T(8,128)(2,1)}, bf16[4,4,96,1536]{3,2,1,0:T(8,128)(2,1)}, u32[]{:S(2)}, u32[]{:S(2)}) collective-permute-start(bf16[4,4,96,1536]{3,2,1,0:T(8,128)(2,1)} %get-tuple-element.137), channel_id=1, source_target_pairs={{0,4},{4,0},{8,12},{12,8},{16,20},{20,16},{24,28},{28,24},{1,5},{5... | collective-permute-start | bytes 14155784 | tf_op jit(solution)/shard_map/ppermute | solution.py:940
  304.6 30.4 %all-to-all-start.2 = ((bf16[4,512,256]{2,1,0:T(8,128)(2,1)}), bf16[4,512,256]{2,1,0:T(8,128)(2,1)S(1)}, u32[]{:S(2)}, u32[]{:S(2)}) async-start(bf16[4,512,256]{2,1,0:T(8,128)(2,1)} %bitcast.204), calls=%async_computation.2 | async-start | bytes 2097152 | tf_op jit(solution)/shard_map/all_to_all | solution.py:1079
  337.4 30.1 %collective-permute-start.13 = (bf16[96,1536]{1,0:T(8,128)(2,1)}, bf16[96,1536]{1,0:T(8,128)(2,1)}, u32[]{:S(2)}, u32[]{:S(2)}) collective-permute-start(bf16[96,1536]{1,0:T(8,128)(2,1)} %get-tuple-element.142), channel_id=1, source_target_pairs={{0,3},{1,0},{2,1},{3,2},{4,7},{5,4},{6,5},{7,6},{8,11},{9,8},{10,9... | collective-permute-start | bytes 884744 | tf_op jit(solution)/shard_map/ppermute | solution.py:883
  338.8 28.6 %collective-permute-start.14 = (bf16[96,1536]{1,0:T(8,128)(2,1)S(1)}, bf16[96,1536]{1,0:T(8,128)(2,1)}, u32[]{:S(2)}, u32[]{:S(2)}) collective-permute-start(bf16[96,1536]{1,0:T(8,128)(2,1)S(1)} %get-tuple-element.143), channel_id=1, source_target_pairs={{0,2},{1,3},{2,0},{3,1},{4,6},{5,7},{6,4},{7,5},{8,10},{9,11},{10,... | collective-permute-start | bytes 884744 | tf_op jit(solution)/shard_map/ppermute | solution.py:883
  338.8 28.6 %collective-permute-start.15 = (bf16[96,1536]{1,0:T(8,128)(2,1)S(1)}, bf16[96,1536]{1,0:T(8,128)(2,1)}, u32[]{:S(2)}, u32[]{:S(2)}) collective-permute-start(bf16[96,1536]{1,0:T(8,128)(2,1)S(1)} %get-tuple-element.144), channel_id=1, source_target_pairs={{0,1},{1,2},{2,3},{3,0},{4,5},{5,6},{6,7},{7,4},{8,9},{9,10},{10,1... | collective-permute-start | bytes 884744 | tf_op jit(solution)/shard_map/ppermute | solution.py:883
  359.6 29.8 %all-to-all-start.3 = ((bf16[4,512,256]{2,1,0:T(8,128)(2,1)}), bf16[4,512,256]{2,1,0:T(8,128)(2,1)S(1)}, u32[]{:S(2)}, u32[]{:S(2)}) async-start(bf16[4,512,256]{2,1,0:T(8,128)(2,1)} %bitcast.205), calls=%async_computation.4 | async-start | bytes 2097152 | tf_op jit(solution)/shard_map/all_to_all | solution.py:1079
  364.5 40.3 %collective-permute-start.16 = (bf16[2,2,96,1536]{3,2,1,0:T(8,128)(2,1)}, bf16[2,2,96,1536]{3,2,1,0:T(8,128)(2,1)S(1)}, u32[]{:S(2)}, u32[]{:S(2)}) collective-permute-start(bf16[2,2,96,1536]{3,2,1,0:T(8,128)(2,1)} %fusion.3), channel_id=1, source_target_pairs={{0,8},{4,12},{8,0},{12,4},{16,24},{20,28},{24,16},{28,20},{1,9},{5... | collective-permute-start | bytes 3538952 | tf_op jit(solution)/shard_map/ppermute | solution.py:940
  366.0 39.1 %collective-permute-start.17 = (bf16[2,2,96,1536]{3,2,1,0:T(8,128)(2,1)}, bf16[2,2,96,1536]{3,2,1,0:T(8,128)(2,1)}, u32[]{:S(2)}, u32[]{:S(2)}) collective-permute-start(bf16[2,2,96,1536]{3,2,1,0:T(8,128)(2,1)} %fusion.4), channel_id=1, source_target_pairs={{0,16},{4,20},{8,24},{12,28},{16,0},{20,4},{24,8},{28,12},{1,17},{... | collective-permute-start | bytes 3538952 | tf_op jit(solution)/shard_map/ppermute | solution.py:940
  389.4 5.7 %copy-start.4 = (bf16[4,512,256]{2,1,0:T(8,128)(2,1)}, bf16[4,512,256]{2,1,0:T(8,128)(2,1)S(1)}, u32[]{:S(2)}) copy-start(bf16[4,512,256]{2,1,0:T(8,128)(2,1)S(1)} %all-to-all-done.3) | copy-start | bytes 3145732
  389.4 28.6 %all-to-all-start.4 = ((bf16[4,512,256]{2,1,0:T(8,128)(2,1)}), bf16[4,512,256]{2,1,0:T(8,128)(2,1)S(1)}, u32[]{:S(2)}, u32[]{:S(2)}) async-start(bf16[4,512,256]{2,1,0:T(8,128)(2,1)} %bitcast.201), calls=%async_computation.5 | async-start | bytes 2097152 | tf_op jit(solution)/shard_map/all_to_all | solution.py:1079
  394.6 100.2 %reduce-scatter.8.cloned.1.call-start = ((), (), s32[]{:S(2)}) async-start(), calls=%async_computation.16 | async-start | bytes 2359296 | tf_op jit(solution)/shard_map/reduce_scatter | solution.py:932
  404.8 2.9 copy-start.9
  418.0 8.8 %copy-start.1 = (bf16[1,512,1024]{2,1,0:T(8,128)(2,1)S(1)}, bf16[1,512,1024]{2,1,0:T(8,128)(2,1)}, u32[]{:S(2)}) copy-start(bf16[1,512,1024]{2,1,0:T(8,128)(2,1)} %param.14) | copy-start | bytes 3145732
  419.0 31.5 %all-to-all-start.5 = ((bf16[4,96,1536]{2,1,0:T(8,128)(2,1)}), bf16[4,96,1536]{2,1,0:T(8,128)(2,1)S(1)}, u32[]{:S(2)}, u32[]{:S(2)}) async-start(bf16[4,96,1536]{2,1,0:T(8,128)(2,1)} %pad_maximum_fusion), calls=%async_computation.7 | async-start | bytes 2359296 | tf_op jit(solution)/shard_map/all_to_all | solution.py:1079
  422.6 82.8 %all-gather.14.cloned.1.call-start = ((), (), s32[]{:S(2)}) async-start(), calls=%async_computation.17 | async-start | bytes 2654208 | tf_op jit(solution)/shard_map/all_gather | solution.py:928
  424.3 21.2 %collective-permute-start.18 = (bf16[2,96,1536]{2,1,0:T(8,128)(2,1)}, bf16[2,96,1536]{2,1,0:T(8,128)(2,1)}, u32[]{:S(2)}, u32[]{:S(2)}) collective-permute-start(bf16[2,96,1536]{2,1,0:T(8,128)(2,1)} %get-tuple-element.189), channel_id=1, source_target_pairs={{0,16},{4,20},{8,24},{12,28},{16,0},{20,4},{24,8},{28,12},{1,17},{... | collective-permute-start | bytes 1769480 | tf_op jit(solution)/shard_map/ppermute | solution.py:940
  425.6 19.9 %collective-permute-start.19 = (bf16[2,96,1536]{2,1,0:T(8,128)(2,1)}, bf16[2,96,1536]{2,1,0:T(8,128)(2,1)}, u32[]{:S(2)}, u32[]{:S(2)}) collective-permute-start(bf16[2,96,1536]{2,1,0:T(8,128)(2,1)} %get-tuple-element.190), channel_id=1, source_target_pairs={{0,8},{4,12},{8,0},{12,4},{16,24},{20,28},{24,16},{28,20},{1,9},{5... | collective-permute-start | bytes 1769480 | tf_op jit(solution)/shard_map/ppermute | solution.py:940
  428.5 22.1 %copy-start.10 = (bf16[2,2,96,1536]{3,2,1,0:T(8,128)(2,1)S(1)}, bf16[2,2,96,1536]{3,2,1,0:T(8,128)(2,1)}, u32[]{:S(2)}) copy-start(bf16[2,2,96,1536]{3,2,1,0:T(8,128)(2,1)} %copy-done.9) | copy-start | bytes 3538948
  450.6 8.0 %collective-permute-start.20 = (bf16[4,4,32,2176]{3,2,1,0:T(8,128)(2,1)}, bf16[4,4,32,2176]{3,2,1,0:T(8,128)(2,1)}, u32[]{:S(2)}, u32[]{:S(2)}) collective-permute-start(bf16[4,4,32,2176]{3,2,1,0:T(8,128)(2,1)} %get-tuple-element.161), channel_id=1, source_target_pairs={{0,4},{4,0},{8,12},{12,8},{16,20},{20,16},{24,28},{28,24},{1,5},{5... | collective-permute-start | bytes 6684680 | tf_op jit(solution)/shard_map/ppermute | solution.py:940
  455.0 33.0 %all-to-all-start.6 = ((bf16[4,96,1536]{2,1,0:T(8,128)(2,1)}), bf16[4,96,1536]{2,1,0:T(8,128)(2,1)S(1)}, u32[]{:S(2)}, u32[]{:S(2)}) async-start(bf16[4,96,1536]{2,1,0:T(8,128)(2,1)} %pad_maximum_fusion.1), calls=%async_computation.8 | async-start | bytes 2359296 | tf_op jit(solution)/shard_map/all_to_all | solution.py:1079
  458.6 80.2 %all-gather.16.cloned.1.call-start = ((), (), s32[]{:S(2)}) async-start(), calls=%async_computation.18 | async-start | bytes 2654208 | tf_op jit(solution)/shard_map/all_gather | solution.py:928
  461.3 18.3 %collective-permute-start.21 = (bf16[2,2,32,2176]{3,2,1,0:T(8,128)(2,1)S(1)}, bf16[2,2,32,2176]{3,2,1,0:T(8,128)(2,1)S(1)}, u32[]{:S(2)}, u32[]{:S(2)}) collective-permute-start(bf16[2,2,32,2176]{3,2,1,0:T(8,128)(2,1)S(1)} %fusion.11), channel_id=1, source_target_pairs={{0,8},{4,12},{8,0},{12,4},{16,24},{20,28},{24,16},{28,20},{1,9},{5... | collective-permute-start | bytes 1671176 | tf_op jit(solution)/shard_map/ppermute | solution.py:940
  462.8 18.8 %collective-permute-start.23 = (bf16[2,2,32,2176]{3,2,1,0:T(8,128)(2,1)S(1)}, bf16[2,2,32,2176]{3,2,1,0:T(8,128)(2,1)S(1)}, u32[]{:S(2)}, u32[]{:S(2)}) collective-permute-start(bf16[2,2,32,2176]{3,2,1,0:T(8,128)(2,1)S(1)} %fusion.12), channel_id=1, source_target_pairs={{0,16},{4,20},{8,24},{12,28},{16,0},{20,4},{24,8},{28,12},{1,17},{... | collective-permute-start | bytes 1671176 | tf_op jit(solution)/shard_map/ppermute | solution.py:940
  483.8 8.8 %collective-permute-start.24 = (bf16[2,32,2176]{2,1,0:T(8,128)(2,1)}, bf16[2,32,2176]{2,1,0:T(8,128)(2,1)}, u32[]{:S(2)}, u32[]{:S(2)}) collective-permute-start(bf16[2,32,2176]{2,1,0:T(8,128)(2,1)} %get-tuple-element.193), channel_id=1, source_target_pairs={{0,8},{4,12},{8,0},{12,4},{16,24},{20,28},{24,16},{28,20},{1,9},{5... | collective-permute-start | bytes 835592 | tf_op jit(solution)/shard_map/ppermute | solution.py:940
  483.9 9.2 %collective-permute-start.22 = (bf16[2,32,2176]{2,1,0:T(8,128)(2,1)}, bf16[2,32,2176]{2,1,0:T(8,128)(2,1)}, u32[]{:S(2)}, u32[]{:S(2)}) collective-permute-start(bf16[2,32,2176]{2,1,0:T(8,128)(2,1)} %get-tuple-element.194), channel_id=1, source_target_pairs={{0,16},{4,20},{8,24},{12,28},{16,0},{20,4},{24,8},{28,12},{1,17},{... | collective-permute-start | bytes 835592 | tf_op jit(solution)/shard_map/ppermute | solution.py:940
  496.9 25.1 %all-to-all-start.7 = ((bf16[4,32,3200]{2,1,0:T(8,128)(2,1)}), bf16[4,32,3200]{2,1,0:T(8,128)(2,1)S(1)}, u32[]{:S(2)}, u32[]{:S(2)}) async-start(bf16[4,32,3200]{2,1,0:T(8,128)(2,1)} %pad_maximum_fusion.5), calls=%async_computation.10 | async-start | bytes 1638400 | tf_op jit(solution)/shard_map/all_to_all | solution.py:1079
  501.8 22.2 %collective-permute-start.31 = (bf16[96,1536]{1,0:T(8,128)(2,1)S(1)}, bf16[96,1536]{1,0:T(8,128)(2,1)S(1)}, u32[]{:S(2)}, u32[]{:S(2)}) collective-permute-start(bf16[96,1536]{1,0:T(8,128)(2,1)S(1)} %reduce_sum.57), channel_id=1, source_target_pairs={{0,24},{4,28},{8,16},{12,20},{16,8},{20,12},{24,0},{28,4},{1,25},{... | collective-permute-start | bytes 884744 | tf_op jit(solution)/shard_map/ppermute | solution.py:940
  503.5 22.1 %collective-permute-start.30 = (bf16[96,1536]{1,0:T(8,128)(2,1)S(1)}, bf16[96,1536]{1,0:T(8,128)(2,1)S(1)}, u32[]{:S(2)}, u32[]{:S(2)}) collective-permute-start(bf16[96,1536]{1,0:T(8,128)(2,1)S(1)} %reduce_sum.57), channel_id=1, source_target_pairs={{0,16},{4,20},{8,24},{12,28},{16,0},{20,4},{24,8},{28,12},{1,17},{... | collective-permute-start | bytes 884744 | tf_op jit(solution)/shard_map/ppermute | solution.py:940
  504.2 21.5 %collective-permute-start.29 = (bf16[96,1536]{1,0:T(8,128)(2,1)S(1)}, bf16[96,1536]{1,0:T(8,128)(2,1)S(1)}, u32[]{:S(2)}, u32[]{:S(2)}) collective-permute-start(bf16[96,1536]{1,0:T(8,128)(2,1)S(1)} %reduce_sum.57), channel_id=1, source_target_pairs={{0,8},{4,12},{8,0},{12,4},{16,24},{20,28},{24,16},{28,20},{1,9},{5... | collective-permute-start | bytes 884744 | tf_op jit(solution)/shard_map/ppermute | solution.py:940
  522.1 9.0 %collective-permute-start.27 = (bf16[32,3200]{1,0:T(8,128)(2,1)S(1)}, bf16[32,3200]{1,0:T(8,128)(2,1)S(1)}, u32[]{:S(2)}, u32[]{:S(2)}) collective-permute-start(bf16[32,3200]{1,0:T(8,128)(2,1)S(1)} %reduce_sum.56), channel_id=1, source_target_pairs={{0,24},{4,28},{8,16},{12,20},{16,8},{20,12},{24,0},{28,4},{1,25},{... | collective-permute-start | bytes 614408 | tf_op jit(solution)/shard_map/ppermute | solution.py:940
  522.7 10.1 %collective-permute-start.26 = (bf16[32,3200]{1,0:T(8,128)(2,1)S(1)}, bf16[32,3200]{1,0:T(8,128)(2,1)S(1)}, u32[]{:S(2)}, u32[]{:S(2)}) collective-permute-start(bf16[32,3200]{1,0:T(8,128)(2,1)S(1)} %reduce_sum.56), channel_id=1, source_target_pairs={{0,16},{4,20},{8,24},{12,28},{16,0},{20,4},{24,8},{28,12},{1,17},{... | collective-permute-start | bytes 614408 | tf_op jit(solution)/shard_map/ppermute | solution.py:940
  524.0 8.9 %collective-permute-start.25 = (bf16[32,3200]{1,0:T(8,128)(2,1)S(1)}, bf16[32,3200]{1,0:T(8,128)(2,1)S(1)}, u32[]{:S(2)}, u32[]{:S(2)}) collective-permute-start(bf16[32,3200]{1,0:T(8,128)(2,1)S(1)} %reduce_sum.56), channel_id=1, source_target_pairs={{0,8},{4,12},{8,0},{12,4},{16,24},{20,28},{24,16},{28,20},{1,9},{5... | collective-permute-start | bytes 614408 | tf_op jit(solution)/shard_map/ppermute | solution.py:940
  527.5 11.3 %copy-start.3 = (bf16[4,96,1536]{2,1,0:T(8,128)(2,1)}, bf16[4,96,1536]{2,1,0:T(8,128)(2,1)S(1)}, u32[]{:S(2)}) copy-start(bf16[4,96,1536]{2,1,0:T(8,128)(2,1)S(1)} %pad_maximum_fusion.2.even) | copy-start | bytes 3538948
  527.5 15.6 %collective-permute-start.32 = (bf16[4,96,1536]{2,1,0:T(8,128)(2,1)S(1)}, bf16[4,96,1536]{2,1,0:T(8,128)(2,1)S(1)}, u32[]{:S(2)}, u32[]{:S(2)}) collective-permute-start(bf16[4,96,1536]{2,1,0:T(8,128)(2,1)S(1)} %pad_maximum_fusion.2.even), channel_id=1, source_target_pairs={{0,4},{4,0},{8,12},{12,8},{16,20},{20,16},{24,28},{28,24},{1,5},{5... | collective-permute-start | bytes 3538952 | tf_op jit(solution)/shard_map/ppermute | solution.py:940
  533.0 2.5 collective-permute-start.28
  (6 other events, 8.7 us)
Sparse Core Ops, SparseCore 0:
  27.6 32.6 all-gather.7
  87.3 91.6 all-gather.9
  181.5 48.8 all-gather.11
  233.7 76.4 reduce-scatter.3
  313.6 89.6 reduce-scatter.5
  406.4 46.8 reduce-scatter.7
  456.0 33.2 all-gather.13
  491.3 34.0 all-gather.15
